TPU v7x, 256 devices: a whole 4x4x8 slice. The times are simulated.
256 devices in a mesh: section: 16 (over y, z_lo), dp: 8 (over z_hi, x), tensor: 2 (over core).
Axes of the slice: x: 4, y: 4, z: 8 (z_hi: 2, z_lo: 4; z = z_hi * 4 + z_lo), core: 2. Of those that a mesh axis runs over, the one named last changes fastest.
Arguments:
- context: bfloat16 [16, 16, 256, 2048], P('section', 'dp'), may hold values from -6 to 6
- queries: bfloat16 [16, 16, 64, 2048], P('section', 'dp'), may hold values from -6 to 6
- lengths: int32 [16, 16], P('section', 'dp'), may hold values from 32 to 256
- norm_gain: float32 [16, 2048], P('section'), may hold values from 0.1 to 1.9
- qkv_weight: bfloat16 [16, 2048, 3, 2048], P('section', 'dp', None, 'tensor')
- out_weight: bfloat16 [16, 2048, 2048], P('section', 'tensor', 'dp'), may hold values from -0.5 to 0.5
Outputs:
- next_context: bfloat16 [16, 16, 256, 2048], P('section', 'dp')
- next_queries: bfloat16 [16, 16, 64, 2048], P('section', 'dp')
All inputs are finite; a program needn't handle non-finite values.
Results may differ from a plain program's by a relative error of at most 0.014.
The roundings to bfloat16 on the way count: a program that leaves them out, or rounds other values in their place, can miss the bound.
Values may be sent and summed in bfloat16 or wider, within the bound.
No kernel may reach another device: no remote copies, remote signals or barrier semaphores. Data moves between devices by JAX's collectives and lax.ppermute only.
A program may use at most 128 MiB of HBM per device.

v0:
```python
import functools
import math

import jax
import jax.numpy as jnp
from jax import lax
from jax.experimental import pallas as pl
from jax.experimental.pallas import tpu as pltpu
from jax.sharding import PartitionSpec as P

HEAD = 128
RING = 4
TAIL = 16
HBM = pl.BlockSpec(memory_space=pltpu.HBM)
SMEM = pl.BlockSpec(memory_space=pltpu.SMEM)
VMEM = pl.BlockSpec(memory_space=pltpu.VMEM)
BF16 = jnp.bfloat16
F32 = jnp.float32


def around_x(array, by):
    pairs = [
        (z * RING + x, z * RING + (x + by) % RING) for z in range(2) for x in range(RING)
    ]
    return lax.ppermute(array, "dp", pairs)


def around_x_of(array, by, sections):
    pairs = []
    for s in sections:
        for z in range(2):
            for x in range(RING):
                base = s * 2 * RING + z * RING
                pairs.append((base + x, base + (x + by) % RING))
    return lax.ppermute(array, ("section", "dp"), pairs)


def across_z(array):
    return lax.ppermute(array, "dp", [(d, (d + RING) % (2 * RING)) for d in range(2 * RING)])


def other_core(array):
    return lax.ppermute(array, "tensor", [(0, 1), (1, 0)])


def relay(array, sections, count):
    return lax.ppermute(array, "section", [(s, (s + 1) % count) for s in sections])


def round_ring(array, cut):
    left, right = around_x(array, 1), around_x(array, -1)
    return left, right, left[:cut], right[cut:]


def after(array, *others):
    return lax.optimization_barrier((array,) + others)[0]


def copy_all(copies):
    for copy in copies:
        copy.start()
    return copies


def wait_all(copies):
    for copy in copies:
        copy.wait()


def call(kernel, outs, in_specs, out_specs, scratch=(), flops=0, moved=0, limit=16):
    return pl.pallas_call(
        kernel,
        out_shape=outs,
        in_specs=in_specs,
        out_specs=out_specs,
        scratch_shapes=list(scratch),
        compiler_params=pltpu.CompilerParams(vmem_limit_bytes=limit * 1024 * 1024),
        cost_estimate=pl.CostEstimate(flops=flops, bytes_accessed=moved, transcendentals=0),
    )


def quarter_kernel(where, weight, *pieces):
    x = where[0]
    width = pieces[0].shape[2]
    for step, piece in enumerate(pieces):
        start = pl.multiple_of(((x + step) % RING) * width, width)
        piece[...] = weight[:, :, pl.ds(start, width)]


def quarters(where, weight):
    planes, rows, columns = weight.shape
    piece = jax.ShapeDtypeStruct((planes, rows, columns // RING), BF16)
    return call(
        quarter_kernel, (piece,) * RING, [SMEM, VMEM], (VMEM,) * RING, moved=4 * weight.size
    )(where, weight)


def norm_kernel(where, context, queries, gain, lengths, ctx_out, qry_out, normed, *scratch):
    ctx, qry, sems = scratch
    core = where[3]
    copies = copy_all(
        [
            pltpu.make_async_copy(context.at[core], ctx, sems.at[0]),
            pltpu.make_async_copy(queries.at[core], qry, sems.at[1]),
        ]
    )
    step = 32

    def rows_of(source, raw, below):
        @pl.loop(0, source.shape[0] // step)
        def _(i):
            first = pl.multiple_of(i * step, step)
            low = source[pl.ds(first, step), :]
            wide = low.astype(F32)
            mean = jnp.mean(wide * wide, axis=-1, keepdims=True)
            normed[pl.ds(below + first, step), :] = (
                wide * lax.rsqrt(mean + 1e-06) * gain[...]
            ).astype(BF16)
            raw[pl.ds(first, step), :] = low

    length = lengths[core].astype(F32)
    normed[pl.ds(normed.shape[0] - TAIL, TAIL), :] = jnp.full(
        (TAIL, normed.shape[1]), length
    ).astype(BF16)
    copies[0].wait()
    rows_of(ctx, ctx_out, 0)
    copies[1].wait()
    rows_of(qry, qry_out, ctx.shape[0])


def norm_scene(where, context, queries, gain, lengths):
    ctx = jax.ShapeDtypeStruct(context.shape[1:], BF16)
    qry = jax.ShapeDtypeStruct(queries.shape[1:], BF16)
    rows = ctx.shape[0] + qry.shape[0] + TAIL
    return call(
        norm_kernel,
        (ctx, qry, jax.ShapeDtypeStruct((rows, ctx.shape[1]), BF16)),
        [SMEM, HBM, HBM, VMEM, SMEM],
        (VMEM,) * 3,
        [
            pltpu.VMEM(ctx.shape, BF16),
            pltpu.VMEM(qry.shape, BF16),
            pltpu.SemaphoreType.DMA((2,)),
        ],
        moved=6 * ctx.size,
    )(where, context, queries, gain, lengths)


def slot_copies(rows, slot, first, count, columns, target, sems, base):
    if slot != 2:
        pieces = [(rows[slot if slot < 2 else 4], first, count, 0)]
    else:
        cut = rows[2].shape[0]
        pieces = []
        if first < cut:
            pieces.append((rows[2], first, min(count, cut - first), 0))
        if first + count > cut:
            skip = max(cut - first, 0)
            pieces.append((rows[3], first + skip - cut, count - skip, skip))
    return [
        pltpu.make_async_copy(
            piece.at[pl.ds(start, size), columns], target.at[pl.ds(at, size)], sems.at[base + i]
        )
        for i, (piece, start, size, at) in enumerate(pieces)
    ]


def row_copies(high, rows, rows_all, sems):
    mem, width = rows_all.shape[0] // RING, rows_all.shape[1]
    columns = pl.ds(pl.multiple_of(high * width, width), width)
    copies = []
    for slot in range(RING):
        target = rows_all.at[pl.ds(slot * mem, mem)]
        copies += slot_copies(rows, slot, 0, mem, columns, target, sems, len(copies))
    return copies


def weight_copies(x, group, weight, sems, base, plane=None):
    copies = []
    for i, piece in enumerate(group):
        step, side = i % RING, i // RING
        _, block, part = piece.shape
        first = pl.multiple_of(((x - step + RING) % RING) * block, block)
        rows, columns = pl.ds(first, block), pl.ds(side * part, part)
        if plane is None:
            source, target = piece, weight.at[:, rows, columns]
        else:
            source, target = piece.at[plane], weight.at[rows, columns]
        copies.append(pltpu.make_async_copy(source, target, sems.at[base + i]))
    return copies


def pieces_of(parts):
    pieces = []
    for own, sides, opposite in (parts[:3], parts[3:]):
        pieces += [own, sides.at[0], opposite, sides.at[1]]
    return pieces


def start_kernel(where, *refs):
    rows, parts = refs[:5], refs[5:11]
    total, rows_all, weight, sems = refs[11:]
    group = pieces_of(parts)
    copies = row_copies(where[1], rows, rows_all, sems)
    copies += weight_copies(where[0], group, weight, sems, 5)
    wait_all(copy_all(copies))

    @pl.when(where[2] == 1)
    def _():
        total[0] = jnp.dot(rows_all[...], weight[0], preferred_element_type=F32)

    @pl.loop(1, 3)
    def _(plane):
        total[plane] = jnp.dot(rows_all[...], weight[plane], preferred_element_type=F32)


def attend_kernel(where, *refs):
    rows, near, far, total_in = refs[:5], refs[5:11], refs[11:17], refs[17]
    outs = refs[18:22]
    rows_all, qry_all, near_query, weight, total, lengths, low, mixed, sems = refs[22:]
    x, z, encoder = where[0], where[1], where[2]
    mem, few = rows_all.shape[0] // RING, qry_all.shape[0] // RING
    width = rows_all.shape[1]
    copies = row_copies(1 - z, rows, rows_all, sems)
    copies += weight_copies(x, pieces_of(far), weight, sems, 5)
    for slot in range(RING):
        copies += slot_copies(
            rows, slot, mem + few, TAIL, pl.ds(0, 128), lengths.at[slot], sems, 13 + slot
        )
    totals = [
        pltpu.make_async_copy(total_in.at[plane], total.at[plane], sems.at[17 + plane])
        for plane in range(3)
    ]
    queries = weight_copies(x, pieces_of(near), near_query, sems, 20, plane=0)
    for slot in range(RING):
        target = qry_all.at[pl.ds(slot * few, few)]
        queries += slot_copies(
            rows, slot, mem, few, pl.ds(0, 2 * width), target, sems, 28 + slot
        )
    copy_all(copies)
    copy_all(totals[1:])

    @pl.when(encoder == 1)
    def _():
        totals[0].start()

    @pl.when(encoder == 0)
    def _():
        copy_all(queries)

    wait_all(copies)
    wait_all(totals[1:])

    @pl.when(encoder == 1)
    def _():
        totals[0].wait()
        low[0] = (
            total[0] + jnp.dot(rows_all[...], weight[0], preferred_element_type=F32)
        ).astype(BF16)

    @pl.when(encoder == 0)
    def _():
        wait_all(queries)
        here = pl.ds(pl.multiple_of(z * width, width), width)
        there = pl.ds(pl.multiple_of((1 - z) * width, width), width)
        low[0, pl.ds(0, RING * few)] = (
            jnp.dot(qry_all[:, here], near_query[...], preferred_element_type=F32)
            + jnp.dot(qry_all[:, there], weight[0], preferred_element_type=F32)
        ).astype(BF16)

    @pl.loop(1, 3)
    def _(plane):
        low[plane] = (
            total[plane] + jnp.dot(rows_all[...], weight[plane], preferred_element_type=F32)
        ).astype(BF16)

    heads = low.shape[2] // HEAD
    scale = 1.0 / math.sqrt(HEAD)

    def heads_of(count):
        column = lax.broadcasted_iota(jnp.int32, (count, mem), 1)

        @pl.loop(0, RING)
        def _(slot):
            own = pl.ds(pl.multiple_of(slot * count, count), count)
            keys = pl.ds(pl.multiple_of(slot * mem, mem), mem)
            length = lengths[slot, pl.ds(0, 1), pl.ds(0, 1)].astype(F32).astype(jnp.int32)
            valid = column < length
            for head in range(heads):
                at = pl.ds(head * HEAD, HEAD)
                scores = (
                    lax.dot_general(
                        low[0, own, at],
                        low[1, keys, at],
                        (((1,), (1,)), ((), ())),
                        preferred_element_type=F32,
                    )
                    * scale
                )
                scores = jnp.where(valid, scores, -1e30)
                expo = jnp.exp(scores - jnp.max(scores, axis=-1, keepdims=True))
                probs = (expo / jnp.sum(expo, axis=-1, keepdims=True)).astype(BF16)
                mixed[slot, pl.ds(0, count), at] = jnp.dot(
                    probs, low[2, keys, at], preferred_element_type=F32
                ).astype(BF16)

    @pl.when(encoder == 1)
    def _():
        heads_of(mem)

    @pl.when(encoder == 0)
    def _():
        heads_of(few)

    wait_all(
        copy_all(
            [
                pltpu.make_async_copy(mixed.at[slot], outs[slot], sems.at[slot])
                for slot in range(RING)
            ]
        )
    )


def start_projections(where, mem, rows, parts):
    width = rows[0].shape[1]
    planes, block, part = parts[0].shape
    return call(
        start_kernel,
        jax.ShapeDtypeStruct((planes, RING * mem, 2 * part), F32),
        [SMEM] + [HBM] * 11,
        VMEM,
        [
            pltpu.VMEM((RING * mem, width // 2), BF16),
            pltpu.VMEM((planes, width // 2, 2 * part), BF16),
            pltpu.SemaphoreType.DMA((13,)),
        ],
        flops=RING * mem * width * planes * 2 * part,
        moved=RING * mem * width + planes * width * 2 * part,
        limit=24,
    )(where, *rows, *parts)


def attend(where, mem, few, rows, near, far, total):
    width = rows[0].shape[1]
    planes, block, part = near[0].shape
    out = jax.ShapeDtypeStruct((mem, 2 * part), BF16)
    operands = (*rows, *near, *far, total)
    return call(
        attend_kernel,
        (out,) * RING,
        [SMEM] + [HBM] * len(operands),
        (HBM,) * RING,
        [
            pltpu.VMEM((RING * mem, width // 2), BF16),
            pltpu.VMEM((RING * few, width), BF16),
            pltpu.VMEM((width // 2, 2 * part), BF16),
            pltpu.VMEM((planes, width // 2, 2 * part), BF16),
            pltpu.VMEM(total.shape, F32),
            pltpu.VMEM((RING, TAIL, 128), BF16),
            pltpu.VMEM((planes, RING * mem, 2 * part), BF16),
            pltpu.VMEM((RING, mem, 2 * part), BF16),
            pltpu.SemaphoreType.DMA((32,)),
        ],
        flops=RING * mem * width * planes * 2 * part,
        moved=RING * mem * width + planes * width * 2 * part,
        limit=30,
    )(where, *operands)


def project_kernel(part, where, context, queries, *refs):
    mixed = refs[:4]
    weights = refs[4:6]
    few_in = refs[6] if part else None
    out, few_out = refs[6 + part : 8 + part]
    heads, weight, base, sems = refs[8 + part :]
    x, encoder, core = where[0], where[2], where[3]
    quarter = mixed[0].shape[1] // 2
    _, inner, block = weights[0].shape
    few = queries.shape[1]
    columns = pl.ds(part * RING * block, RING * block)
    rows_base = pltpu.make_async_copy(context.at[core, :, columns], base, sems.at[0])
    few_base = pltpu.make_async_copy(
        queries.at[core, :, columns], base.at[pl.ds(0, few)], sems.at[0]
    )
    copies = []
    for step in range(RING):
        for side in range(2):
            at = pl.multiple_of(side * inner + ((x + step) % RING) * quarter, quarter)
            copies.append(
                pltpu.make_async_copy(
                    mixed[step].at[:, pl.ds(side * quarter, quarter)],
                    heads.at[:, pl.ds(at, quarter)],
                    sems.at[1 + step * 2 + side],
                )
            )
    pieces = []
    for i in range(RING):
        for side in range(2):
            pieces.append(
                pltpu.make_async_copy(
                    weights[side].at[part * RING + i],
                    weight.at[i, pl.ds(side * inner, inner)],
                    sems.at[9 + i * 2 + side],
                )
            )

    @pl.when(encoder == 1)
    def _():
        rows_base.start()

    @pl.when(encoder == 0)
    def _():
        few_base.start()

    copy_all(copies)
    copy_all(pieces)

    @pl.when(encoder == 1)
    def _():
        rows_base.wait()

    @pl.when(encoder == 0)
    def _():
        few_base.wait()

    if part:
        few_out[:, pl.ds(0, RING * block)] = few_in[...]
    wait_all(copies)
    for i in range(RING):
        wait_all(pieces[2 * i : 2 * i + 2])
        at = pl.ds(i * block, block)
        update = jnp.dot(heads[...], weight[i], preferred_element_type=F32)
        result = (base[:, at].astype(F32) + update).astype(BF16)
        out[:, at] = result
        few_out[:, pl.ds((part * RING + i) * block, block)] = result[:few]


def project(part, where, context, queries, mixed, weights, few_in=()):
    mem, few = context.shape[1], queries.shape[1]
    _, inner, block = weights[0].shape
    return call(
        functools.partial(project_kernel, part),
        (
            jax.ShapeDtypeStruct((mem, RING * block), BF16),
            jax.ShapeDtypeStruct((few, (1 + part) * RING * block), BF16),
        ),
        [SMEM] + [HBM] * 8 + [VMEM] * part,
        (VMEM, VMEM),
        [
            pltpu.VMEM((mem, 2 * inner), BF16),
            pltpu.VMEM((RING, 2 * inner, block), BF16),
            pltpu.VMEM((mem, RING * block), BF16),
            pltpu.SemaphoreType.DMA((17,)),
        ],
        flops=2 * mem * 2 * inner * RING * block,
        moved=2 * (2 * inner * RING * block + 3 * mem * inner),
    )(where, context, queries, *mixed, *weights, *few_in)


def gather_kernel(where, *refs):
    halves = (refs[0:2], refs[2:4])
    ctx_early, qry_early, qry_late = refs[4:6], refs[6:8], refs[8:10]
    ctx_out, qry_out, ctx, qry, sems = refs[10:]
    core, from_encoder = where[3], where[4]
    width = halves[0][0].shape[1]

    def build(rows, few):
        copies = []
        for side in range(2):
            scene = core if side == 0 else 1 - core
            for piece, at in rows[side]:
                target = ctx.at[scene, :, at]
                copies.append(pltpu.make_async_copy(piece, target, sems.at[len(copies)]))
            copies.append(
                pltpu.make_async_copy(few[side], qry.at[scene], sems.at[len(copies)])
            )
        wait_all(copy_all(copies))

    @pl.when(from_encoder == 1)
    def _():
        build(
            [[(halves[i][side], pl.ds(i * width, width)) for i in range(2)] for side in range(2)],
            qry_early,
        )

    @pl.when(from_encoder == 0)
    def _():
        build([[(ctx_early[side], pl.ds(0, 2 * width))] for side in range(2)], qry_late)

    wait_all(
        copy_all(
            [
                pltpu.make_async_copy(ctx, ctx_out, sems.at[0]),
                pltpu.make_async_copy(qry, qry_out, sems.at[1]),
            ]
        )
    )


def gather_result(where, first, second, ctx_early, qry_early, qry_late):
    ctx_shape = (2,) + ctx_early[0].shape
    qry_shape = (2,) + qry_early[0].shape
    return call(
        gather_kernel,
        (jax.ShapeDtypeStruct(ctx_shape, BF16), jax.ShapeDtypeStruct(qry_shape, BF16)),
        [SMEM] + [HBM] * 10,
        (HBM, HBM),
        [
            pltpu.VMEM(ctx_shape, BF16),
            pltpu.VMEM(qry_shape, BF16),
            pltpu.SemaphoreType.DMA((6,)),
        ],
        moved=8 * ctx_early[0].size,
    )(where, *first, *second, *ctx_early, *qry_early, *qry_late)


def both(array):
    return array, other_core(array)


def per_device(context, queries, lengths, norm_gain, qkv_weight, out_weight):
    count = lax.axis_size("section")
    section = lax.axis_index("section")
    place = lax.axis_index("dp")
    core = lax.axis_index("tensor")
    encoders = list(range(count // 2))
    decoders = list(range(count // 2, count))
    before = (section + count - 1) % count
    where = jnp.stack(
        [
            place % RING,
            place // RING,
            (section < count // 2).astype(jnp.int32),
            core,
            (before < count // 2).astype(jnp.int32),
        ]
    ).astype(jnp.int32)
    context, queries = context[0], queries[0]

    mem, few = context.shape[1], queries.shape[1]
    out_all = lax.all_gather(out_weight[0], "dp")

    own = quarters(where, jnp.swapaxes(qkv_weight[0], 0, 1))
    own_other = other_core(own[0])
    far_own = across_z(own[0])
    left, opposite, right = [around_x(own[step], step) for step in range(1, RING)]
    sides = jnp.stack([left, right])

    ctx, qry, normed = norm_scene(
        after(where, *own), context, queries, norm_gain, lengths[0]
    )
    cut = (normed.shape[0] // 32 + 1) * 16
    from_left, from_right, send_left, send_right = round_ring(
        after(normed, far_own, sides, opposite, own_other), cut
    )
    far_sides = across_z(after(sides, far_own))
    far_opposite = across_z(after(opposite, from_left, from_right))
    rows = (
        normed,
        from_left,
        around_x(after(send_left, far_sides), 1),
        around_x(after(send_right, far_sides), -1),
        from_right,
    )
    near = (own[0], sides, opposite, own_other, other_core(sides), other_core(opposite))
    total = start_projections(where, mem, rows, near)
    far = (far_own, far_sides, far_opposite)
    far += (
        other_core(after(far_own, far_sides)),
        other_core(far_sides),
        other_core(after(far_opposite, total)),
    )
    ctx_early = relay(after(ctx, far_opposite), decoders, count)
    qry_early = relay(after(qry, far_opposite), encoders, count)

    mixed = attend(where, mem, few, rows, near, far, total)
    weights = both(after(out_all, mixed[0]))
    mixed = [mixed[0]] + [around_x(mixed[step], -step) for step in range(1, RING)]

    first, few_first = project(0, where, context, queries, mixed, weights)
    first = relay(first, encoders, count)
    second, few_new = project(1, where, context, queries, mixed, weights, (few_first,))
    second = relay(second, encoders, count)
    few_new = relay(few_new, decoders, count)
    ctx_new, qry_new = gather_result(
        where,
        both(first),
        (second, other_core(after(second, few_new))),
        (ctx_early, other_core(after(ctx_early, first))),
        (qry_early, other_core(after(qry_early, first))),
        both(few_new),
    )
    return ctx_new[None], qry_new[None]


def solution(mesh):
    return jax.shard_map(
        per_device,
        mesh=mesh,
        in_specs=(
            P("section", "dp", None, None),
            P("section", "dp", None, None),
            P("section", "dp"),
            P("section", None),
            P("section", "dp", None, "tensor"),
            P("section", "tensor", "dp"),
        ),
        out_specs=(P("section", "dp", None, None), P("section", "dp", None, None)),
        check_vma=False,
    )
```

profile of v0, /device:TPU:17, one launch (start us, length us, event | category | flops | bytes accessed | tf_op | source)
XLA Modules:
  0.0 232.4 jit_solution(16045954761173647109)
XLA Ops:
  7.2 0.0 all-gather.2.cloned.1.call-start
  7.2 0.7 all-gather.2.cloned.1.call-update
  7.9 0.1 stack.40.where
  8.0 1.4 copy-done.4
  9.4 0.8 shard_map.77
  10.2 1.3 collective-permute-start.1
  11.5 1.5 collective-permute-start.2
  13.0 6.9 %collective-permute-start = (bf16[3,256,256]{2,1,0:T(8,128)(2,1)S(1)}, bf16[3,256,256]{2,1,0:T(8,128)(2,1)S(1)}, u32[]{:S(2)}, u32[]{:S(2)}) collective-permute-start(bf16[3,256,256]{2,1,0:T(8,128)(2,1)S(1)} %get-tuple-element.33.refs_5_), channel_id=1, source_target_pairs={{0,8},{2,10},{4,12},{6,14},{8,0},{10,2},{12,4},{14,6},{1,9},{3,11}... | collective-permute-start | bytes 1179656 | tf_op jit(solution)/shard_map/ppermute | solution.py:39
  19.9 1.5 collective-permute-start.3
  21.4 1.8 collective-permute-start.4
  23.2 1.0 copy-done.2
  24.2 0.7 copy-done.5
  24.9 0.7 copy-done.6
  25.6 2.0 shard_map.78
  27.6 0.0 copy-start.7
  27.6 0.1 pad_maximum_fusion.refs_6_
  27.7 1.4 collective-permute-done.refs_11_
  29.1 1.4 collective-permute-done.3.refs_7_
  30.5 0.9 collective-permute-start.5
  31.3 1.8 collective-permute-start.8
  33.1 9.1 %collective-permute-start.6 = (bf16[2,3,256,256]{3,2,1,0:T(8,128)(2,1)S(1)}, bf16[2,3,256,256]{3,2,1,0:T(8,128)(2,1)S(1)}, u32[]{:S(2)}, u32[]{:S(2)}) collective-permute-start(bf16[2,3,256,256]{3,2,1,0:T(8,128)(2,1)S(1)} %pad_maximum_fusion.refs_6_), channel_id=1, source_target_pairs={{0,8},{2,10},{4,12},{6,14},{8,0},{10,2},{12,4},{14,6},{1,9},{3,11}... | collective-permute-start | bytes 2359304 | tf_op jit(solution)/shard_map/ppermute | solution.py:39
  42.3 11.2 %collective-permute-start.10 = (bf16[2,3,256,256]{3,2,1,0:T(8,128)(2,1)S(1)}, bf16[2,3,256,256]{3,2,1,0:T(8,128)(2,1)S(1)}, u32[]{:S(2)}, u32[]{:S(2)}) collective-permute-start(bf16[2,3,256,256]{3,2,1,0:T(8,128)(2,1)S(1)} %pad_maximum_fusion.refs_6_), channel_id=1, source_target_pairs={{0,1},{1,0},{2,3},{3,2},{4,5},{5,4},{6,7},{7,6},{8,9},{9,8},{10,11... | collective-permute-start | bytes 2359304 | tf_op jit(solution)/shard_map/ppermute | solution.py:43
  53.4 8.9 %collective-permute-done.5.refs_1_ = bf16[336,2048]{1,0:T(8,128)(2,1)S(1)} collective-permute-done((bf16[336,2048]{1,0:T(8,128)(2,1)S(1)}, bf16[336,2048]{1,0:T(8,128)(2,1)S(1)}, u32[]{:S(2)}, u32[]{:S(2)}) %collective-permute-start.5) | collective-permute-done | bytes 1376288 | tf_op jit(solution)/shard_map/ppermute | solution.py:25
  62.4 0.1 slice.8
  62.4 2.5 %collective-permute-done.6.refs_12_ = bf16[2,3,256,256]{3,2,1,0:T(8,128)(2,1)S(1)} collective-permute-done((bf16[2,3,256,256]{3,2,1,0:T(8,128)(2,1)S(1)}, bf16[2,3,256,256]{3,2,1,0:T(8,128)(2,1)S(1)}, u32[]{:S(2)}, u32[]{:S(2)}) %collective-permute-start.6) | collective-permute-done | bytes 786464 | tf_op jit(solution)/shard_map/ppermute | solution.py:39
  65.0 1.8 collective-permute-start.7
  66.8 0.1 slice.9
  66.9 1.2 collective-permute-start.9
  68.0 7.5 %collective-permute-start.11 = (bf16[3,256,256]{2,1,0:T(8,128)(2,1)S(1)}, bf16[3,256,256]{2,1,0:T(8,128)(2,1)S(1)}, u32[]{:S(2)}, u32[]{:S(2)}) collective-permute-start(bf16[3,256,256]{2,1,0:T(8,128)(2,1)S(1)} %collective-permute-done.3.refs_7_), channel_id=1, source_target_pairs={{0,1},{1,0},{2,3},{3,2},{4,5},{5,4},{6,7},{7,6},{8,9},{9,8},{10,11... | collective-permute-start | bytes 1179656 | tf_op jit(solution)/shard_map/ppermute | solution.py:43
  75.6 15.5 %collective-permute-start.12 = (bf16[3,256,256]{2,1,0:T(8,128)(2,1)S(1)}, bf16[3,256,256]{2,1,0:T(8,128)(2,1)S(1)}, u32[]{:S(2)}, u32[]{:S(2)}) collective-permute-start(bf16[3,256,256]{2,1,0:T(8,128)(2,1)S(1)} %collective-permute-done.3.refs_7_), channel_id=1, source_target_pairs={{0,8},{2,10},{4,12},{6,14},{8,0},{10,2},{12,4},{14,6},{1,9},{3,11}... | collective-permute-start | bytes 1179656 | tf_op jit(solution)/shard_map/ppermute | solution.py:39
  91.1 0.3 collective-permute-start.14
  91.4 0.2 collective-permute-start.13
  91.6 3.7 %shard_map.79.refs_17_ = f32[3,1024,512]{2,1,0:T(8,128)S(1)} custom-call(s32[5]{0:T(128)S(1)} %stack.40.where, bf16[336,2048]{1,0:T(8,128)(2,1)S(1)} %get-tuple-element.39.refs_0_, bf16[336,2048]{1,0:T(8,128)(2,1)S(1)} %collective-permute-done.5.refs_1_, bf16[176,2048]{1,0:T(8,128)(2,1)S(1)} %collective-permute-done.7.refs_2_, ...), custom_call_target="tpu_custom_call" | custom-call | flops 3221225472 | bytes 5242880 | tf_op jit(solution)/shard_map/pallas_call | solution.py:328
  95.3 40.2 %collective-permute-done.12.refs_13_ = bf16[3,256,256]{2,1,0:T(8,128)(2,1)S(1)} collective-permute-done((bf16[3,256,256]{2,1,0:T(8,128)(2,1)S(1)}, bf16[3,256,256]{2,1,0:T(8,128)(2,1)S(1)}, u32[]{:S(2)}, u32[]{:S(2)}) %collective-permute-start.12) | collective-permute-done | bytes 393248 | tf_op jit(solution)/shard_map/ppermute | solution.py:39
  135.5 0.3 collective-permute-start.15
  135.8 1.4 collective-permute-done.15.refs_16_
  137.3 10.8 %shard_map.80 = (bf16[256,512]{1,0:T(8,128)(2,1)S(1)}, bf16[256,512]{1,0:T(8,128)(2,1)S(1)}, bf16[256,512]{1,0:T(8,128)(2,1)S(1)}, bf16[256,512]{1,0:T(8,128)(2,1)S(1)}) custom-call(s32[5]{0:T(128)S(1)} %stack.40.where, bf16[336,2048]{1,0:T(8,128)(2,1)S(1)} %get-tuple-element.39.refs_0_, bf16[336,2048]{1,0:T(8,128)(2,1)S(1)} %collective-permute-done.5.refs_1_, ...), custom_call_target="tpu_custom_call" | custom-call | flops 3221225472 | bytes 5242880 | tf_op jit(solution)/shard_map/pallas_call | solution.py:349
  148.1 0.7 copy-done.8
  148.8 0.7 copy-done.9
  149.5 9.8 %all-gather.2.cloned.1.call-done.refs_4_ = bf16[8,1024,256]{2,1,0:T(8,128)(2,1)} async-done(((bf16[1,1024,256]{2,1,0:T(8,128)(2,1)}), bf16[8,1024,256]{2,1,0:T(8,128)(2,1)}) %all-gather.2.cloned.1.call-update) | async-done | bytes 4194320 | tf_op jit(solution)/shard_map/all_gather | solution.py:542
  159.3 0.8 collective-permute-start.19
  160.1 3.4 %collective-permute-start.25 = (bf16[256,2048]{1,0:T(8,128)(2,1)}, bf16[256,2048]{1,0:T(8,128)(2,1)S(1)}, u32[]{:S(2)}, u32[]{:S(2)}) collective-permute-start(bf16[256,2048]{1,0:T(8,128)(2,1)} %copy-done.7), channel_id=1, source_target_pairs={{128,144},{144,160},{160,176},{176,192},{192,208},{208,224},{224,2... | collective-permute-start | bytes 3145736 | tf_op jit(solution)/shard_map/ppermute | solution.py:47
  163.6 1.0 collective-permute-start.16
  164.5 1.0 collective-permute-start.17
  165.6 5.7 %collective-permute-done.16.refs_1_ = bf16[256,512]{1,0:T(8,128)(2,1)S(1)} collective-permute-done((bf16[256,512]{1,0:T(8,128)(2,1)}, bf16[256,512]{1,0:T(8,128)(2,1)S(1)}, u32[]{:S(2)}, u32[]{:S(2)}) %collective-permute-start.16) | collective-permute-done | bytes 262176 | tf_op jit(solution)/shard_map/ppermute | solution.py:25
  171.3 2.1 collective-permute-done.17.refs_2_
  173.4 6.7 %collective-permute-done.18.refs_3_ = bf16[256,512]{1,0:T(8,128)(2,1)S(1)} collective-permute-done((bf16[256,512]{1,0:T(8,128)(2,1)S(1)}, bf16[256,512]{1,0:T(8,128)(2,1)S(1)}, u32[]{:S(2)}, u32[]{:S(2)}) %collective-permute-start.18) | collective-permute-done | bytes 262176 | tf_op jit(solution)/shard_map/ppermute | solution.py:25
  180.1 2.2 copy-done.1
  182.3 4.0 %shard_map.81 = (bf16[256,1024]{1,0:T(8,128)(2,1)S(1)}, bf16[64,1024]{1,0:T(8,128)(2,1)S(1)}) custom-call(s32[5]{0:T(128)S(1)} %stack.40.where, bf16[2,256,2048]{2,1,0:T(8,128)(2,1)S(1)} %bitcast.16, bf16[2,64,2048]{2,1,0:T(8,128)(2,1)S(1)} %bitcast.19, bf16[256,512]{1,0:T(8,128)(2,1)S(1)} %get-tuple-element.46.refs_0_, ...), custom_call_target="tpu_custom_call" | custom-call | flops 1073741824 | bytes 5767168 | tf_op jit(solution)/shard_map/pallas_call | solution.py:442
  186.2 1.3 collective-permute-start.20
  187.5 4.0 %shard_map.82 = (bf16[256,1024]{1,0:T(8,128)(2,1)S(1)}, bf16[64,2048]{1,0:T(8,128)(2,1)S(1)}) custom-call(s32[5]{0:T(128)S(1)} %stack.40.where, bf16[2,256,2048]{2,1,0:T(8,128)(2,1)S(1)} %bitcast.17, bf16[2,64,2048]{2,1,0:T(8,128)(2,1)S(1)} %bitcast.20, bf16[256,512]{1,0:T(8,128)(2,1)S(1)} %get-tuple-element.46.refs_0_, ...), custom_call_target="tpu_custom_call" | custom-call | flops 1073741824 | bytes 5767168 | tf_op jit(solution)/shard_map/pallas_call | solution.py:442
  191.5 1.3 collective-permute-start.22
  192.8 11.0 %collective-permute-done.20.refs_0_ = bf16[256,1024]{1,0:T(8,128)(2,1)S(1)} collective-permute-done((bf16[256,1024]{1,0:T(8,128)(2,1)S(1)}, bf16[256,1024]{1,0:T(8,128)(2,1)S(1)}, u32[]{:S(2)}, u32[]{:S(2)}) %collective-permute-start.20) | collective-permute-done | bytes 524320 | tf_op jit(solution)/shard_map/ppermute | solution.py:47
  203.8 2.3 collective-permute-start.26
  206.1 1.3 collective-permute-start.23
  207.4 1.3 collective-permute-start.27
  208.7 4.6 %collective-permute-done.23.refs_8_ = bf16[64,2048]{1,0:T(8,128)(2,1)S(1)} collective-permute-done((bf16[64,2048]{1,0:T(8,128)(2,1)S(1)}, bf16[64,2048]{1,0:T(8,128)(2,1)S(1)}, u32[]{:S(2)}, u32[]{:S(2)}) %collective-permute-start.23) | collective-permute-done | bytes 262176 | tf_op jit(solution)/shard_map/ppermute | solution.py:47
  213.3 1.8 collective-permute-done.22.refs_2_
  215.1 2.3 collective-permute-start.24
  217.4 0.5 collective-permute-start.29
  217.9 2.8 %collective-permute-done.27.refs_6_ = bf16[64,2048]{1,0:T(8,128)(2,1)S(1)} collective-permute-done((bf16[64,2048]{1,0:T(8,128)(2,1)S(1)}, bf16[64,2048]{1,0:T(8,128)(2,1)S(1)}, u32[]{:S(2)}, u32[]{:S(2)}) %collective-permute-start.27) | collective-permute-done | bytes 262176 | tf_op jit(solution)/shard_map/ppermute | solution.py:47
  220.7 1.3 collective-permute-start.28
  222.0 1.2 collective-permute-done.28.refs_7_
  223.2 2.3 shard_map.83
  (30 shorter events, 0.1 us)
Async XLA Ops:
  7.2 16.0 %copy-start = (bf16[1,2,256,2048]{3,2,1,0:T(8,128)(2,1)S(1)}, bf16[1,2,256,2048]{3,2,1,0:T(8,128)(2,1)}, u32[]{:S(2)}) copy-start(bf16[1,2,256,2048]{3,2,1,0:T(8,128)(2,1)} %param.6) | copy-start | bytes 6291460
  7.2 152.1 %all-gather.2.cloned.1.call-start = ((), (), s32[]{:S(2)}) async-start(), calls=%async_computation | async-start | bytes 4718592 | tf_op jit(solution)/shard_map/all_gather | solution.py:542
  8.0 1.4 copy-start.4
  10.2 17.4 %collective-permute-start.1 = (bf16[3,256,256]{2,1,0:T(8,128)(2,1)S(1)}, bf16[3,256,256]{2,1,0:T(8,128)(2,1)S(1)}, u32[]{:S(2)}, u32[]{:S(2)}) collective-permute-start(bf16[3,256,256]{2,1,0:T(8,128)(2,1)S(1)} %get-tuple-element.34), channel_id=1, source_target_pairs={{0,2},{2,4},{4,6},{6,0},{8,10},{10,12},{12,14},{14,8},{1,3},{3,5},... | collective-permute-start | bytes 1179656 | tf_op jit(solution)/shard_map/ppermute | solution.py:25
  11.5 16.1 %collective-permute-start.2 = (bf16[3,256,256]{2,1,0:T(8,128)(2,1)S(1)}, bf16[3,256,256]{2,1,0:T(8,128)(2,1)S(1)}, u32[]{:S(2)}, u32[]{:S(2)}) collective-permute-start(bf16[3,256,256]{2,1,0:T(8,128)(2,1)S(1)} %get-tuple-element.36), channel_id=1, source_target_pairs={{0,6},{2,0},{4,2},{6,4},{8,14},{10,8},{12,10},{14,12},{1,7},{3,1},... | collective-permute-start | bytes 1179656 | tf_op jit(solution)/shard_map/ppermute | solution.py:25
  13.0 16.1 %collective-permute-start = (bf16[3,256,256]{2,1,0:T(8,128)(2,1)S(1)}, bf16[3,256,256]{2,1,0:T(8,128)(2,1)S(1)}, u32[]{:S(2)}, u32[]{:S(2)}) collective-permute-start(bf16[3,256,256]{2,1,0:T(8,128)(2,1)S(1)} %get-tuple-element.33.refs_5_), channel_id=1, source_target_pairs={{0,8},{2,10},{4,12},{6,14},{8,0},{10,2},{12,4},{14,6},{1,9},{3,11}... | collective-permute-start | bytes 1179656 | tf_op jit(solution)/shard_map/ppermute | solution.py:39
  19.9 10.6 %collective-permute-start.3 = (bf16[3,256,256]{2,1,0:T(8,128)(2,1)S(1)}, bf16[3,256,256]{2,1,0:T(8,128)(2,1)S(1)}, u32[]{:S(2)}, u32[]{:S(2)}) collective-permute-start(bf16[3,256,256]{2,1,0:T(8,128)(2,1)S(1)} %get-tuple-element.35), channel_id=1, source_target_pairs={{0,4},{2,6},{4,0},{6,2},{8,12},{10,14},{12,8},{14,10},{1,5},{3,7},... | collective-permute-start | bytes 1179656 | tf_op jit(solution)/shard_map/ppermute | solution.py:25
  21.4 9.1 %collective-permute-start.4 = (bf16[3,256,256]{2,1,0:T(8,128)(2,1)S(1)}, bf16[3,256,256]{2,1,0:T(8,128)(2,1)S(1)}, u32[]{:S(2)}, u32[]{:S(2)}) collective-permute-start(bf16[3,256,256]{2,1,0:T(8,128)(2,1)S(1)} %get-tuple-element.33.refs_5_), channel_id=1, source_target_pairs={{0,1},{1,0},{2,3},{3,2},{4,5},{5,4},{6,7},{7,6},{8,9},{9,8},{10,11... | collective-permute-start | bytes 1179656 | tf_op jit(solution)/shard_map/ppermute | solution.py:43
  23.2 1.0 copy-start.2
  24.2 0.7 copy-start.5
  24.9 0.7 copy-start.6
  27.6 39.3 %copy-start.7 = (bf16[256,2048]{1,0:T(8,128)(2,1)}, bf16[256,2048]{1,0:T(8,128)(2,1)S(1)}, u32[]{:S(2)}) copy-start(bf16[256,2048]{1,0:T(8,128)(2,1)S(1)} %get-tuple-element.57) | copy-start | bytes 3145732
  30.5 31.9 %collective-permute-start.5 = (bf16[336,2048]{1,0:T(8,128)(2,1)S(1)}, bf16[336,2048]{1,0:T(8,128)(2,1)S(1)}, u32[]{:S(2)}, u32[]{:S(2)}) collective-permute-start(bf16[336,2048]{1,0:T(8,128)(2,1)S(1)} %get-tuple-element.39.refs_0_), channel_id=1, source_target_pairs={{0,2},{2,4},{4,6},{6,0},{8,10},{10,12},{12,14},{14,8},{1,3},{3,5},... | collective-permute-start | bytes 4128776 | tf_op jit(solution)/shard_map/ppermute | solution.py:25
  31.3 35.5 %collective-permute-start.8 = (bf16[336,2048]{1,0:T(8,128)(2,1)S(1)}, bf16[336,2048]{1,0:T(8,128)(2,1)S(1)}, u32[]{:S(2)}, u32[]{:S(2)}) collective-permute-start(bf16[336,2048]{1,0:T(8,128)(2,1)S(1)} %get-tuple-element.39.refs_0_), channel_id=1, source_target_pairs={{0,6},{2,0},{4,2},{6,4},{8,14},{10,8},{12,10},{14,12},{1,7},{3,1},... | collective-permute-start | bytes 4128776 | tf_op jit(solution)/shard_map/ppermute | solution.py:25
  33.1 31.8 %collective-permute-start.6 = (bf16[2,3,256,256]{3,2,1,0:T(8,128)(2,1)S(1)}, bf16[2,3,256,256]{3,2,1,0:T(8,128)(2,1)S(1)}, u32[]{:S(2)}, u32[]{:S(2)}) collective-permute-start(bf16[2,3,256,256]{3,2,1,0:T(8,128)(2,1)S(1)} %pad_maximum_fusion.refs_6_), channel_id=1, source_target_pairs={{0,8},{2,10},{4,12},{6,14},{8,0},{10,2},{12,4},{14,6},{1,9},{3,11}... | collective-permute-start | bytes 2359304 | tf_op jit(solution)/shard_map/ppermute | solution.py:39
  42.3 49.2 %collective-permute-start.10 = (bf16[2,3,256,256]{3,2,1,0:T(8,128)(2,1)S(1)}, bf16[2,3,256,256]{3,2,1,0:T(8,128)(2,1)S(1)}, u32[]{:S(2)}, u32[]{:S(2)}) collective-permute-start(bf16[2,3,256,256]{3,2,1,0:T(8,128)(2,1)S(1)} %pad_maximum_fusion.refs_6_), channel_id=1, source_target_pairs={{0,1},{1,0},{2,3},{3,2},{4,5},{5,4},{6,7},{7,6},{8,9},{9,8},{10,11... | collective-permute-start | bytes 2359304 | tf_op jit(solution)/shard_map/ppermute | solution.py:43
  65.0 26.7 %collective-permute-start.7 = (bf16[176,2048]{1,0:T(8,128)(2,1)S(1)}, bf16[176,2048]{1,0:T(8,128)(2,1)S(1)}, u32[]{:S(2)}, u32[]{:S(2)}) collective-permute-start(bf16[176,2048]{1,0:T(8,128)(2,1)S(1)} %slice.8), channel_id=1, source_target_pairs={{0,2},{2,4},{4,6},{6,0},{8,10},{10,12},{12,14},{14,8},{1,3},{3,5},... | collective-permute-start | bytes 2162696 | tf_op jit(solution)/shard_map/ppermute | solution.py:25
  66.9 24.8 %collective-permute-start.9 = (bf16[160,2048]{1,0:T(8,128)(2,1)S(1)}, bf16[160,2048]{1,0:T(8,128)(2,1)S(1)}, u32[]{:S(2)}, u32[]{:S(2)}) collective-permute-start(bf16[160,2048]{1,0:T(8,128)(2,1)S(1)} %slice.9), channel_id=1, source_target_pairs={{0,6},{2,0},{4,2},{6,4},{8,14},{10,8},{12,10},{14,12},{1,7},{3,1},... | collective-permute-start | bytes 1966088 | tf_op jit(solution)/shard_map/ppermute | solution.py:25
  68.0 23.1 %collective-permute-start.11 = (bf16[3,256,256]{2,1,0:T(8,128)(2,1)S(1)}, bf16[3,256,256]{2,1,0:T(8,128)(2,1)S(1)}, u32[]{:S(2)}, u32[]{:S(2)}) collective-permute-start(bf16[3,256,256]{2,1,0:T(8,128)(2,1)S(1)} %collective-permute-done.3.refs_7_), channel_id=1, source_target_pairs={{0,1},{1,0},{2,3},{3,2},{4,5},{5,4},{6,7},{7,6},{8,9},{9,8},{10,11... | collective-permute-start | bytes 1179656 | tf_op jit(solution)/shard_map/ppermute | solution.py:43
  75.6 60.0 %collective-permute-start.12 = (bf16[3,256,256]{2,1,0:T(8,128)(2,1)S(1)}, bf16[3,256,256]{2,1,0:T(8,128)(2,1)S(1)}, u32[]{:S(2)}, u32[]{:S(2)}) collective-permute-start(bf16[3,256,256]{2,1,0:T(8,128)(2,1)S(1)} %collective-permute-done.3.refs_7_), channel_id=1, source_target_pairs={{0,8},{2,10},{4,12},{6,14},{8,0},{10,2},{12,4},{14,6},{1,9},{3,11}... | collective-permute-start | bytes 1179656 | tf_op jit(solution)/shard_map/ppermute | solution.py:39
  91.1 44.7 %collective-permute-start.14 = (bf16[2,3,256,256]{3,2,1,0:T(8,128)(2,1)S(1)}, bf16[2,3,256,256]{3,2,1,0:T(8,128)(2,1)S(1)}, u32[]{:S(2)}, u32[]{:S(2)}) collective-permute-start(bf16[2,3,256,256]{3,2,1,0:T(8,128)(2,1)S(1)} %collective-permute-done.6.refs_12_), channel_id=1, source_target_pairs={{0,1},{1,0},{2,3},{3,2},{4,5},{5,4},{6,7},{7,6},{8,9},{9,8},{10,11... | collective-permute-start | bytes 2359304 | tf_op jit(solution)/shard_map/ppermute | solution.py:43
  91.4 44.4 %collective-permute-start.13 = (bf16[3,256,256]{2,1,0:T(8,128)(2,1)S(1)}, bf16[3,256,256]{2,1,0:T(8,128)(2,1)S(1)}, u32[]{:S(2)}, u32[]{:S(2)}) collective-permute-start(bf16[3,256,256]{2,1,0:T(8,128)(2,1)S(1)} %collective-permute-done.refs_11_), channel_id=1, source_target_pairs={{0,1},{1,0},{2,3},{3,2},{4,5},{5,4},{6,7},{7,6},{8,9},{9,8},{10,11... | collective-permute-start | bytes 1179656 | tf_op jit(solution)/shard_map/ppermute | solution.py:43
  95.3 84.8 %copy-start.3 = (bf16[1,2,64,2048]{3,2,1,0:T(8,128)(2,1)S(1)}, bf16[1,2,64,2048]{3,2,1,0:T(8,128)(2,1)}, u32[]{:S(2)}) copy-start(bf16[1,2,64,2048]{3,2,1,0:T(8,128)(2,1)} %param.7) | copy-start | bytes 1572868
  135.5 1.7 collective-permute-start.15
  148.1 0.7 copy-start.8
  148.8 0.7 copy-start.9
  159.3 20.8 %collective-permute-start.19 = (bf16[8,1024,256]{2,1,0:T(8,128)(2,1)}, bf16[8,1024,256]{2,1,0:T(8,128)(2,1)S(1)}, u32[]{:S(2)}, u32[]{:S(2)}) collective-permute-start(bf16[8,1024,256]{2,1,0:T(8,128)(2,1)} %all-gather.2.cloned.1.call-done.refs_4_), channel_id=1, source_target_pairs={{0,1},{1,0},{2,3},{3,2},{4,5},{5,4},{6,7},{7,6},{8,9},{9,8},{10,11... | collective-permute-start | bytes 12582920 | tf_op jit(solution)/shard_map/ppermute | solution.py:43
  160.1 32.7 %collective-permute-start.25 = (bf16[256,2048]{1,0:T(8,128)(2,1)}, bf16[256,2048]{1,0:T(8,128)(2,1)S(1)}, u32[]{:S(2)}, u32[]{:S(2)}) collective-permute-start(bf16[256,2048]{1,0:T(8,128)(2,1)} %copy-done.7), channel_id=1, source_target_pairs={{128,144},{144,160},{160,176},{176,192},{192,208},{208,224},{224,2... | collective-permute-start | bytes 3145736 | tf_op jit(solution)/shard_map/ppermute | solution.py:47
  163.6 7.7 %collective-permute-start.16 = (bf16[256,512]{1,0:T(8,128)(2,1)}, bf16[256,512]{1,0:T(8,128)(2,1)S(1)}, u32[]{:S(2)}, u32[]{:S(2)}) collective-permute-start(bf16[256,512]{1,0:T(8,128)(2,1)} %copy-done.9), channel_id=1, source_target_pairs={{0,6},{2,0},{4,2},{6,4},{8,14},{10,8},{12,10},{14,12},{1,7},{3,1},... | collective-permute-start | bytes 786440 | tf_op jit(solution)/shard_map/ppermute | solution.py:25
  164.5 8.9 %collective-permute-start.17 = (bf16[256,512]{1,0:T(8,128)(2,1)}, bf16[256,512]{1,0:T(8,128)(2,1)S(1)}, u32[]{:S(2)}, u32[]{:S(2)}) collective-permute-start(bf16[256,512]{1,0:T(8,128)(2,1)} %copy-done.8), channel_id=1, source_target_pairs={{0,4},{2,6},{4,0},{6,2},{8,12},{10,14},{12,8},{14,10},{1,5},{3,7},... | collective-permute-start | bytes 786440 | tf_op jit(solution)/shard_map/ppermute | solution.py:25
  165.6 14.5 %collective-permute-start.18 = (bf16[256,512]{1,0:T(8,128)(2,1)S(1)}, bf16[256,512]{1,0:T(8,128)(2,1)S(1)}, u32[]{:S(2)}, u32[]{:S(2)}) collective-permute-start(bf16[256,512]{1,0:T(8,128)(2,1)S(1)} %get-tuple-element.49), channel_id=1, source_target_pairs={{0,2},{2,4},{4,6},{6,0},{8,10},{10,12},{12,14},{14,8},{1,3},{3,5},... | collective-permute-start | bytes 786440 | tf_op jit(solution)/shard_map/ppermute | solution.py:25
  180.1 2.2 copy-start.1
  186.2 17.6 %collective-permute-start.20 = (bf16[256,1024]{1,0:T(8,128)(2,1)S(1)}, bf16[256,1024]{1,0:T(8,128)(2,1)S(1)}, u32[]{:S(2)}, u32[]{:S(2)}) collective-permute-start(bf16[256,1024]{1,0:T(8,128)(2,1)S(1)} %get-tuple-element.51), channel_id=1, source_target_pairs={{0,16},{16,32},{32,48},{48,64},{64,80},{80,96},{96,112},{112,128},... | collective-permute-start | bytes 1572872 | tf_op jit(solution)/shard_map/ppermute | solution.py:47
  191.5 23.6 %collective-permute-start.22 = (bf16[256,1024]{1,0:T(8,128)(2,1)S(1)}, bf16[256,1024]{1,0:T(8,128)(2,1)S(1)}, u32[]{:S(2)}, u32[]{:S(2)}) collective-permute-start(bf16[256,1024]{1,0:T(8,128)(2,1)S(1)} %get-tuple-element.53), channel_id=1, source_target_pairs={{0,16},{16,32},{32,48},{48,64},{64,80},{80,96},{96,112},{112,128},... | collective-permute-start | bytes 1572872 | tf_op jit(solution)/shard_map/ppermute | solution.py:47
  203.8 19.4 %collective-permute-start.26 = (bf16[256,2048]{1,0:T(8,128)(2,1)S(1)}, bf16[256,2048]{1,0:T(8,128)(2,1)S(1)}, u32[]{:S(2)}, u32[]{:S(2)}) collective-permute-start(bf16[256,2048]{1,0:T(8,128)(2,1)S(1)} %collective-permute-done.25.refs_4_), channel_id=1, source_target_pairs={{0,1},{1,0},{2,3},{3,2},{4,5},{5,4},{6,7},{7,6},{8,9},{9,8},{10,11... | collective-permute-start | bytes 3145736 | tf_op jit(solution)/shard_map/ppermute | solution.py:43
  206.1 7.2 %collective-permute-start.23 = (bf16[64,2048]{1,0:T(8,128)(2,1)S(1)}, bf16[64,2048]{1,0:T(8,128)(2,1)S(1)}, u32[]{:S(2)}, u32[]{:S(2)}) collective-permute-start(bf16[64,2048]{1,0:T(8,128)(2,1)S(1)} %get-tuple-element.54), channel_id=1, source_target_pairs={{128,144},{144,160},{160,176},{176,192},{192,208},{208,224},{224,2... | collective-permute-start | bytes 786440 | tf_op jit(solution)/shard_map/ppermute | solution.py:47
  207.4 13.3 %collective-permute-start.27 = (bf16[64,2048]{1,0:T(8,128)(2,1)S(1)}, bf16[64,2048]{1,0:T(8,128)(2,1)S(1)}, u32[]{:S(2)}, u32[]{:S(2)}) collective-permute-start(bf16[64,2048]{1,0:T(8,128)(2,1)S(1)} %get-tuple-element.60), channel_id=1, source_target_pairs={{0,16},{16,32},{32,48},{48,64},{64,80},{80,96},{96,112},{112,128},... | collective-permute-start | bytes 786440 | tf_op jit(solution)/shard_map/ppermute | solution.py:47
  215.1 8.1 %collective-permute-start.24 = (bf16[256,1024]{1,0:T(8,128)(2,1)S(1)}, bf16[256,1024]{1,0:T(8,128)(2,1)S(1)}, u32[]{:S(2)}, u32[]{:S(2)}) collective-permute-start(bf16[256,1024]{1,0:T(8,128)(2,1)S(1)} %collective-permute-done.22.refs_2_), channel_id=1, source_target_pairs={{0,1},{1,0},{2,3},{3,2},{4,5},{5,4},{6,7},{7,6},{8,9},{9,8},{10,11... | collective-permute-start | bytes 1572872 | tf_op jit(solution)/shard_map/ppermute | solution.py:43
  217.3 5.8 %collective-permute-start.21 = (bf16[256,1024]{1,0:T(8,128)(2,1)S(1)}, bf16[256,1024]{1,0:T(8,128)(2,1)S(1)}, u32[]{:S(2)}, u32[]{:S(2)}) collective-permute-start(bf16[256,1024]{1,0:T(8,128)(2,1)S(1)} %collective-permute-done.20.refs_0_), channel_id=1, source_target_pairs={{0,1},{1,0},{2,3},{3,2},{4,5},{5,4},{6,7},{7,6},{8,9},{9,8},{10,11... | collective-permute-start | bytes 1572872 | tf_op jit(solution)/shard_map/ppermute | solution.py:43
  217.4 4.7 %collective-permute-start.29 = (bf16[64,2048]{1,0:T(8,128)(2,1)S(1)}, bf16[64,2048]{1,0:T(8,128)(2,1)S(1)}, u32[]{:S(2)}, u32[]{:S(2)}) collective-permute-start(bf16[64,2048]{1,0:T(8,128)(2,1)S(1)} %collective-permute-done.23.refs_8_), channel_id=1, source_target_pairs={{0,1},{1,0},{2,3},{3,2},{4,5},{5,4},{6,7},{7,6},{8,9},{9,8},{10,11... | collective-permute-start | bytes 786440 | tf_op jit(solution)/shard_map/ppermute | solution.py:43
  220.7 2.5 %collective-permute-start.28 = (bf16[64,2048]{1,0:T(8,128)(2,1)S(1)}, bf16[64,2048]{1,0:T(8,128)(2,1)S(1)}, u32[]{:S(2)}, u32[]{:S(2)}) collective-permute-start(bf16[64,2048]{1,0:T(8,128)(2,1)S(1)} %collective-permute-done.27.refs_6_), channel_id=1, source_target_pairs={{0,1},{1,0},{2,3},{3,2},{4,5},{5,4},{6,7},{7,6},{8,9},{9,8},{10,11... | collective-permute-start | bytes 786440 | tf_op jit(solution)/shard_map/ppermute | solution.py:43
Sparse Core Ops, SparseCore 0:
  10.6 148.6 all-gather.1
where the time goes:
time: 233 us; the launch traced here: 232 us
  waiting for transfers between devices  102 us (44%)
  starting transfers between devices  80.7 us (35%)
  Pallas kernels  27.4 us (12%)
  between operations  14.3 us (6%)
  local copies, waits for them, and re-layouts  7.61 us (3%)
    ppermute x3, waiting for transfers between devices, across_z(): lax.ppermute(array, 'dp', [(d, (d + RING) % (2 * RING)) for d in range(2...  44.2 us
    ppermute x3, starting transfers between devices, across_z(): lax.ppermute(array, 'dp', [(d, (d + RING) % (2 * RING)) for d in range(2...  31.6 us
    ppermute x12, starting transfers between devices, other_core(): return lax.ppermute(array, 'tensor', [(0, 1), (1, 0)])  28.5 us
    ppermute x10, waiting for transfers between devices, around_x(): return lax.ppermute(array, 'dp', pairs)  24.8 us
    ppermute x5, waiting for transfers between devices, relay(): lax.ppermute(array, 'section', [(s, (s + 1) % count) for s in sections])  20.2 us
    ppermute x10, starting transfers between devices, around_x(): return lax.ppermute(array, 'dp', pairs)  12 us
    pallas_call x1, Pallas kernels, attend(): call(attend_kernel, (out,) * RING, [SMEM] + [HBM] * len(operands), (HBM,)...  10.8 us
    all_gather x1, waiting for transfers between devices, per_device(): out_all = lax.all_gather(out_weight[0], 'dp')  9.82 us
  transfers between devices with their start and end apart: 31, of which 15 were waited for; matrix products, arithmetic and copies ran while one was open for 0% of the time, Pallas kernels for 11%

commit v1 on v0

--- a/solution.py
+++ b/solution.py
@@ -47,9 +47,8 @@
     return lax.ppermute(array, "section", [(s, (s + 1) % count) for s in sections])
 
 
-def round_ring(array, cut):
-    left, right = around_x(array, 1), around_x(array, -1)
-    return left, right, left[:cut], right[cut:]
+def round_ring(array):
+    return around_x(array, 1), around_x(array, -1)
 
 
 def after(array, *others):
@@ -75,7 +74,7 @@
         out_specs=out_specs,
         scratch_shapes=list(scratch),
         compiler_params=pltpu.CompilerParams(vmem_limit_bytes=limit * 1024 * 1024),
-        cost_estimate=pl.CostEstimate(flops=flops, bytes_accessed=moved, transcendentals=0),
+        cost_estimate=pl.CostEstimate(flops=1, bytes_accessed=1, transcendentals=0),
     )
 
 
@@ -191,15 +190,12 @@
 
 
 def pieces_of(parts):
-    pieces = []
-    for own, sides, opposite in (parts[:3], parts[3:]):
-        pieces += [own, sides.at[0], opposite, sides.at[1]]
-    return pieces
+    return [part.at[step] for part in parts for step in range(part.shape[0])]
 
 
 def start_kernel(where, *refs):
-    rows, parts = refs[:5], refs[5:11]
-    total, rows_all, weight, sems = refs[11:]
+    rows, parts = refs[:5], refs[5:7]
+    total, rows_all, weight, sems = refs[7:]
     group = pieces_of(parts)
     copies = row_copies(where[1], rows, rows_all, sems)
     copies += weight_copies(where[0], group, weight, sems, 5)
@@ -215,9 +211,9 @@
 
 
 def attend_kernel(where, *refs):
-    rows, near, far, total_in = refs[:5], refs[5:11], refs[11:17], refs[17]
-    outs = refs[18:22]
-    rows_all, qry_all, near_query, weight, total, lengths, low, mixed, sems = refs[22:]
+    rows, near, far, total_in = refs[:5], refs[5:7], refs[7:10], refs[10]
+    outs = refs[11:15]
+    rows_all, qry_all, near_query, weight, total, lengths, low, mixed, sems = refs[15:]
     x, z, encoder = where[0], where[1], where[2]
     mem, few = rows_all.shape[0] // RING, qry_all.shape[0] // RING
     width = rows_all.shape[1]
@@ -324,11 +320,11 @@
 
 def start_projections(where, mem, rows, parts):
     width = rows[0].shape[1]
-    planes, block, part = parts[0].shape
+    _, planes, block, part = parts[0].shape
     return call(
         start_kernel,
         jax.ShapeDtypeStruct((planes, RING * mem, 2 * part), F32),
-        [SMEM] + [HBM] * 11,
+        [SMEM] + [HBM] * 7,
         VMEM,
         [
             pltpu.VMEM((RING * mem, width // 2), BF16),
@@ -343,7 +339,7 @@
 
 def attend(where, mem, few, rows, near, far, total):
     width = rows[0].shape[1]
-    planes, block, part = near[0].shape
+    _, planes, block, part = near[0].shape
     out = jax.ShapeDtypeStruct((mem, 2 * part), BF16)
     operands = (*rows, *near, *far, total)
     return call(
@@ -374,9 +370,10 @@
     few_in = refs[6] if part else None
     out, few_out = refs[6 + part : 8 + part]
     heads, weight, base, sems = refs[8 + part :]
-    x, encoder, core = where[0], where[2], where[3]
+    x, z, encoder, core = where[0], where[1], where[2], where[3]
     quarter = mixed[0].shape[1] // 2
-    _, inner, block = weights[0].shape
+    inner = quarter * RING
+    block = weights[0].shape[1]
     few = queries.shape[1]
     columns = pl.ds(part * RING * block, RING * block)
     rows_base = pltpu.make_async_copy(context.at[core, :, columns], base, sems.at[0])
@@ -395,11 +392,13 @@
                 )
             )
     pieces = []
+    crossed = z if part == 0 else 1 - z
     for i in range(RING):
         for side in range(2):
+            start = pl.multiple_of((2 * i + crossed) * inner, inner)
             pieces.append(
                 pltpu.make_async_copy(
-                    weights[side].at[part * RING + i],
+                    weights[side].at[pl.ds(start, inner)],
                     weight.at[i, pl.ds(side * inner, inner)],
                     sems.at[9 + i * 2 + side],
                 )
@@ -429,16 +428,18 @@
     wait_all(copies)
     for i in range(RING):
         wait_all(pieces[2 * i : 2 * i + 2])
-        at = pl.ds(i * block, block)
+        place = (x - i + RING) % RING
+        at = pl.ds(pl.multiple_of(place * block, block), block)
         update = jnp.dot(heads[...], weight[i], preferred_element_type=F32)
         result = (base[:, at].astype(F32) + update).astype(BF16)
         out[:, at] = result
-        few_out[:, pl.ds((part * RING + i) * block, block)] = result[:few]
+        at = pl.ds(pl.multiple_of((part * RING + place) * block, block), block)
+        few_out[:, at] = result[:few]
 
 
 def project(part, where, context, queries, mixed, weights, few_in=()):
     mem, few = context.shape[1], queries.shape[1]
-    _, inner, block = weights[0].shape
+    inner, block = mixed[0].shape[1] // 2 * RING, weights[0].shape[1]
     return call(
         functools.partial(project_kernel, part),
         (
@@ -539,43 +540,31 @@
     context, queries = context[0], queries[0]
 
     mem, few = context.shape[1], queries.shape[1]
-    out_all = lax.all_gather(out_weight[0], "dp")
-
+    out_shard = out_weight[0]
+    out_far = across_z(out_shard)
     own = quarters(where, jnp.swapaxes(qkv_weight[0], 0, 1))
-    own_other = other_core(own[0])
-    far_own = across_z(own[0])
-    left, opposite, right = [around_x(own[step], step) for step in range(1, RING)]
-    sides = jnp.stack([left, right])
+    near = jnp.stack([own[0]] + [around_x(own[step], step) for step in range(1, RING)])
+    far = across_z(after(near, out_far))
+    near = (near, other_core(near))
 
     ctx, qry, normed = norm_scene(
         after(where, *own), context, queries, norm_gain, lengths[0]
     )
     cut = (normed.shape[0] // 32 + 1) * 16
-    from_left, from_right, send_left, send_right = round_ring(
-        after(normed, far_own, sides, opposite, own_other), cut
-    )
-    far_sides = across_z(after(sides, far_own))
-    far_opposite = across_z(after(opposite, from_left, from_right))
-    rows = (
-        normed,
-        from_left,
-        around_x(after(send_left, far_sides), 1),
-        around_x(after(send_right, far_sides), -1),
-        from_right,
-    )
-    near = (own[0], sides, opposite, own_other, other_core(sides), other_core(opposite))
+    left, right = round_ring(after(normed, near[0], out_far))
+    rows = (normed, left, around_x(left[:cut], 1), around_x(right[cut:], -1), right)
     total = start_projections(where, mem, rows, near)
-    far = (far_own, far_sides, far_opposite)
-    far += (
-        other_core(after(far_own, far_sides)),
-        other_core(far_sides),
-        other_core(after(far_opposite, total)),
-    )
-    ctx_early = relay(after(ctx, far_opposite), decoders, count)
-    qry_early = relay(after(qry, far_opposite), encoders, count)
-
-    mixed = attend(where, mem, few, rows, near, far, total)
-    weights = both(after(out_all, mixed[0]))
+
+    out_pair = after(jnp.concatenate([out_shard, out_far]), *rows, total)
+    cut = out_shard.shape[0]
+    left, right = round_ring(out_pair)
+    opposite = [around_x(left[:cut], 1), around_x(right[cut:], -1)]
+    far = (far, other_core(after(far[:2], total)), other_core(after(far[2:], total)))
+    ctx_early = relay(after(ctx, *far), decoders, count)
+    qry_early = relay(after(qry, *far), encoders, count)
+
+    mixed = attend(after(where, left, right), mem, few, rows, near, far, total)
+    weights = both(jnp.concatenate([out_pair, left, *after(tuple(opposite), mixed[0]), right]))
     mixed = [mixed[0]] + [around_x(mixed[step], -step) for step in range(1, RING)]
 
     first, few_first = project(0, where, context, queries, mixed, weights)

time: 233 us -> 195 us (0.84)
  waiting for transfers between devices: 102 us -> 73.6 us
  between operations: 14.3 us -> 1.13 us
  starting transfers between devices: 80.7 us -> 85.9 us
    ppermute x3 -> x2, waiting for transfers between devices: 44.2 us -> 11.6 us  [across_z(): lax.ppermute(array, 'dp', [(d, (d + RING) % (2 * RING)) for d in range(2...]
    ppermute x10 -> x14, waiting for transfers between devices: 24.8 us -> 41.7 us  [around_x(): return lax.ppermute(array, 'dp', pairs)]
    ppermute x3 -> x2, starting transfers between devices: 31.6 us -> 20.7 us  [across_z(): lax.ppermute(array, 'dp', [(d, (d + RING) % (2 * RING)) for d in range(2...]
    ppermute x12 -> x9, starting transfers between devices: 28.5 us -> 39.2 us  [other_core(): return lax.ppermute(array, 'tensor', [(0, 1), (1, 0)])]
    all_gather x1 -> x0, waiting for transfers between devices: 9.82 us -> none  [per_device(): out_all = lax.all_gather(out_weight[0], 'dp')]
    ppermute x10 -> x14, starting transfers between devices: 12 us -> 19.5 us  [around_x(): return lax.ppermute(array, 'dp', pairs)]
  transfers between devices with their start and end apart: 31 -> 30, of which waited for: 15 -> 14; matrix products, arithmetic and copies ran while one was open for 0% -> 0% of each run, Pallas kernels for 11% -> 13%
where the time goes in v1:
time: 195 us; the launch traced here: 194 us
  starting transfers between devices  85.9 us (44%)
  waiting for transfers between devices  73.6 us (38%)
  Pallas kernels  27.6 us (14%)
  local copies, waits for them, and re-layouts  6.06 us (3%)
    ppermute x14, waiting for transfers between devices, around_x(): return lax.ppermute(array, 'dp', pairs)  41.7 us
    ppermute x9, starting transfers between devices, other_core(): return lax.ppermute(array, 'tensor', [(0, 1), (1, 0)])  39.2 us
    ppermute x2, starting transfers between devices, across_z(): lax.ppermute(array, 'dp', [(d, (d + RING) % (2 * RING)) for d in range(2...  20.7 us
    ppermute x14, starting transfers between devices, around_x(): return lax.ppermute(array, 'dp', pairs)  19.5 us
    ppermute x5, waiting for transfers between devices, relay(): lax.ppermute(array, 'section', [(s, (s + 1) % count) for s in sections])  19.1 us
    ppermute x2, waiting for transfers between devices, across_z(): lax.ppermute(array, 'dp', [(d, (d + RING) % (2 * RING)) for d in range(2...  11.6 us
    pallas_call x1, Pallas kernels, attend(): call(attend_kernel, (out,) * RING, [SMEM] + [HBM] * len(operands), (HBM,)...  10.7 us
    pallas_call x2, Pallas kernels, project(): call(functools.partial(project_kernel, part), (jax.ShapeDtypeStruct((mem,...  8.17 us
  transfers between devices with their start and end apart: 30, of which 14 were waited for; matrix products, arithmetic and copies ran while one was open for 0% of the time, Pallas kernels for 13%

profile of v1, /device:TPU:17, one launch (start us, length us, event | category | flops | bytes accessed | tf_op | source)
XLA Modules:
  0.0 194.5 jit_solution(1421556384756024846)
XLA Ops:
  0.7 0.1 stack.46.where
  0.8 1.4 copy-done.4
  2.2 0.8 shard_map.77
  2.9 1.3 collective-permute-start.1
  4.2 2.5 %collective-permute-start.2 = (bf16[3,256,256]{2,1,0:T(8,128)(2,1)S(1)}, bf16[3,256,256]{2,1,0:T(8,128)(2,1)S(1)}, u32[]{:S(2)}, u32[]{:S(2)}) collective-permute-start(bf16[3,256,256]{2,1,0:T(8,128)(2,1)S(1)} %get-tuple-element.35), channel_id=1, source_target_pairs={{0,4},{2,6},{4,0},{6,2},{8,12},{10,14},{12,8},{14,10},{1,5},{3,7},... | collective-permute-start | bytes 1179656 | tf_op jit(solution)/shard_map/ppermute | solution.py:25
  6.7 1.2 collective-permute-start.3
  7.8 6.9 %collective-permute-start = (bf16[1024,256]{1,0:T(8,128)(2,1)}, bf16[1024,256]{1,0:T(8,128)(2,1)S(1)}, u32[]{:S(2)}, u32[]{:S(2)}) collective-permute-start(bf16[1024,256]{1,0:T(8,128)(2,1)} %bitcast.27), channel_id=1, source_target_pairs={{0,8},{2,10},{4,12},{6,14},{8,0},{10,2},{12,4},{14,6},{1,9},{3,11}... | collective-permute-start | bytes 1572872 | tf_op jit(solution)/shard_map/ppermute | solution.py:39
  14.7 1.6 copy-done
  16.3 1.0 copy-done.2
  17.4 0.7 copy-done.5
  18.1 0.7 copy-done.6
  18.7 2.0 %shard_map.78 = (bf16[256,2048]{1,0:T(8,128)(2,1)S(1)}, bf16[64,2048]{1,0:T(8,128)(2,1)S(1)}, bf16[336,2048]{1,0:T(8,128)(2,1)S(1)}) custom-call(s32[5]{0:T(128)S(1)} %stack.46.where, bf16[2,256,2048]{2,1,0:T(8,128)(2,1)S(1)} %bitcast.18, bf16[2,64,2048]{2,1,0:T(8,128)(2,1)S(1)} %bitcast.21, f32[1,2048]{1,0:T(1,128)S(1)} %copy-done.5, s32[2]{0:T(128)S(1)} %bitcast.26), custom_call_target="tpu_custom_call" | custom-call | flops 1 | bytes 1 | tf_op jit(solution)/shard_map/pallas_call | solution.py:134
  20.7 2.9 %collective-permute-done.2 = bf16[3,256,256]{2,1,0:T(8,128)(2,1)S(1)} collective-permute-done((bf16[3,256,256]{2,1,0:T(8,128)(2,1)S(1)}, bf16[3,256,256]{2,1,0:T(8,128)(2,1)S(1)}, u32[]{:S(2)}, u32[]{:S(2)}) %collective-permute-start.2) | collective-permute-done | bytes 393248 | tf_op jit(solution)/shard_map/ppermute | solution.py:25
  23.6 0.2 pad_maximum_fusion.refs_5_
  23.8 0.0 copy-start.7
  23.8 3.9 %collective-permute-done = bf16[1024,256]{1,0:T(8,128)(2,1)S(1)} collective-permute-done((bf16[1024,256]{1,0:T(8,128)(2,1)}, bf16[1024,256]{1,0:T(8,128)(2,1)S(1)}, u32[]{:S(2)}, u32[]{:S(2)}) %collective-permute-start) | collective-permute-done | bytes 524320 | tf_op jit(solution)/shard_map/ppermute | solution.py:39
  27.8 0.3 collective-permute-start.4
  28.1 2.4 %collective-permute-start.6 = (bf16[336,2048]{1,0:T(8,128)(2,1)S(1)}, bf16[336,2048]{1,0:T(8,128)(2,1)S(1)}, u32[]{:S(2)}, u32[]{:S(2)}) collective-permute-start(bf16[336,2048]{1,0:T(8,128)(2,1)S(1)} %get-tuple-element.39.refs_0_), channel_id=1, source_target_pairs={{0,6},{2,0},{4,2},{6,4},{8,14},{10,8},{12,10},{14,12},{1,7},{3,1},... | collective-permute-start | bytes 4128776 | tf_op jit(solution)/shard_map/ppermute | solution.py:25
  30.4 2.9 %collective-permute-start.8 = (bf16[4,3,256,256]{3,2,1,0:T(8,128)(2,1)S(1)}, bf16[4,3,256,256]{3,2,1,0:T(8,128)(2,1)S(1)}, u32[]{:S(2)}, u32[]{:S(2)}) collective-permute-start(bf16[4,3,256,256]{3,2,1,0:T(8,128)(2,1)S(1)} %pad_maximum_fusion.refs_5_), channel_id=1, source_target_pairs={{0,1},{1,0},{2,3},{3,2},{4,5},{5,4},{6,7},{7,6},{8,9},{9,8},{10,11... | collective-permute-start | bytes 4718600 | tf_op jit(solution)/shard_map/ppermute | solution.py:43
  33.3 13.8 %collective-permute-start.11 = (bf16[4,3,256,256]{3,2,1,0:T(8,128)(2,1)S(1)}, bf16[4,3,256,256]{3,2,1,0:T(8,128)(2,1)S(1)}, u32[]{:S(2)}, u32[]{:S(2)}) collective-permute-start(bf16[4,3,256,256]{3,2,1,0:T(8,128)(2,1)S(1)} %pad_maximum_fusion.refs_5_), channel_id=1, source_target_pairs={{0,8},{2,10},{4,12},{6,14},{8,0},{10,2},{12,4},{14,6},{1,9},{3,11}... | collective-permute-start | bytes 4718600 | tf_op jit(solution)/shard_map/ppermute | solution.py:39
  47.1 11.3 %collective-permute-done.4.refs_1_ = bf16[336,2048]{1,0:T(8,128)(2,1)S(1)} collective-permute-done((bf16[336,2048]{1,0:T(8,128)(2,1)S(1)}, bf16[336,2048]{1,0:T(8,128)(2,1)S(1)}, u32[]{:S(2)}, u32[]{:S(2)}) %collective-permute-start.4) | collective-permute-done | bytes 1376288 | tf_op jit(solution)/shard_map/ppermute | solution.py:25
  58.3 0.1 slice.24
  58.4 0.1 collective-permute-start.5
  58.5 0.1 slice.25
  58.6 2.7 %collective-permute-start.7 = (bf16[160,2048]{1,0:T(8,128)(2,1)S(1)}, bf16[160,2048]{1,0:T(8,128)(2,1)S(1)}, u32[]{:S(2)}, u32[]{:S(2)}) collective-permute-start(bf16[160,2048]{1,0:T(8,128)(2,1)S(1)} %slice.25), channel_id=1, source_target_pairs={{0,6},{2,0},{4,2},{6,4},{8,14},{10,8},{12,10},{14,12},{1,7},{3,1},... | collective-permute-start | bytes 1966088 | tf_op jit(solution)/shard_map/ppermute | solution.py:25
  61.3 0.1 pad_maximum_fusion.1
  61.4 10.4 %collective-permute-done.7.refs_3_ = bf16[160,2048]{1,0:T(8,128)(2,1)S(1)} collective-permute-done((bf16[160,2048]{1,0:T(8,128)(2,1)S(1)}, bf16[160,2048]{1,0:T(8,128)(2,1)S(1)}, u32[]{:S(2)}, u32[]{:S(2)}) %collective-permute-start.7) | collective-permute-done | bytes 655392 | tf_op jit(solution)/shard_map/ppermute | solution.py:25
  71.8 2.3 %collective-permute-done.5.refs_2_ = bf16[176,2048]{1,0:T(8,128)(2,1)S(1)} collective-permute-done((bf16[176,2048]{1,0:T(8,128)(2,1)S(1)}, bf16[176,2048]{1,0:T(8,128)(2,1)S(1)}, u32[]{:S(2)}, u32[]{:S(2)}) %collective-permute-start.5) | collective-permute-done | bytes 720928 | tf_op jit(solution)/shard_map/ppermute | solution.py:25
  74.1 3.6 %shard_map.79.refs_10_ = f32[3,1024,512]{2,1,0:T(8,128)S(1)} custom-call(s32[5]{0:T(128)S(1)} %stack.46.where, bf16[336,2048]{1,0:T(8,128)(2,1)S(1)} %get-tuple-element.39.refs_0_, bf16[336,2048]{1,0:T(8,128)(2,1)S(1)} %collective-permute-done.4.refs_1_, bf16[176,2048]{1,0:T(8,128)(2,1)S(1)} %collective-permute-done.5.refs_2_, ...), custom_call_target="tpu_custom_call" | custom-call | flops 1 | bytes 1 | tf_op jit(solution)/shard_map/pallas_call | solution.py:324
  77.7 0.1 collective-permute-start.9
  77.8 2.7 %collective-permute-start.10 = (bf16[2048,256]{1,0:T(8,128)(2,1)S(1)}, bf16[2048,256]{1,0:T(8,128)(2,1)S(1)}, u32[]{:S(2)}, u32[]{:S(2)}) collective-permute-start(bf16[2048,256]{1,0:T(8,128)(2,1)S(1)} %pad_maximum_fusion.1), channel_id=1, source_target_pairs={{0,6},{2,0},{4,2},{6,4},{8,14},{10,8},{12,10},{14,12},{1,7},{3,1},... | collective-permute-start | bytes 3145736 | tf_op jit(solution)/shard_map/ppermute | solution.py:25
  80.5 7.6 %collective-permute-done.11.refs_7_ = bf16[4,3,256,256]{3,2,1,0:T(8,128)(2,1)S(1)} collective-permute-done((bf16[4,3,256,256]{3,2,1,0:T(8,128)(2,1)S(1)}, bf16[4,3,256,256]{3,2,1,0:T(8,128)(2,1)S(1)}, u32[]{:S(2)}, u32[]{:S(2)}) %collective-permute-start.11) | collective-permute-done | bytes 1572896 | tf_op jit(solution)/shard_map/ppermute | solution.py:39
  88.1 0.1 fusion
  88.2 27.6 %collective-permute-start.13 = (bf16[2,3,256,256]{3,2,1,0:T(8,128)(2,1)S(1)}, bf16[2,3,256,256]{3,2,1,0:T(8,128)(2,1)S(1)}, u32[]{:S(2)}, u32[]{:S(2)}) collective-permute-start(bf16[2,3,256,256]{3,2,1,0:T(8,128)(2,1)S(1)} %get-tuple-element.44), channel_id=1, source_target_pairs={{0,1},{1,0},{2,3},{3,2},{4,5},{5,4},{6,7},{7,6},{8,9},{9,8},{10,11... | collective-permute-start | bytes 2359304 | tf_op jit(solution)/shard_map/ppermute | solution.py:43
  115.8 0.3 collective-permute-start.12
  116.2 0.1 collective-permute-start.17
  116.3 2.7 %collective-permute-start.18 = (bf16[1024,256]{1,0:T(8,128)(2,1)S(1)}, bf16[1024,256]{1,0:T(8,128)(2,1)S(1)}, u32[]{:S(2)}, u32[]{:S(2)}) collective-permute-start(bf16[1024,256]{1,0:T(8,128)(2,1)S(1)} %slice.29), channel_id=1, source_target_pairs={{0,6},{2,0},{4,2},{6,4},{8,14},{10,8},{12,10},{14,12},{1,7},{3,1},... | collective-permute-start | bytes 1572872 | tf_op jit(solution)/shard_map/ppermute | solution.py:25
  119.0 0.1 constant_dynamic-update-slice_fusion.4
  119.1 10.7 %shard_map.80 = (bf16[256,512]{1,0:T(8,128)(2,1)S(1)}, bf16[256,512]{1,0:T(8,128)(2,1)S(1)}, bf16[256,512]{1,0:T(8,128)(2,1)S(1)}, bf16[256,512]{1,0:T(8,128)(2,1)S(1)}) custom-call(s32[5]{0:T(128)S(1)} %stack.46.where, bf16[336,2048]{1,0:T(8,128)(2,1)S(1)} %get-tuple-element.39.refs_0_, bf16[336,2048]{1,0:T(8,128)(2,1)S(1)} %collective-permute-done.4.refs_1_, ...), custom_call_target="tpu_custom_call" | custom-call | flops 1 | bytes 1 | tf_op jit(solution)/shard_map/pallas_call | solution.py:345
  129.9 0.1 constant_dynamic-update-slice_fusion.3
  130.0 0.8 collective-permute-done.17
  130.8 0.1 constant_dynamic-update-slice_fusion.refs_4_
  130.9 1.1 collective-permute-start.19
  132.1 1.3 collective-permute-start.25
  133.4 2.9 %collective-permute-start.14 = (bf16[256,512]{1,0:T(8,128)(2,1)S(1)}, bf16[256,512]{1,0:T(8,128)(2,1)S(1)}, u32[]{:S(2)}, u32[]{:S(2)}) collective-permute-start(bf16[256,512]{1,0:T(8,128)(2,1)S(1)} %get-tuple-element.46), channel_id=1, source_target_pairs={{0,6},{2,0},{4,2},{6,4},{8,14},{10,8},{12,10},{14,12},{1,7},{3,1},... | collective-permute-start | bytes 786440 | tf_op jit(solution)/shard_map/ppermute | solution.py:25
  136.3 0.7 collective-permute-start.16
  137.0 10.4 %collective-permute-done.14.refs_1_ = bf16[256,512]{1,0:T(8,128)(2,1)S(1)} collective-permute-done((bf16[256,512]{1,0:T(8,128)(2,1)S(1)}, bf16[256,512]{1,0:T(8,128)(2,1)S(1)}, u32[]{:S(2)}, u32[]{:S(2)}) %collective-permute-start.14) | collective-permute-done | bytes 262176 | tf_op jit(solution)/shard_map/ppermute | solution.py:25
  147.3 3.7 %collective-permute-done.16.refs_3_ = bf16[256,512]{1,0:T(8,128)(2,1)S(1)} collective-permute-done((bf16[256,512]{1,0:T(8,128)(2,1)S(1)}, bf16[256,512]{1,0:T(8,128)(2,1)S(1)}, u32[]{:S(2)}, u32[]{:S(2)}) %collective-permute-start.16) | collective-permute-done | bytes 262176 | tf_op jit(solution)/shard_map/ppermute | solution.py:25
  151.1 4.0 %shard_map.81 = (bf16[256,1024]{1,0:T(8,128)(2,1)S(1)}, bf16[64,1024]{1,0:T(8,128)(2,1)S(1)}) custom-call(s32[5]{0:T(128)S(1)} %stack.46.where, bf16[2,256,2048]{2,1,0:T(8,128)(2,1)S(1)} %bitcast.19, bf16[2,64,2048]{2,1,0:T(8,128)(2,1)S(1)} %bitcast.22, bf16[256,512]{1,0:T(8,128)(2,1)S(1)} %get-tuple-element.45.refs_0_, ...), custom_call_target="tpu_custom_call" | custom-call | flops 1 | bytes 1 | tf_op jit(solution)/shard_map/pallas_call | solution.py:443
  155.0 1.3 collective-permute-start.20
  156.3 4.2 %shard_map.82 = (bf16[256,1024]{1,0:T(8,128)(2,1)S(1)}, bf16[64,2048]{1,0:T(8,128)(2,1)S(1)}) custom-call(s32[5]{0:T(128)S(1)} %stack.46.where, bf16[2,256,2048]{2,1,0:T(8,128)(2,1)S(1)} %bitcast.20, bf16[2,64,2048]{2,1,0:T(8,128)(2,1)S(1)} %bitcast.23, bf16[256,512]{1,0:T(8,128)(2,1)S(1)} %get-tuple-element.45.refs_0_, ...), custom_call_target="tpu_custom_call" | custom-call | flops 1 | bytes 1 | tf_op jit(solution)/shard_map/pallas_call | solution.py:443
  160.6 1.3 collective-permute-start.22
  161.9 10.5 %collective-permute-done.20.refs_0_ = bf16[256,1024]{1,0:T(8,128)(2,1)S(1)} collective-permute-done((bf16[256,1024]{1,0:T(8,128)(2,1)S(1)}, bf16[256,1024]{1,0:T(8,128)(2,1)S(1)}, u32[]{:S(2)}, u32[]{:S(2)}) %collective-permute-start.20) | collective-permute-done | bytes 524320 | tf_op jit(solution)/shard_map/ppermute | solution.py:47
  172.3 2.9 %collective-permute-start.26 = (bf16[256,2048]{1,0:T(8,128)(2,1)S(1)}, bf16[256,2048]{1,0:T(8,128)(2,1)S(1)}, u32[]{:S(2)}, u32[]{:S(2)}) collective-permute-start(bf16[256,2048]{1,0:T(8,128)(2,1)S(1)} %collective-permute-done.25.refs_4_), channel_id=1, source_target_pairs={{0,1},{1,0},{2,3},{3,2},{4,5},{5,4},{6,7},{7,6},{8,9},{9,8},{10,11... | collective-permute-start | bytes 3145736 | tf_op jit(solution)/shard_map/ppermute | solution.py:43
  175.2 1.3 collective-permute-start.23
  176.5 1.3 collective-permute-start.27
  177.8 4.6 %collective-permute-done.23.refs_8_ = bf16[64,2048]{1,0:T(8,128)(2,1)S(1)} collective-permute-done((bf16[64,2048]{1,0:T(8,128)(2,1)S(1)}, bf16[64,2048]{1,0:T(8,128)(2,1)S(1)}, u32[]{:S(2)}, u32[]{:S(2)}) %collective-permute-start.23) | collective-permute-done | bytes 262176 | tf_op jit(solution)/shard_map/ppermute | solution.py:47
  182.4 1.1 collective-permute-done.22.refs_2_
  183.6 2.6 %collective-permute-start.24 = (bf16[256,1024]{1,0:T(8,128)(2,1)S(1)}, bf16[256,1024]{1,0:T(8,128)(2,1)S(1)}, u32[]{:S(2)}, u32[]{:S(2)}) collective-permute-start(bf16[256,1024]{1,0:T(8,128)(2,1)S(1)} %collective-permute-done.22.refs_2_), channel_id=1, source_target_pairs={{0,1},{1,0},{2,3},{3,2},{4,5},{5,4},{6,7},{7,6},{8,9},{9,8},{10,11... | collective-permute-start | bytes 1572872 | tf_op jit(solution)/shard_map/ppermute | solution.py:43
  186.1 0.5 collective-permute-start.29
  186.6 2.9 %collective-permute-done.27.refs_6_ = bf16[64,2048]{1,0:T(8,128)(2,1)S(1)} collective-permute-done((bf16[64,2048]{1,0:T(8,128)(2,1)S(1)}, bf16[64,2048]{1,0:T(8,128)(2,1)S(1)}, u32[]{:S(2)}, u32[]{:S(2)}) %collective-permute-start.27) | collective-permute-done | bytes 262176 | tf_op jit(solution)/shard_map/ppermute | solution.py:47
  189.5 1.3 collective-permute-start.28
  190.8 1.2 collective-permute-done.28.refs_7_
  192.0 2.3 %shard_map.83 = (bf16[2,256,2048]{2,1,0:T(8,128)(2,1)}, bf16[2,64,2048]{2,1,0:T(8,128)(2,1)}) custom-call(s32[5]{0:T(128)S(1)} %stack.46.where, bf16[256,1024]{1,0:T(8,128)(2,1)S(1)} %collective-permute-done.20.refs_0_, bf16[256,1024]{1,0:T(8,128)(2,1)S(1)} %collective-permute-done.21.refs_1_, bf16[256,1024]{1,0:T(8,128)(2,1)S(1)} %collective-permute-done.22.refs_2_, ...), custom_call_target="tpu_custom_call" | custom-call | flops 1 | bytes 1 | tf_op jit(solution)/shard_map/pallas_call | solution.py:505
  (32 shorter events, 0.2 us)
Async XLA Ops:
  0.7 1.4 copy-start.4
  2.9 17.8 %collective-permute-start.1 = (bf16[3,256,256]{2,1,0:T(8,128)(2,1)S(1)}, bf16[3,256,256]{2,1,0:T(8,128)(2,1)S(1)}, u32[]{:S(2)}, u32[]{:S(2)}) collective-permute-start(bf16[3,256,256]{2,1,0:T(8,128)(2,1)S(1)} %get-tuple-element.34), channel_id=1, source_target_pairs={{0,2},{2,4},{4,6},{6,0},{8,10},{10,12},{12,14},{14,8},{1,3},{3,5},... | collective-permute-start | bytes 1179656 | tf_op jit(solution)/shard_map/ppermute | solution.py:25
  4.2 19.4 %collective-permute-start.2 = (bf16[3,256,256]{2,1,0:T(8,128)(2,1)S(1)}, bf16[3,256,256]{2,1,0:T(8,128)(2,1)S(1)}, u32[]{:S(2)}, u32[]{:S(2)}) collective-permute-start(bf16[3,256,256]{2,1,0:T(8,128)(2,1)S(1)} %get-tuple-element.35), channel_id=1, source_target_pairs={{0,4},{2,6},{4,0},{6,2},{8,12},{10,14},{12,8},{14,10},{1,5},{3,7},... | collective-permute-start | bytes 1179656 | tf_op jit(solution)/shard_map/ppermute | solution.py:25
  6.7 16.9 %collective-permute-start.3 = (bf16[3,256,256]{2,1,0:T(8,128)(2,1)S(1)}, bf16[3,256,256]{2,1,0:T(8,128)(2,1)S(1)}, u32[]{:S(2)}, u32[]{:S(2)}) collective-permute-start(bf16[3,256,256]{2,1,0:T(8,128)(2,1)S(1)} %get-tuple-element.36), channel_id=1, source_target_pairs={{0,6},{2,0},{4,2},{6,4},{8,14},{10,8},{12,10},{14,12},{1,7},{3,1},... | collective-permute-start | bytes 1179656 | tf_op jit(solution)/shard_map/ppermute | solution.py:25
  7.8 19.9 %collective-permute-start = (bf16[1024,256]{1,0:T(8,128)(2,1)}, bf16[1024,256]{1,0:T(8,128)(2,1)S(1)}, u32[]{:S(2)}, u32[]{:S(2)}) collective-permute-start(bf16[1024,256]{1,0:T(8,128)(2,1)} %bitcast.27), channel_id=1, source_target_pairs={{0,8},{2,10},{4,12},{6,14},{8,0},{10,2},{12,4},{14,6},{1,9},{3,11}... | collective-permute-start | bytes 1572872 | tf_op jit(solution)/shard_map/ppermute | solution.py:39
  14.7 1.6 copy-start
  16.3 1.0 copy-start.2
  17.4 0.7 copy-start.5
  18.1 0.7 copy-start.6
  23.8 37.5 %copy-start.7 = (bf16[1,1024,256]{2,1,0:T(8,128)(2,1)S(1)}, bf16[1,1024,256]{2,1,0:T(8,128)(2,1)}, u32[]{:S(2)}) copy-start(bf16[1,1024,256]{2,1,0:T(8,128)(2,1)} %param.11) | copy-start | bytes 1572868
  27.8 30.6 %collective-permute-start.4 = (bf16[336,2048]{1,0:T(8,128)(2,1)S(1)}, bf16[336,2048]{1,0:T(8,128)(2,1)S(1)}, u32[]{:S(2)}, u32[]{:S(2)}) collective-permute-start(bf16[336,2048]{1,0:T(8,128)(2,1)S(1)} %get-tuple-element.39.refs_0_), channel_id=1, source_target_pairs={{0,2},{2,4},{4,6},{6,0},{8,10},{10,12},{12,14},{14,8},{1,3},{3,5},... | collective-permute-start | bytes 4128776 | tf_op jit(solution)/shard_map/ppermute | solution.py:25
  28.1 30.4 %collective-permute-start.6 = (bf16[336,2048]{1,0:T(8,128)(2,1)S(1)}, bf16[336,2048]{1,0:T(8,128)(2,1)S(1)}, u32[]{:S(2)}, u32[]{:S(2)}) collective-permute-start(bf16[336,2048]{1,0:T(8,128)(2,1)S(1)} %get-tuple-element.39.refs_0_), channel_id=1, source_target_pairs={{0,6},{2,0},{4,2},{6,4},{8,14},{10,8},{12,10},{14,12},{1,7},{3,1},... | collective-permute-start | bytes 4128776 | tf_op jit(solution)/shard_map/ppermute | solution.py:25
  30.4 30.9 %collective-permute-start.8 = (bf16[4,3,256,256]{3,2,1,0:T(8,128)(2,1)S(1)}, bf16[4,3,256,256]{3,2,1,0:T(8,128)(2,1)S(1)}, u32[]{:S(2)}, u32[]{:S(2)}) collective-permute-start(bf16[4,3,256,256]{3,2,1,0:T(8,128)(2,1)S(1)} %pad_maximum_fusion.refs_5_), channel_id=1, source_target_pairs={{0,1},{1,0},{2,3},{3,2},{4,5},{5,4},{6,7},{7,6},{8,9},{9,8},{10,11... | collective-permute-start | bytes 4718600 | tf_op jit(solution)/shard_map/ppermute | solution.py:43
  33.3 54.8 %collective-permute-start.11 = (bf16[4,3,256,256]{3,2,1,0:T(8,128)(2,1)S(1)}, bf16[4,3,256,256]{3,2,1,0:T(8,128)(2,1)S(1)}, u32[]{:S(2)}, u32[]{:S(2)}) collective-permute-start(bf16[4,3,256,256]{3,2,1,0:T(8,128)(2,1)S(1)} %pad_maximum_fusion.refs_5_), channel_id=1, source_target_pairs={{0,8},{2,10},{4,12},{6,14},{8,0},{10,2},{12,4},{14,6},{1,9},{3,11}... | collective-permute-start | bytes 4718600 | tf_op jit(solution)/shard_map/ppermute | solution.py:39
  58.4 15.7 %collective-permute-start.5 = (bf16[176,2048]{1,0:T(8,128)(2,1)S(1)}, bf16[176,2048]{1,0:T(8,128)(2,1)S(1)}, u32[]{:S(2)}, u32[]{:S(2)}) collective-permute-start(bf16[176,2048]{1,0:T(8,128)(2,1)S(1)} %slice.24), channel_id=1, source_target_pairs={{0,2},{2,4},{4,6},{6,0},{8,10},{10,12},{12,14},{14,8},{1,3},{3,5},... | collective-permute-start | bytes 2162696 | tf_op jit(solution)/shard_map/ppermute | solution.py:25
  58.6 13.2 %collective-permute-start.7 = (bf16[160,2048]{1,0:T(8,128)(2,1)S(1)}, bf16[160,2048]{1,0:T(8,128)(2,1)S(1)}, u32[]{:S(2)}, u32[]{:S(2)}) collective-permute-start(bf16[160,2048]{1,0:T(8,128)(2,1)S(1)} %slice.25), channel_id=1, source_target_pairs={{0,6},{2,0},{4,2},{6,4},{8,14},{10,8},{12,10},{14,12},{1,7},{3,1},... | collective-permute-start | bytes 1966088 | tf_op jit(solution)/shard_map/ppermute | solution.py:25
  77.7 38.4 %collective-permute-start.9 = (bf16[2048,256]{1,0:T(8,128)(2,1)S(1)}, bf16[2048,256]{1,0:T(8,128)(2,1)S(1)}, u32[]{:S(2)}, u32[]{:S(2)}) collective-permute-start(bf16[2048,256]{1,0:T(8,128)(2,1)S(1)} %pad_maximum_fusion.1), channel_id=1, source_target_pairs={{0,2},{2,4},{4,6},{6,0},{8,10},{10,12},{12,14},{14,8},{1,3},{3,5},... | collective-permute-start | bytes 3145736 | tf_op jit(solution)/shard_map/ppermute | solution.py:25
  77.8 38.5 %collective-permute-start.10 = (bf16[2048,256]{1,0:T(8,128)(2,1)S(1)}, bf16[2048,256]{1,0:T(8,128)(2,1)S(1)}, u32[]{:S(2)}, u32[]{:S(2)}) collective-permute-start(bf16[2048,256]{1,0:T(8,128)(2,1)S(1)} %pad_maximum_fusion.1), channel_id=1, source_target_pairs={{0,6},{2,0},{4,2},{6,4},{8,14},{10,8},{12,10},{14,12},{1,7},{3,1},... | collective-permute-start | bytes 3145736 | tf_op jit(solution)/shard_map/ppermute | solution.py:25
  88.2 30.9 %collective-permute-start.13 = (bf16[2,3,256,256]{3,2,1,0:T(8,128)(2,1)S(1)}, bf16[2,3,256,256]{3,2,1,0:T(8,128)(2,1)S(1)}, u32[]{:S(2)}, u32[]{:S(2)}) collective-permute-start(bf16[2,3,256,256]{3,2,1,0:T(8,128)(2,1)S(1)} %get-tuple-element.44), channel_id=1, source_target_pairs={{0,1},{1,0},{2,3},{3,2},{4,5},{5,4},{6,7},{7,6},{8,9},{9,8},{10,11... | collective-permute-start | bytes 2359304 | tf_op jit(solution)/shard_map/ppermute | solution.py:43
  115.8 3.3 %collective-permute-start.12 = (bf16[2,3,256,256]{3,2,1,0:T(8,128)(2,1)S(1)}, bf16[2,3,256,256]{3,2,1,0:T(8,128)(2,1)S(1)}, u32[]{:S(2)}, u32[]{:S(2)}) collective-permute-start(bf16[2,3,256,256]{3,2,1,0:T(8,128)(2,1)S(1)} %get-tuple-element.43), channel_id=1, source_target_pairs={{0,1},{1,0},{2,3},{3,2},{4,5},{5,4},{6,7},{7,6},{8,9},{9,8},{10,11... | collective-permute-start | bytes 2359304 | tf_op jit(solution)/shard_map/ppermute | solution.py:43
  116.2 14.6 %collective-permute-start.17 = (bf16[1024,256]{1,0:T(8,128)(2,1)S(1)}, bf16[1024,256]{1,0:T(8,128)(2,1)S(1)}, u32[]{:S(2)}, u32[]{:S(2)}) collective-permute-start(bf16[1024,256]{1,0:T(8,128)(2,1)S(1)} %slice.28), channel_id=1, source_target_pairs={{0,2},{2,4},{4,6},{6,0},{8,10},{10,12},{12,14},{14,8},{1,3},{3,5},... | collective-permute-start | bytes 1572872 | tf_op jit(solution)/shard_map/ppermute | solution.py:25
  116.3 14.4 %collective-permute-start.18 = (bf16[1024,256]{1,0:T(8,128)(2,1)S(1)}, bf16[1024,256]{1,0:T(8,128)(2,1)S(1)}, u32[]{:S(2)}, u32[]{:S(2)}) collective-permute-start(bf16[1024,256]{1,0:T(8,128)(2,1)S(1)} %slice.29), channel_id=1, source_target_pairs={{0,6},{2,0},{4,2},{6,4},{8,14},{10,8},{12,10},{14,12},{1,7},{3,1},... | collective-permute-start | bytes 1572872 | tf_op jit(solution)/shard_map/ppermute | solution.py:25
  130.8 20.3 %copy-start.1 = (bf16[1,2,256,2048]{3,2,1,0:T(8,128)(2,1)S(1)}, bf16[1,2,256,2048]{3,2,1,0:T(8,128)(2,1)}, u32[]{:S(2)}) copy-start(bf16[1,2,256,2048]{3,2,1,0:T(8,128)(2,1)} %param.6) | copy-start | bytes 6291460
  130.8 20.3 %copy-start.3 = (bf16[1,2,64,2048]{3,2,1,0:T(8,128)(2,1)S(1)}, bf16[1,2,64,2048]{3,2,1,0:T(8,128)(2,1)}, u32[]{:S(2)}) copy-start(bf16[1,2,64,2048]{3,2,1,0:T(8,128)(2,1)} %param.7) | copy-start | bytes 1572868
  130.9 20.1 %collective-permute-start.19 = (bf16[8192,256]{1,0:T(8,128)(2,1)S(1)}, bf16[8192,256]{1,0:T(8,128)(2,1)S(1)}, u32[]{:S(2)}, u32[]{:S(2)}) collective-permute-start(bf16[8192,256]{1,0:T(8,128)(2,1)S(1)} %constant_dynamic-update-slice_fusion.refs_4_), channel_id=1, source_target_pairs={{0,1},{1,0},{2,3},{3,2},{4,5},{5,4},{6,7},{7,6},{8,9},{9,8},{10,11... | collective-permute-start | bytes 12582920 | tf_op jit(solution)/shard_map/ppermute | solution.py:43
  132.1 29.8 %collective-permute-start.25 = (bf16[256,2048]{1,0:T(8,128)(2,1)S(1)}, bf16[256,2048]{1,0:T(8,128)(2,1)S(1)}, u32[]{:S(2)}, u32[]{:S(2)}) collective-permute-start(bf16[256,2048]{1,0:T(8,128)(2,1)S(1)} %get-tuple-element.57), channel_id=1, source_target_pairs={{128,144},{144,160},{160,176},{176,192},{192,208},{208,224},{224,2... | collective-permute-start | bytes 3145736 | tf_op jit(solution)/shard_map/ppermute | solution.py:47
  133.4 13.9 %collective-permute-start.14 = (bf16[256,512]{1,0:T(8,128)(2,1)S(1)}, bf16[256,512]{1,0:T(8,128)(2,1)S(1)}, u32[]{:S(2)}, u32[]{:S(2)}) collective-permute-start(bf16[256,512]{1,0:T(8,128)(2,1)S(1)} %get-tuple-element.46), channel_id=1, source_target_pairs={{0,6},{2,0},{4,2},{6,4},{8,14},{10,8},{12,10},{14,12},{1,7},{3,1},... | collective-permute-start | bytes 786440 | tf_op jit(solution)/shard_map/ppermute | solution.py:25
  136.3 11.0 %collective-permute-start.15 = (bf16[256,512]{1,0:T(8,128)(2,1)S(1)}, bf16[256,512]{1,0:T(8,128)(2,1)S(1)}, u32[]{:S(2)}, u32[]{:S(2)}) collective-permute-start(bf16[256,512]{1,0:T(8,128)(2,1)S(1)} %get-tuple-element.47), channel_id=1, source_target_pairs={{0,4},{2,6},{4,0},{6,2},{8,12},{10,14},{12,8},{14,10},{1,5},{3,7},... | collective-permute-start | bytes 786440 | tf_op jit(solution)/shard_map/ppermute | solution.py:25
  136.3 14.8 %collective-permute-start.16 = (bf16[256,512]{1,0:T(8,128)(2,1)S(1)}, bf16[256,512]{1,0:T(8,128)(2,1)S(1)}, u32[]{:S(2)}, u32[]{:S(2)}) collective-permute-start(bf16[256,512]{1,0:T(8,128)(2,1)S(1)} %get-tuple-element.48), channel_id=1, source_target_pairs={{0,2},{2,4},{4,6},{6,0},{8,10},{10,12},{12,14},{14,8},{1,3},{3,5},... | collective-permute-start | bytes 786440 | tf_op jit(solution)/shard_map/ppermute | solution.py:25
  155.0 17.3 %collective-permute-start.20 = (bf16[256,1024]{1,0:T(8,128)(2,1)S(1)}, bf16[256,1024]{1,0:T(8,128)(2,1)S(1)}, u32[]{:S(2)}, u32[]{:S(2)}) collective-permute-start(bf16[256,1024]{1,0:T(8,128)(2,1)S(1)} %get-tuple-element.51), channel_id=1, source_target_pairs={{0,16},{16,32},{32,48},{48,64},{64,80},{80,96},{96,112},{112,128},... | collective-permute-start | bytes 1572872 | tf_op jit(solution)/shard_map/ppermute | solution.py:47
  160.6 23.0 %collective-permute-start.22 = (bf16[256,1024]{1,0:T(8,128)(2,1)S(1)}, bf16[256,1024]{1,0:T(8,128)(2,1)S(1)}, u32[]{:S(2)}, u32[]{:S(2)}) collective-permute-start(bf16[256,1024]{1,0:T(8,128)(2,1)S(1)} %get-tuple-element.53), channel_id=1, source_target_pairs={{0,16},{16,32},{32,48},{48,64},{64,80},{80,96},{96,112},{112,128},... | collective-permute-start | bytes 1572872 | tf_op jit(solution)/shard_map/ppermute | solution.py:47
  172.3 19.7 %collective-permute-start.26 = (bf16[256,2048]{1,0:T(8,128)(2,1)S(1)}, bf16[256,2048]{1,0:T(8,128)(2,1)S(1)}, u32[]{:S(2)}, u32[]{:S(2)}) collective-permute-start(bf16[256,2048]{1,0:T(8,128)(2,1)S(1)} %collective-permute-done.25.refs_4_), channel_id=1, source_target_pairs={{0,1},{1,0},{2,3},{3,2},{4,5},{5,4},{6,7},{7,6},{8,9},{9,8},{10,11... | collective-permute-start | bytes 3145736 | tf_op jit(solution)/shard_map/ppermute | solution.py:43
  175.2 7.2 %collective-permute-start.23 = (bf16[64,2048]{1,0:T(8,128)(2,1)S(1)}, bf16[64,2048]{1,0:T(8,128)(2,1)S(1)}, u32[]{:S(2)}, u32[]{:S(2)}) collective-permute-start(bf16[64,2048]{1,0:T(8,128)(2,1)S(1)} %get-tuple-element.54), channel_id=1, source_target_pairs={{128,144},{144,160},{160,176},{176,192},{192,208},{208,224},{224,2... | collective-permute-start | bytes 786440 | tf_op jit(solution)/shard_map/ppermute | solution.py:47
  176.5 13.0 %collective-permute-start.27 = (bf16[64,2048]{1,0:T(8,128)(2,1)S(1)}, bf16[64,2048]{1,0:T(8,128)(2,1)S(1)}, u32[]{:S(2)}, u32[]{:S(2)}) collective-permute-start(bf16[64,2048]{1,0:T(8,128)(2,1)S(1)} %get-tuple-element.60), channel_id=1, source_target_pairs={{0,16},{16,32},{32,48},{48,64},{64,80},{80,96},{96,112},{112,128},... | collective-permute-start | bytes 786440 | tf_op jit(solution)/shard_map/ppermute | solution.py:47
  183.6 8.4 %collective-permute-start.24 = (bf16[256,1024]{1,0:T(8,128)(2,1)S(1)}, bf16[256,1024]{1,0:T(8,128)(2,1)S(1)}, u32[]{:S(2)}, u32[]{:S(2)}) collective-permute-start(bf16[256,1024]{1,0:T(8,128)(2,1)S(1)} %collective-permute-done.22.refs_2_), channel_id=1, source_target_pairs={{0,1},{1,0},{2,3},{3,2},{4,5},{5,4},{6,7},{7,6},{8,9},{9,8},{10,11... | collective-permute-start | bytes 1572872 | tf_op jit(solution)/shard_map/ppermute | solution.py:43
  186.1 5.9 %collective-permute-start.21 = (bf16[256,1024]{1,0:T(8,128)(2,1)S(1)}, bf16[256,1024]{1,0:T(8,128)(2,1)S(1)}, u32[]{:S(2)}, u32[]{:S(2)}) collective-permute-start(bf16[256,1024]{1,0:T(8,128)(2,1)S(1)} %collective-permute-done.20.refs_0_), channel_id=1, source_target_pairs={{0,1},{1,0},{2,3},{3,2},{4,5},{5,4},{6,7},{7,6},{8,9},{9,8},{10,11... | collective-permute-start | bytes 1572872 | tf_op jit(solution)/shard_map/ppermute | solution.py:43
  186.1 4.7 %collective-permute-start.29 = (bf16[64,2048]{1,0:T(8,128)(2,1)S(1)}, bf16[64,2048]{1,0:T(8,128)(2,1)S(1)}, u32[]{:S(2)}, u32[]{:S(2)}) collective-permute-start(bf16[64,2048]{1,0:T(8,128)(2,1)S(1)} %collective-permute-done.23.refs_8_), channel_id=1, source_target_pairs={{0,1},{1,0},{2,3},{3,2},{4,5},{5,4},{6,7},{7,6},{8,9},{9,8},{10,11... | collective-permute-start | bytes 786440 | tf_op jit(solution)/shard_map/ppermute | solution.py:43
  189.5 2.5 %collective-permute-start.28 = (bf16[64,2048]{1,0:T(8,128)(2,1)S(1)}, bf16[64,2048]{1,0:T(8,128)(2,1)S(1)}, u32[]{:S(2)}, u32[]{:S(2)}) collective-permute-start(bf16[64,2048]{1,0:T(8,128)(2,1)S(1)} %collective-permute-done.27.refs_6_), channel_id=1, source_target_pairs={{0,1},{1,0},{2,3},{3,2},{4,5},{5,4},{6,7},{7,6},{8,9},{9,8},{10,11... | collective-permute-start | bytes 786440 | tf_op jit(solution)/shard_map/ppermute | solution.py:43

commit v2 on v1

--- a/solution.py
+++ b/solution.py
@@ -48,7 +48,7 @@
 
 
 def round_ring(array):
-    return around_x(array, 1), around_x(array, -1)
+    return (array,) + tuple(around_x(array, step) for step in range(1, RING))
 
 
 def after(array, *others):
@@ -145,130 +145,89 @@
     )(where, context, queries, gain, lengths)
 
 
-def slot_copies(rows, slot, first, count, columns, target, sems, base):
-    if slot != 2:
-        pieces = [(rows[slot if slot < 2 else 4], first, count, 0)]
-    else:
-        cut = rows[2].shape[0]
-        pieces = []
-        if first < cut:
-            pieces.append((rows[2], first, min(count, cut - first), 0))
-        if first + count > cut:
-            skip = max(cut - first, 0)
-            pieces.append((rows[3], first + skip - cut, count - skip, skip))
-    return [
-        pltpu.make_async_copy(
-            piece.at[pl.ds(start, size), columns], target.at[pl.ds(at, size)], sems.at[base + i]
+def start_kernel(where, *refs):
+    rows, parts = refs[:4], refs[4:6]
+    total, far_rows, far_qry, lengths, near_rows, near_qry, weight, sems = refs[6:]
+    x, z = where[0], where[1]
+    mem, few = far_rows.shape[0] // RING, far_qry.shape[0] // RING
+    width = far_rows.shape[1]
+    copies = []
+
+    def take(slot, first, count, columns, target):
+        source = rows[slot].at[pl.ds(first, count), columns]
+        copies.append(pltpu.make_async_copy(source, target, sems.at[len(copies)]))
+
+    for part, first in ((parts[0], 0), (parts[1], parts[0].shape[3])):
+        for step in range(RING):
+            _, _, block, columns = part.shape
+            at = pl.multiple_of(((x - step + RING) % RING) * block, block)
+            target = weight.at[:, pl.ds(at, block), pl.ds(first, columns)]
+            copies.append(
+                pltpu.make_async_copy(part.at[step], target, sems.at[len(copies)])
+            )
+    for slot in range(RING):
+        columns = pl.ds(pl.multiple_of(z * width, width), width)
+        take(slot, 0, mem, columns, near_rows.at[pl.ds(slot * mem, mem)])
+        take(slot, mem, few, columns, near_qry.at[pl.ds(slot * few, few)])
+        take(slot, mem + few, TAIL, pl.ds(0, 128), lengths.at[slot])
+    for step in range(RING):
+        at = ((1 - z) * RING + (x - step + RING) % RING) * block
+        columns = pl.ds(pl.multiple_of(at, block), block)
+        here = pl.ds(step * block, block)
+        for slot in range(RING):
+            take(slot, 0, mem, columns, far_rows.at[pl.ds(slot * mem, mem), here])
+            take(slot, mem, few, columns, far_qry.at[pl.ds(slot * few, few), here])
+    wait_all(copy_all(copies))
+
+    @pl.when(where[2] == 1)
+    def _():
+        total[0] = jnp.dot(near_rows[...], weight[0], preferred_element_type=F32)
+
+    @pl.when(where[2] == 0)
+    def _():
+        total[0, pl.ds(0, RING * few)] = jnp.dot(
+            near_qry[...], weight[0], preferred_element_type=F32
         )
-        for i, (piece, start, size, at) in enumerate(pieces)
-    ]
-
-
-def row_copies(high, rows, rows_all, sems):
-    mem, width = rows_all.shape[0] // RING, rows_all.shape[1]
-    columns = pl.ds(pl.multiple_of(high * width, width), width)
-    copies = []
-    for slot in range(RING):
-        target = rows_all.at[pl.ds(slot * mem, mem)]
-        copies += slot_copies(rows, slot, 0, mem, columns, target, sems, len(copies))
-    return copies
-
-
-def weight_copies(x, group, weight, sems, base, plane=None):
-    copies = []
-    for i, piece in enumerate(group):
-        step, side = i % RING, i // RING
-        _, block, part = piece.shape
-        first = pl.multiple_of(((x - step + RING) % RING) * block, block)
-        rows, columns = pl.ds(first, block), pl.ds(side * part, part)
-        if plane is None:
-            source, target = piece, weight.at[:, rows, columns]
-        else:
-            source, target = piece.at[plane], weight.at[rows, columns]
-        copies.append(pltpu.make_async_copy(source, target, sems.at[base + i]))
-    return copies
-
-
-def pieces_of(parts):
-    return [part.at[step] for part in parts for step in range(part.shape[0])]
-
-
-def start_kernel(where, *refs):
-    rows, parts = refs[:5], refs[5:7]
-    total, rows_all, weight, sems = refs[7:]
-    group = pieces_of(parts)
-    copies = row_copies(where[1], rows, rows_all, sems)
-    copies += weight_copies(where[0], group, weight, sems, 5)
-    wait_all(copy_all(copies))
-
-    @pl.when(where[2] == 1)
-    def _():
-        total[0] = jnp.dot(rows_all[...], weight[0], preferred_element_type=F32)
 
     @pl.loop(1, 3)
     def _(plane):
-        total[plane] = jnp.dot(rows_all[...], weight[plane], preferred_element_type=F32)
-
-
-def attend_kernel(where, *refs):
-    rows, near, far, total_in = refs[:5], refs[5:7], refs[7:10], refs[10]
-    outs = refs[11:15]
-    rows_all, qry_all, near_query, weight, total, lengths, low, mixed, sems = refs[15:]
-    x, z, encoder = where[0], where[1], where[2]
-    mem, few = rows_all.shape[0] // RING, qry_all.shape[0] // RING
-    width = rows_all.shape[1]
-    copies = row_copies(1 - z, rows, rows_all, sems)
-    copies += weight_copies(x, pieces_of(far), weight, sems, 5)
-    for slot in range(RING):
-        copies += slot_copies(
-            rows, slot, mem + few, TAIL, pl.ds(0, 128), lengths.at[slot], sems, 13 + slot
-        )
-    totals = [
-        pltpu.make_async_copy(total_in.at[plane], total.at[plane], sems.at[17 + plane])
-        for plane in range(3)
-    ]
-    queries = weight_copies(x, pieces_of(near), near_query, sems, 20, plane=0)
-    for slot in range(RING):
-        target = qry_all.at[pl.ds(slot * few, few)]
-        queries += slot_copies(
-            rows, slot, mem, few, pl.ds(0, 2 * width), target, sems, 28 + slot
-        )
-    copy_all(copies)
-    copy_all(totals[1:])
+        total[plane] = jnp.dot(near_rows[...], weight[plane], preferred_element_type=F32)
+
+
+def attend_kernel(where, total, rows, qry, lengths, *refs):
+    sides = (refs[:1], refs[1:3])
+    outs = refs[3:7]
+    low, mixed = refs[7:]
+    mem, few = mixed.shape[1], qry.shape[0] // RING
+    encoder = where[2]
+
+    def add_half(plane, source, count):
+        for side, pieces in enumerate(sides):
+            part = pieces[0].shape[3]
+            at = pl.ds(side * part, part)
+            result = total[plane, pl.ds(0, count), at]
+            first = 0
+            for piece in pieces:
+                depth = piece.shape[0] * piece.shape[2]
+                result += jnp.dot(
+                    source[:, pl.ds(first, depth)],
+                    piece[:, plane].reshape(depth, part),
+                    preferred_element_type=F32,
+                )
+                first += depth
+            low[plane, pl.ds(0, count), at] = result.astype(BF16)
 
     @pl.when(encoder == 1)
     def _():
-        totals[0].start()
+        add_half(0, rows, RING * mem)
 
     @pl.when(encoder == 0)
     def _():
-        copy_all(queries)
-
-    wait_all(copies)
-    wait_all(totals[1:])
-
-    @pl.when(encoder == 1)
-    def _():
-        totals[0].wait()
-        low[0] = (
-            total[0] + jnp.dot(rows_all[...], weight[0], preferred_element_type=F32)
-        ).astype(BF16)
-
-    @pl.when(encoder == 0)
-    def _():
-        wait_all(queries)
-        here = pl.ds(pl.multiple_of(z * width, width), width)
-        there = pl.ds(pl.multiple_of((1 - z) * width, width), width)
-        low[0, pl.ds(0, RING * few)] = (
-            jnp.dot(qry_all[:, here], near_query[...], preferred_element_type=F32)
-            + jnp.dot(qry_all[:, there], weight[0], preferred_element_type=F32)
-        ).astype(BF16)
+        add_half(0, qry, RING * few)
 
     @pl.loop(1, 3)
     def _(plane):
-        low[plane] = (
-            total[plane] + jnp.dot(rows_all[...], weight[plane], preferred_element_type=F32)
-        ).astype(BF16)
+        add_half(plane, rows, RING * mem)
 
     heads = low.shape[2] // HEAD
     scale = 1.0 / math.sqrt(HEAD)
@@ -308,60 +267,49 @@
     def _():
         heads_of(few)
 
-    wait_all(
-        copy_all(
-            [
-                pltpu.make_async_copy(mixed.at[slot], outs[slot], sems.at[slot])
-                for slot in range(RING)
-            ]
-        )
-    )
-
-
-def start_projections(where, mem, rows, parts):
+    for slot in range(RING):
+        outs[slot][...] = mixed[slot]
+
+
+def start_projections(where, mem, few, rows, parts):
     width = rows[0].shape[1]
     _, planes, block, part = parts[0].shape
+    half = width // 2
     return call(
         start_kernel,
-        jax.ShapeDtypeStruct((planes, RING * mem, 2 * part), F32),
-        [SMEM] + [HBM] * 7,
-        VMEM,
-        [
-            pltpu.VMEM((RING * mem, width // 2), BF16),
-            pltpu.VMEM((planes, width // 2, 2 * part), BF16),
-            pltpu.SemaphoreType.DMA((13,)),
+        (
+            jax.ShapeDtypeStruct((planes, RING * mem, 2 * part), F32),
+            jax.ShapeDtypeStruct((RING * mem, half), BF16),
+            jax.ShapeDtypeStruct((RING * few, half), BF16),
+            jax.ShapeDtypeStruct((RING, TAIL, 128), BF16),
+        ),
+        [SMEM] + [HBM] * 6,
+        (VMEM,) * 4,
+        [
+            pltpu.VMEM((RING * mem, half), BF16),
+            pltpu.VMEM((RING * few, half), BF16),
+            pltpu.VMEM((planes, half, 2 * part), BF16),
+            pltpu.SemaphoreType.DMA((64,)),
         ],
-        flops=RING * mem * width * planes * 2 * part,
-        moved=RING * mem * width + planes * width * 2 * part,
-        limit=24,
+        limit=14,
     )(where, *rows, *parts)
 
 
-def attend(where, mem, few, rows, near, far, total):
-    width = rows[0].shape[1]
-    _, planes, block, part = near[0].shape
-    out = jax.ShapeDtypeStruct((mem, 2 * part), BF16)
-    operands = (*rows, *near, *far, total)
+def attend(where, mem, started, far):
+    total = started[0]
+    planes, _, columns = total.shape
+    out = jax.ShapeDtypeStruct((mem, columns), BF16)
     return call(
         attend_kernel,
         (out,) * RING,
-        [SMEM] + [HBM] * len(operands),
-        (HBM,) * RING,
-        [
-            pltpu.VMEM((RING * mem, width // 2), BF16),
-            pltpu.VMEM((RING * few, width), BF16),
-            pltpu.VMEM((width // 2, 2 * part), BF16),
-            pltpu.VMEM((planes, width // 2, 2 * part), BF16),
-            pltpu.VMEM(total.shape, F32),
-            pltpu.VMEM((RING, TAIL, 128), BF16),
-            pltpu.VMEM((planes, RING * mem, 2 * part), BF16),
-            pltpu.VMEM((RING, mem, 2 * part), BF16),
-            pltpu.SemaphoreType.DMA((32,)),
+        [SMEM] + [VMEM] * 7,
+        (VMEM,) * RING,
+        [
+            pltpu.VMEM((planes, RING * mem, columns), BF16),
+            pltpu.VMEM((RING, mem, columns), BF16),
         ],
-        flops=RING * mem * width * planes * 2 * part,
-        moved=RING * mem * width + planes * width * 2 * part,
-        limit=30,
-    )(where, *operands)
+        limit=14,
+    )(where, *started, *far)
 
 
 def project_kernel(part, where, context, queries, *refs):
@@ -543,41 +491,45 @@
     out_shard = out_weight[0]
     out_far = across_z(out_shard)
     own = quarters(where, jnp.swapaxes(qkv_weight[0], 0, 1))
-    near = jnp.stack([own[0]] + [around_x(own[step], step) for step in range(1, RING)])
-    far = across_z(after(near, out_far))
-    near = (near, other_core(near))
+    out_pair = jnp.concatenate([out_shard, out_far])
+    near = [own[0]] + [around_x(own[step], step) for step in range(1, RING)]
+    arrived = near[1:]
+    near = jnp.stack(near)
+    far = across_z(after(near, out_pair))
 
     ctx, qry, normed = norm_scene(
         after(where, *own), context, queries, norm_gain, lengths[0]
     )
-    cut = (normed.shape[0] // 32 + 1) * 16
-    left, right = round_ring(after(normed, near[0], out_far))
-    rows = (normed, left, around_x(left[:cut], 1), around_x(right[cut:], -1), right)
-    total = start_projections(where, mem, rows, near)
-
-    out_pair = after(jnp.concatenate([out_shard, out_far]), *rows, total)
-    cut = out_shard.shape[0]
-    left, right = round_ring(out_pair)
-    opposite = [around_x(left[:cut], 1), around_x(right[cut:], -1)]
-    far = (far, other_core(after(far[:2], total)), other_core(after(far[2:], total)))
-    ctx_early = relay(after(ctx, *far), decoders, count)
-    qry_early = relay(after(qry, *far), encoders, count)
-
-    mixed = attend(after(where, left, right), mem, few, rows, near, far, total)
-    weights = both(jnp.concatenate([out_pair, left, *after(tuple(opposite), mixed[0]), right]))
+    rows = round_ring(after(normed, out_pair, *arrived))
+    started = start_projections(where, mem, few, rows, (near, other_core(near)))
+
+    weights = round_ring(after(out_pair, *rows, started[0]))
+    far = (
+        far,
+        other_core(after(far[:2], started[0], *weights)),
+        other_core(after(far[2:], started[0], *weights)),
+    )
+    weights = both(jnp.concatenate(after(weights, *far)))
+
+    mixed = attend(where, mem, started, far)
+    ctx_early = relay(after(ctx, mixed[0]), decoders, count)
+    qry_early = relay(after(qry, mixed[0]), encoders, count)
     mixed = [mixed[0]] + [around_x(mixed[step], -step) for step in range(1, RING)]
 
-    first, few_first = project(0, where, context, queries, mixed, weights)
+    first, few_first = project(
+        0, after(where, qry_early), context, queries, mixed, weights
+    )
     first = relay(first, encoders, count)
     second, few_new = project(1, where, context, queries, mixed, weights, (few_first,))
-    second = relay(second, encoders, count)
+    qry_early = (qry_early, other_core(qry_early))
+    second = relay(after(second, qry_early[1]), encoders, count)
     few_new = relay(few_new, decoders, count)
     ctx_new, qry_new = gather_result(
         where,
         both(first),
         (second, other_core(after(second, few_new))),
         (ctx_early, other_core(after(ctx_early, first))),
-        (qry_early, other_core(after(qry_early, first))),
+        qry_early,
         both(few_new),
     )
     return ctx_new[None], qry_new[None]

time: 195 us -> 231 us (1.18)
  waiting for transfers between devices: 73.6 us -> 142 us
  starting transfers between devices: 85.9 us -> 52.3 us
    ppermute x14 -> x12, waiting for transfers between devices: 41.7 us -> 115 us  [around_x(): return lax.ppermute(array, 'dp', pairs)]
    ppermute x9, starting transfers between devices: 39.2 us -> 8.34 us  [other_core(): return lax.ppermute(array, 'tensor', [(0, 1), (1, 0)])]
    ppermute x5, starting transfers between devices: 6.51 us -> 16.4 us  [relay(): lax.ppermute(array, 'section', [(s, (s + 1) % count) for s in sections])]
    ppermute x2, waiting for transfers between devices: 11.6 us -> 2.32 us  [across_z(): lax.ppermute(array, 'dp', [(d, (d + RING) % (2 * RING)) for d in range(2...]
    ppermute x2, starting transfers between devices: 20.7 us -> 13.2 us  [across_z(): lax.ppermute(array, 'dp', [(d, (d + RING) % (2 * RING)) for d in range(2...]
    ppermute x14 -> x12, starting transfers between devices: 19.5 us -> 14.4 us  [around_x(): return lax.ppermute(array, 'dp', pairs)]
    ppermute x9, waiting for transfers between devices: 1.18 us -> 5.2 us  [other_core(): return lax.ppermute(array, 'tensor', [(0, 1), (1, 0)])]
    unnamed x20 -> x19, local copies, waits for them, and re-layouts: 5.61 us -> 5.61 us
  transfers between devices with their start and end apart: 30 -> 28, of which waited for: 14 -> 17; matrix products, arithmetic and copies ran while one was open for 0% -> 0% of each run, Pallas kernels for 13% -> 11%
where the time goes in v2:
time: 231 us; the launch traced here: 228 us
  waiting for transfers between devices  142 us (61%)
  starting transfers between devices  52.3 us (23%)
  Pallas kernels  27.3 us (12%)
  local copies, waits for them, and re-layouts  5.87 us (3%)
    ppermute x12, waiting for transfers between devices, around_x(): return lax.ppermute(array, 'dp', pairs)  115 us
    ppermute x5, waiting for transfers between devices, relay(): lax.ppermute(array, 'section', [(s, (s + 1) % count) for s in sections])  18.9 us
    ppermute x5, starting transfers between devices, relay(): lax.ppermute(array, 'section', [(s, (s + 1) % count) for s in sections])  16.4 us
    ppermute x12, starting transfers between devices, around_x(): return lax.ppermute(array, 'dp', pairs)  14.4 us
    ppermute x2, starting transfers between devices, across_z(): lax.ppermute(array, 'dp', [(d, (d + RING) % (2 * RING)) for d in range(2...  13.2 us
    pallas_call x1, Pallas kernels, attend(): call(attend_kernel, (out,) * RING, [SMEM] + [VMEM] * 7, (VMEM,) * RING, [...  9.22 us
    ppermute x9, starting transfers between devices, other_core(): return lax.ppermute(array, 'tensor', [(0, 1), (1, 0)])  8.34 us
    pallas_call x2, Pallas kernels, project(): call(functools.partial(project_kernel, part), (jax.ShapeDtypeStruct((mem,...  7.94 us
  transfers between devices with their start and end apart: 28, of which 17 were waited for; matrix products, arithmetic and copies ran while one was open for 0% of the time, Pallas kernels for 11%

profile of v2, /device:TPU:17, one launch (start us, length us, event | category | flops | bytes accessed | tf_op | source)
XLA Modules:
  0.0 228.4 jit_solution(5612684577487288713)
XLA Ops:
  0.7 0.1 stack.46.where
  0.8 1.4 copy-done.4
  2.2 0.8 shard_map.77
  2.9 1.3 collective-permute-start.1
  4.2 2.5 %collective-permute-start.2 = (bf16[3,256,256]{2,1,0:T(8,128)(2,1)S(1)}, bf16[3,256,256]{2,1,0:T(8,128)(2,1)S(1)}, u32[]{:S(2)}, u32[]{:S(2)}) collective-permute-start(bf16[3,256,256]{2,1,0:T(8,128)(2,1)S(1)} %get-tuple-element.41), channel_id=1, source_target_pairs={{0,4},{2,6},{4,0},{6,2},{8,12},{10,14},{12,8},{14,10},{1,5},{3,7},... | collective-permute-start | bytes 1179656 | tf_op jit(solution)/shard_map/ppermute | solution.py:25
  6.7 1.2 collective-permute-start.3
  7.8 6.9 %collective-permute-start = (bf16[1024,256]{1,0:T(8,128)(2,1)}, bf16[1024,256]{1,0:T(8,128)(2,1)S(1)}, u32[]{:S(2)}, u32[]{:S(2)}) collective-permute-start(bf16[1024,256]{1,0:T(8,128)(2,1)} %bitcast.27), channel_id=1, source_target_pairs={{0,8},{2,10},{4,12},{6,14},{8,0},{10,2},{12,4},{14,6},{1,9},{3,11}... | collective-permute-start | bytes 1572872 | tf_op jit(solution)/shard_map/ppermute | solution.py:39
  14.7 1.6 copy-done
  16.3 1.0 copy-done.2
  17.4 0.7 copy-done.5
  18.1 0.7 copy-done.6
  18.7 2.0 shard_map.78
  20.7 0.0 copy-start.7
  20.7 0.0 collective-permute-done.1
  20.7 2.9 %collective-permute-done.2 = bf16[3,256,256]{2,1,0:T(8,128)(2,1)S(1)} collective-permute-done((bf16[3,256,256]{2,1,0:T(8,128)(2,1)S(1)}, bf16[3,256,256]{2,1,0:T(8,128)(2,1)S(1)}, u32[]{:S(2)}, u32[]{:S(2)}) %collective-permute-start.2) | collective-permute-done | bytes 393248 | tf_op jit(solution)/shard_map/ppermute | solution.py:25
  23.6 0.2 pad_maximum_fusion.refs_4_
  23.8 1.6 collective-permute-start.7
  25.4 2.3 %collective-permute-done = bf16[1024,256]{1,0:T(8,128)(2,1)S(1)} collective-permute-done((bf16[1024,256]{1,0:T(8,128)(2,1)}, bf16[1024,256]{1,0:T(8,128)(2,1)S(1)}, u32[]{:S(2)}, u32[]{:S(2)}) %collective-permute-start) | collective-permute-done | bytes 524320 | tf_op jit(solution)/shard_map/ppermute | solution.py:39
  27.8 0.1 pad_maximum_fusion.1
  27.8 0.4 collective-permute-start.4
  28.2 1.2 collective-permute-start.5
  29.4 1.3 collective-permute-start.6
  30.7 6.2 %collective-permute-start.8 = (bf16[4,3,256,256]{3,2,1,0:T(8,128)(2,1)S(1)}, bf16[4,3,256,256]{3,2,1,0:T(8,128)(2,1)S(1)}, u32[]{:S(2)}, u32[]{:S(2)}) collective-permute-start(bf16[4,3,256,256]{3,2,1,0:T(8,128)(2,1)S(1)} %pad_maximum_fusion.refs_4_), channel_id=1, source_target_pairs={{0,8},{2,10},{4,12},{6,14},{8,0},{10,2},{12,4},{14,6},{1,9},{3,11}... | collective-permute-start | bytes 4718600 | tf_op jit(solution)/shard_map/ppermute | solution.py:39
  37.0 22.4 %collective-permute-done.4.refs_1_ = bf16[336,2048]{1,0:T(8,128)(2,1)S(1)} collective-permute-done((bf16[336,2048]{1,0:T(8,128)(2,1)S(1)}, bf16[336,2048]{1,0:T(8,128)(2,1)S(1)}, u32[]{:S(2)}, u32[]{:S(2)}) %collective-permute-start.4) | collective-permute-done | bytes 1376288 | tf_op jit(solution)/shard_map/ppermute | solution.py:25
  59.4 27.8 %collective-permute-done.5.refs_2_ = bf16[336,2048]{1,0:T(8,128)(2,1)S(1)} collective-permute-done((bf16[336,2048]{1,0:T(8,128)(2,1)S(1)}, bf16[336,2048]{1,0:T(8,128)(2,1)S(1)}, u32[]{:S(2)}, u32[]{:S(2)}) %collective-permute-start.5) | collective-permute-done | bytes 1376288 | tf_op jit(solution)/shard_map/ppermute | solution.py:25
  87.1 2.8 %collective-permute-done.6.refs_3_ = bf16[336,2048]{1,0:T(8,128)(2,1)S(1)} collective-permute-done((bf16[336,2048]{1,0:T(8,128)(2,1)S(1)}, bf16[336,2048]{1,0:T(8,128)(2,1)S(1)}, u32[]{:S(2)}, u32[]{:S(2)}) %collective-permute-start.6) | collective-permute-done | bytes 1376288 | tf_op jit(solution)/shard_map/ppermute | solution.py:25
  89.9 5.1 %shard_map.79 = (f32[3,1024,512]{2,1,0:T(8,128)S(1)}, bf16[1024,1024]{1,0:T(8,128)(2,1)S(1)}, bf16[256,1024]{1,0:T(8,128)(2,1)S(1)}, bf16[4,16,128]{2,1,0:T(8,128)(2,1)S(1)}) custom-call(s32[5]{0:T(128)S(1)} %stack.46.where, bf16[336,2048]{1,0:T(8,128)(2,1)S(1)} %get-tuple-element.46.refs_0_, bf16[336,2048]{1,0:T(8,128)(2,1)S(1)} %collective-permute-done.4.refs_1_, ...), custom_call_target="tpu_custom_call" | custom-call | flops 1 | bytes 1 | tf_op jit(solution)/shard_map/pallas_call | solution.py:278
  95.1 1.5 collective-permute-start.9
  96.6 3.1 %collective-permute-start.10 = (bf16[2048,256]{1,0:T(8,128)(2,1)S(1)}, bf16[2048,256]{1,0:T(8,128)(2,1)S(1)}, u32[]{:S(2)}, u32[]{:S(2)}) collective-permute-start(bf16[2048,256]{1,0:T(8,128)(2,1)S(1)} %pad_maximum_fusion.1), channel_id=1, source_target_pairs={{0,4},{2,6},{4,0},{6,2},{8,12},{10,14},{12,8},{14,10},{1,5},{3,7},... | collective-permute-start | bytes 3145736 | tf_op jit(solution)/shard_map/ppermute | solution.py:25
  99.7 0.1 fusion
  99.8 20.7 %collective-permute-done.9 = bf16[2048,256]{1,0:T(8,128)(2,1)S(1)} collective-permute-done((bf16[2048,256]{1,0:T(8,128)(2,1)S(1)}, bf16[2048,256]{1,0:T(8,128)(2,1)S(1)}, u32[]{:S(2)}, u32[]{:S(2)}) %collective-permute-start.9) | collective-permute-done | bytes 1048608 | tf_op jit(solution)/shard_map/ppermute | solution.py:25
  120.5 24.2 %collective-permute-done.10 = bf16[2048,256]{1,0:T(8,128)(2,1)S(1)} collective-permute-done((bf16[2048,256]{1,0:T(8,128)(2,1)S(1)}, bf16[2048,256]{1,0:T(8,128)(2,1)S(1)}, u32[]{:S(2)}, u32[]{:S(2)}) %collective-permute-start.10) | collective-permute-done | bytes 1048608 | tf_op jit(solution)/shard_map/ppermute | solution.py:25
  144.7 1.5 collective-permute-start.12
  146.3 0.0 collective-permute-start.13
  146.3 1.9 collective-permute-done.12.refs_1_
  148.2 1.1 collective-permute-done.13.refs_2_
  149.3 0.1 constant_dynamic-update-slice_fusion.3
  149.4 0.1 constant_dynamic-update-slice_fusion.2
  149.5 0.1 constant_dynamic-update-slice_fusion.1
  149.5 0.1 constant_dynamic-update-slice_fusion.refs_4_
  149.6 0.5 collective-permute-start.18
  150.1 9.2 %shard_map.80 = (bf16[256,512]{1,0:T(8,128)(2,1)S(1)}, bf16[256,512]{1,0:T(8,128)(2,1)S(1)}, bf16[256,512]{1,0:T(8,128)(2,1)S(1)}, bf16[256,512]{1,0:T(8,128)(2,1)S(1)}) custom-call(s32[5]{0:T(128)S(1)} %stack.46.where, f32[3,1024,512]{2,1,0:T(8,128)S(1)} %get-tuple-element.47.total, bf16[1024,1024]{1,0:T(8,128)(2,1)S(1)} %get-tuple-element.48.rows, ...), custom_call_target="tpu_custom_call" | custom-call | flops 1 | bytes 1 | tf_op jit(solution)/shard_map/pallas_call | solution.py:302
  159.3 1.3 collective-permute-start.14
  160.6 11.2 %collective-permute-start.25 = (bf16[256,2048]{1,0:T(8,128)(2,1)S(1)}, bf16[256,2048]{1,0:T(8,128)(2,1)S(1)}, u32[]{:S(2)}, u32[]{:S(2)}) collective-permute-start(bf16[256,2048]{1,0:T(8,128)(2,1)S(1)} %get-tuple-element.72), channel_id=1, source_target_pairs={{128,144},{144,160},{160,176},{176,192},{192,208},{208,224},{224,2... | collective-permute-start | bytes 3145736 | tf_op jit(solution)/shard_map/ppermute | solution.py:47
  171.8 2.0 collective-permute-start.15
  173.8 0.9 collective-permute-done.14.refs_6_
  174.7 4.7 %collective-permute-done.15.refs_1_ = bf16[256,512]{1,0:T(8,128)(2,1)S(1)} collective-permute-done((bf16[256,512]{1,0:T(8,128)(2,1)S(1)}, bf16[256,512]{1,0:T(8,128)(2,1)S(1)}, u32[]{:S(2)}, u32[]{:S(2)}) %collective-permute-start.15) | collective-permute-done | bytes 262176 | tf_op jit(solution)/shard_map/ppermute | solution.py:25
  179.4 3.1 %collective-permute-done.16.refs_2_ = bf16[256,512]{1,0:T(8,128)(2,1)S(1)} collective-permute-done((bf16[256,512]{1,0:T(8,128)(2,1)S(1)}, bf16[256,512]{1,0:T(8,128)(2,1)S(1)}, u32[]{:S(2)}, u32[]{:S(2)}) %collective-permute-start.16) | collective-permute-done | bytes 262176 | tf_op jit(solution)/shard_map/ppermute | solution.py:25
  182.5 6.7 %collective-permute-done.17.refs_3_ = bf16[256,512]{1,0:T(8,128)(2,1)S(1)} collective-permute-done((bf16[256,512]{1,0:T(8,128)(2,1)S(1)}, bf16[256,512]{1,0:T(8,128)(2,1)S(1)}, u32[]{:S(2)}, u32[]{:S(2)}) %collective-permute-start.17) | collective-permute-done | bytes 262176 | tf_op jit(solution)/shard_map/ppermute | solution.py:25
  189.2 4.0 %shard_map.81 = (bf16[256,1024]{1,0:T(8,128)(2,1)S(1)}, bf16[64,1024]{1,0:T(8,128)(2,1)S(1)}) custom-call(s32[5]{0:T(128)S(1)} %stack.46.where, bf16[2,256,2048]{2,1,0:T(8,128)(2,1)S(1)} %bitcast.19, bf16[2,64,2048]{2,1,0:T(8,128)(2,1)S(1)} %bitcast.22, bf16[256,512]{1,0:T(8,128)(2,1)S(1)} %get-tuple-element.55.refs_0_, ...), custom_call_target="tpu_custom_call" | custom-call | flops 1 | bytes 1 | tf_op jit(solution)/shard_map/pallas_call | solution.py:391
  193.1 1.3 collective-permute-start.19
  194.4 0.6 collective-permute-start.21
  195.0 4.0 %shard_map.82 = (bf16[256,1024]{1,0:T(8,128)(2,1)S(1)}, bf16[64,2048]{1,0:T(8,128)(2,1)S(1)}) custom-call(s32[5]{0:T(128)S(1)} %stack.46.where, bf16[2,256,2048]{2,1,0:T(8,128)(2,1)S(1)} %bitcast.20, bf16[2,64,2048]{2,1,0:T(8,128)(2,1)S(1)} %bitcast.23, bf16[256,512]{1,0:T(8,128)(2,1)S(1)} %get-tuple-element.55.refs_0_, ...), custom_call_target="tpu_custom_call" | custom-call | flops 1 | bytes 1 | tf_op jit(solution)/shard_map/pallas_call | solution.py:391
  199.0 1.3 collective-permute-start.22
  200.3 10.4 %collective-permute-done.19.refs_0_ = bf16[256,1024]{1,0:T(8,128)(2,1)S(1)} collective-permute-done((bf16[256,1024]{1,0:T(8,128)(2,1)S(1)}, bf16[256,1024]{1,0:T(8,128)(2,1)S(1)}, u32[]{:S(2)}, u32[]{:S(2)}) %collective-permute-start.19) | collective-permute-done | bytes 524320 | tf_op jit(solution)/shard_map/ppermute | solution.py:47
  210.7 2.3 collective-permute-start.26
  213.0 1.3 collective-permute-start.23
  214.3 5.9 %collective-permute-done.23.refs_8_ = bf16[64,2048]{1,0:T(8,128)(2,1)S(1)} collective-permute-done((bf16[64,2048]{1,0:T(8,128)(2,1)S(1)}, bf16[64,2048]{1,0:T(8,128)(2,1)S(1)}, u32[]{:S(2)}, u32[]{:S(2)}) %collective-permute-start.23) | collective-permute-done | bytes 262176 | tf_op jit(solution)/shard_map/ppermute | solution.py:47
  220.2 1.8 collective-permute-done.22.refs_2_
  222.0 1.3 collective-permute-start.20
  223.3 0.0 collective-permute-start.24
  223.3 0.5 collective-permute-start.27
  223.8 2.2 collective-permute-done.27.refs_9_
  226.0 2.3 %shard_map.83 = (bf16[2,256,2048]{2,1,0:T(8,128)(2,1)}, bf16[2,64,2048]{2,1,0:T(8,128)(2,1)}) custom-call(s32[5]{0:T(128)S(1)} %stack.46.where, bf16[256,1024]{1,0:T(8,128)(2,1)S(1)} %collective-permute-done.19.refs_0_, bf16[256,1024]{1,0:T(8,128)(2,1)S(1)} %collective-permute-done.20.refs_1_, bf16[256,1024]{1,0:T(8,128)(2,1)S(1)} %collective-permute-done.22.refs_2_, ...), custom_call_target="tpu_custom_call" | custom-call | flops 1 | bytes 1 | tf_op jit(solution)/shard_map/pallas_call | solution.py:453
  (23 shorter events, 0.1 us)
Async XLA Ops:
  0.7 1.4 copy-start.4
  2.9 17.8 %collective-permute-start.1 = (bf16[3,256,256]{2,1,0:T(8,128)(2,1)S(1)}, bf16[3,256,256]{2,1,0:T(8,128)(2,1)S(1)}, u32[]{:S(2)}, u32[]{:S(2)}) collective-permute-start(bf16[3,256,256]{2,1,0:T(8,128)(2,1)S(1)} %get-tuple-element.40), channel_id=1, source_target_pairs={{0,2},{2,4},{4,6},{6,0},{8,10},{10,12},{12,14},{14,8},{1,3},{3,5},... | collective-permute-start | bytes 1179656 | tf_op jit(solution)/shard_map/ppermute | solution.py:25
  4.2 19.4 %collective-permute-start.2 = (bf16[3,256,256]{2,1,0:T(8,128)(2,1)S(1)}, bf16[3,256,256]{2,1,0:T(8,128)(2,1)S(1)}, u32[]{:S(2)}, u32[]{:S(2)}) collective-permute-start(bf16[3,256,256]{2,1,0:T(8,128)(2,1)S(1)} %get-tuple-element.41), channel_id=1, source_target_pairs={{0,4},{2,6},{4,0},{6,2},{8,12},{10,14},{12,8},{14,10},{1,5},{3,7},... | collective-permute-start | bytes 1179656 | tf_op jit(solution)/shard_map/ppermute | solution.py:25
  6.7 16.9 %collective-permute-start.3 = (bf16[3,256,256]{2,1,0:T(8,128)(2,1)S(1)}, bf16[3,256,256]{2,1,0:T(8,128)(2,1)S(1)}, u32[]{:S(2)}, u32[]{:S(2)}) collective-permute-start(bf16[3,256,256]{2,1,0:T(8,128)(2,1)S(1)} %get-tuple-element.42), channel_id=1, source_target_pairs={{0,6},{2,0},{4,2},{6,4},{8,14},{10,8},{12,10},{14,12},{1,7},{3,1},... | collective-permute-start | bytes 1179656 | tf_op jit(solution)/shard_map/ppermute | solution.py:25
  7.8 19.9 %collective-permute-start = (bf16[1024,256]{1,0:T(8,128)(2,1)}, bf16[1024,256]{1,0:T(8,128)(2,1)S(1)}, u32[]{:S(2)}, u32[]{:S(2)}) collective-permute-start(bf16[1024,256]{1,0:T(8,128)(2,1)} %bitcast.27), channel_id=1, source_target_pairs={{0,8},{2,10},{4,12},{6,14},{8,0},{10,2},{12,4},{14,6},{1,9},{3,11}... | collective-permute-start | bytes 1572872 | tf_op jit(solution)/shard_map/ppermute | solution.py:39
  14.7 1.6 copy-start
  16.3 1.0 copy-start.2
  17.4 0.7 copy-start.5
  18.1 0.7 copy-start.6
  20.7 7.1 %copy-start.7 = (bf16[1,1024,256]{2,1,0:T(8,128)(2,1)S(1)}, bf16[1,1024,256]{2,1,0:T(8,128)(2,1)}, u32[]{:S(2)}) copy-start(bf16[1,1024,256]{2,1,0:T(8,128)(2,1)} %param.11) | copy-start | bytes 1572868
  23.8 66.1 %collective-permute-start.7 = (bf16[4,3,256,256]{3,2,1,0:T(8,128)(2,1)S(1)}, bf16[4,3,256,256]{3,2,1,0:T(8,128)(2,1)S(1)}, u32[]{:S(2)}, u32[]{:S(2)}) collective-permute-start(bf16[4,3,256,256]{3,2,1,0:T(8,128)(2,1)S(1)} %pad_maximum_fusion.refs_4_), channel_id=1, source_target_pairs={{0,1},{1,0},{2,3},{3,2},{4,5},{5,4},{6,7},{7,6},{8,9},{9,8},{10,11... | collective-permute-start | bytes 4718600 | tf_op jit(solution)/shard_map/ppermute | solution.py:43
  27.8 31.5 %collective-permute-start.4 = (bf16[336,2048]{1,0:T(8,128)(2,1)S(1)}, bf16[336,2048]{1,0:T(8,128)(2,1)S(1)}, u32[]{:S(2)}, u32[]{:S(2)}) collective-permute-start(bf16[336,2048]{1,0:T(8,128)(2,1)S(1)} %get-tuple-element.46.refs_0_), channel_id=1, source_target_pairs={{0,2},{2,4},{4,6},{6,0},{8,10},{10,12},{12,14},{14,8},{1,3},{3,5},... | collective-permute-start | bytes 4128776 | tf_op jit(solution)/shard_map/ppermute | solution.py:25
  28.2 58.9 %collective-permute-start.5 = (bf16[336,2048]{1,0:T(8,128)(2,1)S(1)}, bf16[336,2048]{1,0:T(8,128)(2,1)S(1)}, u32[]{:S(2)}, u32[]{:S(2)}) collective-permute-start(bf16[336,2048]{1,0:T(8,128)(2,1)S(1)} %get-tuple-element.46.refs_0_), channel_id=1, source_target_pairs={{0,4},{2,6},{4,0},{6,2},{8,12},{10,14},{12,8},{14,10},{1,5},{3,7},... | collective-permute-start | bytes 4128776 | tf_op jit(solution)/shard_map/ppermute | solution.py:25
  29.4 60.5 %collective-permute-start.6 = (bf16[336,2048]{1,0:T(8,128)(2,1)S(1)}, bf16[336,2048]{1,0:T(8,128)(2,1)S(1)}, u32[]{:S(2)}, u32[]{:S(2)}) collective-permute-start(bf16[336,2048]{1,0:T(8,128)(2,1)S(1)} %get-tuple-element.46.refs_0_), channel_id=1, source_target_pairs={{0,6},{2,0},{4,2},{6,4},{8,14},{10,8},{12,10},{14,12},{1,7},{3,1},... | collective-permute-start | bytes 4128776 | tf_op jit(solution)/shard_map/ppermute | solution.py:25
  30.7 69.0 %collective-permute-start.8 = (bf16[4,3,256,256]{3,2,1,0:T(8,128)(2,1)S(1)}, bf16[4,3,256,256]{3,2,1,0:T(8,128)(2,1)S(1)}, u32[]{:S(2)}, u32[]{:S(2)}) collective-permute-start(bf16[4,3,256,256]{3,2,1,0:T(8,128)(2,1)S(1)} %pad_maximum_fusion.refs_4_), channel_id=1, source_target_pairs={{0,8},{2,10},{4,12},{6,14},{8,0},{10,2},{12,4},{14,6},{1,9},{3,11}... | collective-permute-start | bytes 4718600 | tf_op jit(solution)/shard_map/ppermute | solution.py:39
  95.1 25.4 %collective-permute-start.9 = (bf16[2048,256]{1,0:T(8,128)(2,1)S(1)}, bf16[2048,256]{1,0:T(8,128)(2,1)S(1)}, u32[]{:S(2)}, u32[]{:S(2)}) collective-permute-start(bf16[2048,256]{1,0:T(8,128)(2,1)S(1)} %pad_maximum_fusion.1), channel_id=1, source_target_pairs={{0,2},{2,4},{4,6},{6,0},{8,10},{10,12},{12,14},{14,8},{1,3},{3,5},... | collective-permute-start | bytes 3145736 | tf_op jit(solution)/shard_map/ppermute | solution.py:25
  96.6 48.2 %collective-permute-start.10 = (bf16[2048,256]{1,0:T(8,128)(2,1)S(1)}, bf16[2048,256]{1,0:T(8,128)(2,1)S(1)}, u32[]{:S(2)}, u32[]{:S(2)}) collective-permute-start(bf16[2048,256]{1,0:T(8,128)(2,1)S(1)} %pad_maximum_fusion.1), channel_id=1, source_target_pairs={{0,4},{2,6},{4,0},{6,2},{8,12},{10,14},{12,8},{14,10},{1,5},{3,7},... | collective-permute-start | bytes 3145736 | tf_op jit(solution)/shard_map/ppermute | solution.py:25
  99.7 45.0 %collective-permute-start.11 = (bf16[2048,256]{1,0:T(8,128)(2,1)S(1)}, bf16[2048,256]{1,0:T(8,128)(2,1)S(1)}, u32[]{:S(2)}, u32[]{:S(2)}) collective-permute-start(bf16[2048,256]{1,0:T(8,128)(2,1)S(1)} %pad_maximum_fusion.1), channel_id=1, source_target_pairs={{0,6},{2,0},{4,2},{6,4},{8,14},{10,8},{12,10},{14,12},{1,7},{3,1},... | collective-permute-start | bytes 3145736 | tf_op jit(solution)/shard_map/ppermute | solution.py:25
  144.7 3.4 %collective-permute-start.12 = (bf16[2,3,256,256]{3,2,1,0:T(8,128)(2,1)S(1)}, bf16[2,3,256,256]{3,2,1,0:T(8,128)(2,1)S(1)}, u32[]{:S(2)}, u32[]{:S(2)}) collective-permute-start(bf16[2,3,256,256]{3,2,1,0:T(8,128)(2,1)S(1)} %get-tuple-element.53), channel_id=1, source_target_pairs={{0,1},{1,0},{2,3},{3,2},{4,5},{5,4},{6,7},{7,6},{8,9},{9,8},{10,11... | collective-permute-start | bytes 2359304 | tf_op jit(solution)/shard_map/ppermute | solution.py:43
  146.3 3.0 %collective-permute-start.13 = (bf16[2,3,256,256]{3,2,1,0:T(8,128)(2,1)S(1)}, bf16[2,3,256,256]{3,2,1,0:T(8,128)(2,1)S(1)}, u32[]{:S(2)}, u32[]{:S(2)}) collective-permute-start(bf16[2,3,256,256]{3,2,1,0:T(8,128)(2,1)S(1)} %get-tuple-element.54), channel_id=1, source_target_pairs={{0,1},{1,0},{2,3},{3,2},{4,5},{5,4},{6,7},{7,6},{8,9},{9,8},{10,11... | collective-permute-start | bytes 2359304 | tf_op jit(solution)/shard_map/ppermute | solution.py:43
  149.6 39.5 %collective-permute-start.18 = (bf16[8192,256]{1,0:T(8,128)(2,1)S(1)}, bf16[8192,256]{1,0:T(8,128)(2,1)S(1)}, u32[]{:S(2)}, u32[]{:S(2)}) collective-permute-start(bf16[8192,256]{1,0:T(8,128)(2,1)S(1)} %constant_dynamic-update-slice_fusion.refs_4_), channel_id=1, source_target_pairs={{0,1},{1,0},{2,3},{3,2},{4,5},{5,4},{6,7},{7,6},{8,9},{9,8},{10,11... | collective-permute-start | bytes 12582920 | tf_op jit(solution)/shard_map/ppermute | solution.py:43
  150.1 39.1 %copy-start.1 = (bf16[1,2,256,2048]{3,2,1,0:T(8,128)(2,1)S(1)}, bf16[1,2,256,2048]{3,2,1,0:T(8,128)(2,1)}, u32[]{:S(2)}) copy-start(bf16[1,2,256,2048]{3,2,1,0:T(8,128)(2,1)} %param.6) | copy-start | bytes 6291460
  150.1 39.1 %copy-start.3 = (bf16[1,2,64,2048]{3,2,1,0:T(8,128)(2,1)S(1)}, bf16[1,2,64,2048]{3,2,1,0:T(8,128)(2,1)}, u32[]{:S(2)}) copy-start(bf16[1,2,64,2048]{3,2,1,0:T(8,128)(2,1)} %param.7) | copy-start | bytes 1572868
  159.3 15.4 %collective-permute-start.14 = (bf16[64,2048]{1,0:T(8,128)(2,1)S(1)}, bf16[64,2048]{1,0:T(8,128)(2,1)S(1)}, u32[]{:S(2)}, u32[]{:S(2)}) collective-permute-start(bf16[64,2048]{1,0:T(8,128)(2,1)S(1)} %get-tuple-element.56), channel_id=1, source_target_pairs={{0,16},{16,32},{32,48},{48,64},{64,80},{80,96},{96,112},{112,128},... | collective-permute-start | bytes 786440 | tf_op jit(solution)/shard_map/ppermute | solution.py:47
  160.6 39.7 %collective-permute-start.25 = (bf16[256,2048]{1,0:T(8,128)(2,1)S(1)}, bf16[256,2048]{1,0:T(8,128)(2,1)S(1)}, u32[]{:S(2)}, u32[]{:S(2)}) collective-permute-start(bf16[256,2048]{1,0:T(8,128)(2,1)S(1)} %get-tuple-element.72), channel_id=1, source_target_pairs={{128,144},{144,160},{160,176},{176,192},{192,208},{208,224},{224,2... | collective-permute-start | bytes 3145736 | tf_op jit(solution)/shard_map/ppermute | solution.py:47
  171.8 7.5 %collective-permute-start.15 = (bf16[256,512]{1,0:T(8,128)(2,1)S(1)}, bf16[256,512]{1,0:T(8,128)(2,1)S(1)}, u32[]{:S(2)}, u32[]{:S(2)}) collective-permute-start(bf16[256,512]{1,0:T(8,128)(2,1)S(1)} %get-tuple-element.58), channel_id=1, source_target_pairs={{0,6},{2,0},{4,2},{6,4},{8,14},{10,8},{12,10},{14,12},{1,7},{3,1},... | collective-permute-start | bytes 786440 | tf_op jit(solution)/shard_map/ppermute | solution.py:25
  173.8 8.7 %collective-permute-start.16 = (bf16[256,512]{1,0:T(8,128)(2,1)S(1)}, bf16[256,512]{1,0:T(8,128)(2,1)S(1)}, u32[]{:S(2)}, u32[]{:S(2)}) collective-permute-start(bf16[256,512]{1,0:T(8,128)(2,1)S(1)} %get-tuple-element.59), channel_id=1, source_target_pairs={{0,4},{2,6},{4,0},{6,2},{8,12},{10,14},{12,8},{14,10},{1,5},{3,7},... | collective-permute-start | bytes 786440 | tf_op jit(solution)/shard_map/ppermute | solution.py:25
  174.7 14.5 %collective-permute-start.17 = (bf16[256,512]{1,0:T(8,128)(2,1)S(1)}, bf16[256,512]{1,0:T(8,128)(2,1)S(1)}, u32[]{:S(2)}, u32[]{:S(2)}) collective-permute-start(bf16[256,512]{1,0:T(8,128)(2,1)S(1)} %get-tuple-element.60), channel_id=1, source_target_pairs={{0,2},{2,4},{4,6},{6,0},{8,10},{10,12},{12,14},{14,8},{1,3},{3,5},... | collective-permute-start | bytes 786440 | tf_op jit(solution)/shard_map/ppermute | solution.py:25
  193.1 17.6 %collective-permute-start.19 = (bf16[256,1024]{1,0:T(8,128)(2,1)S(1)}, bf16[256,1024]{1,0:T(8,128)(2,1)S(1)}, u32[]{:S(2)}, u32[]{:S(2)}) collective-permute-start(bf16[256,1024]{1,0:T(8,128)(2,1)S(1)} %get-tuple-element.65), channel_id=1, source_target_pairs={{0,16},{16,32},{32,48},{48,64},{64,80},{80,96},{96,112},{112,128},... | collective-permute-start | bytes 1572872 | tf_op jit(solution)/shard_map/ppermute | solution.py:47
  194.4 4.6 %collective-permute-start.21 = (bf16[64,2048]{1,0:T(8,128)(2,1)S(1)}, bf16[64,2048]{1,0:T(8,128)(2,1)S(1)}, u32[]{:S(2)}, u32[]{:S(2)}) collective-permute-start(bf16[64,2048]{1,0:T(8,128)(2,1)S(1)} %collective-permute-done.14.refs_6_), channel_id=1, source_target_pairs={{0,1},{1,0},{2,3},{3,2},{4,5},{5,4},{6,7},{7,6},{8,9},{9,8},{10,11... | collective-permute-start | bytes 786440 | tf_op jit(solution)/shard_map/ppermute | solution.py:43
  199.0 22.9 %collective-permute-start.22 = (bf16[256,1024]{1,0:T(8,128)(2,1)S(1)}, bf16[256,1024]{1,0:T(8,128)(2,1)S(1)}, u32[]{:S(2)}, u32[]{:S(2)}) collective-permute-start(bf16[256,1024]{1,0:T(8,128)(2,1)S(1)} %get-tuple-element.68), channel_id=1, source_target_pairs={{0,16},{16,32},{32,48},{48,64},{64,80},{80,96},{96,112},{112,128},... | collective-permute-start | bytes 1572872 | tf_op jit(solution)/shard_map/ppermute | solution.py:47
  210.7 15.2 %collective-permute-start.26 = (bf16[256,2048]{1,0:T(8,128)(2,1)S(1)}, bf16[256,2048]{1,0:T(8,128)(2,1)S(1)}, u32[]{:S(2)}, u32[]{:S(2)}) collective-permute-start(bf16[256,2048]{1,0:T(8,128)(2,1)S(1)} %collective-permute-done.25.refs_4_), channel_id=1, source_target_pairs={{0,1},{1,0},{2,3},{3,2},{4,5},{5,4},{6,7},{7,6},{8,9},{9,8},{10,11... | collective-permute-start | bytes 3145736 | tf_op jit(solution)/shard_map/ppermute | solution.py:43
  213.0 7.2 %collective-permute-start.23 = (bf16[64,2048]{1,0:T(8,128)(2,1)S(1)}, bf16[64,2048]{1,0:T(8,128)(2,1)S(1)}, u32[]{:S(2)}, u32[]{:S(2)}) collective-permute-start(bf16[64,2048]{1,0:T(8,128)(2,1)S(1)} %get-tuple-element.69), channel_id=1, source_target_pairs={{128,144},{144,160},{160,176},{176,192},{192,208},{208,224},{224,2... | collective-permute-start | bytes 786440 | tf_op jit(solution)/shard_map/ppermute | solution.py:47
  222.0 4.0 %collective-permute-start.20 = (bf16[256,1024]{1,0:T(8,128)(2,1)S(1)}, bf16[256,1024]{1,0:T(8,128)(2,1)S(1)}, u32[]{:S(2)}, u32[]{:S(2)}) collective-permute-start(bf16[256,1024]{1,0:T(8,128)(2,1)S(1)} %collective-permute-done.19.refs_0_), channel_id=1, source_target_pairs={{0,1},{1,0},{2,3},{3,2},{4,5},{5,4},{6,7},{7,6},{8,9},{9,8},{10,11... | collective-permute-start | bytes 1572872 | tf_op jit(solution)/shard_map/ppermute | solution.py:43
  223.3 2.7 %collective-permute-start.24 = (bf16[256,1024]{1,0:T(8,128)(2,1)S(1)}, bf16[256,1024]{1,0:T(8,128)(2,1)S(1)}, u32[]{:S(2)}, u32[]{:S(2)}) collective-permute-start(bf16[256,1024]{1,0:T(8,128)(2,1)S(1)} %collective-permute-done.22.refs_2_), channel_id=1, source_target_pairs={{0,1},{1,0},{2,3},{3,2},{4,5},{5,4},{6,7},{7,6},{8,9},{9,8},{10,11... | collective-permute-start | bytes 1572872 | tf_op jit(solution)/shard_map/ppermute | solution.py:43
  223.3 2.7 %collective-permute-start.27 = (bf16[64,2048]{1,0:T(8,128)(2,1)S(1)}, bf16[64,2048]{1,0:T(8,128)(2,1)S(1)}, u32[]{:S(2)}, u32[]{:S(2)}) collective-permute-start(bf16[64,2048]{1,0:T(8,128)(2,1)S(1)} %collective-permute-done.23.refs_8_), channel_id=1, source_target_pairs={{0,1},{1,0},{2,3},{3,2},{4,5},{5,4},{6,7},{7,6},{8,9},{9,8},{10,11... | collective-permute-start | bytes 786440 | tf_op jit(solution)/shard_map/ppermute | solution.py:43

commit v3 on v2

--- a/solution.py
+++ b/solution.py
@@ -47,8 +47,9 @@
     return lax.ppermute(array, "section", [(s, (s + 1) % count) for s in sections])
 
 
-def round_ring(array):
-    return (array,) + tuple(around_x(array, step) for step in range(1, RING))
+def round_ring(array, cut):
+    left, right = around_x(array, 1), around_x(array, -1)
+    return array, left, around_x(left[:cut], 1), around_x(right[cut:], -1), right
 
 
 def after(array, *others):
@@ -146,16 +147,28 @@
 
 
 def start_kernel(where, *refs):
-    rows, parts = refs[:4], refs[4:6]
-    total, far_rows, far_qry, lengths, near_rows, near_qry, weight, sems = refs[6:]
+    rows, parts = refs[:5], refs[5:7]
+    total, far_rows, far_qry, lengths, near_rows, near_qry, weight, sems = refs[7:]
     x, z = where[0], where[1]
     mem, few = far_rows.shape[0] // RING, far_qry.shape[0] // RING
     width = far_rows.shape[1]
     copies = []
 
     def take(slot, first, count, columns, target):
-        source = rows[slot].at[pl.ds(first, count), columns]
-        copies.append(pltpu.make_async_copy(source, target, sems.at[len(copies)]))
+        cut = rows[2].shape[0]
+        pieces = [(rows[slot if slot < 2 else 4], first, count, 0)]
+        if slot == 2:
+            low = min(max(cut - first, 0), count)
+            pieces = [(rows[2], first, low, 0), (rows[3], first + low - cut, count - low, low)]
+        for source, start, size, at in pieces:
+            if size > 0:
+                copies.append(
+                    pltpu.make_async_copy(
+                        source.at[pl.ds(start, size), columns],
+                        target.at[pl.ds(at, size)],
+                        sems.at[len(copies)],
+                    )
+                )
 
     for part, first in ((parts[0], 0), (parts[1], parts[0].shape[3])):
         for step in range(RING):
@@ -195,9 +208,9 @@
 
 
 def attend_kernel(where, total, rows, qry, lengths, *refs):
-    sides = (refs[:1], refs[1:3])
-    outs = refs[3:7]
-    low, mixed = refs[7:]
+    sides = (refs[:1], refs[1:5])
+    outs = refs[5:9]
+    low, mixed = refs[9:]
     mem, few = mixed.shape[1], qry.shape[0] // RING
     encoder = where[2]
 
@@ -283,7 +296,7 @@
             jax.ShapeDtypeStruct((RING * few, half), BF16),
             jax.ShapeDtypeStruct((RING, TAIL, 128), BF16),
         ),
-        [SMEM] + [HBM] * 6,
+        [SMEM] + [HBM] * 7,
         (VMEM,) * 4,
         [
             pltpu.VMEM((RING * mem, half), BF16),
@@ -302,7 +315,7 @@
     return call(
         attend_kernel,
         (out,) * RING,
-        [SMEM] + [VMEM] * 7,
+        [SMEM] + [VMEM] * 9,
         (VMEM,) * RING,
         [
             pltpu.VMEM((planes, RING * mem, columns), BF16),
@@ -500,25 +513,20 @@
     ctx, qry, normed = norm_scene(
         after(where, *own), context, queries, norm_gain, lengths[0]
     )
-    rows = round_ring(after(normed, out_pair, *arrived))
+    cut = (normed.shape[0] // 32 + 1) * 16
+    rows = round_ring(after(normed, out_pair, *arrived), cut)
     started = start_projections(where, mem, few, rows, (near, other_core(near)))
 
-    weights = round_ring(after(out_pair, *rows, started[0]))
-    far = (
-        far,
-        other_core(after(far[:2], started[0], *weights)),
-        other_core(after(far[2:], started[0], *weights)),
-    )
-    weights = both(jnp.concatenate(after(weights, *far)))
-
-    mixed = attend(where, mem, started, far)
-    ctx_early = relay(after(ctx, mixed[0]), decoders, count)
-    qry_early = relay(after(qry, mixed[0]), encoders, count)
+    weights = round_ring(after(out_pair, *rows, started[0]), out_shard.shape[0])
+    far_other = [other_core(after(far[step : step + 1], started[0])) for step in range(RING)]
+
+    mixed = attend(after(where, weights[1], weights[4]), mem, started, (far, *far_other))
+    weights = both(jnp.concatenate(after(weights, mixed[0])))
     mixed = [mixed[0]] + [around_x(mixed[step], -step) for step in range(1, RING)]
-
-    first, few_first = project(
-        0, after(where, qry_early), context, queries, mixed, weights
-    )
+    ctx_early = relay(after(ctx, *mixed), decoders, count)
+    qry_early = relay(after(qry, *mixed), encoders, count)
+
+    first, few_first = project(0, where, context, queries, mixed, weights)
     first = relay(first, encoders, count)
     second, few_new = project(1, where, context, queries, mixed, weights, (few_first,))
     qry_early = (qry_early, other_core(qry_early))

time: 231 us -> 196 us (0.85)
  the two profiles are of different devices: /device:TPU:17 before, /device:TPU:1 now
where the time goes in v3:
time: 196 us; the launch traced here: 195 us
  waiting for transfers between devices  87.5 us (45%)
  starting transfers between devices  72.6 us (37%)
  Pallas kernels  27.9 us (14%)
  local copies, waits for them, and re-layouts  6.06 us (3%)
    ppermute x14, waiting for transfers between devices, around_x(): return lax.ppermute(array, 'dp', pairs)  59.4 us
    ppermute x11, starting transfers between devices, other_core(): return lax.ppermute(array, 'tensor', [(0, 1), (1, 0)])  31.6 us
    ppermute x5, waiting for transfers between devices, relay(): lax.ppermute(array, 'section', [(s, (s + 1) % count) for s in sections])  23.8 us
    ppermute x14, starting transfers between devices, around_x(): return lax.ppermute(array, 'dp', pairs)  18.1 us
    ppermute x2, starting transfers between devices, across_z(): lax.ppermute(array, 'dp', [(d, (d + RING) % (2 * RING)) for d in range(2...  12.6 us
    ppermute x5, starting transfers between devices, relay(): lax.ppermute(array, 'section', [(s, (s + 1) % count) for s in sections])  10.3 us
    pallas_call x1, Pallas kernels, attend(): call(attend_kernel, (out,) * RING, [SMEM] + [VMEM] * 9, (VMEM,) * RING, [...  8.9 us
    pallas_call x2, Pallas kernels, project(): call(functools.partial(project_kernel, part), (jax.ShapeDtypeStruct((mem,...  7.97 us
  transfers between devices with their start and end apart: 32, of which 14 were waited for; matrix products, arithmetic and copies ran while one was open for 0% of the time, Pallas kernels for 13%

profile of v3, /device:TPU:1, one launch (start us, length us, event | category | flops | bytes accessed | tf_op | source)
XLA Modules:
  0.0 195.5 jit_solution(18285442822995372086)
XLA Ops:
  0.6 7.8 %collective-permute-start = (bf16[1024,256]{1,0:T(8,128)(2,1)}, bf16[1024,256]{1,0:T(8,128)(2,1)S(1)}, u32[]{:S(2)}, u32[]{:S(2)}) collective-permute-start(bf16[1024,256]{1,0:T(8,128)(2,1)} %bitcast.27), channel_id=1, source_target_pairs={{0,8},{2,10},{4,12},{6,14},{8,0},{10,2},{12,4},{14,6},{1,9},{3,11}... | collective-permute-start | bytes 1572872 | tf_op jit(solution)/shard_map/ppermute | solution.py:39
  8.5 0.1 stack.46.where
  8.5 1.4 copy-done.4
  9.9 0.8 shard_map.77
  10.7 1.3 collective-permute-start.1
  12.0 2.5 %collective-permute-start.2 = (bf16[3,256,256]{2,1,0:T(8,128)(2,1)S(1)}, bf16[3,256,256]{2,1,0:T(8,128)(2,1)S(1)}, u32[]{:S(2)}, u32[]{:S(2)}) collective-permute-start(bf16[3,256,256]{2,1,0:T(8,128)(2,1)S(1)} %get-tuple-element.44), channel_id=1, source_target_pairs={{0,4},{2,6},{4,0},{6,2},{8,12},{10,14},{12,8},{14,10},{1,5},{3,7},... | collective-permute-start | bytes 1179656 | tf_op jit(solution)/shard_map/ppermute | solution.py:25
  14.4 1.2 collective-permute-start.3
  15.6 1.6 copy-done
  17.2 1.0 copy-done.2
  18.2 0.7 copy-done.5
  18.9 0.7 copy-done.6
  19.6 2.0 %shard_map.78 = (bf16[256,2048]{1,0:T(8,128)(2,1)S(1)}, bf16[64,2048]{1,0:T(8,128)(2,1)S(1)}, bf16[336,2048]{1,0:T(8,128)(2,1)S(1)}) custom-call(s32[5]{0:T(128)S(1)} %stack.46.where, bf16[2,256,2048]{2,1,0:T(8,128)(2,1)S(1)} %bitcast.18, bf16[2,64,2048]{2,1,0:T(8,128)(2,1)S(1)} %bitcast.21, f32[1,2048]{1,0:T(1,128)S(1)} %copy-done.5, s32[2]{0:T(128)S(1)} %bitcast.26), custom_call_target="tpu_custom_call" | custom-call | flops 1 | bytes 1 | tf_op jit(solution)/shard_map/pallas_call | solution.py:135
  21.6 0.3 collective-permute-done
  21.9 0.1 pad_maximum_fusion.1
  22.0 9.1 %collective-permute-done.2 = bf16[3,256,256]{2,1,0:T(8,128)(2,1)S(1)} collective-permute-done((bf16[3,256,256]{2,1,0:T(8,128)(2,1)S(1)}, bf16[3,256,256]{2,1,0:T(8,128)(2,1)S(1)}, u32[]{:S(2)}, u32[]{:S(2)}) %collective-permute-start.2) | collective-permute-done | bytes 393248 | tf_op jit(solution)/shard_map/ppermute | solution.py:25
  31.1 1.7 collective-permute-start.4
  32.8 1.7 collective-permute-start.6
  34.4 0.2 pad_maximum_fusion.refs_5_
  34.6 1.8 collective-permute-start.8
  36.5 4.8 %collective-permute-start.11 = (bf16[4,3,256,256]{3,2,1,0:T(8,128)(2,1)S(1)}, bf16[4,3,256,256]{3,2,1,0:T(8,128)(2,1)S(1)}, u32[]{:S(2)}, u32[]{:S(2)}) collective-permute-start(bf16[4,3,256,256]{3,2,1,0:T(8,128)(2,1)S(1)} %pad_maximum_fusion.refs_5_), channel_id=1, source_target_pairs={{0,8},{2,10},{4,12},{6,14},{8,0},{10,2},{12,4},{14,6},{1,9},{3,11}... | collective-permute-start | bytes 4718600 | tf_op jit(solution)/shard_map/ppermute | solution.py:39
  41.3 22.2 %collective-permute-done.4.refs_1_ = bf16[336,2048]{1,0:T(8,128)(2,1)S(1)} collective-permute-done((bf16[336,2048]{1,0:T(8,128)(2,1)S(1)}, bf16[336,2048]{1,0:T(8,128)(2,1)S(1)}, u32[]{:S(2)}, u32[]{:S(2)}) %collective-permute-start.4) | collective-permute-done | bytes 1376288 | tf_op jit(solution)/shard_map/ppermute | solution.py:25
  63.5 0.1 slice.32
  63.5 0.1 collective-permute-start.5
  63.7 2.7 %collective-permute-start.7 = (bf16[160,2048]{1,0:T(8,128)(2,1)S(1)}, bf16[160,2048]{1,0:T(8,128)(2,1)S(1)}, u32[]{:S(2)}, u32[]{:S(2)}) collective-permute-start(bf16[160,2048]{1,0:T(8,128)(2,1)S(1)} %slice.33), channel_id=1, source_target_pairs={{0,6},{2,0},{4,2},{6,4},{8,14},{10,8},{12,10},{14,12},{1,7},{3,1},... | collective-permute-start | bytes 1966088 | tf_op jit(solution)/shard_map/ppermute | solution.py:25
  66.4 11.6 %collective-permute-done.7.refs_3_ = bf16[160,2048]{1,0:T(8,128)(2,1)S(1)} collective-permute-done((bf16[160,2048]{1,0:T(8,128)(2,1)S(1)}, bf16[160,2048]{1,0:T(8,128)(2,1)S(1)}, u32[]{:S(2)}, u32[]{:S(2)}) %collective-permute-start.7) | collective-permute-done | bytes 655392 | tf_op jit(solution)/shard_map/ppermute | solution.py:25
  78.1 2.3 %collective-permute-done.5.refs_2_ = bf16[176,2048]{1,0:T(8,128)(2,1)S(1)} collective-permute-done((bf16[176,2048]{1,0:T(8,128)(2,1)S(1)}, bf16[176,2048]{1,0:T(8,128)(2,1)S(1)}, u32[]{:S(2)}, u32[]{:S(2)}) %collective-permute-start.5) | collective-permute-done | bytes 720928 | tf_op jit(solution)/shard_map/ppermute | solution.py:25
  80.3 6.0 %shard_map.79 = (f32[3,1024,512]{2,1,0:T(8,128)S(1)}, bf16[1024,1024]{1,0:T(8,128)(2,1)S(1)}, bf16[256,1024]{1,0:T(8,128)(2,1)S(1)}, bf16[4,16,128]{2,1,0:T(8,128)(2,1)S(1)}) custom-call(s32[5]{0:T(128)S(1)} %stack.46.where, bf16[336,2048]{1,0:T(8,128)(2,1)S(1)} %get-tuple-element.48.refs_0_, bf16[336,2048]{1,0:T(8,128)(2,1)S(1)} %collective-permute-done.4.refs_1_, ...), custom_call_target="tpu_custom_call" | custom-call | flops 1 | bytes 1 | tf_op jit(solution)/shard_map/pallas_call | solution.py:291
  86.3 0.1 collective-permute-start.9
  86.4 2.7 %collective-permute-start.10 = (bf16[2048,256]{1,0:T(8,128)(2,1)S(1)}, bf16[2048,256]{1,0:T(8,128)(2,1)S(1)}, u32[]{:S(2)}, u32[]{:S(2)}) collective-permute-start(bf16[2048,256]{1,0:T(8,128)(2,1)S(1)} %pad_maximum_fusion.1), channel_id=1, source_target_pairs={{0,6},{2,0},{4,2},{6,4},{8,14},{10,8},{12,10},{14,12},{1,7},{3,1},... | collective-permute-start | bytes 3145736 | tf_op jit(solution)/shard_map/ppermute | solution.py:25
  89.1 0.1 fusion
  89.2 21.0 %collective-permute-start.12 = (bf16[1,3,256,256]{3,2,1,0:T(8,128)(2,1)S(1)}, bf16[1,3,256,256]{3,2,1,0:T(8,128)(2,1)S(1)}, u32[]{:S(2)}, u32[]{:S(2)}) collective-permute-start(bf16[1,3,256,256]{3,2,1,0:T(8,128)(2,1)S(1)} %get-tuple-element.56), channel_id=1, source_target_pairs={{0,1},{1,0},{2,3},{3,2},{4,5},{5,4},{6,7},{7,6},{8,9},{9,8},{10,11... | collective-permute-start | bytes 1179656 | tf_op jit(solution)/shard_map/ppermute | solution.py:43
  110.2 0.1 collective-permute-start.19
  110.4 2.7 %collective-permute-start.20 = (bf16[1024,256]{1,0:T(8,128)(2,1)S(1)}, bf16[1024,256]{1,0:T(8,128)(2,1)S(1)}, u32[]{:S(2)}, u32[]{:S(2)}) collective-permute-start(bf16[1024,256]{1,0:T(8,128)(2,1)S(1)} %slice.39), channel_id=1, source_target_pairs={{0,6},{2,0},{4,2},{6,4},{8,14},{10,8},{12,10},{14,12},{1,7},{3,1},... | collective-permute-start | bytes 1572872 | tf_op jit(solution)/shard_map/ppermute | solution.py:25
  113.1 3.5 %collective-permute-start.13 = (bf16[1,3,256,256]{3,2,1,0:T(8,128)(2,1)S(1)}, bf16[1,3,256,256]{3,2,1,0:T(8,128)(2,1)S(1)}, u32[]{:S(2)}, u32[]{:S(2)}) collective-permute-start(bf16[1,3,256,256]{3,2,1,0:T(8,128)(2,1)S(1)} %get-tuple-element.57), channel_id=1, source_target_pairs={{0,1},{1,0},{2,3},{3,2},{4,5},{5,4},{6,7},{7,6},{8,9},{9,8},{10,11... | collective-permute-start | bytes 1179656 | tf_op jit(solution)/shard_map/ppermute | solution.py:43
  116.7 0.5 collective-permute-start.15
  117.2 0.8 collective-permute-done.13.refs_2_
  118.0 0.6 collective-permute-done.14.refs_3_
  118.6 0.6 collective-permute-done.15.refs_4_
  119.1 8.9 %shard_map.80 = (bf16[256,512]{1,0:T(8,128)(2,1)S(1)}, bf16[256,512]{1,0:T(8,128)(2,1)S(1)}, bf16[256,512]{1,0:T(8,128)(2,1)S(1)}, bf16[256,512]{1,0:T(8,128)(2,1)S(1)}) custom-call(s32[5]{0:T(128)S(1)} %stack.46.where, f32[3,1024,512]{2,1,0:T(8,128)S(1)} %get-tuple-element.49.total, bf16[1024,1024]{1,0:T(8,128)(2,1)S(1)} %get-tuple-element.52.rows, ...), custom_call_target="tpu_custom_call" | custom-call | flops 1 | bytes 1 | tf_op jit(solution)/shard_map/pallas_call | solution.py:315
  128.1 0.1 constant_dynamic-update-slice_fusion.4
  128.1 0.1 constant_dynamic-update-slice_fusion.3
  128.3 0.1 constant_dynamic-update-slice_fusion.refs_4_
  128.4 0.5 collective-permute-start.21
  128.9 0.2 collective-permute-start.16
  129.1 0.1 collective-permute-start.17
  129.2 1.1 collective-permute-start.18
  130.3 6.3 %collective-permute-done.16.refs_1_ = bf16[256,512]{1,0:T(8,128)(2,1)S(1)} collective-permute-done((bf16[256,512]{1,0:T(8,128)(2,1)S(1)}, bf16[256,512]{1,0:T(8,128)(2,1)S(1)}, u32[]{:S(2)}, u32[]{:S(2)}) %collective-permute-start.16) | collective-permute-done | bytes 262176 | tf_op jit(solution)/shard_map/ppermute | solution.py:25
  136.6 1.6 collective-permute-done.17.refs_2_
  138.2 6.3 %collective-permute-done.18.refs_3_ = bf16[256,512]{1,0:T(8,128)(2,1)S(1)} collective-permute-done((bf16[256,512]{1,0:T(8,128)(2,1)S(1)}, bf16[256,512]{1,0:T(8,128)(2,1)S(1)}, u32[]{:S(2)}, u32[]{:S(2)}) %collective-permute-start.18) | collective-permute-done | bytes 262176 | tf_op jit(solution)/shard_map/ppermute | solution.py:25
  144.5 1.3 collective-permute-start.29
  145.7 2.8 %collective-permute-start.24 = (bf16[64,2048]{1,0:T(8,128)(2,1)S(1)}, bf16[64,2048]{1,0:T(8,128)(2,1)S(1)}, u32[]{:S(2)}, u32[]{:S(2)}) collective-permute-start(bf16[64,2048]{1,0:T(8,128)(2,1)S(1)} %get-tuple-element.73), channel_id=1, source_target_pairs={{0,16},{16,32},{32,48},{48,64},{64,80},{80,96},{96,112},{112,128},... | collective-permute-start | bytes 786440 | tf_op jit(solution)/shard_map/ppermute | solution.py:47
  148.6 4.0 %shard_map.81 = (bf16[256,1024]{1,0:T(8,128)(2,1)S(1)}, bf16[64,1024]{1,0:T(8,128)(2,1)S(1)}) custom-call(s32[5]{0:T(128)S(1)} %stack.46.where, bf16[2,256,2048]{2,1,0:T(8,128)(2,1)S(1)} %bitcast.19, bf16[2,64,2048]{2,1,0:T(8,128)(2,1)S(1)} %bitcast.22, bf16[256,512]{1,0:T(8,128)(2,1)S(1)} %get-tuple-element.60.refs_0_, ...), custom_call_target="tpu_custom_call" | custom-call | flops 1 | bytes 1 | tf_op jit(solution)/shard_map/pallas_call | solution.py:404
  152.6 3.1 %collective-permute-start.22 = (bf16[256,1024]{1,0:T(8,128)(2,1)S(1)}, bf16[256,1024]{1,0:T(8,128)(2,1)S(1)}, u32[]{:S(2)}, u32[]{:S(2)}) collective-permute-start(bf16[256,1024]{1,0:T(8,128)(2,1)S(1)} %get-tuple-element.69), channel_id=1, source_target_pairs={{0,16},{16,32},{32,48},{48,64},{64,80},{80,96},{96,112},{112,128},... | collective-permute-start | bytes 1572872 | tf_op jit(solution)/shard_map/ppermute | solution.py:47
  155.7 1.6 collective-permute-start.25
  157.3 4.0 %shard_map.82 = (bf16[256,1024]{1,0:T(8,128)(2,1)S(1)}, bf16[64,2048]{1,0:T(8,128)(2,1)S(1)}) custom-call(s32[5]{0:T(128)S(1)} %stack.46.where, bf16[2,256,2048]{2,1,0:T(8,128)(2,1)S(1)} %bitcast.20, bf16[2,64,2048]{2,1,0:T(8,128)(2,1)S(1)} %bitcast.23, bf16[256,512]{1,0:T(8,128)(2,1)S(1)} %get-tuple-element.60.refs_0_, ...), custom_call_target="tpu_custom_call" | custom-call | flops 1 | bytes 1 | tf_op jit(solution)/shard_map/pallas_call | solution.py:404
  161.4 1.8 collective-permute-start.26
  163.2 11.3 %collective-permute-done.29.refs_4_ = bf16[256,2048]{1,0:T(8,128)(2,1)S(1)} collective-permute-done((bf16[256,2048]{1,0:T(8,128)(2,1)S(1)}, bf16[256,2048]{1,0:T(8,128)(2,1)S(1)}, u32[]{:S(2)}, u32[]{:S(2)}) %collective-permute-start.29) | collective-permute-done | bytes 1048608 | tf_op jit(solution)/shard_map/ppermute | solution.py:47
  174.5 1.3 collective-permute-start.30
  175.8 1.3 collective-permute-start.27
  177.1 12.4 %collective-permute-done.27.refs_8_ = bf16[64,2048]{1,0:T(8,128)(2,1)S(1)} collective-permute-done((bf16[64,2048]{1,0:T(8,128)(2,1)S(1)}, bf16[64,2048]{1,0:T(8,128)(2,1)S(1)}, u32[]{:S(2)}, u32[]{:S(2)}) %collective-permute-start.27) | collective-permute-done | bytes 262176 | tf_op jit(solution)/shard_map/ppermute | solution.py:47
  189.6 0.8 collective-permute-start.23
  190.3 0.5 collective-permute-start.31
  190.9 2.2 %collective-permute-done.31.refs_9_ = bf16[64,2048]{1,0:T(8,128)(2,1)S(1)} collective-permute-done((bf16[64,2048]{1,0:T(8,128)(2,1)S(1)}, bf16[64,2048]{1,0:T(8,128)(2,1)S(1)}, u32[]{:S(2)}, u32[]{:S(2)}) %collective-permute-start.31) | collective-permute-done | bytes 262176 | tf_op jit(solution)/shard_map/ppermute | solution.py:43
  193.0 2.3 %shard_map.83 = (bf16[2,256,2048]{2,1,0:T(8,128)(2,1)}, bf16[2,64,2048]{2,1,0:T(8,128)(2,1)}) custom-call(s32[5]{0:T(128)S(1)} %stack.46.where, bf16[256,1024]{1,0:T(8,128)(2,1)S(1)} %collective-permute-done.22.refs_0_, bf16[256,1024]{1,0:T(8,128)(2,1)S(1)} %collective-permute-done.23.refs_1_, bf16[256,1024]{1,0:T(8,128)(2,1)S(1)} %collective-permute-done.26.refs_2_, ...), custom_call_target="tpu_custom_call" | custom-call | flops 1 | bytes 1 | tf_op jit(solution)/shard_map/pallas_call | solution.py:466
  (36 shorter events, 0.3 us)
Async XLA Ops:
  0.6 21.2 %collective-permute-start = (bf16[1024,256]{1,0:T(8,128)(2,1)}, bf16[1024,256]{1,0:T(8,128)(2,1)S(1)}, u32[]{:S(2)}, u32[]{:S(2)}) collective-permute-start(bf16[1024,256]{1,0:T(8,128)(2,1)} %bitcast.27), channel_id=1, source_target_pairs={{0,8},{2,10},{4,12},{6,14},{8,0},{10,2},{12,4},{14,6},{1,9},{3,11}... | collective-permute-start | bytes 1572872 | tf_op jit(solution)/shard_map/ppermute | solution.py:39
  8.5 1.4 copy-start.4
  9.9 11.9 %copy-start.7 = (bf16[1,1024,256]{2,1,0:T(8,128)(2,1)S(1)}, bf16[1,1024,256]{2,1,0:T(8,128)(2,1)}, u32[]{:S(2)}) copy-start(bf16[1,1024,256]{2,1,0:T(8,128)(2,1)} %param.11) | copy-start | bytes 1572868
  10.7 11.2 %collective-permute-start.1 = (bf16[3,256,256]{2,1,0:T(8,128)(2,1)S(1)}, bf16[3,256,256]{2,1,0:T(8,128)(2,1)S(1)}, u32[]{:S(2)}, u32[]{:S(2)}) collective-permute-start(bf16[3,256,256]{2,1,0:T(8,128)(2,1)S(1)} %get-tuple-element.43), channel_id=1, source_target_pairs={{0,2},{2,4},{4,6},{6,0},{8,10},{10,12},{12,14},{14,8},{1,3},{3,5},... | collective-permute-start | bytes 1179656 | tf_op jit(solution)/shard_map/ppermute | solution.py:25
  12.0 19.1 %collective-permute-start.2 = (bf16[3,256,256]{2,1,0:T(8,128)(2,1)S(1)}, bf16[3,256,256]{2,1,0:T(8,128)(2,1)S(1)}, u32[]{:S(2)}, u32[]{:S(2)}) collective-permute-start(bf16[3,256,256]{2,1,0:T(8,128)(2,1)S(1)} %get-tuple-element.44), channel_id=1, source_target_pairs={{0,4},{2,6},{4,0},{6,2},{8,12},{10,14},{12,8},{14,10},{1,5},{3,7},... | collective-permute-start | bytes 1179656 | tf_op jit(solution)/shard_map/ppermute | solution.py:25
  14.4 16.6 %collective-permute-start.3 = (bf16[3,256,256]{2,1,0:T(8,128)(2,1)S(1)}, bf16[3,256,256]{2,1,0:T(8,128)(2,1)S(1)}, u32[]{:S(2)}, u32[]{:S(2)}) collective-permute-start(bf16[3,256,256]{2,1,0:T(8,128)(2,1)S(1)} %get-tuple-element.45), channel_id=1, source_target_pairs={{0,6},{2,0},{4,2},{6,4},{8,14},{10,8},{12,10},{14,12},{1,7},{3,1},... | collective-permute-start | bytes 1179656 | tf_op jit(solution)/shard_map/ppermute | solution.py:25
  15.6 1.6 copy-start
  17.2 1.0 copy-start.2
  18.2 0.7 copy-start.5
  18.9 0.7 copy-start.6
  31.1 32.4 %collective-permute-start.4 = (bf16[336,2048]{1,0:T(8,128)(2,1)S(1)}, bf16[336,2048]{1,0:T(8,128)(2,1)S(1)}, u32[]{:S(2)}, u32[]{:S(2)}) collective-permute-start(bf16[336,2048]{1,0:T(8,128)(2,1)S(1)} %get-tuple-element.48.refs_0_), channel_id=1, source_target_pairs={{0,2},{2,4},{4,6},{6,0},{8,10},{10,12},{12,14},{14,8},{1,3},{3,5},... | collective-permute-start | bytes 4128776 | tf_op jit(solution)/shard_map/ppermute | solution.py:25
  32.8 30.9 %collective-permute-start.6 = (bf16[336,2048]{1,0:T(8,128)(2,1)S(1)}, bf16[336,2048]{1,0:T(8,128)(2,1)S(1)}, u32[]{:S(2)}, u32[]{:S(2)}) collective-permute-start(bf16[336,2048]{1,0:T(8,128)(2,1)S(1)} %get-tuple-element.48.refs_0_), channel_id=1, source_target_pairs={{0,6},{2,0},{4,2},{6,4},{8,14},{10,8},{12,10},{14,12},{1,7},{3,1},... | collective-permute-start | bytes 4128776 | tf_op jit(solution)/shard_map/ppermute | solution.py:25
  34.6 31.8 %collective-permute-start.8 = (bf16[4,3,256,256]{3,2,1,0:T(8,128)(2,1)S(1)}, bf16[4,3,256,256]{3,2,1,0:T(8,128)(2,1)S(1)}, u32[]{:S(2)}, u32[]{:S(2)}) collective-permute-start(bf16[4,3,256,256]{3,2,1,0:T(8,128)(2,1)S(1)} %pad_maximum_fusion.refs_5_), channel_id=1, source_target_pairs={{0,1},{1,0},{2,3},{3,2},{4,5},{5,4},{6,7},{7,6},{8,9},{9,8},{10,11... | collective-permute-start | bytes 4718600 | tf_op jit(solution)/shard_map/ppermute | solution.py:43
  36.5 52.6 %collective-permute-start.11 = (bf16[4,3,256,256]{3,2,1,0:T(8,128)(2,1)S(1)}, bf16[4,3,256,256]{3,2,1,0:T(8,128)(2,1)S(1)}, u32[]{:S(2)}, u32[]{:S(2)}) collective-permute-start(bf16[4,3,256,256]{3,2,1,0:T(8,128)(2,1)S(1)} %pad_maximum_fusion.refs_5_), channel_id=1, source_target_pairs={{0,8},{2,10},{4,12},{6,14},{8,0},{10,2},{12,4},{14,6},{1,9},{3,11}... | collective-permute-start | bytes 4718600 | tf_op jit(solution)/shard_map/ppermute | solution.py:39
  63.5 16.8 %collective-permute-start.5 = (bf16[176,2048]{1,0:T(8,128)(2,1)S(1)}, bf16[176,2048]{1,0:T(8,128)(2,1)S(1)}, u32[]{:S(2)}, u32[]{:S(2)}) collective-permute-start(bf16[176,2048]{1,0:T(8,128)(2,1)S(1)} %slice.32), channel_id=1, source_target_pairs={{0,2},{2,4},{4,6},{6,0},{8,10},{10,12},{12,14},{14,8},{1,3},{3,5},... | collective-permute-start | bytes 2162696 | tf_op jit(solution)/shard_map/ppermute | solution.py:25
  63.7 14.4 %collective-permute-start.7 = (bf16[160,2048]{1,0:T(8,128)(2,1)S(1)}, bf16[160,2048]{1,0:T(8,128)(2,1)S(1)}, u32[]{:S(2)}, u32[]{:S(2)}) collective-permute-start(bf16[160,2048]{1,0:T(8,128)(2,1)S(1)} %slice.33), channel_id=1, source_target_pairs={{0,6},{2,0},{4,2},{6,4},{8,14},{10,8},{12,10},{14,12},{1,7},{3,1},... | collective-permute-start | bytes 1966088 | tf_op jit(solution)/shard_map/ppermute | solution.py:25
  86.3 23.9 %collective-permute-start.9 = (bf16[2048,256]{1,0:T(8,128)(2,1)S(1)}, bf16[2048,256]{1,0:T(8,128)(2,1)S(1)}, u32[]{:S(2)}, u32[]{:S(2)}) collective-permute-start(bf16[2048,256]{1,0:T(8,128)(2,1)S(1)} %pad_maximum_fusion.1), channel_id=1, source_target_pairs={{0,2},{2,4},{4,6},{6,0},{8,10},{10,12},{12,14},{14,8},{1,3},{3,5},... | collective-permute-start | bytes 3145736 | tf_op jit(solution)/shard_map/ppermute | solution.py:25
  86.4 23.9 %collective-permute-start.10 = (bf16[2048,256]{1,0:T(8,128)(2,1)S(1)}, bf16[2048,256]{1,0:T(8,128)(2,1)S(1)}, u32[]{:S(2)}, u32[]{:S(2)}) collective-permute-start(bf16[2048,256]{1,0:T(8,128)(2,1)S(1)} %pad_maximum_fusion.1), channel_id=1, source_target_pairs={{0,6},{2,0},{4,2},{6,4},{8,14},{10,8},{12,10},{14,12},{1,7},{3,1},... | collective-permute-start | bytes 3145736 | tf_op jit(solution)/shard_map/ppermute | solution.py:25
  89.2 27.5 %collective-permute-start.12 = (bf16[1,3,256,256]{3,2,1,0:T(8,128)(2,1)S(1)}, bf16[1,3,256,256]{3,2,1,0:T(8,128)(2,1)S(1)}, u32[]{:S(2)}, u32[]{:S(2)}) collective-permute-start(bf16[1,3,256,256]{3,2,1,0:T(8,128)(2,1)S(1)} %get-tuple-element.56), channel_id=1, source_target_pairs={{0,1},{1,0},{2,3},{3,2},{4,5},{5,4},{6,7},{7,6},{8,9},{9,8},{10,11... | collective-permute-start | bytes 1179656 | tf_op jit(solution)/shard_map/ppermute | solution.py:43
  110.2 17.8 %collective-permute-start.19 = (bf16[1024,256]{1,0:T(8,128)(2,1)S(1)}, bf16[1024,256]{1,0:T(8,128)(2,1)S(1)}, u32[]{:S(2)}, u32[]{:S(2)}) collective-permute-start(bf16[1024,256]{1,0:T(8,128)(2,1)S(1)} %slice.38), channel_id=1, source_target_pairs={{0,2},{2,4},{4,6},{6,0},{8,10},{10,12},{12,14},{14,8},{1,3},{3,5},... | collective-permute-start | bytes 1572872 | tf_op jit(solution)/shard_map/ppermute | solution.py:25
  110.4 17.7 %collective-permute-start.20 = (bf16[1024,256]{1,0:T(8,128)(2,1)S(1)}, bf16[1024,256]{1,0:T(8,128)(2,1)S(1)}, u32[]{:S(2)}, u32[]{:S(2)}) collective-permute-start(bf16[1024,256]{1,0:T(8,128)(2,1)S(1)} %slice.39), channel_id=1, source_target_pairs={{0,6},{2,0},{4,2},{6,4},{8,14},{10,8},{12,10},{14,12},{1,7},{3,1},... | collective-permute-start | bytes 1572872 | tf_op jit(solution)/shard_map/ppermute | solution.py:25
  113.1 4.9 %collective-permute-start.13 = (bf16[1,3,256,256]{3,2,1,0:T(8,128)(2,1)S(1)}, bf16[1,3,256,256]{3,2,1,0:T(8,128)(2,1)S(1)}, u32[]{:S(2)}, u32[]{:S(2)}) collective-permute-start(bf16[1,3,256,256]{3,2,1,0:T(8,128)(2,1)S(1)} %get-tuple-element.57), channel_id=1, source_target_pairs={{0,1},{1,0},{2,3},{3,2},{4,5},{5,4},{6,7},{7,6},{8,9},{9,8},{10,11... | collective-permute-start | bytes 1179656 | tf_op jit(solution)/shard_map/ppermute | solution.py:43
  116.6 1.9 collective-permute-start.14
  116.7 2.5 %collective-permute-start.15 = (bf16[1,3,256,256]{3,2,1,0:T(8,128)(2,1)S(1)}, bf16[1,3,256,256]{3,2,1,0:T(8,128)(2,1)S(1)}, u32[]{:S(2)}, u32[]{:S(2)}) collective-permute-start(bf16[1,3,256,256]{3,2,1,0:T(8,128)(2,1)S(1)} %get-tuple-element.59), channel_id=1, source_target_pairs={{0,1},{1,0},{2,3},{3,2},{4,5},{5,4},{6,7},{7,6},{8,9},{9,8},{10,11... | collective-permute-start | bytes 1179656 | tf_op jit(solution)/shard_map/ppermute | solution.py:43
  128.2 20.3 %copy-start.1 = (bf16[1,2,256,2048]{3,2,1,0:T(8,128)(2,1)S(1)}, bf16[1,2,256,2048]{3,2,1,0:T(8,128)(2,1)}, u32[]{:S(2)}) copy-start(bf16[1,2,256,2048]{3,2,1,0:T(8,128)(2,1)} %param.6) | copy-start | bytes 6291460
  128.2 20.3 %copy-start.3 = (bf16[1,2,64,2048]{3,2,1,0:T(8,128)(2,1)S(1)}, bf16[1,2,64,2048]{3,2,1,0:T(8,128)(2,1)}, u32[]{:S(2)}) copy-start(bf16[1,2,64,2048]{3,2,1,0:T(8,128)(2,1)} %param.7) | copy-start | bytes 1572868
  128.4 20.1 %collective-permute-start.21 = (bf16[8192,256]{1,0:T(8,128)(2,1)S(1)}, bf16[8192,256]{1,0:T(8,128)(2,1)S(1)}, u32[]{:S(2)}, u32[]{:S(2)}) collective-permute-start(bf16[8192,256]{1,0:T(8,128)(2,1)S(1)} %constant_dynamic-update-slice_fusion.refs_4_), channel_id=1, source_target_pairs={{0,1},{1,0},{2,3},{3,2},{4,5},{5,4},{6,7},{7,6},{8,9},{9,8},{10,11... | collective-permute-start | bytes 12582920 | tf_op jit(solution)/shard_map/ppermute | solution.py:43
  128.9 7.8 %collective-permute-start.16 = (bf16[256,512]{1,0:T(8,128)(2,1)S(1)}, bf16[256,512]{1,0:T(8,128)(2,1)S(1)}, u32[]{:S(2)}, u32[]{:S(2)}) collective-permute-start(bf16[256,512]{1,0:T(8,128)(2,1)S(1)} %get-tuple-element.61), channel_id=1, source_target_pairs={{0,6},{2,0},{4,2},{6,4},{8,14},{10,8},{12,10},{14,12},{1,7},{3,1},... | collective-permute-start | bytes 786440 | tf_op jit(solution)/shard_map/ppermute | solution.py:25
  129.1 9.1 %collective-permute-start.17 = (bf16[256,512]{1,0:T(8,128)(2,1)S(1)}, bf16[256,512]{1,0:T(8,128)(2,1)S(1)}, u32[]{:S(2)}, u32[]{:S(2)}) collective-permute-start(bf16[256,512]{1,0:T(8,128)(2,1)S(1)} %get-tuple-element.62), channel_id=1, source_target_pairs={{0,4},{2,6},{4,0},{6,2},{8,12},{10,14},{12,8},{14,10},{1,5},{3,7},... | collective-permute-start | bytes 786440 | tf_op jit(solution)/shard_map/ppermute | solution.py:25
  129.2 15.3 %collective-permute-start.18 = (bf16[256,512]{1,0:T(8,128)(2,1)S(1)}, bf16[256,512]{1,0:T(8,128)(2,1)S(1)}, u32[]{:S(2)}, u32[]{:S(2)}) collective-permute-start(bf16[256,512]{1,0:T(8,128)(2,1)S(1)} %get-tuple-element.63), channel_id=1, source_target_pairs={{0,2},{2,4},{4,6},{6,0},{8,10},{10,12},{12,14},{14,8},{1,3},{3,5},... | collective-permute-start | bytes 786440 | tf_op jit(solution)/shard_map/ppermute | solution.py:25
  144.5 30.0 %collective-permute-start.29 = (bf16[256,2048]{1,0:T(8,128)(2,1)S(1)}, bf16[256,2048]{1,0:T(8,128)(2,1)S(1)}, u32[]{:S(2)}, u32[]{:S(2)}) collective-permute-start(bf16[256,2048]{1,0:T(8,128)(2,1)S(1)} %get-tuple-element.78), channel_id=1, source_target_pairs={{128,144},{144,160},{160,176},{176,192},{192,208},{208,224},{224,2... | collective-permute-start | bytes 3145736 | tf_op jit(solution)/shard_map/ppermute | solution.py:47
  145.7 10.0 %collective-permute-start.24 = (bf16[64,2048]{1,0:T(8,128)(2,1)S(1)}, bf16[64,2048]{1,0:T(8,128)(2,1)S(1)}, u32[]{:S(2)}, u32[]{:S(2)}) collective-permute-start(bf16[64,2048]{1,0:T(8,128)(2,1)S(1)} %get-tuple-element.73), channel_id=1, source_target_pairs={{0,16},{16,32},{32,48},{48,64},{64,80},{80,96},{96,112},{112,128},... | collective-permute-start | bytes 786440 | tf_op jit(solution)/shard_map/ppermute | solution.py:47
  152.6 21.9 %collective-permute-start.22 = (bf16[256,1024]{1,0:T(8,128)(2,1)S(1)}, bf16[256,1024]{1,0:T(8,128)(2,1)S(1)}, u32[]{:S(2)}, u32[]{:S(2)}) collective-permute-start(bf16[256,1024]{1,0:T(8,128)(2,1)S(1)} %get-tuple-element.69), channel_id=1, source_target_pairs={{0,16},{16,32},{32,48},{48,64},{64,80},{80,96},{96,112},{112,128},... | collective-permute-start | bytes 1572872 | tf_op jit(solution)/shard_map/ppermute | solution.py:47
  155.7 5.6 %collective-permute-start.25 = (bf16[64,2048]{1,0:T(8,128)(2,1)S(1)}, bf16[64,2048]{1,0:T(8,128)(2,1)S(1)}, u32[]{:S(2)}, u32[]{:S(2)}) collective-permute-start(bf16[64,2048]{1,0:T(8,128)(2,1)S(1)} %collective-permute-done.24.refs_6_), channel_id=1, source_target_pairs={{0,1},{1,0},{2,3},{3,2},{4,5},{5,4},{6,7},{7,6},{8,9},{9,8},{10,11... | collective-permute-start | bytes 786440 | tf_op jit(solution)/shard_map/ppermute | solution.py:43
  161.4 28.2 %collective-permute-start.26 = (bf16[256,1024]{1,0:T(8,128)(2,1)S(1)}, bf16[256,1024]{1,0:T(8,128)(2,1)S(1)}, u32[]{:S(2)}, u32[]{:S(2)}) collective-permute-start(bf16[256,1024]{1,0:T(8,128)(2,1)S(1)} %get-tuple-element.74), channel_id=1, source_target_pairs={{0,16},{16,32},{32,48},{48,64},{64,80},{80,96},{96,112},{112,128},... | collective-permute-start | bytes 1572872 | tf_op jit(solution)/shard_map/ppermute | solution.py:47
  174.5 18.5 %collective-permute-start.30 = (bf16[256,2048]{1,0:T(8,128)(2,1)S(1)}, bf16[256,2048]{1,0:T(8,128)(2,1)S(1)}, u32[]{:S(2)}, u32[]{:S(2)}) collective-permute-start(bf16[256,2048]{1,0:T(8,128)(2,1)S(1)} %collective-permute-done.29.refs_4_), channel_id=1, source_target_pairs={{0,1},{1,0},{2,3},{3,2},{4,5},{5,4},{6,7},{7,6},{8,9},{9,8},{10,11... | collective-permute-start | bytes 3145736 | tf_op jit(solution)/shard_map/ppermute | solution.py:43
  175.8 13.7 %collective-permute-start.27 = (bf16[64,2048]{1,0:T(8,128)(2,1)S(1)}, bf16[64,2048]{1,0:T(8,128)(2,1)S(1)}, u32[]{:S(2)}, u32[]{:S(2)}) collective-permute-start(bf16[64,2048]{1,0:T(8,128)(2,1)S(1)} %get-tuple-element.75), channel_id=1, source_target_pairs={{128,144},{144,160},{160,176},{176,192},{192,208},{208,224},{224,2... | collective-permute-start | bytes 786440 | tf_op jit(solution)/shard_map/ppermute | solution.py:47
  189.6 3.5 %collective-permute-start.23 = (bf16[256,1024]{1,0:T(8,128)(2,1)S(1)}, bf16[256,1024]{1,0:T(8,128)(2,1)S(1)}, u32[]{:S(2)}, u32[]{:S(2)}) collective-permute-start(bf16[256,1024]{1,0:T(8,128)(2,1)S(1)} %collective-permute-done.22.refs_0_), channel_id=1, source_target_pairs={{0,1},{1,0},{2,3},{3,2},{4,5},{5,4},{6,7},{7,6},{8,9},{9,8},{10,11... | collective-permute-start | bytes 1572872 | tf_op jit(solution)/shard_map/ppermute | solution.py:43
  190.3 2.7 %collective-permute-start.28 = (bf16[256,1024]{1,0:T(8,128)(2,1)S(1)}, bf16[256,1024]{1,0:T(8,128)(2,1)S(1)}, u32[]{:S(2)}, u32[]{:S(2)}) collective-permute-start(bf16[256,1024]{1,0:T(8,128)(2,1)S(1)} %collective-permute-done.26.refs_2_), channel_id=1, source_target_pairs={{0,1},{1,0},{2,3},{3,2},{4,5},{5,4},{6,7},{7,6},{8,9},{9,8},{10,11... | collective-permute-start | bytes 1572872 | tf_op jit(solution)/shard_map/ppermute | solution.py:43
  190.3 2.7 %collective-permute-start.31 = (bf16[64,2048]{1,0:T(8,128)(2,1)S(1)}, bf16[64,2048]{1,0:T(8,128)(2,1)S(1)}, u32[]{:S(2)}, u32[]{:S(2)}) collective-permute-start(bf16[64,2048]{1,0:T(8,128)(2,1)S(1)} %collective-permute-done.27.refs_8_), channel_id=1, source_target_pairs={{0,1},{1,0},{2,3},{3,2},{4,5},{5,4},{6,7},{7,6},{8,9},{9,8},{10,11... | collective-permute-start | bytes 786440 | tf_op jit(solution)/shard_map/ppermute | solution.py:43

commit v4 on v3

--- a/solution.py
+++ b/solution.py
@@ -67,7 +67,7 @@
         copy.wait()
 
 
-def call(kernel, outs, in_specs, out_specs, scratch=(), flops=0, moved=0, limit=16):
+def call(kernel, outs, in_specs, out_specs, scratch=(), limit=16):
     return pl.pallas_call(
         kernel,
         out_shape=outs,
@@ -91,11 +91,13 @@
     planes, rows, columns = weight.shape
     piece = jax.ShapeDtypeStruct((planes, rows, columns // RING), BF16)
     return call(
-        quarter_kernel, (piece,) * RING, [SMEM, VMEM], (VMEM,) * RING, moved=4 * weight.size
+        quarter_kernel, (piece,) * RING, [SMEM, VMEM], (VMEM,) * RING
     )(where, weight)
 
 
-def norm_kernel(where, context, queries, gain, lengths, ctx_out, qry_out, normed, *scratch):
+def norm_kernel(
+    where, context, queries, gain, lengths, ctx_out, qry_out, normed, qry_normed, *scratch
+):
     ctx, qry, sems = scratch
     core = where[3]
     copies = copy_all(
@@ -106,14 +108,14 @@
     )
     step = 32
 
-    def rows_of(source, raw, below):
+    def rows_of(source, raw, target):
         @pl.loop(0, source.shape[0] // step)
         def _(i):
             first = pl.multiple_of(i * step, step)
             low = source[pl.ds(first, step), :]
             wide = low.astype(F32)
             mean = jnp.mean(wide * wide, axis=-1, keepdims=True)
-            normed[pl.ds(below + first, step), :] = (
+            target[pl.ds(first, step), :] = (
                 wide * lax.rsqrt(mean + 1e-06) * gain[...]
             ).astype(BF16)
             raw[pl.ds(first, step), :] = low
@@ -123,36 +125,39 @@
         (TAIL, normed.shape[1]), length
     ).astype(BF16)
     copies[0].wait()
-    rows_of(ctx, ctx_out, 0)
+    rows_of(ctx, ctx_out, normed)
     copies[1].wait()
-    rows_of(qry, qry_out, ctx.shape[0])
+    rows_of(qry, qry_out, qry_normed)
 
 
 def norm_scene(where, context, queries, gain, lengths):
     ctx = jax.ShapeDtypeStruct(context.shape[1:], BF16)
     qry = jax.ShapeDtypeStruct(queries.shape[1:], BF16)
-    rows = ctx.shape[0] + qry.shape[0] + TAIL
+    rows = ctx.shape[0] + TAIL
     return call(
         norm_kernel,
-        (ctx, qry, jax.ShapeDtypeStruct((rows, ctx.shape[1]), BF16)),
+        (ctx, qry, jax.ShapeDtypeStruct((rows, ctx.shape[1]), BF16), qry),
         [SMEM, HBM, HBM, VMEM, SMEM],
-        (VMEM,) * 3,
+        (VMEM,) * 4,
         [
             pltpu.VMEM(ctx.shape, BF16),
             pltpu.VMEM(qry.shape, BF16),
             pltpu.SemaphoreType.DMA((2,)),
         ],
-        moved=6 * ctx.size,
     )(where, context, queries, gain, lengths)
 
 
 def start_kernel(where, *refs):
-    rows, parts = refs[:5], refs[5:7]
-    total, far_rows, far_qry, lengths, near_rows, near_qry, weight, sems = refs[7:]
+    rows, queries, parts = refs[:5], refs[5:9], refs[9:11]
+    total, far_rows, far_qry, lengths, near_rows, near_qry, weight, sems = refs[11:]
     x, z = where[0], where[1]
     mem, few = far_rows.shape[0] // RING, far_qry.shape[0] // RING
     width = far_rows.shape[1]
     copies = []
+
+    def take_queries(slot, columns, target):
+        source = queries[slot].at[:, columns]
+        copies.append(pltpu.make_async_copy(source, target, sems.at[len(copies)]))
 
     def take(slot, first, count, columns, target):
         cut = rows[2].shape[0]
@@ -181,15 +186,15 @@
     for slot in range(RING):
         columns = pl.ds(pl.multiple_of(z * width, width), width)
         take(slot, 0, mem, columns, near_rows.at[pl.ds(slot * mem, mem)])
-        take(slot, mem, few, columns, near_qry.at[pl.ds(slot * few, few)])
-        take(slot, mem + few, TAIL, pl.ds(0, 128), lengths.at[slot])
+        take_queries(slot, columns, near_qry.at[pl.ds(slot * few, few)])
+        take(slot, mem, TAIL, pl.ds(0, 128), lengths.at[slot])
     for step in range(RING):
         at = ((1 - z) * RING + (x - step + RING) % RING) * block
         columns = pl.ds(pl.multiple_of(at, block), block)
         here = pl.ds(step * block, block)
         for slot in range(RING):
             take(slot, 0, mem, columns, far_rows.at[pl.ds(slot * mem, mem), here])
-            take(slot, mem, few, columns, far_qry.at[pl.ds(slot * few, few), here])
+            take_queries(slot, columns, far_qry.at[pl.ds(slot * few, few), here])
     wait_all(copy_all(copies))
 
     @pl.when(where[2] == 1)
@@ -208,9 +213,9 @@
 
 
 def attend_kernel(where, total, rows, qry, lengths, *refs):
-    sides = (refs[:1], refs[1:5])
-    outs = refs[5:9]
-    low, mixed = refs[9:]
+    sides = (refs[:1], refs[1:3])
+    outs = refs[3:7]
+    low, mixed = refs[7:]
     mem, few = mixed.shape[1], qry.shape[0] // RING
     encoder = where[2]
 
@@ -284,7 +289,7 @@
         outs[slot][...] = mixed[slot]
 
 
-def start_projections(where, mem, few, rows, parts):
+def start_projections(where, mem, few, rows, queries, parts):
     width = rows[0].shape[1]
     _, planes, block, part = parts[0].shape
     half = width // 2
@@ -296,7 +301,7 @@
             jax.ShapeDtypeStruct((RING * few, half), BF16),
             jax.ShapeDtypeStruct((RING, TAIL, 128), BF16),
         ),
-        [SMEM] + [HBM] * 7,
+        [SMEM] + [HBM] * 11,
         (VMEM,) * 4,
         [
             pltpu.VMEM((RING * mem, half), BF16),
@@ -305,7 +310,7 @@
             pltpu.SemaphoreType.DMA((64,)),
         ],
         limit=14,
-    )(where, *rows, *parts)
+    )(where, *rows, *queries, *parts)
 
 
 def attend(where, mem, started, far):
@@ -315,7 +320,7 @@
     return call(
         attend_kernel,
         (out,) * RING,
-        [SMEM] + [VMEM] * 9,
+        [SMEM] + [VMEM] * 7,
         (VMEM,) * RING,
         [
             pltpu.VMEM((planes, RING * mem, columns), BF16),
@@ -330,7 +335,7 @@
     weights = refs[4:6]
     few_in = refs[6] if part else None
     out, few_out = refs[6 + part : 8 + part]
-    heads, weight, base, sems = refs[8 + part :]
+    heads, base, sems = refs[8 + part :]
     x, z, encoder, core = where[0], where[1], where[2], where[3]
     quarter = mixed[0].shape[1] // 2
     inner = quarter * RING
@@ -352,18 +357,7 @@
                     sems.at[1 + step * 2 + side],
                 )
             )
-    pieces = []
     crossed = z if part == 0 else 1 - z
-    for i in range(RING):
-        for side in range(2):
-            start = pl.multiple_of((2 * i + crossed) * inner, inner)
-            pieces.append(
-                pltpu.make_async_copy(
-                    weights[side].at[pl.ds(start, inner)],
-                    weight.at[i, pl.ds(side * inner, inner)],
-                    sems.at[9 + i * 2 + side],
-                )
-            )
 
     @pl.when(encoder == 1)
     def _():
@@ -374,7 +368,6 @@
         few_base.start()
 
     copy_all(copies)
-    copy_all(pieces)
 
     @pl.when(encoder == 1)
     def _():
@@ -388,10 +381,17 @@
         few_out[:, pl.ds(0, RING * block)] = few_in[...]
     wait_all(copies)
     for i in range(RING):
-        wait_all(pieces[2 * i : 2 * i + 2])
         place = (x - i + RING) % RING
+        start = pl.ds(pl.multiple_of((2 * i + crossed) * inner, inner), inner)
         at = pl.ds(pl.multiple_of(place * block, block), block)
-        update = jnp.dot(heads[...], weight[i], preferred_element_type=F32)
+        update = sum(
+            jnp.dot(
+                heads[:, pl.ds(side * inner, inner)],
+                weights[side][start, :],
+                preferred_element_type=F32,
+            )
+            for side in range(2)
+        )
         result = (base[:, at].astype(F32) + update).astype(BF16)
         out[:, at] = result
         at = pl.ds(pl.multiple_of((part * RING + place) * block, block), block)
@@ -407,16 +407,13 @@
             jax.ShapeDtypeStruct((mem, RING * block), BF16),
             jax.ShapeDtypeStruct((few, (1 + part) * RING * block), BF16),
         ),
-        [SMEM] + [HBM] * 8 + [VMEM] * part,
+        [SMEM] + [HBM] * 6 + [VMEM] * (2 + part),
         (VMEM, VMEM),
         [
             pltpu.VMEM((mem, 2 * inner), BF16),
-            pltpu.VMEM((RING, 2 * inner, block), BF16),
             pltpu.VMEM((mem, RING * block), BF16),
-            pltpu.SemaphoreType.DMA((17,)),
+            pltpu.SemaphoreType.DMA((9,)),
         ],
-        flops=2 * mem * 2 * inner * RING * block,
-        moved=2 * (2 * inner * RING * block + 3 * mem * inner),
     )(where, context, queries, *mixed, *weights, *few_in)
 
 
@@ -473,7 +470,6 @@
             pltpu.VMEM(qry_shape, BF16),
             pltpu.SemaphoreType.DMA((6,)),
         ],
-        moved=8 * ctx_early[0].size,
     )(where, *first, *second, *ctx_early, *qry_early, *qry_late)
 
 
@@ -510,15 +506,17 @@
     near = jnp.stack(near)
     far = across_z(after(near, out_pair))
 
-    ctx, qry, normed = norm_scene(
+    ctx, qry, normed, qry_normed = norm_scene(
         after(where, *own), context, queries, norm_gain, lengths[0]
     )
     cut = (normed.shape[0] // 32 + 1) * 16
     rows = round_ring(after(normed, out_pair, *arrived), cut)
-    started = start_projections(where, mem, few, rows, (near, other_core(near)))
+    qry_sent = after(qry_normed, rows[1], rows[4])
+    qry_rows = [qry_normed] + [around_x_of(qry_sent, step, decoders) for step in range(1, RING)]
+    started = start_projections(where, mem, few, rows, qry_rows, (near, other_core(near)))
 
     weights = round_ring(after(out_pair, *rows, started[0]), out_shard.shape[0])
-    far_other = [other_core(after(far[step : step + 1], started[0])) for step in range(RING)]
+    far_other = [other_core(after(far[i : i + 2], started[0])) for i in (0, 2)]
 
     mixed = attend(after(where, weights[1], weights[4]), mem, started, (far, *far_other))
     weights = both(jnp.concatenate(after(weights, mixed[0])))

time: 196 us -> 203 us (1.036)
  starting transfers between devices: 72.6 us -> 78.1 us
  waiting for transfers between devices: 87.5 us -> 92.5 us
  Pallas kernels: 27.9 us -> 24.3 us
    ppermute x5, waiting for transfers between devices: 23.8 us -> 32.5 us  [relay(): lax.ppermute(array, 'section', [(s, (s + 1) % count) for s in sections])]
    ppermute x14, waiting for transfers between devices: 59.4 us -> 52.2 us  [around_x(): return lax.ppermute(array, 'dp', pairs)]
    ppermute x2, waiting for transfers between devices: 0.29 us -> 5.55 us  [across_z(): lax.ppermute(array, 'dp', [(d, (d + RING) % (2 * RING)) for d in range(2...]
    pallas_call x2, Pallas kernels: 7.97 us -> 4.34 us  [project(): call(functools.partial(project_kernel, part), (jax.ShapeDtypeStruct((mem,...]
    ppermute x5, starting transfers between devices: 10.3 us -> 13.2 us  [relay(): lax.ppermute(array, 'section', [(s, (s + 1) % count) for s in sections])]
    ppermute x11 -> x9, waiting for transfers between devices: 4.13 us -> 2.19 us  [other_core(): return lax.ppermute(array, 'tensor', [(0, 1), (1, 0)])]
    ppermute x11 -> x9, starting transfers between devices: 31.6 us -> 30.3 us  [other_core(): return lax.ppermute(array, 'tensor', [(0, 1), (1, 0)])]
  transfers between devices with their start and end apart: 32 -> 33, of which waited for: 14 -> 12; matrix products, arithmetic and copies ran while one was open for 0% -> 0% of each run, Pallas kernels for 13% -> 11%
where the time goes in v4:
time: 203 us; the launch traced here: 202 us
  waiting for transfers between devices  92.5 us (46%)
  starting transfers between devices  78.1 us (38%)
  Pallas kernels  24.3 us (12%)
  local copies, waits for them, and re-layouts  6.02 us (3%)
    ppermute x14, waiting for transfers between devices, around_x(): return lax.ppermute(array, 'dp', pairs)  52.2 us
    ppermute x5, waiting for transfers between devices, relay(): lax.ppermute(array, 'section', [(s, (s + 1) % count) for s in sections])  32.5 us
    ppermute x9, starting transfers between devices, other_core(): return lax.ppermute(array, 'tensor', [(0, 1), (1, 0)])  30.3 us
    ppermute x14, starting transfers between devices, around_x(): return lax.ppermute(array, 'dp', pairs)  20 us
    ppermute x5, starting transfers between devices, relay(): lax.ppermute(array, 'section', [(s, (s + 1) % count) for s in sections])  13.2 us
    ppermute x2, starting transfers between devices, across_z(): lax.ppermute(array, 'dp', [(d, (d + RING) % (2 * RING)) for d in range(2...  12.6 us
    pallas_call x1, Pallas kernels, attend(): call(attend_kernel, (out,) * RING, [SMEM] + [VMEM] * 7, (VMEM,) * RING, [...  8.9 us
    pallas_call x1, Pallas kernels, start_projections(): call(start_kernel, (jax.ShapeDtypeStruct((planes, RING * mem, 2 * part),...  5.99 us
  transfers between devices with their start and end apart: 33, of which 12 were waited for; matrix products, arithmetic and copies ran while one was open for 0% of the time, Pallas kernels for 11%

profile of v4, /device:TPU:1, one launch (start us, length us, event | category | flops | bytes accessed | tf_op | source)
XLA Modules:
  0.0 202.2 jit_solution(3361335766230079275)
XLA Ops:
  0.6 7.8 %collective-permute-start = (bf16[1024,256]{1,0:T(8,128)(2,1)}, bf16[1024,256]{1,0:T(8,128)(2,1)S(1)}, u32[]{:S(2)}, u32[]{:S(2)}) collective-permute-start(bf16[1024,256]{1,0:T(8,128)(2,1)} %bitcast.27), channel_id=1, source_target_pairs={{0,8},{2,10},{4,12},{6,14},{8,0},{10,2},{12,4},{14,6},{1,9},{3,11}... | collective-permute-start | bytes 1572872 | tf_op jit(solution)/shard_map/ppermute | solution.py:39
  8.5 0.1 stack.46.where
  8.5 1.4 copy-done.4
  9.9 0.8 shard_map.77
  10.7 1.3 collective-permute-start.1
  12.0 2.5 %collective-permute-start.2 = (bf16[3,256,256]{2,1,0:T(8,128)(2,1)S(1)}, bf16[3,256,256]{2,1,0:T(8,128)(2,1)S(1)}, u32[]{:S(2)}, u32[]{:S(2)}) collective-permute-start(bf16[3,256,256]{2,1,0:T(8,128)(2,1)S(1)} %get-tuple-element.44), channel_id=1, source_target_pairs={{0,4},{2,6},{4,0},{6,2},{8,12},{10,14},{12,8},{14,10},{1,5},{3,7},... | collective-permute-start | bytes 1179656 | tf_op jit(solution)/shard_map/ppermute | solution.py:25
  14.4 1.2 collective-permute-start.3
  15.6 1.6 copy-done
  17.2 1.0 copy-done.2
  18.2 0.7 copy-done.5
  18.9 0.7 copy-done.6
  19.6 2.0 shard_map.78
  21.6 0.3 collective-permute-done
  21.9 0.1 pad_maximum_fusion.1
  22.0 9.1 %collective-permute-done.2 = bf16[3,256,256]{2,1,0:T(8,128)(2,1)S(1)} collective-permute-done((bf16[3,256,256]{2,1,0:T(8,128)(2,1)S(1)}, bf16[3,256,256]{2,1,0:T(8,128)(2,1)S(1)}, u32[]{:S(2)}, u32[]{:S(2)}) %collective-permute-start.2) | collective-permute-done | bytes 393248 | tf_op jit(solution)/shard_map/ppermute | solution.py:25
  31.1 1.7 collective-permute-start.4
  32.8 1.7 collective-permute-start.6
  34.4 0.2 pad_maximum_fusion.refs_9_
  34.6 1.8 collective-permute-start.11
  36.5 4.8 %collective-permute-start.14 = (bf16[4,3,256,256]{3,2,1,0:T(8,128)(2,1)S(1)}, bf16[4,3,256,256]{3,2,1,0:T(8,128)(2,1)S(1)}, u32[]{:S(2)}, u32[]{:S(2)}) collective-permute-start(bf16[4,3,256,256]{3,2,1,0:T(8,128)(2,1)S(1)} %pad_maximum_fusion.refs_9_), channel_id=1, source_target_pairs={{0,8},{2,10},{4,12},{6,14},{8,0},{10,2},{12,4},{14,6},{1,9},{3,11}... | collective-permute-start | bytes 4718600 | tf_op jit(solution)/shard_map/ppermute | solution.py:39
  41.3 16.6 %collective-permute-done.4.refs_1_ = bf16[272,2048]{1,0:T(8,128)(2,1)S(1)} collective-permute-done((bf16[272,2048]{1,0:T(8,128)(2,1)S(1)}, bf16[272,2048]{1,0:T(8,128)(2,1)S(1)}, u32[]{:S(2)}, u32[]{:S(2)}) %collective-permute-start.4) | collective-permute-done | bytes 1114144 | tf_op jit(solution)/shard_map/ppermute | solution.py:25
  57.8 0.7 collective-permute-start.10
  58.6 0.7 collective-permute-start.5
  59.2 0.7 collective-permute-start.8
  60.0 2.2 %collective-permute-start.7 = (bf16[128,2048]{1,0:T(8,128)(2,1)S(1)}, bf16[128,2048]{1,0:T(8,128)(2,1)S(1)}, u32[]{:S(2)}, u32[]{:S(2)}) collective-permute-start(bf16[128,2048]{1,0:T(8,128)(2,1)S(1)} %slice.25), channel_id=1, source_target_pairs={{0,6},{2,0},{4,2},{6,4},{8,14},{10,8},{12,10},{14,12},{1,7},{3,1},... | collective-permute-start | bytes 1572872 | tf_op jit(solution)/shard_map/ppermute | solution.py:25
  62.1 0.7 collective-permute-start.9
  62.8 9.4 %collective-permute-done.7.refs_3_ = bf16[128,2048]{1,0:T(8,128)(2,1)S(1)} collective-permute-done((bf16[128,2048]{1,0:T(8,128)(2,1)S(1)}, bf16[128,2048]{1,0:T(8,128)(2,1)S(1)}, u32[]{:S(2)}, u32[]{:S(2)}) %collective-permute-start.7) | collective-permute-done | bytes 524320 | tf_op jit(solution)/shard_map/ppermute | solution.py:25
  72.2 0.3 collective-permute-done.5.refs_2_
  72.6 6.0 %shard_map.79 = (f32[3,1024,512]{2,1,0:T(8,128)S(1)}, bf16[1024,1024]{1,0:T(8,128)(2,1)S(1)}, bf16[256,1024]{1,0:T(8,128)(2,1)S(1)}, bf16[4,16,128]{2,1,0:T(8,128)(2,1)S(1)}) custom-call(s32[5]{0:T(128)S(1)} %stack.46.where, bf16[272,2048]{1,0:T(8,128)(2,1)S(1)} %get-tuple-element.48.refs_0_, bf16[272,2048]{1,0:T(8,128)(2,1)S(1)} %collective-permute-done.4.refs_1_, ...), custom_call_target="tpu_custom_call" | custom-call | flops 1 | bytes 1 | tf_op jit(solution)/shard_map/pallas_call | solution.py:296
  78.6 1.2 collective-permute-start.12
  79.8 1.6 collective-permute-start.13
  81.3 5.3 %collective-permute-done.14.refs_0_ = bf16[4,3,256,256]{3,2,1,0:T(8,128)(2,1)S(1)} collective-permute-done((bf16[4,3,256,256]{3,2,1,0:T(8,128)(2,1)S(1)}, bf16[4,3,256,256]{3,2,1,0:T(8,128)(2,1)S(1)}, u32[]{:S(2)}, u32[]{:S(2)}) %collective-permute-start.14) | collective-permute-done | bytes 1572896 | tf_op jit(solution)/shard_map/ppermute | solution.py:39
  86.6 0.1 fusion
  86.7 23.3 %collective-permute-start.16 = (bf16[2,3,256,256]{3,2,1,0:T(8,128)(2,1)S(1)}, bf16[2,3,256,256]{3,2,1,0:T(8,128)(2,1)S(1)}, u32[]{:S(2)}, u32[]{:S(2)}) collective-permute-start(bf16[2,3,256,256]{3,2,1,0:T(8,128)(2,1)S(1)} %get-tuple-element.59), channel_id=1, source_target_pairs={{0,1},{1,0},{2,3},{3,2},{4,5},{5,4},{6,7},{7,6},{8,9},{9,8},{10,11... | collective-permute-start | bytes 2359304 | tf_op jit(solution)/shard_map/ppermute | solution.py:43
  110.0 0.1 collective-permute-start.15
  110.1 0.1 collective-permute-start.20
  110.3 2.7 %collective-permute-start.21 = (bf16[1024,256]{1,0:T(8,128)(2,1)S(1)}, bf16[1024,256]{1,0:T(8,128)(2,1)S(1)}, u32[]{:S(2)}, u32[]{:S(2)}) collective-permute-start(bf16[1024,256]{1,0:T(8,128)(2,1)S(1)} %slice.29), channel_id=1, source_target_pairs={{0,6},{2,0},{4,2},{6,4},{8,14},{10,8},{12,10},{14,12},{1,7},{3,1},... | collective-permute-start | bytes 1572872 | tf_op jit(solution)/shard_map/ppermute | solution.py:25
  113.0 0.0 collective-permute-done.15.refs_1_
  113.0 8.9 %shard_map.80 = (bf16[256,512]{1,0:T(8,128)(2,1)S(1)}, bf16[256,512]{1,0:T(8,128)(2,1)S(1)}, bf16[256,512]{1,0:T(8,128)(2,1)S(1)}, bf16[256,512]{1,0:T(8,128)(2,1)S(1)}) custom-call(s32[5]{0:T(128)S(1)} %stack.46.where, f32[3,1024,512]{2,1,0:T(8,128)S(1)} %get-tuple-element.51.total, bf16[1024,1024]{1,0:T(8,128)(2,1)S(1)} %get-tuple-element.54.rows, ...), custom_call_target="tpu_custom_call" | custom-call | flops 1 | bytes 1 | tf_op jit(solution)/shard_map/pallas_call | solution.py:320
  122.0 2.6 %collective-permute-done.20 = bf16[1024,256]{1,0:T(8,128)(2,1)S(1)} collective-permute-done((bf16[1024,256]{1,0:T(8,128)(2,1)S(1)}, bf16[1024,256]{1,0:T(8,128)(2,1)S(1)}, u32[]{:S(2)}, u32[]{:S(2)}) %collective-permute-start.20) | collective-permute-done | bytes 524320 | tf_op jit(solution)/shard_map/ppermute | solution.py:25
  124.5 0.1 constant_dynamic-update-slice_fusion.4
  124.6 0.1 constant_dynamic-update-slice_fusion.3
  124.7 0.0 copy-start.3
  124.8 0.1 constant_dynamic-update-slice_fusion.refs_4_
  124.9 1.3 collective-permute-start.22
  126.2 2.8 %collective-permute-start.17 = (bf16[256,512]{1,0:T(8,128)(2,1)S(1)}, bf16[256,512]{1,0:T(8,128)(2,1)S(1)}, u32[]{:S(2)}, u32[]{:S(2)}) collective-permute-start(bf16[256,512]{1,0:T(8,128)(2,1)S(1)} %get-tuple-element.61), channel_id=1, source_target_pairs={{0,6},{2,0},{4,2},{6,4},{8,14},{10,8},{12,10},{14,12},{1,7},{3,1},... | collective-permute-start | bytes 786440 | tf_op jit(solution)/shard_map/ppermute | solution.py:25
  129.0 0.6 collective-permute-start.19
  129.6 10.6 %collective-permute-done.17.refs_1_ = bf16[256,512]{1,0:T(8,128)(2,1)S(1)} collective-permute-done((bf16[256,512]{1,0:T(8,128)(2,1)S(1)}, bf16[256,512]{1,0:T(8,128)(2,1)S(1)}, u32[]{:S(2)}, u32[]{:S(2)}) %collective-permute-start.17) | collective-permute-done | bytes 262176 | tf_op jit(solution)/shard_map/ppermute | solution.py:25
  140.1 3.7 %collective-permute-done.19.refs_3_ = bf16[256,512]{1,0:T(8,128)(2,1)S(1)} collective-permute-done((bf16[256,512]{1,0:T(8,128)(2,1)S(1)}, bf16[256,512]{1,0:T(8,128)(2,1)S(1)}, u32[]{:S(2)}, u32[]{:S(2)}) %collective-permute-start.19) | collective-permute-done | bytes 262176 | tf_op jit(solution)/shard_map/ppermute | solution.py:25
  143.8 1.3 collective-permute-start.30
  145.1 3.4 %collective-permute-start.25 = (bf16[64,2048]{1,0:T(8,128)(2,1)S(1)}, bf16[64,2048]{1,0:T(8,128)(2,1)S(1)}, u32[]{:S(2)}, u32[]{:S(2)}) collective-permute-start(bf16[64,2048]{1,0:T(8,128)(2,1)S(1)} %get-tuple-element.73), channel_id=1, source_target_pairs={{0,16},{16,32},{32,48},{48,64},{64,80},{80,96},{96,112},{112,128},... | collective-permute-start | bytes 786440 | tf_op jit(solution)/shard_map/ppermute | solution.py:47
  148.5 2.2 %shard_map.81 = (bf16[256,1024]{1,0:T(8,128)(2,1)S(1)}, bf16[64,1024]{1,0:T(8,128)(2,1)S(1)}) custom-call(s32[5]{0:T(128)S(1)} %stack.46.where, bf16[2,256,2048]{2,1,0:T(8,128)(2,1)S(1)} %bitcast.19, bf16[2,64,2048]{2,1,0:T(8,128)(2,1)S(1)} %bitcast.22, bf16[256,512]{1,0:T(8,128)(2,1)S(1)} %get-tuple-element.60.refs_0_, ...), custom_call_target="tpu_custom_call" | custom-call | flops 1 | bytes 1 | tf_op jit(solution)/shard_map/pallas_call | solution.py:404
  150.7 3.1 %collective-permute-start.23 = (bf16[256,1024]{1,0:T(8,128)(2,1)S(1)}, bf16[256,1024]{1,0:T(8,128)(2,1)S(1)}, u32[]{:S(2)}, u32[]{:S(2)}) collective-permute-start(bf16[256,1024]{1,0:T(8,128)(2,1)S(1)} %get-tuple-element.69), channel_id=1, source_target_pairs={{0,16},{16,32},{32,48},{48,64},{64,80},{80,96},{96,112},{112,128},... | collective-permute-start | bytes 1572872 | tf_op jit(solution)/shard_map/ppermute | solution.py:47
  153.8 1.4 collective-permute-start.26
  155.2 2.2 %shard_map.82 = (bf16[256,1024]{1,0:T(8,128)(2,1)S(1)}, bf16[64,2048]{1,0:T(8,128)(2,1)S(1)}) custom-call(s32[5]{0:T(128)S(1)} %stack.46.where, bf16[2,256,2048]{2,1,0:T(8,128)(2,1)S(1)} %bitcast.20, bf16[2,64,2048]{2,1,0:T(8,128)(2,1)S(1)} %bitcast.23, bf16[256,512]{1,0:T(8,128)(2,1)S(1)} %get-tuple-element.60.refs_0_, ...), custom_call_target="tpu_custom_call" | custom-call | flops 1 | bytes 1 | tf_op jit(solution)/shard_map/pallas_call | solution.py:404
  157.4 4.1 %collective-permute-start.27 = (bf16[256,1024]{1,0:T(8,128)(2,1)S(1)}, bf16[256,1024]{1,0:T(8,128)(2,1)S(1)}, u32[]{:S(2)}, u32[]{:S(2)}) collective-permute-start(bf16[256,1024]{1,0:T(8,128)(2,1)S(1)} %get-tuple-element.74), channel_id=1, source_target_pairs={{0,16},{16,32},{32,48},{48,64},{64,80},{80,96},{96,112},{112,128},... | collective-permute-start | bytes 1572872 | tf_op jit(solution)/shard_map/ppermute | solution.py:47
  161.5 20.1 %collective-permute-done.30.refs_4_ = bf16[256,2048]{1,0:T(8,128)(2,1)S(1)} collective-permute-done((bf16[256,2048]{1,0:T(8,128)(2,1)S(1)}, bf16[256,2048]{1,0:T(8,128)(2,1)S(1)}, u32[]{:S(2)}, u32[]{:S(2)}) %collective-permute-start.30) | collective-permute-done | bytes 1048608 | tf_op jit(solution)/shard_map/ppermute | solution.py:47
  181.6 1.0 collective-permute-start.31
  182.6 1.3 collective-permute-start.28
  183.9 12.4 %collective-permute-done.28.refs_8_ = bf16[64,2048]{1,0:T(8,128)(2,1)S(1)} collective-permute-done((bf16[64,2048]{1,0:T(8,128)(2,1)S(1)}, bf16[64,2048]{1,0:T(8,128)(2,1)S(1)}, u32[]{:S(2)}, u32[]{:S(2)}) %collective-permute-start.28) | collective-permute-done | bytes 262176 | tf_op jit(solution)/shard_map/ppermute | solution.py:47
  196.3 0.8 collective-permute-start.29
  197.1 0.5 collective-permute-start.32
  197.6 2.2 %collective-permute-done.32.refs_9_ = bf16[64,2048]{1,0:T(8,128)(2,1)S(1)} collective-permute-done((bf16[64,2048]{1,0:T(8,128)(2,1)S(1)}, bf16[64,2048]{1,0:T(8,128)(2,1)S(1)}, u32[]{:S(2)}, u32[]{:S(2)}) %collective-permute-start.32) | collective-permute-done | bytes 262176 | tf_op jit(solution)/shard_map/ppermute | solution.py:43
  199.8 2.3 %shard_map.83 = (bf16[2,256,2048]{2,1,0:T(8,128)(2,1)}, bf16[2,64,2048]{2,1,0:T(8,128)(2,1)}) custom-call(s32[5]{0:T(128)S(1)} %stack.46.where, bf16[256,1024]{1,0:T(8,128)(2,1)S(1)} %collective-permute-done.23.refs_0_, bf16[256,1024]{1,0:T(8,128)(2,1)S(1)} %collective-permute-done.24.refs_1_, bf16[256,1024]{1,0:T(8,128)(2,1)S(1)} %collective-permute-done.27.refs_2_, ...), custom_call_target="tpu_custom_call" | custom-call | flops 1 | bytes 1 | tf_op jit(solution)/shard_map/pallas_call | solution.py:463
  (38 shorter events, 0.3 us)
Async XLA Ops:
  0.6 21.2 %collective-permute-start = (bf16[1024,256]{1,0:T(8,128)(2,1)}, bf16[1024,256]{1,0:T(8,128)(2,1)S(1)}, u32[]{:S(2)}, u32[]{:S(2)}) collective-permute-start(bf16[1024,256]{1,0:T(8,128)(2,1)} %bitcast.27), channel_id=1, source_target_pairs={{0,8},{2,10},{4,12},{6,14},{8,0},{10,2},{12,4},{14,6},{1,9},{3,11}... | collective-permute-start | bytes 1572872 | tf_op jit(solution)/shard_map/ppermute | solution.py:39
  8.5 1.4 copy-start.4
  9.9 11.9 %copy-start.7 = (bf16[1,1024,256]{2,1,0:T(8,128)(2,1)S(1)}, bf16[1,1024,256]{2,1,0:T(8,128)(2,1)}, u32[]{:S(2)}) copy-start(bf16[1,1024,256]{2,1,0:T(8,128)(2,1)} %param.11) | copy-start | bytes 1572868
  10.7 11.2 %collective-permute-start.1 = (bf16[3,256,256]{2,1,0:T(8,128)(2,1)S(1)}, bf16[3,256,256]{2,1,0:T(8,128)(2,1)S(1)}, u32[]{:S(2)}, u32[]{:S(2)}) collective-permute-start(bf16[3,256,256]{2,1,0:T(8,128)(2,1)S(1)} %get-tuple-element.43), channel_id=1, source_target_pairs={{0,2},{2,4},{4,6},{6,0},{8,10},{10,12},{12,14},{14,8},{1,3},{3,5},... | collective-permute-start | bytes 1179656 | tf_op jit(solution)/shard_map/ppermute | solution.py:25
  12.0 19.1 %collective-permute-start.2 = (bf16[3,256,256]{2,1,0:T(8,128)(2,1)S(1)}, bf16[3,256,256]{2,1,0:T(8,128)(2,1)S(1)}, u32[]{:S(2)}, u32[]{:S(2)}) collective-permute-start(bf16[3,256,256]{2,1,0:T(8,128)(2,1)S(1)} %get-tuple-element.44), channel_id=1, source_target_pairs={{0,4},{2,6},{4,0},{6,2},{8,12},{10,14},{12,8},{14,10},{1,5},{3,7},... | collective-permute-start | bytes 1179656 | tf_op jit(solution)/shard_map/ppermute | solution.py:25
  14.4 16.6 %collective-permute-start.3 = (bf16[3,256,256]{2,1,0:T(8,128)(2,1)S(1)}, bf16[3,256,256]{2,1,0:T(8,128)(2,1)S(1)}, u32[]{:S(2)}, u32[]{:S(2)}) collective-permute-start(bf16[3,256,256]{2,1,0:T(8,128)(2,1)S(1)} %get-tuple-element.45), channel_id=1, source_target_pairs={{0,6},{2,0},{4,2},{6,4},{8,14},{10,8},{12,10},{14,12},{1,7},{3,1},... | collective-permute-start | bytes 1179656 | tf_op jit(solution)/shard_map/ppermute | solution.py:25
  15.6 1.6 copy-start
  17.2 1.0 copy-start.2
  18.2 0.7 copy-start.5
  18.9 0.7 copy-start.6
  31.1 26.8 %collective-permute-start.4 = (bf16[272,2048]{1,0:T(8,128)(2,1)S(1)}, bf16[272,2048]{1,0:T(8,128)(2,1)S(1)}, u32[]{:S(2)}, u32[]{:S(2)}) collective-permute-start(bf16[272,2048]{1,0:T(8,128)(2,1)S(1)} %get-tuple-element.48.refs_0_), channel_id=1, source_target_pairs={{0,2},{2,4},{4,6},{6,0},{8,10},{10,12},{12,14},{14,8},{1,3},{3,5},... | collective-permute-start | bytes 3342344 | tf_op jit(solution)/shard_map/ppermute | solution.py:25
  32.8 25.1 %collective-permute-start.6 = (bf16[272,2048]{1,0:T(8,128)(2,1)S(1)}, bf16[272,2048]{1,0:T(8,128)(2,1)S(1)}, u32[]{:S(2)}, u32[]{:S(2)}) collective-permute-start(bf16[272,2048]{1,0:T(8,128)(2,1)S(1)} %get-tuple-element.48.refs_0_), channel_id=1, source_target_pairs={{0,6},{2,0},{4,2},{6,4},{8,14},{10,8},{12,10},{14,12},{1,7},{3,1},... | collective-permute-start | bytes 3342344 | tf_op jit(solution)/shard_map/ppermute | solution.py:25
  34.6 28.2 %collective-permute-start.11 = (bf16[4,3,256,256]{3,2,1,0:T(8,128)(2,1)S(1)}, bf16[4,3,256,256]{3,2,1,0:T(8,128)(2,1)S(1)}, u32[]{:S(2)}, u32[]{:S(2)}) collective-permute-start(bf16[4,3,256,256]{3,2,1,0:T(8,128)(2,1)S(1)} %pad_maximum_fusion.refs_9_), channel_id=1, source_target_pairs={{0,1},{1,0},{2,3},{3,2},{4,5},{5,4},{6,7},{7,6},{8,9},{9,8},{10,11... | collective-permute-start | bytes 4718600 | tf_op jit(solution)/shard_map/ppermute | solution.py:43
  36.5 50.1 %collective-permute-start.14 = (bf16[4,3,256,256]{3,2,1,0:T(8,128)(2,1)S(1)}, bf16[4,3,256,256]{3,2,1,0:T(8,128)(2,1)S(1)}, u32[]{:S(2)}, u32[]{:S(2)}) collective-permute-start(bf16[4,3,256,256]{3,2,1,0:T(8,128)(2,1)S(1)} %pad_maximum_fusion.refs_9_), channel_id=1, source_target_pairs={{0,8},{2,10},{4,12},{6,14},{8,0},{10,2},{12,4},{14,6},{1,9},{3,11}... | collective-permute-start | bytes 4718600 | tf_op jit(solution)/shard_map/ppermute | solution.py:39
  57.8 2.1 %collective-permute-start.10 = (bf16[64,2048]{1,0:T(8,128)(2,1)S(1)}, bf16[64,2048]{1,0:T(8,128)(2,1)S(1)}, u32[]{:S(2)}, u32[]{:S(2)}) collective-permute-start(bf16[64,2048]{1,0:T(8,128)(2,1)S(1)} %get-tuple-element.50.refs_5_), channel_id=1, source_target_pairs={{128,134},{130,128},{132,130},{134,132},{136,142},{138,136},{140,1... | collective-permute-start | bytes 786440 | tf_op jit(solution)/shard_map/ppermute | solution.py:35
  58.6 14.0 %collective-permute-start.5 = (bf16[144,2048]{1,0:T(8,128)(2,1)S(1)}, bf16[144,2048]{1,0:T(8,128)(2,1)S(1)}, u32[]{:S(2)}, u32[]{:S(2)}) collective-permute-start(bf16[144,2048]{1,0:T(8,128)(2,1)S(1)} %slice.24), channel_id=1, source_target_pairs={{0,2},{2,4},{4,6},{6,0},{8,10},{10,12},{12,14},{14,8},{1,3},{3,5},... | collective-permute-start | bytes 1769480 | tf_op jit(solution)/shard_map/ppermute | solution.py:25
  59.2 2.9 %collective-permute-start.8 = (bf16[64,2048]{1,0:T(8,128)(2,1)S(1)}, bf16[64,2048]{1,0:T(8,128)(2,1)S(1)}, u32[]{:S(2)}, u32[]{:S(2)}) collective-permute-start(bf16[64,2048]{1,0:T(8,128)(2,1)S(1)} %get-tuple-element.50.refs_5_), channel_id=1, source_target_pairs={{128,130},{130,132},{132,134},{134,128},{136,138},{138,140},{140,1... | collective-permute-start | bytes 786440 | tf_op jit(solution)/shard_map/ppermute | solution.py:35
  60.0 12.3 %collective-permute-start.7 = (bf16[128,2048]{1,0:T(8,128)(2,1)S(1)}, bf16[128,2048]{1,0:T(8,128)(2,1)S(1)}, u32[]{:S(2)}, u32[]{:S(2)}) collective-permute-start(bf16[128,2048]{1,0:T(8,128)(2,1)S(1)} %slice.25), channel_id=1, source_target_pairs={{0,6},{2,0},{4,2},{6,4},{8,14},{10,8},{12,10},{14,12},{1,7},{3,1},... | collective-permute-start | bytes 1572872 | tf_op jit(solution)/shard_map/ppermute | solution.py:25
  62.1 0.7 collective-permute-start.9
  78.6 31.5 %collective-permute-start.12 = (bf16[2048,256]{1,0:T(8,128)(2,1)S(1)}, bf16[2048,256]{1,0:T(8,128)(2,1)S(1)}, u32[]{:S(2)}, u32[]{:S(2)}) collective-permute-start(bf16[2048,256]{1,0:T(8,128)(2,1)S(1)} %pad_maximum_fusion.1), channel_id=1, source_target_pairs={{0,2},{2,4},{4,6},{6,0},{8,10},{10,12},{12,14},{14,8},{1,3},{3,5},... | collective-permute-start | bytes 3145736 | tf_op jit(solution)/shard_map/ppermute | solution.py:25
  79.8 30.5 %collective-permute-start.13 = (bf16[2048,256]{1,0:T(8,128)(2,1)S(1)}, bf16[2048,256]{1,0:T(8,128)(2,1)S(1)}, u32[]{:S(2)}, u32[]{:S(2)}) collective-permute-start(bf16[2048,256]{1,0:T(8,128)(2,1)S(1)} %pad_maximum_fusion.1), channel_id=1, source_target_pairs={{0,6},{2,0},{4,2},{6,4},{8,14},{10,8},{12,10},{14,12},{1,7},{3,1},... | collective-permute-start | bytes 3145736 | tf_op jit(solution)/shard_map/ppermute | solution.py:25
  86.7 26.3 %collective-permute-start.16 = (bf16[2,3,256,256]{3,2,1,0:T(8,128)(2,1)S(1)}, bf16[2,3,256,256]{3,2,1,0:T(8,128)(2,1)S(1)}, u32[]{:S(2)}, u32[]{:S(2)}) collective-permute-start(bf16[2,3,256,256]{3,2,1,0:T(8,128)(2,1)S(1)} %get-tuple-element.59), channel_id=1, source_target_pairs={{0,1},{1,0},{2,3},{3,2},{4,5},{5,4},{6,7},{7,6},{8,9},{9,8},{10,11... | collective-permute-start | bytes 2359304 | tf_op jit(solution)/shard_map/ppermute | solution.py:43
  110.0 3.0 %collective-permute-start.15 = (bf16[2,3,256,256]{3,2,1,0:T(8,128)(2,1)S(1)}, bf16[2,3,256,256]{3,2,1,0:T(8,128)(2,1)S(1)}, u32[]{:S(2)}, u32[]{:S(2)}) collective-permute-start(bf16[2,3,256,256]{3,2,1,0:T(8,128)(2,1)S(1)} %get-tuple-element.58), channel_id=1, source_target_pairs={{0,1},{1,0},{2,3},{3,2},{4,5},{5,4},{6,7},{7,6},{8,9},{9,8},{10,11... | collective-permute-start | bytes 2359304 | tf_op jit(solution)/shard_map/ppermute | solution.py:43
  110.1 14.4 %collective-permute-start.20 = (bf16[1024,256]{1,0:T(8,128)(2,1)S(1)}, bf16[1024,256]{1,0:T(8,128)(2,1)S(1)}, u32[]{:S(2)}, u32[]{:S(2)}) collective-permute-start(bf16[1024,256]{1,0:T(8,128)(2,1)S(1)} %slice.28), channel_id=1, source_target_pairs={{0,2},{2,4},{4,6},{6,0},{8,10},{10,12},{12,14},{14,8},{1,3},{3,5},... | collective-permute-start | bytes 1572872 | tf_op jit(solution)/shard_map/ppermute | solution.py:25
  110.3 14.2 %collective-permute-start.21 = (bf16[1024,256]{1,0:T(8,128)(2,1)S(1)}, bf16[1024,256]{1,0:T(8,128)(2,1)S(1)}, u32[]{:S(2)}, u32[]{:S(2)}) collective-permute-start(bf16[1024,256]{1,0:T(8,128)(2,1)S(1)} %slice.29), channel_id=1, source_target_pairs={{0,6},{2,0},{4,2},{6,4},{8,14},{10,8},{12,10},{14,12},{1,7},{3,1},... | collective-permute-start | bytes 1572872 | tf_op jit(solution)/shard_map/ppermute | solution.py:25
  124.7 23.8 %copy-start.1 = (bf16[1,2,256,2048]{3,2,1,0:T(8,128)(2,1)S(1)}, bf16[1,2,256,2048]{3,2,1,0:T(8,128)(2,1)}, u32[]{:S(2)}) copy-start(bf16[1,2,256,2048]{3,2,1,0:T(8,128)(2,1)} %param.6) | copy-start | bytes 6291460
  124.7 23.8 %copy-start.3 = (bf16[1,2,64,2048]{3,2,1,0:T(8,128)(2,1)S(1)}, bf16[1,2,64,2048]{3,2,1,0:T(8,128)(2,1)}, u32[]{:S(2)}) copy-start(bf16[1,2,64,2048]{3,2,1,0:T(8,128)(2,1)} %param.7) | copy-start | bytes 1572868
  124.9 23.6 %collective-permute-start.22 = (bf16[8192,256]{1,0:T(8,128)(2,1)S(1)}, bf16[8192,256]{1,0:T(8,128)(2,1)S(1)}, u32[]{:S(2)}, u32[]{:S(2)}) collective-permute-start(bf16[8192,256]{1,0:T(8,128)(2,1)S(1)} %constant_dynamic-update-slice_fusion.refs_4_), channel_id=1, source_target_pairs={{0,1},{1,0},{2,3},{3,2},{4,5},{5,4},{6,7},{7,6},{8,9},{9,8},{10,11... | collective-permute-start | bytes 12582920 | tf_op jit(solution)/shard_map/ppermute | solution.py:43
  126.2 13.9 %collective-permute-start.17 = (bf16[256,512]{1,0:T(8,128)(2,1)S(1)}, bf16[256,512]{1,0:T(8,128)(2,1)S(1)}, u32[]{:S(2)}, u32[]{:S(2)}) collective-permute-start(bf16[256,512]{1,0:T(8,128)(2,1)S(1)} %get-tuple-element.61), channel_id=1, source_target_pairs={{0,6},{2,0},{4,2},{6,4},{8,14},{10,8},{12,10},{14,12},{1,7},{3,1},... | collective-permute-start | bytes 786440 | tf_op jit(solution)/shard_map/ppermute | solution.py:25
  129.0 11.1 %collective-permute-start.18 = (bf16[256,512]{1,0:T(8,128)(2,1)S(1)}, bf16[256,512]{1,0:T(8,128)(2,1)S(1)}, u32[]{:S(2)}, u32[]{:S(2)}) collective-permute-start(bf16[256,512]{1,0:T(8,128)(2,1)S(1)} %get-tuple-element.62), channel_id=1, source_target_pairs={{0,4},{2,6},{4,0},{6,2},{8,12},{10,14},{12,8},{14,10},{1,5},{3,7},... | collective-permute-start | bytes 786440 | tf_op jit(solution)/shard_map/ppermute | solution.py:25
  129.0 14.8 %collective-permute-start.19 = (bf16[256,512]{1,0:T(8,128)(2,1)S(1)}, bf16[256,512]{1,0:T(8,128)(2,1)S(1)}, u32[]{:S(2)}, u32[]{:S(2)}) collective-permute-start(bf16[256,512]{1,0:T(8,128)(2,1)S(1)} %get-tuple-element.63), channel_id=1, source_target_pairs={{0,2},{2,4},{4,6},{6,0},{8,10},{10,12},{12,14},{14,8},{1,3},{3,5},... | collective-permute-start | bytes 786440 | tf_op jit(solution)/shard_map/ppermute | solution.py:25
  143.8 37.8 %collective-permute-start.30 = (bf16[256,2048]{1,0:T(8,128)(2,1)S(1)}, bf16[256,2048]{1,0:T(8,128)(2,1)S(1)}, u32[]{:S(2)}, u32[]{:S(2)}) collective-permute-start(bf16[256,2048]{1,0:T(8,128)(2,1)S(1)} %get-tuple-element.78), channel_id=1, source_target_pairs={{128,144},{144,160},{160,176},{176,192},{192,208},{208,224},{224,2... | collective-permute-start | bytes 3145736 | tf_op jit(solution)/shard_map/ppermute | solution.py:47
  145.1 8.7 %collective-permute-start.25 = (bf16[64,2048]{1,0:T(8,128)(2,1)S(1)}, bf16[64,2048]{1,0:T(8,128)(2,1)S(1)}, u32[]{:S(2)}, u32[]{:S(2)}) collective-permute-start(bf16[64,2048]{1,0:T(8,128)(2,1)S(1)} %get-tuple-element.73), channel_id=1, source_target_pairs={{0,16},{16,32},{32,48},{48,64},{64,80},{80,96},{96,112},{112,128},... | collective-permute-start | bytes 786440 | tf_op jit(solution)/shard_map/ppermute | solution.py:47
  150.7 30.9 %collective-permute-start.23 = (bf16[256,1024]{1,0:T(8,128)(2,1)S(1)}, bf16[256,1024]{1,0:T(8,128)(2,1)S(1)}, u32[]{:S(2)}, u32[]{:S(2)}) collective-permute-start(bf16[256,1024]{1,0:T(8,128)(2,1)S(1)} %get-tuple-element.69), channel_id=1, source_target_pairs={{0,16},{16,32},{32,48},{48,64},{64,80},{80,96},{96,112},{112,128},... | collective-permute-start | bytes 1572872 | tf_op jit(solution)/shard_map/ppermute | solution.py:47
  153.8 3.6 %collective-permute-start.26 = (bf16[64,2048]{1,0:T(8,128)(2,1)S(1)}, bf16[64,2048]{1,0:T(8,128)(2,1)S(1)}, u32[]{:S(2)}, u32[]{:S(2)}) collective-permute-start(bf16[64,2048]{1,0:T(8,128)(2,1)S(1)} %collective-permute-done.25.refs_6_), channel_id=1, source_target_pairs={{0,1},{1,0},{2,3},{3,2},{4,5},{5,4},{6,7},{7,6},{8,9},{9,8},{10,11... | collective-permute-start | bytes 786440 | tf_op jit(solution)/shard_map/ppermute | solution.py:43
  157.4 38.9 %collective-permute-start.27 = (bf16[256,1024]{1,0:T(8,128)(2,1)S(1)}, bf16[256,1024]{1,0:T(8,128)(2,1)S(1)}, u32[]{:S(2)}, u32[]{:S(2)}) collective-permute-start(bf16[256,1024]{1,0:T(8,128)(2,1)S(1)} %get-tuple-element.74), channel_id=1, source_target_pairs={{0,16},{16,32},{32,48},{48,64},{64,80},{80,96},{96,112},{112,128},... | collective-permute-start | bytes 1572872 | tf_op jit(solution)/shard_map/ppermute | solution.py:47
  181.6 18.2 %collective-permute-start.31 = (bf16[256,2048]{1,0:T(8,128)(2,1)S(1)}, bf16[256,2048]{1,0:T(8,128)(2,1)S(1)}, u32[]{:S(2)}, u32[]{:S(2)}) collective-permute-start(bf16[256,2048]{1,0:T(8,128)(2,1)S(1)} %collective-permute-done.30.refs_4_), channel_id=1, source_target_pairs={{0,1},{1,0},{2,3},{3,2},{4,5},{5,4},{6,7},{7,6},{8,9},{9,8},{10,11... | collective-permute-start | bytes 3145736 | tf_op jit(solution)/shard_map/ppermute | solution.py:43
  182.6 13.7 %collective-permute-start.28 = (bf16[64,2048]{1,0:T(8,128)(2,1)S(1)}, bf16[64,2048]{1,0:T(8,128)(2,1)S(1)}, u32[]{:S(2)}, u32[]{:S(2)}) collective-permute-start(bf16[64,2048]{1,0:T(8,128)(2,1)S(1)} %get-tuple-element.75), channel_id=1, source_target_pairs={{128,144},{144,160},{160,176},{176,192},{192,208},{208,224},{224,2... | collective-permute-start | bytes 786440 | tf_op jit(solution)/shard_map/ppermute | solution.py:47
  196.3 3.5 %collective-permute-start.29 = (bf16[256,1024]{1,0:T(8,128)(2,1)S(1)}, bf16[256,1024]{1,0:T(8,128)(2,1)S(1)}, u32[]{:S(2)}, u32[]{:S(2)}) collective-permute-start(bf16[256,1024]{1,0:T(8,128)(2,1)S(1)} %collective-permute-done.27.refs_2_), channel_id=1, source_target_pairs={{0,1},{1,0},{2,3},{3,2},{4,5},{5,4},{6,7},{7,6},{8,9},{9,8},{10,11... | collective-permute-start | bytes 1572872 | tf_op jit(solution)/shard_map/ppermute | solution.py:43
  197.1 2.7 %collective-permute-start.24 = (bf16[256,1024]{1,0:T(8,128)(2,1)S(1)}, bf16[256,1024]{1,0:T(8,128)(2,1)S(1)}, u32[]{:S(2)}, u32[]{:S(2)}) collective-permute-start(bf16[256,1024]{1,0:T(8,128)(2,1)S(1)} %collective-permute-done.23.refs_0_), channel_id=1, source_target_pairs={{0,1},{1,0},{2,3},{3,2},{4,5},{5,4},{6,7},{7,6},{8,9},{9,8},{10,11... | collective-permute-start | bytes 1572872 | tf_op jit(solution)/shard_map/ppermute | solution.py:43
  197.1 2.7 %collective-permute-start.32 = (bf16[64,2048]{1,0:T(8,128)(2,1)S(1)}, bf16[64,2048]{1,0:T(8,128)(2,1)S(1)}, u32[]{:S(2)}, u32[]{:S(2)}) collective-permute-start(bf16[64,2048]{1,0:T(8,128)(2,1)S(1)} %collective-permute-done.28.refs_8_), channel_id=1, source_target_pairs={{0,1},{1,0},{2,3},{3,2},{4,5},{5,4},{6,7},{7,6},{8,9},{9,8},{10,11... | collective-permute-start | bytes 786440 | tf_op jit(solution)/shard_map/ppermute | solution.py:43

commit v5 on v4

--- a/solution.py
+++ b/solution.py
@@ -25,16 +25,6 @@
     return lax.ppermute(array, "dp", pairs)
 
 
-def around_x_of(array, by, sections):
-    pairs = []
-    for s in sections:
-        for z in range(2):
-            for x in range(RING):
-                base = s * 2 * RING + z * RING
-                pairs.append((base + x, base + (x + by) % RING))
-    return lax.ppermute(array, ("section", "dp"), pairs)
-
-
 def across_z(array):
     return lax.ppermute(array, "dp", [(d, (d + RING) % (2 * RING)) for d in range(2 * RING)])
 
@@ -47,8 +37,8 @@
     return lax.ppermute(array, "section", [(s, (s + 1) % count) for s in sections])
 
 
-def round_ring(array, cut):
-    left, right = around_x(array, 1), around_x(array, -1)
+def round_ring(array, cut, *before_right):
+    left, right = around_x(array, 1), around_x(after(array, *before_right), -1)
     return array, left, around_x(left[:cut], 1), around_x(right[cut:], -1), right
 
 
@@ -95,9 +85,7 @@
     )(where, weight)
 
 
-def norm_kernel(
-    where, context, queries, gain, lengths, ctx_out, qry_out, normed, qry_normed, *scratch
-):
+def norm_kernel(where, context, queries, gain, lengths, ctx_out, qry_out, normed, *scratch):
     ctx, qry, sems = scratch
     core = where[3]
     copies = copy_all(
@@ -108,14 +96,14 @@
     )
     step = 32
 
-    def rows_of(source, raw, target):
+    def rows_of(source, raw, below):
         @pl.loop(0, source.shape[0] // step)
         def _(i):
             first = pl.multiple_of(i * step, step)
             low = source[pl.ds(first, step), :]
             wide = low.astype(F32)
             mean = jnp.mean(wide * wide, axis=-1, keepdims=True)
-            target[pl.ds(first, step), :] = (
+            normed[pl.ds(below + first, step), :] = (
                 wide * lax.rsqrt(mean + 1e-06) * gain[...]
             ).astype(BF16)
             raw[pl.ds(first, step), :] = low
@@ -125,20 +113,20 @@
         (TAIL, normed.shape[1]), length
     ).astype(BF16)
     copies[0].wait()
-    rows_of(ctx, ctx_out, normed)
+    rows_of(ctx, ctx_out, 0)
     copies[1].wait()
-    rows_of(qry, qry_out, qry_normed)
+    rows_of(qry, qry_out, ctx.shape[0])
 
 
 def norm_scene(where, context, queries, gain, lengths):
     ctx = jax.ShapeDtypeStruct(context.shape[1:], BF16)
     qry = jax.ShapeDtypeStruct(queries.shape[1:], BF16)
-    rows = ctx.shape[0] + TAIL
+    rows = ctx.shape[0] + qry.shape[0] + TAIL
     return call(
         norm_kernel,
-        (ctx, qry, jax.ShapeDtypeStruct((rows, ctx.shape[1]), BF16), qry),
+        (ctx, qry, jax.ShapeDtypeStruct((rows, ctx.shape[1]), BF16)),
         [SMEM, HBM, HBM, VMEM, SMEM],
-        (VMEM,) * 4,
+        (VMEM,) * 3,
         [
             pltpu.VMEM(ctx.shape, BF16),
             pltpu.VMEM(qry.shape, BF16),
@@ -148,16 +136,12 @@
 
 
 def start_kernel(where, *refs):
-    rows, queries, parts = refs[:5], refs[5:9], refs[9:11]
-    total, far_rows, far_qry, lengths, near_rows, near_qry, weight, sems = refs[11:]
+    rows, parts = refs[:5], refs[5:7]
+    total, far_rows, far_qry, lengths, near_rows, near_qry, weight, sems = refs[7:]
     x, z = where[0], where[1]
     mem, few = far_rows.shape[0] // RING, far_qry.shape[0] // RING
     width = far_rows.shape[1]
     copies = []
-
-    def take_queries(slot, columns, target):
-        source = queries[slot].at[:, columns]
-        copies.append(pltpu.make_async_copy(source, target, sems.at[len(copies)]))
 
     def take(slot, first, count, columns, target):
         cut = rows[2].shape[0]
@@ -186,15 +170,15 @@
     for slot in range(RING):
         columns = pl.ds(pl.multiple_of(z * width, width), width)
         take(slot, 0, mem, columns, near_rows.at[pl.ds(slot * mem, mem)])
-        take_queries(slot, columns, near_qry.at[pl.ds(slot * few, few)])
-        take(slot, mem, TAIL, pl.ds(0, 128), lengths.at[slot])
+        take(slot, mem, few, columns, near_qry.at[pl.ds(slot * few, few)])
+        take(slot, mem + few, TAIL, pl.ds(0, 128), lengths.at[slot])
     for step in range(RING):
         at = ((1 - z) * RING + (x - step + RING) % RING) * block
         columns = pl.ds(pl.multiple_of(at, block), block)
         here = pl.ds(step * block, block)
         for slot in range(RING):
             take(slot, 0, mem, columns, far_rows.at[pl.ds(slot * mem, mem), here])
-            take_queries(slot, columns, far_qry.at[pl.ds(slot * few, few), here])
+            take(slot, mem, few, columns, far_qry.at[pl.ds(slot * few, few), here])
     wait_all(copy_all(copies))
 
     @pl.when(where[2] == 1)
@@ -289,7 +273,7 @@
         outs[slot][...] = mixed[slot]
 
 
-def start_projections(where, mem, few, rows, queries, parts):
+def start_projections(where, mem, few, rows, parts):
     width = rows[0].shape[1]
     _, planes, block, part = parts[0].shape
     half = width // 2
@@ -301,7 +285,7 @@
             jax.ShapeDtypeStruct((RING * few, half), BF16),
             jax.ShapeDtypeStruct((RING, TAIL, 128), BF16),
         ),
-        [SMEM] + [HBM] * 11,
+        [SMEM] + [HBM] * 7,
         (VMEM,) * 4,
         [
             pltpu.VMEM((RING * mem, half), BF16),
@@ -310,7 +294,7 @@
             pltpu.SemaphoreType.DMA((64,)),
         ],
         limit=14,
-    )(where, *rows, *queries, *parts)
+    )(where, *rows, *parts)
 
 
 def attend(where, mem, started, far):
@@ -506,16 +490,14 @@
     near = jnp.stack(near)
     far = across_z(after(near, out_pair))
 
-    ctx, qry, normed, qry_normed = norm_scene(
+    ctx, qry, normed = norm_scene(
         after(where, *own), context, queries, norm_gain, lengths[0]
     )
     cut = (normed.shape[0] // 32 + 1) * 16
     rows = round_ring(after(normed, out_pair, *arrived), cut)
-    qry_sent = after(qry_normed, rows[1], rows[4])
-    qry_rows = [qry_normed] + [around_x_of(qry_sent, step, decoders) for step in range(1, RING)]
-    started = start_projections(where, mem, few, rows, qry_rows, (near, other_core(near)))
-
-    weights = round_ring(after(out_pair, *rows, started[0]), out_shard.shape[0])
+    started = start_projections(where, mem, few, rows, (near, other_core(near)))
+
+    weights = round_ring(after(out_pair, *rows), out_shard.shape[0], started[0])
     far_other = [other_core(after(far[i : i + 2], started[0])) for i in (0, 2)]
 
     mixed = attend(after(where, weights[1], weights[4]), mem, started, (far, *far_other))

time: 203 us -> 195 us (0.961)
  waiting for transfers between devices: 92.5 us -> 88.4 us
  starting transfers between devices: 78.1 us -> 74.2 us
    ppermute x5, waiting for transfers between devices: 32.5 us -> 24.8 us  [relay(): lax.ppermute(array, 'section', [(s, (s + 1) % count) for s in sections])]
    ppermute x14, waiting for transfers between devices: 52.2 us -> 59.9 us  [around_x(): return lax.ppermute(array, 'dp', pairs)]
    ppermute x2, waiting for transfers between devices: 5.55 us -> 0.29 us  [across_z(): lax.ppermute(array, 'dp', [(d, (d + RING) % (2 * RING)) for d in range(2...]
    ppermute x14, starting transfers between devices: 20 us -> 16 us  [around_x(): return lax.ppermute(array, 'dp', pairs)]
    ppermute x9, starting transfers between devices: 30.3 us -> 32.6 us  [other_core(): return lax.ppermute(array, 'tensor', [(0, 1), (1, 0)])]
  transfers between devices with their start and end apart: 33 -> 30, of which waited for: 12 -> 14; matrix products, arithmetic and copies ran while one was open for 0% -> 0% of each run, Pallas kernels for 11% -> 11%
where the time goes in v5:
time: 195 us; the launch traced here: 194 us
  waiting for transfers between devices  88.4 us (45%)
  starting transfers between devices  74.2 us (38%)
  Pallas kernels  24.2 us (12%)
  local copies, waits for them, and re-layouts  6.06 us (3%)
    ppermute x14, waiting for transfers between devices, around_x(): return lax.ppermute(array, 'dp', pairs)  59.9 us
    ppermute x9, starting transfers between devices, other_core(): return lax.ppermute(array, 'tensor', [(0, 1), (1, 0)])  32.6 us
    ppermute x5, waiting for transfers between devices, relay(): lax.ppermute(array, 'section', [(s, (s + 1) % count) for s in sections])  24.8 us
    ppermute x14, starting transfers between devices, around_x(): return lax.ppermute(array, 'dp', pairs)  16 us
    ppermute x5, starting transfers between devices, relay(): lax.ppermute(array, 'section', [(s, (s + 1) % count) for s in sections])  13.1 us
    ppermute x2, starting transfers between devices, across_z(): lax.ppermute(array, 'dp', [(d, (d + RING) % (2 * RING)) for d in range(2...  12.6 us
    pallas_call x1, Pallas kernels, attend(): call(attend_kernel, (out,) * RING, [SMEM] + [VMEM] * 7, (VMEM,) * RING, [...  8.91 us
    pallas_call x1, Pallas kernels, start_projections(): call(start_kernel, (jax.ShapeDtypeStruct((planes, RING * mem, 2 * part),...  5.95 us
  transfers between devices with their start and end apart: 30, of which 14 were waited for; matrix products, arithmetic and copies ran while one was open for 0% of the time, Pallas kernels for 11%

profile of v5, /device:TPU:1, one launch (start us, length us, event | category | flops | bytes accessed | tf_op | source)
XLA Modules:
  0.0 194.2 jit_solution(650283347895102348)
XLA Ops:
  0.6 7.8 %collective-permute-start = (bf16[1024,256]{1,0:T(8,128)(2,1)}, bf16[1024,256]{1,0:T(8,128)(2,1)S(1)}, u32[]{:S(2)}, u32[]{:S(2)}) collective-permute-start(bf16[1024,256]{1,0:T(8,128)(2,1)} %bitcast.27), channel_id=1, source_target_pairs={{0,8},{2,10},{4,12},{6,14},{8,0},{10,2},{12,4},{14,6},{1,9},{3,11}... | collective-permute-start | bytes 1572872 | tf_op jit(solution)/shard_map/ppermute | solution.py:29
  8.5 0.1 stack.46.where
  8.5 1.4 copy-done.4
  9.9 0.8 shard_map.77
  10.7 1.3 collective-permute-start.1
  12.0 2.5 %collective-permute-start.2 = (bf16[3,256,256]{2,1,0:T(8,128)(2,1)S(1)}, bf16[3,256,256]{2,1,0:T(8,128)(2,1)S(1)}, u32[]{:S(2)}, u32[]{:S(2)}) collective-permute-start(bf16[3,256,256]{2,1,0:T(8,128)(2,1)S(1)} %get-tuple-element.43), channel_id=1, source_target_pairs={{0,4},{2,6},{4,0},{6,2},{8,12},{10,14},{12,8},{14,10},{1,5},{3,7},... | collective-permute-start | bytes 1179656 | tf_op jit(solution)/shard_map/ppermute | solution.py:25
  14.4 1.2 collective-permute-start.3
  15.6 1.6 copy-done
  17.2 1.0 copy-done.2
  18.2 0.7 copy-done.5
  18.9 0.7 copy-done.6
  19.6 2.0 %shard_map.78 = (bf16[256,2048]{1,0:T(8,128)(2,1)S(1)}, bf16[64,2048]{1,0:T(8,128)(2,1)S(1)}, bf16[336,2048]{1,0:T(8,128)(2,1)S(1)}) custom-call(s32[5]{0:T(128)S(1)} %stack.46.where, bf16[2,256,2048]{2,1,0:T(8,128)(2,1)S(1)} %bitcast.18, bf16[2,64,2048]{2,1,0:T(8,128)(2,1)S(1)} %bitcast.21, f32[1,2048]{1,0:T(1,128)S(1)} %copy-done.5, s32[2]{0:T(128)S(1)} %bitcast.26), custom_call_target="tpu_custom_call" | custom-call | flops 1 | bytes 1 | tf_op jit(solution)/shard_map/pallas_call | solution.py:125
  21.6 0.3 collective-permute-done
  21.9 0.1 pad_maximum_fusion.1
  22.0 9.1 %collective-permute-done.2 = bf16[3,256,256]{2,1,0:T(8,128)(2,1)S(1)} collective-permute-done((bf16[3,256,256]{2,1,0:T(8,128)(2,1)S(1)}, bf16[3,256,256]{2,1,0:T(8,128)(2,1)S(1)}, u32[]{:S(2)}, u32[]{:S(2)}) %collective-permute-start.2) | collective-permute-done | bytes 393248 | tf_op jit(solution)/shard_map/ppermute | solution.py:25
  31.1 1.7 collective-permute-start.4
  32.8 1.7 collective-permute-start.6
  34.4 0.2 pad_maximum_fusion.refs_5_
  34.6 1.8 collective-permute-start.9
  36.5 4.8 %collective-permute-start.11 = (bf16[4,3,256,256]{3,2,1,0:T(8,128)(2,1)S(1)}, bf16[4,3,256,256]{3,2,1,0:T(8,128)(2,1)S(1)}, u32[]{:S(2)}, u32[]{:S(2)}) collective-permute-start(bf16[4,3,256,256]{3,2,1,0:T(8,128)(2,1)S(1)} %pad_maximum_fusion.refs_5_), channel_id=1, source_target_pairs={{0,8},{2,10},{4,12},{6,14},{8,0},{10,2},{12,4},{14,6},{1,9},{3,11}... | collective-permute-start | bytes 4718600 | tf_op jit(solution)/shard_map/ppermute | solution.py:29
  41.3 22.2 %collective-permute-done.4.refs_1_ = bf16[336,2048]{1,0:T(8,128)(2,1)S(1)} collective-permute-done((bf16[336,2048]{1,0:T(8,128)(2,1)S(1)}, bf16[336,2048]{1,0:T(8,128)(2,1)S(1)}, u32[]{:S(2)}, u32[]{:S(2)}) %collective-permute-start.4) | collective-permute-done | bytes 1376288 | tf_op jit(solution)/shard_map/ppermute | solution.py:25
  63.5 0.1 slice.24
  63.5 0.1 collective-permute-start.5
  63.6 0.1 slice.25
  63.7 2.7 %collective-permute-start.7 = (bf16[160,2048]{1,0:T(8,128)(2,1)S(1)}, bf16[160,2048]{1,0:T(8,128)(2,1)S(1)}, u32[]{:S(2)}, u32[]{:S(2)}) collective-permute-start(bf16[160,2048]{1,0:T(8,128)(2,1)S(1)} %slice.25), channel_id=1, source_target_pairs={{0,6},{2,0},{4,2},{6,4},{8,14},{10,8},{12,10},{14,12},{1,7},{3,1},... | collective-permute-start | bytes 1966088 | tf_op jit(solution)/shard_map/ppermute | solution.py:25
  66.4 11.6 %collective-permute-done.7.refs_3_ = bf16[160,2048]{1,0:T(8,128)(2,1)S(1)} collective-permute-done((bf16[160,2048]{1,0:T(8,128)(2,1)S(1)}, bf16[160,2048]{1,0:T(8,128)(2,1)S(1)}, u32[]{:S(2)}, u32[]{:S(2)}) %collective-permute-start.7) | collective-permute-done | bytes 655392 | tf_op jit(solution)/shard_map/ppermute | solution.py:25
  78.1 2.3 %collective-permute-done.5.refs_2_ = bf16[176,2048]{1,0:T(8,128)(2,1)S(1)} collective-permute-done((bf16[176,2048]{1,0:T(8,128)(2,1)S(1)}, bf16[176,2048]{1,0:T(8,128)(2,1)S(1)}, u32[]{:S(2)}, u32[]{:S(2)}) %collective-permute-start.5) | collective-permute-done | bytes 720928 | tf_op jit(solution)/shard_map/ppermute | solution.py:25
  80.3 6.0 %shard_map.79 = (f32[3,1024,512]{2,1,0:T(8,128)S(1)}, bf16[1024,1024]{1,0:T(8,128)(2,1)S(1)}, bf16[256,1024]{1,0:T(8,128)(2,1)S(1)}, bf16[4,16,128]{2,1,0:T(8,128)(2,1)S(1)}) custom-call(s32[5]{0:T(128)S(1)} %stack.46.where, bf16[336,2048]{1,0:T(8,128)(2,1)S(1)} %get-tuple-element.47.refs_0_, bf16[336,2048]{1,0:T(8,128)(2,1)S(1)} %collective-permute-done.4.refs_1_, ...), custom_call_target="tpu_custom_call" | custom-call | flops 1 | bytes 1 | tf_op jit(solution)/shard_map/pallas_call | solution.py:280
  86.3 1.8 collective-permute-start.10
  88.1 0.1 fusion
  88.3 21.9 %collective-permute-start.13 = (bf16[2,3,256,256]{3,2,1,0:T(8,128)(2,1)S(1)}, bf16[2,3,256,256]{3,2,1,0:T(8,128)(2,1)S(1)}, u32[]{:S(2)}, u32[]{:S(2)}) collective-permute-start(bf16[2,3,256,256]{3,2,1,0:T(8,128)(2,1)S(1)} %get-tuple-element.57), channel_id=1, source_target_pairs={{0,1},{1,0},{2,3},{3,2},{4,5},{5,4},{6,7},{7,6},{8,9},{9,8},{10,11... | collective-permute-start | bytes 2359304 | tf_op jit(solution)/shard_map/ppermute | solution.py:33
  110.2 0.1 collective-permute-start.12
  110.3 1.4 collective-permute-start.18
  111.8 0.2 collective-permute-start.17
  112.0 0.1 collective-permute-done.13.refs_2_
  112.1 1.1 collective-permute-done.12.refs_1_
  113.2 8.9 %shard_map.80 = (bf16[256,512]{1,0:T(8,128)(2,1)S(1)}, bf16[256,512]{1,0:T(8,128)(2,1)S(1)}, bf16[256,512]{1,0:T(8,128)(2,1)S(1)}, bf16[256,512]{1,0:T(8,128)(2,1)S(1)}) custom-call(s32[5]{0:T(128)S(1)} %stack.46.where, f32[3,1024,512]{2,1,0:T(8,128)S(1)} %get-tuple-element.49.total, bf16[1024,1024]{1,0:T(8,128)(2,1)S(1)} %get-tuple-element.52.rows, ...), custom_call_target="tpu_custom_call" | custom-call | flops 1 | bytes 1 | tf_op jit(solution)/shard_map/pallas_call | solution.py:304
  122.1 0.0 collective-permute-done.18
  122.2 0.7 collective-permute-done.17
  122.9 0.1 constant_dynamic-update-slice_fusion.4
  123.0 0.1 constant_dynamic-update-slice_fusion.3
  123.0 0.0 copy-start.1
  123.2 0.1 constant_dynamic-update-slice_fusion.refs_4_
  123.2 4.6 %collective-permute-start.19 = (bf16[8192,256]{1,0:T(8,128)(2,1)S(1)}, bf16[8192,256]{1,0:T(8,128)(2,1)S(1)}, u32[]{:S(2)}, u32[]{:S(2)}) collective-permute-start(bf16[8192,256]{1,0:T(8,128)(2,1)S(1)} %constant_dynamic-update-slice_fusion.refs_4_), channel_id=1, source_target_pairs={{0,1},{1,0},{2,3},{3,2},{4,5},{5,4},{6,7},{7,6},{8,9},{9,8},{10,11... | collective-permute-start | bytes 12582920 | tf_op jit(solution)/shard_map/ppermute | solution.py:33
  127.8 0.7 collective-permute-start.15
  128.6 0.7 collective-permute-start.16
  129.3 6.4 %collective-permute-done.14.refs_1_ = bf16[256,512]{1,0:T(8,128)(2,1)S(1)} collective-permute-done((bf16[256,512]{1,0:T(8,128)(2,1)S(1)}, bf16[256,512]{1,0:T(8,128)(2,1)S(1)}, u32[]{:S(2)}, u32[]{:S(2)}) %collective-permute-start.14) | collective-permute-done | bytes 262176 | tf_op jit(solution)/shard_map/ppermute | solution.py:25
  135.7 1.3 collective-permute-done.15.refs_2_
  137.0 6.2 %collective-permute-done.16.refs_3_ = bf16[256,512]{1,0:T(8,128)(2,1)S(1)} collective-permute-done((bf16[256,512]{1,0:T(8,128)(2,1)S(1)}, bf16[256,512]{1,0:T(8,128)(2,1)S(1)}, u32[]{:S(2)}, u32[]{:S(2)}) %collective-permute-start.16) | collective-permute-done | bytes 262176 | tf_op jit(solution)/shard_map/ppermute | solution.py:25
  143.2 1.3 collective-permute-start.27
  144.5 3.3 %collective-permute-start.22 = (bf16[64,2048]{1,0:T(8,128)(2,1)S(1)}, bf16[64,2048]{1,0:T(8,128)(2,1)S(1)}, u32[]{:S(2)}, u32[]{:S(2)}) collective-permute-start(bf16[64,2048]{1,0:T(8,128)(2,1)S(1)} %get-tuple-element.71), channel_id=1, source_target_pairs={{0,16},{16,32},{32,48},{48,64},{64,80},{80,96},{96,112},{112,128},... | collective-permute-start | bytes 786440 | tf_op jit(solution)/shard_map/ppermute | solution.py:37
  147.8 2.2 %shard_map.81 = (bf16[256,1024]{1,0:T(8,128)(2,1)S(1)}, bf16[64,1024]{1,0:T(8,128)(2,1)S(1)}) custom-call(s32[5]{0:T(128)S(1)} %stack.46.where, bf16[2,256,2048]{2,1,0:T(8,128)(2,1)S(1)} %bitcast.19, bf16[2,64,2048]{2,1,0:T(8,128)(2,1)S(1)} %bitcast.22, bf16[256,512]{1,0:T(8,128)(2,1)S(1)} %get-tuple-element.58.refs_0_, ...), custom_call_target="tpu_custom_call" | custom-call | flops 1 | bytes 1 | tf_op jit(solution)/shard_map/pallas_call | solution.py:388
  150.0 3.1 %collective-permute-start.20 = (bf16[256,1024]{1,0:T(8,128)(2,1)S(1)}, bf16[256,1024]{1,0:T(8,128)(2,1)S(1)}, u32[]{:S(2)}, u32[]{:S(2)}) collective-permute-start(bf16[256,1024]{1,0:T(8,128)(2,1)S(1)} %get-tuple-element.67), channel_id=1, source_target_pairs={{0,16},{16,32},{32,48},{48,64},{64,80},{80,96},{96,112},{112,128},... | collective-permute-start | bytes 1572872 | tf_op jit(solution)/shard_map/ppermute | solution.py:37
  153.1 1.5 collective-permute-start.23
  154.6 2.2 %shard_map.82 = (bf16[256,1024]{1,0:T(8,128)(2,1)S(1)}, bf16[64,2048]{1,0:T(8,128)(2,1)S(1)}) custom-call(s32[5]{0:T(128)S(1)} %stack.46.where, bf16[2,256,2048]{2,1,0:T(8,128)(2,1)S(1)} %bitcast.20, bf16[2,64,2048]{2,1,0:T(8,128)(2,1)S(1)} %bitcast.23, bf16[256,512]{1,0:T(8,128)(2,1)S(1)} %get-tuple-element.58.refs_0_, ...), custom_call_target="tpu_custom_call" | custom-call | flops 1 | bytes 1 | tf_op jit(solution)/shard_map/pallas_call | solution.py:388
  156.8 4.1 %collective-permute-start.24 = (bf16[256,1024]{1,0:T(8,128)(2,1)S(1)}, bf16[256,1024]{1,0:T(8,128)(2,1)S(1)}, u32[]{:S(2)}, u32[]{:S(2)}) collective-permute-start(bf16[256,1024]{1,0:T(8,128)(2,1)S(1)} %get-tuple-element.72), channel_id=1, source_target_pairs={{0,16},{16,32},{32,48},{48,64},{64,80},{80,96},{96,112},{112,128},... | collective-permute-start | bytes 1572872 | tf_op jit(solution)/shard_map/ppermute | solution.py:37
  160.9 12.3 %collective-permute-done.27.refs_4_ = bf16[256,2048]{1,0:T(8,128)(2,1)S(1)} collective-permute-done((bf16[256,2048]{1,0:T(8,128)(2,1)S(1)}, bf16[256,2048]{1,0:T(8,128)(2,1)S(1)}, u32[]{:S(2)}, u32[]{:S(2)}) %collective-permute-start.27) | collective-permute-done | bytes 1048608 | tf_op jit(solution)/shard_map/ppermute | solution.py:37
  173.3 1.3 collective-permute-start.28
  174.6 1.3 collective-permute-start.25
  175.9 12.4 %collective-permute-done.25.refs_8_ = bf16[64,2048]{1,0:T(8,128)(2,1)S(1)} collective-permute-done((bf16[64,2048]{1,0:T(8,128)(2,1)S(1)}, bf16[64,2048]{1,0:T(8,128)(2,1)S(1)}, u32[]{:S(2)}, u32[]{:S(2)}) %collective-permute-start.25) | collective-permute-done | bytes 262176 | tf_op jit(solution)/shard_map/ppermute | solution.py:37
  188.3 0.8 collective-permute-start.26
  189.1 0.5 collective-permute-start.29
  189.6 2.2 %collective-permute-done.29.refs_9_ = bf16[64,2048]{1,0:T(8,128)(2,1)S(1)} collective-permute-done((bf16[64,2048]{1,0:T(8,128)(2,1)S(1)}, bf16[64,2048]{1,0:T(8,128)(2,1)S(1)}, u32[]{:S(2)}, u32[]{:S(2)}) %collective-permute-start.29) | collective-permute-done | bytes 262176 | tf_op jit(solution)/shard_map/ppermute | solution.py:33
  191.8 2.3 %shard_map.83 = (bf16[2,256,2048]{2,1,0:T(8,128)(2,1)}, bf16[2,64,2048]{2,1,0:T(8,128)(2,1)}) custom-call(s32[5]{0:T(128)S(1)} %stack.46.where, bf16[256,1024]{1,0:T(8,128)(2,1)S(1)} %collective-permute-done.20.refs_0_, bf16[256,1024]{1,0:T(8,128)(2,1)S(1)} %collective-permute-done.21.refs_1_, bf16[256,1024]{1,0:T(8,128)(2,1)S(1)} %collective-permute-done.24.refs_2_, ...), custom_call_target="tpu_custom_call" | custom-call | flops 1 | bytes 1 | tf_op jit(solution)/shard_map/pallas_call | solution.py:447
  (32 shorter events, 0.2 us)
Async XLA Ops:
  0.6 21.2 %collective-permute-start = (bf16[1024,256]{1,0:T(8,128)(2,1)}, bf16[1024,256]{1,0:T(8,128)(2,1)S(1)}, u32[]{:S(2)}, u32[]{:S(2)}) collective-permute-start(bf16[1024,256]{1,0:T(8,128)(2,1)} %bitcast.27), channel_id=1, source_target_pairs={{0,8},{2,10},{4,12},{6,14},{8,0},{10,2},{12,4},{14,6},{1,9},{3,11}... | collective-permute-start | bytes 1572872 | tf_op jit(solution)/shard_map/ppermute | solution.py:29
  8.5 1.4 copy-start.4
  9.9 11.9 %copy-start.7 = (bf16[1,1024,256]{2,1,0:T(8,128)(2,1)S(1)}, bf16[1,1024,256]{2,1,0:T(8,128)(2,1)}, u32[]{:S(2)}) copy-start(bf16[1,1024,256]{2,1,0:T(8,128)(2,1)} %param.11) | copy-start | bytes 1572868
  10.7 11.2 %collective-permute-start.1 = (bf16[3,256,256]{2,1,0:T(8,128)(2,1)S(1)}, bf16[3,256,256]{2,1,0:T(8,128)(2,1)S(1)}, u32[]{:S(2)}, u32[]{:S(2)}) collective-permute-start(bf16[3,256,256]{2,1,0:T(8,128)(2,1)S(1)} %get-tuple-element.42), channel_id=1, source_target_pairs={{0,2},{2,4},{4,6},{6,0},{8,10},{10,12},{12,14},{14,8},{1,3},{3,5},... | collective-permute-start | bytes 1179656 | tf_op jit(solution)/shard_map/ppermute | solution.py:25
  12.0 19.1 %collective-permute-start.2 = (bf16[3,256,256]{2,1,0:T(8,128)(2,1)S(1)}, bf16[3,256,256]{2,1,0:T(8,128)(2,1)S(1)}, u32[]{:S(2)}, u32[]{:S(2)}) collective-permute-start(bf16[3,256,256]{2,1,0:T(8,128)(2,1)S(1)} %get-tuple-element.43), channel_id=1, source_target_pairs={{0,4},{2,6},{4,0},{6,2},{8,12},{10,14},{12,8},{14,10},{1,5},{3,7},... | collective-permute-start | bytes 1179656 | tf_op jit(solution)/shard_map/ppermute | solution.py:25
  14.4 16.6 %collective-permute-start.3 = (bf16[3,256,256]{2,1,0:T(8,128)(2,1)S(1)}, bf16[3,256,256]{2,1,0:T(8,128)(2,1)S(1)}, u32[]{:S(2)}, u32[]{:S(2)}) collective-permute-start(bf16[3,256,256]{2,1,0:T(8,128)(2,1)S(1)} %get-tuple-element.44), channel_id=1, source_target_pairs={{0,6},{2,0},{4,2},{6,4},{8,14},{10,8},{12,10},{14,12},{1,7},{3,1},... | collective-permute-start | bytes 1179656 | tf_op jit(solution)/shard_map/ppermute | solution.py:25
  15.6 1.6 copy-start
  17.2 1.0 copy-start.2
  18.2 0.7 copy-start.5
  18.9 0.7 copy-start.6
  31.1 32.4 %collective-permute-start.4 = (bf16[336,2048]{1,0:T(8,128)(2,1)S(1)}, bf16[336,2048]{1,0:T(8,128)(2,1)S(1)}, u32[]{:S(2)}, u32[]{:S(2)}) collective-permute-start(bf16[336,2048]{1,0:T(8,128)(2,1)S(1)} %get-tuple-element.47.refs_0_), channel_id=1, source_target_pairs={{0,2},{2,4},{4,6},{6,0},{8,10},{10,12},{12,14},{14,8},{1,3},{3,5},... | collective-permute-start | bytes 4128776 | tf_op jit(solution)/shard_map/ppermute | solution.py:25
  32.8 30.9 %collective-permute-start.6 = (bf16[336,2048]{1,0:T(8,128)(2,1)S(1)}, bf16[336,2048]{1,0:T(8,128)(2,1)S(1)}, u32[]{:S(2)}, u32[]{:S(2)}) collective-permute-start(bf16[336,2048]{1,0:T(8,128)(2,1)S(1)} %get-tuple-element.47.refs_0_), channel_id=1, source_target_pairs={{0,6},{2,0},{4,2},{6,4},{8,14},{10,8},{12,10},{14,12},{1,7},{3,1},... | collective-permute-start | bytes 4128776 | tf_op jit(solution)/shard_map/ppermute | solution.py:25
  34.6 31.8 %collective-permute-start.9 = (bf16[4,3,256,256]{3,2,1,0:T(8,128)(2,1)S(1)}, bf16[4,3,256,256]{3,2,1,0:T(8,128)(2,1)S(1)}, u32[]{:S(2)}, u32[]{:S(2)}) collective-permute-start(bf16[4,3,256,256]{3,2,1,0:T(8,128)(2,1)S(1)} %pad_maximum_fusion.refs_5_), channel_id=1, source_target_pairs={{0,1},{1,0},{2,3},{3,2},{4,5},{5,4},{6,7},{7,6},{8,9},{9,8},{10,11... | collective-permute-start | bytes 4718600 | tf_op jit(solution)/shard_map/ppermute | solution.py:33
  36.5 51.7 %collective-permute-start.11 = (bf16[4,3,256,256]{3,2,1,0:T(8,128)(2,1)S(1)}, bf16[4,3,256,256]{3,2,1,0:T(8,128)(2,1)S(1)}, u32[]{:S(2)}, u32[]{:S(2)}) collective-permute-start(bf16[4,3,256,256]{3,2,1,0:T(8,128)(2,1)S(1)} %pad_maximum_fusion.refs_5_), channel_id=1, source_target_pairs={{0,8},{2,10},{4,12},{6,14},{8,0},{10,2},{12,4},{14,6},{1,9},{3,11}... | collective-permute-start | bytes 4718600 | tf_op jit(solution)/shard_map/ppermute | solution.py:29
  63.5 16.8 %collective-permute-start.5 = (bf16[176,2048]{1,0:T(8,128)(2,1)S(1)}, bf16[176,2048]{1,0:T(8,128)(2,1)S(1)}, u32[]{:S(2)}, u32[]{:S(2)}) collective-permute-start(bf16[176,2048]{1,0:T(8,128)(2,1)S(1)} %slice.24), channel_id=1, source_target_pairs={{0,2},{2,4},{4,6},{6,0},{8,10},{10,12},{12,14},{14,8},{1,3},{3,5},... | collective-permute-start | bytes 2162696 | tf_op jit(solution)/shard_map/ppermute | solution.py:25
  63.7 14.4 %collective-permute-start.7 = (bf16[160,2048]{1,0:T(8,128)(2,1)S(1)}, bf16[160,2048]{1,0:T(8,128)(2,1)S(1)}, u32[]{:S(2)}, u32[]{:S(2)}) collective-permute-start(bf16[160,2048]{1,0:T(8,128)(2,1)S(1)} %slice.25), channel_id=1, source_target_pairs={{0,6},{2,0},{4,2},{6,4},{8,14},{10,8},{12,10},{14,12},{1,7},{3,1},... | collective-permute-start | bytes 1966088 | tf_op jit(solution)/shard_map/ppermute | solution.py:25
  86.3 24.0 %collective-permute-start.10 = (bf16[2048,256]{1,0:T(8,128)(2,1)S(1)}, bf16[2048,256]{1,0:T(8,128)(2,1)S(1)}, u32[]{:S(2)}, u32[]{:S(2)}) collective-permute-start(bf16[2048,256]{1,0:T(8,128)(2,1)S(1)} %pad_maximum_fusion.1), channel_id=1, source_target_pairs={{0,6},{2,0},{4,2},{6,4},{8,14},{10,8},{12,10},{14,12},{1,7},{3,1},... | collective-permute-start | bytes 3145736 | tf_op jit(solution)/shard_map/ppermute | solution.py:25
  88.1 23.6 %collective-permute-start.8 = (bf16[2048,256]{1,0:T(8,128)(2,1)S(1)}, bf16[2048,256]{1,0:T(8,128)(2,1)S(1)}, u32[]{:S(2)}, u32[]{:S(2)}) collective-permute-start(bf16[2048,256]{1,0:T(8,128)(2,1)S(1)} %pad_maximum_fusion.1), channel_id=1, source_target_pairs={{0,2},{2,4},{4,6},{6,0},{8,10},{10,12},{12,14},{14,8},{1,3},{3,5},... | collective-permute-start | bytes 3145736 | tf_op jit(solution)/shard_map/ppermute | solution.py:25
  88.3 23.8 %collective-permute-start.13 = (bf16[2,3,256,256]{3,2,1,0:T(8,128)(2,1)S(1)}, bf16[2,3,256,256]{3,2,1,0:T(8,128)(2,1)S(1)}, u32[]{:S(2)}, u32[]{:S(2)}) collective-permute-start(bf16[2,3,256,256]{3,2,1,0:T(8,128)(2,1)S(1)} %get-tuple-element.57), channel_id=1, source_target_pairs={{0,1},{1,0},{2,3},{3,2},{4,5},{5,4},{6,7},{7,6},{8,9},{9,8},{10,11... | collective-permute-start | bytes 2359304 | tf_op jit(solution)/shard_map/ppermute | solution.py:33
  110.2 3.0 %collective-permute-start.12 = (bf16[2,3,256,256]{3,2,1,0:T(8,128)(2,1)S(1)}, bf16[2,3,256,256]{3,2,1,0:T(8,128)(2,1)S(1)}, u32[]{:S(2)}, u32[]{:S(2)}) collective-permute-start(bf16[2,3,256,256]{3,2,1,0:T(8,128)(2,1)S(1)} %get-tuple-element.56), channel_id=1, source_target_pairs={{0,1},{1,0},{2,3},{3,2},{4,5},{5,4},{6,7},{7,6},{8,9},{9,8},{10,11... | collective-permute-start | bytes 2359304 | tf_op jit(solution)/shard_map/ppermute | solution.py:33
  110.3 11.8 %collective-permute-start.18 = (bf16[1024,256]{1,0:T(8,128)(2,1)S(1)}, bf16[1024,256]{1,0:T(8,128)(2,1)S(1)}, u32[]{:S(2)}, u32[]{:S(2)}) collective-permute-start(bf16[1024,256]{1,0:T(8,128)(2,1)S(1)} %slice.29), channel_id=1, source_target_pairs={{0,6},{2,0},{4,2},{6,4},{8,14},{10,8},{12,10},{14,12},{1,7},{3,1},... | collective-permute-start | bytes 1572872 | tf_op jit(solution)/shard_map/ppermute | solution.py:25
  111.8 11.1 %collective-permute-start.17 = (bf16[1024,256]{1,0:T(8,128)(2,1)S(1)}, bf16[1024,256]{1,0:T(8,128)(2,1)S(1)}, u32[]{:S(2)}, u32[]{:S(2)}) collective-permute-start(bf16[1024,256]{1,0:T(8,128)(2,1)S(1)} %slice.28), channel_id=1, source_target_pairs={{0,2},{2,4},{4,6},{6,0},{8,10},{10,12},{12,14},{14,8},{1,3},{3,5},... | collective-permute-start | bytes 1572872 | tf_op jit(solution)/shard_map/ppermute | solution.py:25
  123.0 24.8 %copy-start.1 = (bf16[1,2,256,2048]{3,2,1,0:T(8,128)(2,1)S(1)}, bf16[1,2,256,2048]{3,2,1,0:T(8,128)(2,1)}, u32[]{:S(2)}) copy-start(bf16[1,2,256,2048]{3,2,1,0:T(8,128)(2,1)} %param.6) | copy-start | bytes 6291460
  123.1 24.8 %copy-start.3 = (bf16[1,2,64,2048]{3,2,1,0:T(8,128)(2,1)S(1)}, bf16[1,2,64,2048]{3,2,1,0:T(8,128)(2,1)}, u32[]{:S(2)}) copy-start(bf16[1,2,64,2048]{3,2,1,0:T(8,128)(2,1)} %param.7) | copy-start | bytes 1572868
  123.2 24.6 %collective-permute-start.19 = (bf16[8192,256]{1,0:T(8,128)(2,1)S(1)}, bf16[8192,256]{1,0:T(8,128)(2,1)S(1)}, u32[]{:S(2)}, u32[]{:S(2)}) collective-permute-start(bf16[8192,256]{1,0:T(8,128)(2,1)S(1)} %constant_dynamic-update-slice_fusion.refs_4_), channel_id=1, source_target_pairs={{0,1},{1,0},{2,3},{3,2},{4,5},{5,4},{6,7},{7,6},{8,9},{9,8},{10,11... | collective-permute-start | bytes 12582920 | tf_op jit(solution)/shard_map/ppermute | solution.py:33
  127.8 7.9 %collective-permute-start.14 = (bf16[256,512]{1,0:T(8,128)(2,1)S(1)}, bf16[256,512]{1,0:T(8,128)(2,1)S(1)}, u32[]{:S(2)}, u32[]{:S(2)}) collective-permute-start(bf16[256,512]{1,0:T(8,128)(2,1)S(1)} %get-tuple-element.59), channel_id=1, source_target_pairs={{0,6},{2,0},{4,2},{6,4},{8,14},{10,8},{12,10},{14,12},{1,7},{3,1},... | collective-permute-start | bytes 786440 | tf_op jit(solution)/shard_map/ppermute | solution.py:25
  127.8 9.1 %collective-permute-start.15 = (bf16[256,512]{1,0:T(8,128)(2,1)S(1)}, bf16[256,512]{1,0:T(8,128)(2,1)S(1)}, u32[]{:S(2)}, u32[]{:S(2)}) collective-permute-start(bf16[256,512]{1,0:T(8,128)(2,1)S(1)} %get-tuple-element.60), channel_id=1, source_target_pairs={{0,4},{2,6},{4,0},{6,2},{8,12},{10,14},{12,8},{14,10},{1,5},{3,7},... | collective-permute-start | bytes 786440 | tf_op jit(solution)/shard_map/ppermute | solution.py:25
  128.6 14.6 %collective-permute-start.16 = (bf16[256,512]{1,0:T(8,128)(2,1)S(1)}, bf16[256,512]{1,0:T(8,128)(2,1)S(1)}, u32[]{:S(2)}, u32[]{:S(2)}) collective-permute-start(bf16[256,512]{1,0:T(8,128)(2,1)S(1)} %get-tuple-element.61), channel_id=1, source_target_pairs={{0,2},{2,4},{4,6},{6,0},{8,10},{10,12},{12,14},{14,8},{1,3},{3,5},... | collective-permute-start | bytes 786440 | tf_op jit(solution)/shard_map/ppermute | solution.py:25
  143.2 30.0 %collective-permute-start.27 = (bf16[256,2048]{1,0:T(8,128)(2,1)S(1)}, bf16[256,2048]{1,0:T(8,128)(2,1)S(1)}, u32[]{:S(2)}, u32[]{:S(2)}) collective-permute-start(bf16[256,2048]{1,0:T(8,128)(2,1)S(1)} %get-tuple-element.76), channel_id=1, source_target_pairs={{128,144},{144,160},{160,176},{176,192},{192,208},{208,224},{224,2... | collective-permute-start | bytes 3145736 | tf_op jit(solution)/shard_map/ppermute | solution.py:37
  144.5 8.6 %collective-permute-start.22 = (bf16[64,2048]{1,0:T(8,128)(2,1)S(1)}, bf16[64,2048]{1,0:T(8,128)(2,1)S(1)}, u32[]{:S(2)}, u32[]{:S(2)}) collective-permute-start(bf16[64,2048]{1,0:T(8,128)(2,1)S(1)} %get-tuple-element.71), channel_id=1, source_target_pairs={{0,16},{16,32},{32,48},{48,64},{64,80},{80,96},{96,112},{112,128},... | collective-permute-start | bytes 786440 | tf_op jit(solution)/shard_map/ppermute | solution.py:37
  150.0 23.2 %collective-permute-start.20 = (bf16[256,1024]{1,0:T(8,128)(2,1)S(1)}, bf16[256,1024]{1,0:T(8,128)(2,1)S(1)}, u32[]{:S(2)}, u32[]{:S(2)}) collective-permute-start(bf16[256,1024]{1,0:T(8,128)(2,1)S(1)} %get-tuple-element.67), channel_id=1, source_target_pairs={{0,16},{16,32},{32,48},{48,64},{64,80},{80,96},{96,112},{112,128},... | collective-permute-start | bytes 1572872 | tf_op jit(solution)/shard_map/ppermute | solution.py:37
  153.1 3.7 %collective-permute-start.23 = (bf16[64,2048]{1,0:T(8,128)(2,1)S(1)}, bf16[64,2048]{1,0:T(8,128)(2,1)S(1)}, u32[]{:S(2)}, u32[]{:S(2)}) collective-permute-start(bf16[64,2048]{1,0:T(8,128)(2,1)S(1)} %collective-permute-done.22.refs_6_), channel_id=1, source_target_pairs={{0,1},{1,0},{2,3},{3,2},{4,5},{5,4},{6,7},{7,6},{8,9},{9,8},{10,11... | collective-permute-start | bytes 786440 | tf_op jit(solution)/shard_map/ppermute | solution.py:33
  156.8 31.5 %collective-permute-start.24 = (bf16[256,1024]{1,0:T(8,128)(2,1)S(1)}, bf16[256,1024]{1,0:T(8,128)(2,1)S(1)}, u32[]{:S(2)}, u32[]{:S(2)}) collective-permute-start(bf16[256,1024]{1,0:T(8,128)(2,1)S(1)} %get-tuple-element.72), channel_id=1, source_target_pairs={{0,16},{16,32},{32,48},{48,64},{64,80},{80,96},{96,112},{112,128},... | collective-permute-start | bytes 1572872 | tf_op jit(solution)/shard_map/ppermute | solution.py:37
  173.3 18.5 %collective-permute-start.28 = (bf16[256,2048]{1,0:T(8,128)(2,1)S(1)}, bf16[256,2048]{1,0:T(8,128)(2,1)S(1)}, u32[]{:S(2)}, u32[]{:S(2)}) collective-permute-start(bf16[256,2048]{1,0:T(8,128)(2,1)S(1)} %collective-permute-done.27.refs_4_), channel_id=1, source_target_pairs={{0,1},{1,0},{2,3},{3,2},{4,5},{5,4},{6,7},{7,6},{8,9},{9,8},{10,11... | collective-permute-start | bytes 3145736 | tf_op jit(solution)/shard_map/ppermute | solution.py:33
  174.6 13.7 %collective-permute-start.25 = (bf16[64,2048]{1,0:T(8,128)(2,1)S(1)}, bf16[64,2048]{1,0:T(8,128)(2,1)S(1)}, u32[]{:S(2)}, u32[]{:S(2)}) collective-permute-start(bf16[64,2048]{1,0:T(8,128)(2,1)S(1)} %get-tuple-element.73), channel_id=1, source_target_pairs={{128,144},{144,160},{160,176},{176,192},{192,208},{208,224},{224,2... | collective-permute-start | bytes 786440 | tf_op jit(solution)/shard_map/ppermute | solution.py:37
  188.3 3.5 %collective-permute-start.26 = (bf16[256,1024]{1,0:T(8,128)(2,1)S(1)}, bf16[256,1024]{1,0:T(8,128)(2,1)S(1)}, u32[]{:S(2)}, u32[]{:S(2)}) collective-permute-start(bf16[256,1024]{1,0:T(8,128)(2,1)S(1)} %collective-permute-done.24.refs_2_), channel_id=1, source_target_pairs={{0,1},{1,0},{2,3},{3,2},{4,5},{5,4},{6,7},{7,6},{8,9},{9,8},{10,11... | collective-permute-start | bytes 1572872 | tf_op jit(solution)/shard_map/ppermute | solution.py:33
  189.1 2.7 %collective-permute-start.21 = (bf16[256,1024]{1,0:T(8,128)(2,1)S(1)}, bf16[256,1024]{1,0:T(8,128)(2,1)S(1)}, u32[]{:S(2)}, u32[]{:S(2)}) collective-permute-start(bf16[256,1024]{1,0:T(8,128)(2,1)S(1)} %collective-permute-done.20.refs_0_), channel_id=1, source_target_pairs={{0,1},{1,0},{2,3},{3,2},{4,5},{5,4},{6,7},{7,6},{8,9},{9,8},{10,11... | collective-permute-start | bytes 1572872 | tf_op jit(solution)/shard_map/ppermute | solution.py:33
  189.1 2.7 %collective-permute-start.29 = (bf16[64,2048]{1,0:T(8,128)(2,1)S(1)}, bf16[64,2048]{1,0:T(8,128)(2,1)S(1)}, u32[]{:S(2)}, u32[]{:S(2)}) collective-permute-start(bf16[64,2048]{1,0:T(8,128)(2,1)S(1)} %collective-permute-done.25.refs_8_), channel_id=1, source_target_pairs={{0,1},{1,0},{2,3},{3,2},{4,5},{5,4},{6,7},{7,6},{8,9},{9,8},{10,11... | collective-permute-start | bytes 786440 | tf_op jit(solution)/shard_map/ppermute | solution.py:33

commit v6 on v5

--- a/solution.py
+++ b/solution.py
@@ -500,10 +500,10 @@
     weights = round_ring(after(out_pair, *rows), out_shard.shape[0], started[0])
     far_other = [other_core(after(far[i : i + 2], started[0])) for i in (0, 2)]
 
+    ctx_early = relay(after(ctx, *far_other), decoders, count)
     mixed = attend(after(where, weights[1], weights[4]), mem, started, (far, *far_other))
     weights = both(jnp.concatenate(after(weights, mixed[0])))
     mixed = [mixed[0]] + [around_x(mixed[step], -step) for step in range(1, RING)]
-    ctx_early = relay(after(ctx, *mixed), decoders, count)
     qry_early = relay(after(qry, *mixed), encoders, count)
 
     first, few_first = project(0, where, context, queries, mixed, weights)
@@ -516,7 +516,7 @@
         where,
         both(first),
         (second, other_core(after(second, few_new))),
-        (ctx_early, other_core(after(ctx_early, first))),
+        (ctx_early, other_core(after(ctx_early, few_new))),
         qry_early,
         both(few_new),
     )

time: 195 us -> 202 us (1.036)
  the two profiles are of different devices: /device:TPU:1 before, /device:TPU:17 now
where the time goes in v6:
time: 202 us; the launch traced here: 201 us
  waiting for transfers between devices  101 us (50%)
  starting transfers between devices  69.8 us (35%)
  Pallas kernels  23.7 us (12%)
  local copies, waits for them, and re-layouts  6.06 us (3%)
    ppermute x14, waiting for transfers between devices, around_x(): return lax.ppermute(array, 'dp', pairs)  61 us
    ppermute x5, waiting for transfers between devices, relay(): lax.ppermute(array, 'section', [(s, (s + 1) % count) for s in sections])  36.5 us
    ppermute x9, starting transfers between devices, other_core(): return lax.ppermute(array, 'tensor', [(0, 1), (1, 0)])  28.7 us
    ppermute x14, starting transfers between devices, around_x(): return lax.ppermute(array, 'dp', pairs)  20.1 us
    ppermute x2, starting transfers between devices, across_z(): lax.ppermute(array, 'dp', [(d, (d + RING) % (2 * RING)) for d in range(2...  11.8 us
    pallas_call x1, Pallas kernels, attend(): call(attend_kernel, (out,) * RING, [SMEM] + [VMEM] * 7, (VMEM,) * RING, [...  9.23 us
    ppermute x5, starting transfers between devices, relay(): lax.ppermute(array, 'section', [(s, (s + 1) % count) for s in sections])  9.12 us
    unnamed x20, local copies, waits for them, and re-layouts  5.62 us
  transfers between devices with their start and end apart: 30, of which 13 were waited for; matrix products, arithmetic and copies ran while one was open for 0% of the time, Pallas kernels for 11%

profile of v6, /device:TPU:17, one launch (start us, length us, event | category | flops | bytes accessed | tf_op | source)
XLA Modules:
  0.0 201.4 jit_solution(9624257459641357772)
XLA Ops:
  0.6 7.0 %collective-permute-start = (bf16[1024,256]{1,0:T(8,128)(2,1)}, bf16[1024,256]{1,0:T(8,128)(2,1)S(1)}, u32[]{:S(2)}, u32[]{:S(2)}) collective-permute-start(bf16[1024,256]{1,0:T(8,128)(2,1)} %bitcast.27), channel_id=1, source_target_pairs={{0,8},{2,10},{4,12},{6,14},{8,0},{10,2},{12,4},{14,6},{1,9},{3,11}... | collective-permute-start | bytes 1572872 | tf_op jit(solution)/shard_map/ppermute | solution.py:29
  7.6 0.1 stack.46.where
  7.7 1.4 copy-done.4
  9.1 0.8 shard_map.77
  9.9 1.3 collective-permute-start.1
  11.2 2.5 %collective-permute-start.2 = (bf16[3,256,256]{2,1,0:T(8,128)(2,1)S(1)}, bf16[3,256,256]{2,1,0:T(8,128)(2,1)S(1)}, u32[]{:S(2)}, u32[]{:S(2)}) collective-permute-start(bf16[3,256,256]{2,1,0:T(8,128)(2,1)S(1)} %get-tuple-element.43), channel_id=1, source_target_pairs={{0,4},{2,6},{4,0},{6,2},{8,12},{10,14},{12,8},{14,10},{1,5},{3,7},... | collective-permute-start | bytes 1179656 | tf_op jit(solution)/shard_map/ppermute | solution.py:25
  13.6 1.2 collective-permute-start.3
  14.8 1.6 copy-done
  16.4 1.0 copy-done.2
  17.4 0.7 copy-done.5
  18.1 0.7 copy-done.6
  18.8 2.0 shard_map.78
  20.8 0.8 collective-permute-done
  21.6 0.1 pad_maximum_fusion.1
  21.7 8.6 %collective-permute-done.2 = bf16[3,256,256]{2,1,0:T(8,128)(2,1)S(1)} collective-permute-done((bf16[3,256,256]{2,1,0:T(8,128)(2,1)S(1)}, bf16[3,256,256]{2,1,0:T(8,128)(2,1)S(1)}, u32[]{:S(2)}, u32[]{:S(2)}) %collective-permute-start.2) | collective-permute-done | bytes 393248 | tf_op jit(solution)/shard_map/ppermute | solution.py:25
  30.2 1.7 collective-permute-start.4
  31.9 1.7 collective-permute-start.6
  33.6 0.2 pad_maximum_fusion.refs_5_
  33.8 1.8 collective-permute-start.9
  35.6 4.8 %collective-permute-start.11 = (bf16[4,3,256,256]{3,2,1,0:T(8,128)(2,1)S(1)}, bf16[4,3,256,256]{3,2,1,0:T(8,128)(2,1)S(1)}, u32[]{:S(2)}, u32[]{:S(2)}) collective-permute-start(bf16[4,3,256,256]{3,2,1,0:T(8,128)(2,1)S(1)} %pad_maximum_fusion.refs_5_), channel_id=1, source_target_pairs={{0,8},{2,10},{4,12},{6,14},{8,0},{10,2},{12,4},{14,6},{1,9},{3,11}... | collective-permute-start | bytes 4718600 | tf_op jit(solution)/shard_map/ppermute | solution.py:29
  40.4 22.2 %collective-permute-done.4.refs_1_ = bf16[336,2048]{1,0:T(8,128)(2,1)S(1)} collective-permute-done((bf16[336,2048]{1,0:T(8,128)(2,1)S(1)}, bf16[336,2048]{1,0:T(8,128)(2,1)S(1)}, u32[]{:S(2)}, u32[]{:S(2)}) %collective-permute-start.4) | collective-permute-done | bytes 1376288 | tf_op jit(solution)/shard_map/ppermute | solution.py:25
  62.6 0.1 slice.24
  62.7 0.1 collective-permute-start.5
  62.8 0.1 slice.25
  62.9 2.7 %collective-permute-start.7 = (bf16[160,2048]{1,0:T(8,128)(2,1)S(1)}, bf16[160,2048]{1,0:T(8,128)(2,1)S(1)}, u32[]{:S(2)}, u32[]{:S(2)}) collective-permute-start(bf16[160,2048]{1,0:T(8,128)(2,1)S(1)} %slice.25), channel_id=1, source_target_pairs={{0,6},{2,0},{4,2},{6,4},{8,14},{10,8},{12,10},{14,12},{1,7},{3,1},... | collective-permute-start | bytes 1966088 | tf_op jit(solution)/shard_map/ppermute | solution.py:25
  65.6 11.6 %collective-permute-done.7.refs_3_ = bf16[160,2048]{1,0:T(8,128)(2,1)S(1)} collective-permute-done((bf16[160,2048]{1,0:T(8,128)(2,1)S(1)}, bf16[160,2048]{1,0:T(8,128)(2,1)S(1)}, u32[]{:S(2)}, u32[]{:S(2)}) %collective-permute-start.7) | collective-permute-done | bytes 655392 | tf_op jit(solution)/shard_map/ppermute | solution.py:25
  77.2 2.3 %collective-permute-done.5.refs_2_ = bf16[176,2048]{1,0:T(8,128)(2,1)S(1)} collective-permute-done((bf16[176,2048]{1,0:T(8,128)(2,1)S(1)}, bf16[176,2048]{1,0:T(8,128)(2,1)S(1)}, u32[]{:S(2)}, u32[]{:S(2)}) %collective-permute-start.5) | collective-permute-done | bytes 720928 | tf_op jit(solution)/shard_map/ppermute | solution.py:25
  79.5 5.2 %shard_map.79 = (f32[3,1024,512]{2,1,0:T(8,128)S(1)}, bf16[1024,1024]{1,0:T(8,128)(2,1)S(1)}, bf16[256,1024]{1,0:T(8,128)(2,1)S(1)}, bf16[4,16,128]{2,1,0:T(8,128)(2,1)S(1)}) custom-call(s32[5]{0:T(128)S(1)} %stack.46.where, bf16[336,2048]{1,0:T(8,128)(2,1)S(1)} %get-tuple-element.47.refs_0_, bf16[336,2048]{1,0:T(8,128)(2,1)S(1)} %collective-permute-done.4.refs_1_, ...), custom_call_target="tpu_custom_call" | custom-call | flops 1 | bytes 1 | tf_op jit(solution)/shard_map/pallas_call | solution.py:280
  84.7 2.7 %collective-permute-start.10 = (bf16[2048,256]{1,0:T(8,128)(2,1)S(1)}, bf16[2048,256]{1,0:T(8,128)(2,1)S(1)}, u32[]{:S(2)}, u32[]{:S(2)}) collective-permute-start(bf16[2048,256]{1,0:T(8,128)(2,1)S(1)} %pad_maximum_fusion.1), channel_id=1, source_target_pairs={{0,6},{2,0},{4,2},{6,4},{8,14},{10,8},{12,10},{14,12},{1,7},{3,1},... | collective-permute-start | bytes 3145736 | tf_op jit(solution)/shard_map/ppermute | solution.py:25
  87.4 0.1 fusion
  87.5 21.9 %collective-permute-start.12 = (bf16[2,3,256,256]{3,2,1,0:T(8,128)(2,1)S(1)}, bf16[2,3,256,256]{3,2,1,0:T(8,128)(2,1)S(1)}, u32[]{:S(2)}, u32[]{:S(2)}) collective-permute-start(bf16[2,3,256,256]{3,2,1,0:T(8,128)(2,1)S(1)} %get-tuple-element.56), channel_id=1, source_target_pairs={{0,1},{1,0},{2,3},{3,2},{4,5},{5,4},{6,7},{7,6},{8,9},{9,8},{10,11... | collective-permute-start | bytes 2359304 | tf_op jit(solution)/shard_map/ppermute | solution.py:33
  109.4 0.1 collective-permute-start.13
  109.5 0.1 collective-permute-start.17
  109.6 2.7 %collective-permute-start.18 = (bf16[1024,256]{1,0:T(8,128)(2,1)S(1)}, bf16[1024,256]{1,0:T(8,128)(2,1)S(1)}, u32[]{:S(2)}, u32[]{:S(2)}) collective-permute-start(bf16[1024,256]{1,0:T(8,128)(2,1)S(1)} %slice.29), channel_id=1, source_target_pairs={{0,6},{2,0},{4,2},{6,4},{8,14},{10,8},{12,10},{14,12},{1,7},{3,1},... | collective-permute-start | bytes 1572872 | tf_op jit(solution)/shard_map/ppermute | solution.py:25
  112.4 0.0 collective-permute-done.13.refs_2_
  112.4 9.2 %shard_map.80 = (bf16[256,512]{1,0:T(8,128)(2,1)S(1)}, bf16[256,512]{1,0:T(8,128)(2,1)S(1)}, bf16[256,512]{1,0:T(8,128)(2,1)S(1)}, bf16[256,512]{1,0:T(8,128)(2,1)S(1)}) custom-call(s32[5]{0:T(128)S(1)} %stack.46.where, f32[3,1024,512]{2,1,0:T(8,128)S(1)} %get-tuple-element.49.total, bf16[1024,1024]{1,0:T(8,128)(2,1)S(1)} %get-tuple-element.52.rows, ...), custom_call_target="tpu_custom_call" | custom-call | flops 1 | bytes 1 | tf_op jit(solution)/shard_map/pallas_call | solution.py:304
  121.6 2.3 %collective-permute-done.17 = bf16[1024,256]{1,0:T(8,128)(2,1)S(1)} collective-permute-done((bf16[1024,256]{1,0:T(8,128)(2,1)S(1)}, bf16[1024,256]{1,0:T(8,128)(2,1)S(1)}, u32[]{:S(2)}, u32[]{:S(2)}) %collective-permute-start.17) | collective-permute-done | bytes 524320 | tf_op jit(solution)/shard_map/ppermute | solution.py:25
  123.9 0.1 constant_dynamic-update-slice_fusion.4
  124.0 0.1 constant_dynamic-update-slice_fusion.3
  124.0 0.0 copy-start.1
  124.1 0.0 copy-start.3
  124.2 0.1 constant_dynamic-update-slice_fusion.refs_4_
  124.2 1.3 collective-permute-start.19
  125.6 4.0 %collective-permute-start.27 = (bf16[256,2048]{1,0:T(8,128)(2,1)S(1)}, bf16[256,2048]{1,0:T(8,128)(2,1)S(1)}, u32[]{:S(2)}, u32[]{:S(2)}) collective-permute-start(bf16[256,2048]{1,0:T(8,128)(2,1)S(1)} %get-tuple-element.76), channel_id=1, source_target_pairs={{128,144},{144,160},{160,176},{176,192},{192,208},{208,224},{224,2... | collective-permute-start | bytes 3145736 | tf_op jit(solution)/shard_map/ppermute | solution.py:37
  129.5 2.9 %collective-permute-start.14 = (bf16[256,512]{1,0:T(8,128)(2,1)S(1)}, bf16[256,512]{1,0:T(8,128)(2,1)S(1)}, u32[]{:S(2)}, u32[]{:S(2)}) collective-permute-start(bf16[256,512]{1,0:T(8,128)(2,1)S(1)} %get-tuple-element.59), channel_id=1, source_target_pairs={{0,6},{2,0},{4,2},{6,4},{8,14},{10,8},{12,10},{14,12},{1,7},{3,1},... | collective-permute-start | bytes 786440 | tf_op jit(solution)/shard_map/ppermute | solution.py:25
  132.4 0.7 collective-permute-start.16
  133.1 10.0 %collective-permute-done.14.refs_1_ = bf16[256,512]{1,0:T(8,128)(2,1)S(1)} collective-permute-done((bf16[256,512]{1,0:T(8,128)(2,1)S(1)}, bf16[256,512]{1,0:T(8,128)(2,1)S(1)}, u32[]{:S(2)}, u32[]{:S(2)}) %collective-permute-start.14) | collective-permute-done | bytes 262176 | tf_op jit(solution)/shard_map/ppermute | solution.py:25
  143.1 4.0 %collective-permute-done.16.refs_3_ = bf16[256,512]{1,0:T(8,128)(2,1)S(1)} collective-permute-done((bf16[256,512]{1,0:T(8,128)(2,1)S(1)}, bf16[256,512]{1,0:T(8,128)(2,1)S(1)}, u32[]{:S(2)}, u32[]{:S(2)}) %collective-permute-start.16) | collective-permute-done | bytes 262176 | tf_op jit(solution)/shard_map/ppermute | solution.py:25
  147.1 1.3 collective-permute-start.22
  148.4 10.3 %collective-permute-done.22.refs_6_ = bf16[64,2048]{1,0:T(8,128)(2,1)S(1)} collective-permute-done((bf16[64,2048]{1,0:T(8,128)(2,1)S(1)}, bf16[64,2048]{1,0:T(8,128)(2,1)S(1)}, u32[]{:S(2)}, u32[]{:S(2)}) %collective-permute-start.22) | collective-permute-done | bytes 262176 | tf_op jit(solution)/shard_map/ppermute | solution.py:37
  158.7 1.7 collective-permute-start.23
  160.5 2.2 %shard_map.81 = (bf16[256,1024]{1,0:T(8,128)(2,1)S(1)}, bf16[64,1024]{1,0:T(8,128)(2,1)S(1)}) custom-call(s32[5]{0:T(128)S(1)} %stack.46.where, bf16[2,256,2048]{2,1,0:T(8,128)(2,1)S(1)} %bitcast.19, bf16[2,64,2048]{2,1,0:T(8,128)(2,1)S(1)} %bitcast.22, bf16[256,512]{1,0:T(8,128)(2,1)S(1)} %get-tuple-element.58.refs_0_, ...), custom_call_target="tpu_custom_call" | custom-call | flops 1 | bytes 1 | tf_op jit(solution)/shard_map/pallas_call | solution.py:388
  162.6 2.2 %shard_map.82 = (bf16[256,1024]{1,0:T(8,128)(2,1)S(1)}, bf16[64,2048]{1,0:T(8,128)(2,1)S(1)}) custom-call(s32[5]{0:T(128)S(1)} %stack.46.where, bf16[2,256,2048]{2,1,0:T(8,128)(2,1)S(1)} %bitcast.20, bf16[2,64,2048]{2,1,0:T(8,128)(2,1)S(1)} %bitcast.23, bf16[256,512]{1,0:T(8,128)(2,1)S(1)} %get-tuple-element.58.refs_0_, ...), custom_call_target="tpu_custom_call" | custom-call | flops 1 | bytes 1 | tf_op jit(solution)/shard_map/pallas_call | solution.py:388
  164.8 1.3 collective-permute-start.25
  166.1 1.3 collective-permute-start.24
  167.4 1.3 collective-permute-start.20
  168.7 3.3 %collective-permute-done.25.refs_8_ = bf16[64,2048]{1,0:T(8,128)(2,1)S(1)} collective-permute-done((bf16[64,2048]{1,0:T(8,128)(2,1)S(1)}, bf16[64,2048]{1,0:T(8,128)(2,1)S(1)}, u32[]{:S(2)}, u32[]{:S(2)}) %collective-permute-start.25) | collective-permute-done | bytes 262176 | tf_op jit(solution)/shard_map/ppermute | solution.py:37
  172.0 0.6 collective-permute-start.28
  172.6 11.7 %collective-permute-done.24.refs_2_ = bf16[256,1024]{1,0:T(8,128)(2,1)S(1)} collective-permute-done((bf16[256,1024]{1,0:T(8,128)(2,1)S(1)}, bf16[256,1024]{1,0:T(8,128)(2,1)S(1)}, u32[]{:S(2)}, u32[]{:S(2)}) %collective-permute-start.24) | collective-permute-done | bytes 524320 | tf_op jit(solution)/shard_map/ppermute | solution.py:37
  184.2 11.2 %collective-permute-done.20.refs_0_ = bf16[256,1024]{1,0:T(8,128)(2,1)S(1)} collective-permute-done((bf16[256,1024]{1,0:T(8,128)(2,1)S(1)}, bf16[256,1024]{1,0:T(8,128)(2,1)S(1)}, u32[]{:S(2)}, u32[]{:S(2)}) %collective-permute-start.20) | collective-permute-done | bytes 524320 | tf_op jit(solution)/shard_map/ppermute | solution.py:37
  195.5 0.8 collective-permute-start.21
  196.3 0.5 collective-permute-start.29
  196.8 2.2 %collective-permute-done.29.refs_9_ = bf16[64,2048]{1,0:T(8,128)(2,1)S(1)} collective-permute-done((bf16[64,2048]{1,0:T(8,128)(2,1)S(1)}, bf16[64,2048]{1,0:T(8,128)(2,1)S(1)}, u32[]{:S(2)}, u32[]{:S(2)}) %collective-permute-start.29) | collective-permute-done | bytes 262176 | tf_op jit(solution)/shard_map/ppermute | solution.py:33
  198.9 2.3 %shard_map.83 = (bf16[2,256,2048]{2,1,0:T(8,128)(2,1)}, bf16[2,64,2048]{2,1,0:T(8,128)(2,1)}) custom-call(s32[5]{0:T(128)S(1)} %stack.46.where, bf16[256,1024]{1,0:T(8,128)(2,1)S(1)} %collective-permute-done.20.refs_0_, bf16[256,1024]{1,0:T(8,128)(2,1)S(1)} %collective-permute-done.21.refs_1_, bf16[256,1024]{1,0:T(8,128)(2,1)S(1)} %collective-permute-done.24.refs_2_, ...), custom_call_target="tpu_custom_call" | custom-call | flops 1 | bytes 1 | tf_op jit(solution)/shard_map/pallas_call | solution.py:447
  (32 shorter events, 0.2 us)
Async XLA Ops:
  0.6 21.0 %collective-permute-start = (bf16[1024,256]{1,0:T(8,128)(2,1)}, bf16[1024,256]{1,0:T(8,128)(2,1)S(1)}, u32[]{:S(2)}, u32[]{:S(2)}) collective-permute-start(bf16[1024,256]{1,0:T(8,128)(2,1)} %bitcast.27), channel_id=1, source_target_pairs={{0,8},{2,10},{4,12},{6,14},{8,0},{10,2},{12,4},{14,6},{1,9},{3,11}... | collective-permute-start | bytes 1572872 | tf_op jit(solution)/shard_map/ppermute | solution.py:29
  7.7 1.4 copy-start.4
  9.1 12.5 %copy-start.7 = (bf16[1,1024,256]{2,1,0:T(8,128)(2,1)S(1)}, bf16[1,1024,256]{2,1,0:T(8,128)(2,1)}, u32[]{:S(2)}) copy-start(bf16[1,1024,256]{2,1,0:T(8,128)(2,1)} %param.11) | copy-start | bytes 1572868
  9.9 11.8 %collective-permute-start.1 = (bf16[3,256,256]{2,1,0:T(8,128)(2,1)S(1)}, bf16[3,256,256]{2,1,0:T(8,128)(2,1)S(1)}, u32[]{:S(2)}, u32[]{:S(2)}) collective-permute-start(bf16[3,256,256]{2,1,0:T(8,128)(2,1)S(1)} %get-tuple-element.42), channel_id=1, source_target_pairs={{0,2},{2,4},{4,6},{6,0},{8,10},{10,12},{12,14},{14,8},{1,3},{3,5},... | collective-permute-start | bytes 1179656 | tf_op jit(solution)/shard_map/ppermute | solution.py:25
  11.2 19.1 %collective-permute-start.2 = (bf16[3,256,256]{2,1,0:T(8,128)(2,1)S(1)}, bf16[3,256,256]{2,1,0:T(8,128)(2,1)S(1)}, u32[]{:S(2)}, u32[]{:S(2)}) collective-permute-start(bf16[3,256,256]{2,1,0:T(8,128)(2,1)S(1)} %get-tuple-element.43), channel_id=1, source_target_pairs={{0,4},{2,6},{4,0},{6,2},{8,12},{10,14},{12,8},{14,10},{1,5},{3,7},... | collective-permute-start | bytes 1179656 | tf_op jit(solution)/shard_map/ppermute | solution.py:25
  13.6 16.6 %collective-permute-start.3 = (bf16[3,256,256]{2,1,0:T(8,128)(2,1)S(1)}, bf16[3,256,256]{2,1,0:T(8,128)(2,1)S(1)}, u32[]{:S(2)}, u32[]{:S(2)}) collective-permute-start(bf16[3,256,256]{2,1,0:T(8,128)(2,1)S(1)} %get-tuple-element.44), channel_id=1, source_target_pairs={{0,6},{2,0},{4,2},{6,4},{8,14},{10,8},{12,10},{14,12},{1,7},{3,1},... | collective-permute-start | bytes 1179656 | tf_op jit(solution)/shard_map/ppermute | solution.py:25
  14.8 1.6 copy-start
  16.4 1.0 copy-start.2
  17.4 0.7 copy-start.5
  18.1 0.7 copy-start.6
  30.2 32.4 %collective-permute-start.4 = (bf16[336,2048]{1,0:T(8,128)(2,1)S(1)}, bf16[336,2048]{1,0:T(8,128)(2,1)S(1)}, u32[]{:S(2)}, u32[]{:S(2)}) collective-permute-start(bf16[336,2048]{1,0:T(8,128)(2,1)S(1)} %get-tuple-element.47.refs_0_), channel_id=1, source_target_pairs={{0,2},{2,4},{4,6},{6,0},{8,10},{10,12},{12,14},{14,8},{1,3},{3,5},... | collective-permute-start | bytes 4128776 | tf_op jit(solution)/shard_map/ppermute | solution.py:25
  31.9 30.9 %collective-permute-start.6 = (bf16[336,2048]{1,0:T(8,128)(2,1)S(1)}, bf16[336,2048]{1,0:T(8,128)(2,1)S(1)}, u32[]{:S(2)}, u32[]{:S(2)}) collective-permute-start(bf16[336,2048]{1,0:T(8,128)(2,1)S(1)} %get-tuple-element.47.refs_0_), channel_id=1, source_target_pairs={{0,6},{2,0},{4,2},{6,4},{8,14},{10,8},{12,10},{14,12},{1,7},{3,1},... | collective-permute-start | bytes 4128776 | tf_op jit(solution)/shard_map/ppermute | solution.py:25
  33.8 45.7 %collective-permute-start.9 = (bf16[4,3,256,256]{3,2,1,0:T(8,128)(2,1)S(1)}, bf16[4,3,256,256]{3,2,1,0:T(8,128)(2,1)S(1)}, u32[]{:S(2)}, u32[]{:S(2)}) collective-permute-start(bf16[4,3,256,256]{3,2,1,0:T(8,128)(2,1)S(1)} %pad_maximum_fusion.refs_5_), channel_id=1, source_target_pairs={{0,1},{1,0},{2,3},{3,2},{4,5},{5,4},{6,7},{7,6},{8,9},{9,8},{10,11... | collective-permute-start | bytes 4718600 | tf_op jit(solution)/shard_map/ppermute | solution.py:33
  35.6 51.8 %collective-permute-start.11 = (bf16[4,3,256,256]{3,2,1,0:T(8,128)(2,1)S(1)}, bf16[4,3,256,256]{3,2,1,0:T(8,128)(2,1)S(1)}, u32[]{:S(2)}, u32[]{:S(2)}) collective-permute-start(bf16[4,3,256,256]{3,2,1,0:T(8,128)(2,1)S(1)} %pad_maximum_fusion.refs_5_), channel_id=1, source_target_pairs={{0,8},{2,10},{4,12},{6,14},{8,0},{10,2},{12,4},{14,6},{1,9},{3,11}... | collective-permute-start | bytes 4718600 | tf_op jit(solution)/shard_map/ppermute | solution.py:29
  62.7 16.8 %collective-permute-start.5 = (bf16[176,2048]{1,0:T(8,128)(2,1)S(1)}, bf16[176,2048]{1,0:T(8,128)(2,1)S(1)}, u32[]{:S(2)}, u32[]{:S(2)}) collective-permute-start(bf16[176,2048]{1,0:T(8,128)(2,1)S(1)} %slice.24), channel_id=1, source_target_pairs={{0,2},{2,4},{4,6},{6,0},{8,10},{10,12},{12,14},{14,8},{1,3},{3,5},... | collective-permute-start | bytes 2162696 | tf_op jit(solution)/shard_map/ppermute | solution.py:25
  62.9 14.4 %collective-permute-start.7 = (bf16[160,2048]{1,0:T(8,128)(2,1)S(1)}, bf16[160,2048]{1,0:T(8,128)(2,1)S(1)}, u32[]{:S(2)}, u32[]{:S(2)}) collective-permute-start(bf16[160,2048]{1,0:T(8,128)(2,1)S(1)} %slice.25), channel_id=1, source_target_pairs={{0,6},{2,0},{4,2},{6,4},{8,14},{10,8},{12,10},{14,12},{1,7},{3,1},... | collective-permute-start | bytes 1966088 | tf_op jit(solution)/shard_map/ppermute | solution.py:25
  79.5 30.0 %collective-permute-start.8 = (bf16[2048,256]{1,0:T(8,128)(2,1)S(1)}, bf16[2048,256]{1,0:T(8,128)(2,1)S(1)}, u32[]{:S(2)}, u32[]{:S(2)}) collective-permute-start(bf16[2048,256]{1,0:T(8,128)(2,1)S(1)} %pad_maximum_fusion.1), channel_id=1, source_target_pairs={{0,2},{2,4},{4,6},{6,0},{8,10},{10,12},{12,14},{14,8},{1,3},{3,5},... | collective-permute-start | bytes 3145736 | tf_op jit(solution)/shard_map/ppermute | solution.py:25
  84.7 24.9 %collective-permute-start.10 = (bf16[2048,256]{1,0:T(8,128)(2,1)S(1)}, bf16[2048,256]{1,0:T(8,128)(2,1)S(1)}, u32[]{:S(2)}, u32[]{:S(2)}) collective-permute-start(bf16[2048,256]{1,0:T(8,128)(2,1)S(1)} %pad_maximum_fusion.1), channel_id=1, source_target_pairs={{0,6},{2,0},{4,2},{6,4},{8,14},{10,8},{12,10},{14,12},{1,7},{3,1},... | collective-permute-start | bytes 3145736 | tf_op jit(solution)/shard_map/ppermute | solution.py:25
  87.5 24.9 %collective-permute-start.12 = (bf16[2,3,256,256]{3,2,1,0:T(8,128)(2,1)S(1)}, bf16[2,3,256,256]{3,2,1,0:T(8,128)(2,1)S(1)}, u32[]{:S(2)}, u32[]{:S(2)}) collective-permute-start(bf16[2,3,256,256]{3,2,1,0:T(8,128)(2,1)S(1)} %get-tuple-element.56), channel_id=1, source_target_pairs={{0,1},{1,0},{2,3},{3,2},{4,5},{5,4},{6,7},{7,6},{8,9},{9,8},{10,11... | collective-permute-start | bytes 2359304 | tf_op jit(solution)/shard_map/ppermute | solution.py:33
  109.4 3.0 %collective-permute-start.13 = (bf16[2,3,256,256]{3,2,1,0:T(8,128)(2,1)S(1)}, bf16[2,3,256,256]{3,2,1,0:T(8,128)(2,1)S(1)}, u32[]{:S(2)}, u32[]{:S(2)}) collective-permute-start(bf16[2,3,256,256]{3,2,1,0:T(8,128)(2,1)S(1)} %get-tuple-element.57), channel_id=1, source_target_pairs={{0,1},{1,0},{2,3},{3,2},{4,5},{5,4},{6,7},{7,6},{8,9},{9,8},{10,11... | collective-permute-start | bytes 2359304 | tf_op jit(solution)/shard_map/ppermute | solution.py:33
  109.5 14.4 %collective-permute-start.17 = (bf16[1024,256]{1,0:T(8,128)(2,1)S(1)}, bf16[1024,256]{1,0:T(8,128)(2,1)S(1)}, u32[]{:S(2)}, u32[]{:S(2)}) collective-permute-start(bf16[1024,256]{1,0:T(8,128)(2,1)S(1)} %slice.28), channel_id=1, source_target_pairs={{0,2},{2,4},{4,6},{6,0},{8,10},{10,12},{12,14},{14,8},{1,3},{3,5},... | collective-permute-start | bytes 1572872 | tf_op jit(solution)/shard_map/ppermute | solution.py:25
  109.6 14.2 %collective-permute-start.18 = (bf16[1024,256]{1,0:T(8,128)(2,1)S(1)}, bf16[1024,256]{1,0:T(8,128)(2,1)S(1)}, u32[]{:S(2)}, u32[]{:S(2)}) collective-permute-start(bf16[1024,256]{1,0:T(8,128)(2,1)S(1)} %slice.29), channel_id=1, source_target_pairs={{0,6},{2,0},{4,2},{6,4},{8,14},{10,8},{12,10},{14,12},{1,7},{3,1},... | collective-permute-start | bytes 1572872 | tf_op jit(solution)/shard_map/ppermute | solution.py:25
  124.0 36.4 %copy-start.1 = (bf16[1,2,256,2048]{3,2,1,0:T(8,128)(2,1)S(1)}, bf16[1,2,256,2048]{3,2,1,0:T(8,128)(2,1)}, u32[]{:S(2)}) copy-start(bf16[1,2,256,2048]{3,2,1,0:T(8,128)(2,1)} %param.6) | copy-start | bytes 6291460
  124.1 36.4 %copy-start.3 = (bf16[1,2,64,2048]{3,2,1,0:T(8,128)(2,1)S(1)}, bf16[1,2,64,2048]{3,2,1,0:T(8,128)(2,1)}, u32[]{:S(2)}) copy-start(bf16[1,2,64,2048]{3,2,1,0:T(8,128)(2,1)} %param.7) | copy-start | bytes 1572868
  124.2 36.2 %collective-permute-start.19 = (bf16[8192,256]{1,0:T(8,128)(2,1)S(1)}, bf16[8192,256]{1,0:T(8,128)(2,1)S(1)}, u32[]{:S(2)}, u32[]{:S(2)}) collective-permute-start(bf16[8192,256]{1,0:T(8,128)(2,1)S(1)} %constant_dynamic-update-slice_fusion.refs_4_), channel_id=1, source_target_pairs={{0,1},{1,0},{2,3},{3,2},{4,5},{5,4},{6,7},{7,6},{8,9},{9,8},{10,11... | collective-permute-start | bytes 12582920 | tf_op jit(solution)/shard_map/ppermute | solution.py:33
  125.6 43.1 %collective-permute-start.27 = (bf16[256,2048]{1,0:T(8,128)(2,1)S(1)}, bf16[256,2048]{1,0:T(8,128)(2,1)S(1)}, u32[]{:S(2)}, u32[]{:S(2)}) collective-permute-start(bf16[256,2048]{1,0:T(8,128)(2,1)S(1)} %get-tuple-element.76), channel_id=1, source_target_pairs={{128,144},{144,160},{160,176},{176,192},{192,208},{208,224},{224,2... | collective-permute-start | bytes 3145736 | tf_op jit(solution)/shard_map/ppermute | solution.py:37
  129.5 13.6 %collective-permute-start.14 = (bf16[256,512]{1,0:T(8,128)(2,1)S(1)}, bf16[256,512]{1,0:T(8,128)(2,1)S(1)}, u32[]{:S(2)}, u32[]{:S(2)}) collective-permute-start(bf16[256,512]{1,0:T(8,128)(2,1)S(1)} %get-tuple-element.59), channel_id=1, source_target_pairs={{0,6},{2,0},{4,2},{6,4},{8,14},{10,8},{12,10},{14,12},{1,7},{3,1},... | collective-permute-start | bytes 786440 | tf_op jit(solution)/shard_map/ppermute | solution.py:25
  132.4 10.7 %collective-permute-start.15 = (bf16[256,512]{1,0:T(8,128)(2,1)S(1)}, bf16[256,512]{1,0:T(8,128)(2,1)S(1)}, u32[]{:S(2)}, u32[]{:S(2)}) collective-permute-start(bf16[256,512]{1,0:T(8,128)(2,1)S(1)} %get-tuple-element.60), channel_id=1, source_target_pairs={{0,4},{2,6},{4,0},{6,2},{8,12},{10,14},{12,8},{14,10},{1,5},{3,7},... | collective-permute-start | bytes 786440 | tf_op jit(solution)/shard_map/ppermute | solution.py:25
  132.4 14.7 %collective-permute-start.16 = (bf16[256,512]{1,0:T(8,128)(2,1)S(1)}, bf16[256,512]{1,0:T(8,128)(2,1)S(1)}, u32[]{:S(2)}, u32[]{:S(2)}) collective-permute-start(bf16[256,512]{1,0:T(8,128)(2,1)S(1)} %get-tuple-element.61), channel_id=1, source_target_pairs={{0,2},{2,4},{4,6},{6,0},{8,10},{10,12},{12,14},{14,8},{1,3},{3,5},... | collective-permute-start | bytes 786440 | tf_op jit(solution)/shard_map/ppermute | solution.py:25
  147.1 11.6 %collective-permute-start.22 = (bf16[64,2048]{1,0:T(8,128)(2,1)S(1)}, bf16[64,2048]{1,0:T(8,128)(2,1)S(1)}, u32[]{:S(2)}, u32[]{:S(2)}) collective-permute-start(bf16[64,2048]{1,0:T(8,128)(2,1)S(1)} %get-tuple-element.71), channel_id=1, source_target_pairs={{0,16},{16,32},{32,48},{48,64},{64,80},{80,96},{96,112},{112,128},... | collective-permute-start | bytes 786440 | tf_op jit(solution)/shard_map/ppermute | solution.py:37
  158.7 7.4 %collective-permute-start.23 = (bf16[64,2048]{1,0:T(8,128)(2,1)S(1)}, bf16[64,2048]{1,0:T(8,128)(2,1)S(1)}, u32[]{:S(2)}, u32[]{:S(2)}) collective-permute-start(bf16[64,2048]{1,0:T(8,128)(2,1)S(1)} %collective-permute-done.22.refs_6_), channel_id=1, source_target_pairs={{0,1},{1,0},{2,3},{3,2},{4,5},{5,4},{6,7},{7,6},{8,9},{9,8},{10,11... | collective-permute-start | bytes 786440 | tf_op jit(solution)/shard_map/ppermute | solution.py:33
  164.8 7.2 %collective-permute-start.25 = (bf16[64,2048]{1,0:T(8,128)(2,1)S(1)}, bf16[64,2048]{1,0:T(8,128)(2,1)S(1)}, u32[]{:S(2)}, u32[]{:S(2)}) collective-permute-start(bf16[64,2048]{1,0:T(8,128)(2,1)S(1)} %get-tuple-element.73), channel_id=1, source_target_pairs={{128,144},{144,160},{160,176},{176,192},{192,208},{208,224},{224,2... | collective-permute-start | bytes 786440 | tf_op jit(solution)/shard_map/ppermute | solution.py:37
  166.1 18.1 %collective-permute-start.24 = (bf16[256,1024]{1,0:T(8,128)(2,1)S(1)}, bf16[256,1024]{1,0:T(8,128)(2,1)S(1)}, u32[]{:S(2)}, u32[]{:S(2)}) collective-permute-start(bf16[256,1024]{1,0:T(8,128)(2,1)S(1)} %get-tuple-element.72), channel_id=1, source_target_pairs={{0,16},{16,32},{32,48},{48,64},{64,80},{80,96},{96,112},{112,128},... | collective-permute-start | bytes 1572872 | tf_op jit(solution)/shard_map/ppermute | solution.py:37
  167.4 28.1 %collective-permute-start.20 = (bf16[256,1024]{1,0:T(8,128)(2,1)S(1)}, bf16[256,1024]{1,0:T(8,128)(2,1)S(1)}, u32[]{:S(2)}, u32[]{:S(2)}) collective-permute-start(bf16[256,1024]{1,0:T(8,128)(2,1)S(1)} %get-tuple-element.67), channel_id=1, source_target_pairs={{0,16},{16,32},{32,48},{48,64},{64,80},{80,96},{96,112},{112,128},... | collective-permute-start | bytes 1572872 | tf_op jit(solution)/shard_map/ppermute | solution.py:37
  172.0 26.9 %collective-permute-start.28 = (bf16[256,2048]{1,0:T(8,128)(2,1)S(1)}, bf16[256,2048]{1,0:T(8,128)(2,1)S(1)}, u32[]{:S(2)}, u32[]{:S(2)}) collective-permute-start(bf16[256,2048]{1,0:T(8,128)(2,1)S(1)} %collective-permute-done.27.refs_4_), channel_id=1, source_target_pairs={{0,1},{1,0},{2,3},{3,2},{4,5},{5,4},{6,7},{7,6},{8,9},{9,8},{10,11... | collective-permute-start | bytes 3145736 | tf_op jit(solution)/shard_map/ppermute | solution.py:33
  195.5 3.5 %collective-permute-start.21 = (bf16[256,1024]{1,0:T(8,128)(2,1)S(1)}, bf16[256,1024]{1,0:T(8,128)(2,1)S(1)}, u32[]{:S(2)}, u32[]{:S(2)}) collective-permute-start(bf16[256,1024]{1,0:T(8,128)(2,1)S(1)} %collective-permute-done.20.refs_0_), channel_id=1, source_target_pairs={{0,1},{1,0},{2,3},{3,2},{4,5},{5,4},{6,7},{7,6},{8,9},{9,8},{10,11... | collective-permute-start | bytes 1572872 | tf_op jit(solution)/shard_map/ppermute | solution.py:33
  196.3 2.7 %collective-permute-start.26 = (bf16[256,1024]{1,0:T(8,128)(2,1)S(1)}, bf16[256,1024]{1,0:T(8,128)(2,1)S(1)}, u32[]{:S(2)}, u32[]{:S(2)}) collective-permute-start(bf16[256,1024]{1,0:T(8,128)(2,1)S(1)} %collective-permute-done.24.refs_2_), channel_id=1, source_target_pairs={{0,1},{1,0},{2,3},{3,2},{4,5},{5,4},{6,7},{7,6},{8,9},{9,8},{10,11... | collective-permute-start | bytes 1572872 | tf_op jit(solution)/shard_map/ppermute | solution.py:33
  196.3 2.7 %collective-permute-start.29 = (bf16[64,2048]{1,0:T(8,128)(2,1)S(1)}, bf16[64,2048]{1,0:T(8,128)(2,1)S(1)}, u32[]{:S(2)}, u32[]{:S(2)}) collective-permute-start(bf16[64,2048]{1,0:T(8,128)(2,1)S(1)} %collective-permute-done.25.refs_8_), channel_id=1, source_target_pairs={{0,1},{1,0},{2,3},{3,2},{4,5},{5,4},{6,7},{7,6},{8,9},{9,8},{10,11... | collective-permute-start | bytes 786440 | tf_op jit(solution)/shard_map/ppermute | solution.py:33

commit v7 on v6

--- a/solution.py
+++ b/solution.py
@@ -516,7 +516,7 @@
         where,
         both(first),
         (second, other_core(after(second, few_new))),
-        (ctx_early, other_core(after(ctx_early, few_new))),
+        (ctx_early, other_core(after(ctx_early, first, few_new))),
         qry_early,
         both(few_new),
     )

time: 202 us -> 190 us (0.941)
  waiting for transfers between devices: 101 us -> 87.1 us
    ppermute x5, waiting for transfers between devices: 36.5 us -> 23.1 us  [relay(): lax.ppermute(array, 'section', [(s, (s + 1) % count) for s in sections])]
  transfers between devices with their start and end apart: 30 -> 30, of which waited for: 13 -> 12; matrix products, arithmetic and copies ran while one was open for 0% -> 0% of each run, Pallas kernels for 11% -> 11%
where the time goes in v7:
time: 190 us; the launch traced here: 189 us
  waiting for transfers between devices  87.1 us (46%)
  starting transfers between devices  71 us (37%)
  Pallas kernels  23.7 us (12%)
  local copies, waits for them, and re-layouts  6.06 us (3%)
    ppermute x14, waiting for transfers between devices, around_x(): return lax.ppermute(array, 'dp', pairs)  61 us
    ppermute x9, starting transfers between devices, other_core(): return lax.ppermute(array, 'tensor', [(0, 1), (1, 0)])  30 us
    ppermute x5, waiting for transfers between devices, relay(): lax.ppermute(array, 'section', [(s, (s + 1) % count) for s in sections])  23.1 us
    ppermute x14, starting transfers between devices, around_x(): return lax.ppermute(array, 'dp', pairs)  20.1 us
    ppermute x2, starting transfers between devices, across_z(): lax.ppermute(array, 'dp', [(d, (d + RING) % (2 * RING)) for d in range(2...  11.8 us
    pallas_call x1, Pallas kernels, attend(): call(attend_kernel, (out,) * RING, [SMEM] + [VMEM] * 7, (VMEM,) * RING, [...  9.23 us
    ppermute x5, starting transfers between devices, relay(): lax.ppermute(array, 'section', [(s, (s + 1) % count) for s in sections])  9.12 us
    unnamed x20, local copies, waits for them, and re-layouts  5.62 us
  transfers between devices with their start and end apart: 30, of which 12 were waited for; matrix products, arithmetic and copies ran while one was open for 0% of the time, Pallas kernels for 11%

profile of v7, /device:TPU:17, one launch (start us, length us, event | category | flops | bytes accessed | tf_op | source)
XLA Modules:
  0.0 189.3 jit_solution(16341732557106101794)
XLA Ops:
  0.6 7.0 %collective-permute-start = (bf16[1024,256]{1,0:T(8,128)(2,1)}, bf16[1024,256]{1,0:T(8,128)(2,1)S(1)}, u32[]{:S(2)}, u32[]{:S(2)}) collective-permute-start(bf16[1024,256]{1,0:T(8,128)(2,1)} %bitcast.27), channel_id=1, source_target_pairs={{0,8},{2,10},{4,12},{6,14},{8,0},{10,2},{12,4},{14,6},{1,9},{3,11}... | collective-permute-start | bytes 1572872 | tf_op jit(solution)/shard_map/ppermute | solution.py:29
  7.6 0.1 stack.46.where
  7.7 1.4 copy-done.4
  9.1 0.8 shard_map.77
  9.9 1.3 collective-permute-start.1
  11.2 2.5 %collective-permute-start.2 = (bf16[3,256,256]{2,1,0:T(8,128)(2,1)S(1)}, bf16[3,256,256]{2,1,0:T(8,128)(2,1)S(1)}, u32[]{:S(2)}, u32[]{:S(2)}) collective-permute-start(bf16[3,256,256]{2,1,0:T(8,128)(2,1)S(1)} %get-tuple-element.43), channel_id=1, source_target_pairs={{0,4},{2,6},{4,0},{6,2},{8,12},{10,14},{12,8},{14,10},{1,5},{3,7},... | collective-permute-start | bytes 1179656 | tf_op jit(solution)/shard_map/ppermute | solution.py:25
  13.6 1.2 collective-permute-start.3
  14.8 1.6 copy-done
  16.4 1.0 copy-done.2
  17.4 0.7 copy-done.5
  18.1 0.7 copy-done.6
  18.8 2.0 %shard_map.78 = (bf16[256,2048]{1,0:T(8,128)(2,1)S(1)}, bf16[64,2048]{1,0:T(8,128)(2,1)S(1)}, bf16[336,2048]{1,0:T(8,128)(2,1)S(1)}) custom-call(s32[5]{0:T(128)S(1)} %stack.46.where, bf16[2,256,2048]{2,1,0:T(8,128)(2,1)S(1)} %bitcast.18, bf16[2,64,2048]{2,1,0:T(8,128)(2,1)S(1)} %bitcast.21, f32[1,2048]{1,0:T(1,128)S(1)} %copy-done.5, s32[2]{0:T(128)S(1)} %bitcast.26), custom_call_target="tpu_custom_call" | custom-call | flops 1 | bytes 1 | tf_op jit(solution)/shard_map/pallas_call | solution.py:125
  20.8 0.8 collective-permute-done
  21.6 0.1 pad_maximum_fusion.1
  21.7 8.6 %collective-permute-done.2 = bf16[3,256,256]{2,1,0:T(8,128)(2,1)S(1)} collective-permute-done((bf16[3,256,256]{2,1,0:T(8,128)(2,1)S(1)}, bf16[3,256,256]{2,1,0:T(8,128)(2,1)S(1)}, u32[]{:S(2)}, u32[]{:S(2)}) %collective-permute-start.2) | collective-permute-done | bytes 393248 | tf_op jit(solution)/shard_map/ppermute | solution.py:25
  30.2 1.7 collective-permute-start.4
  31.9 1.7 collective-permute-start.6
  33.6 0.2 pad_maximum_fusion.refs_5_
  33.8 1.8 collective-permute-start.9
  35.6 4.8 %collective-permute-start.11 = (bf16[4,3,256,256]{3,2,1,0:T(8,128)(2,1)S(1)}, bf16[4,3,256,256]{3,2,1,0:T(8,128)(2,1)S(1)}, u32[]{:S(2)}, u32[]{:S(2)}) collective-permute-start(bf16[4,3,256,256]{3,2,1,0:T(8,128)(2,1)S(1)} %pad_maximum_fusion.refs_5_), channel_id=1, source_target_pairs={{0,8},{2,10},{4,12},{6,14},{8,0},{10,2},{12,4},{14,6},{1,9},{3,11}... | collective-permute-start | bytes 4718600 | tf_op jit(solution)/shard_map/ppermute | solution.py:29
  40.4 22.2 %collective-permute-done.4.refs_1_ = bf16[336,2048]{1,0:T(8,128)(2,1)S(1)} collective-permute-done((bf16[336,2048]{1,0:T(8,128)(2,1)S(1)}, bf16[336,2048]{1,0:T(8,128)(2,1)S(1)}, u32[]{:S(2)}, u32[]{:S(2)}) %collective-permute-start.4) | collective-permute-done | bytes 1376288 | tf_op jit(solution)/shard_map/ppermute | solution.py:25
  62.6 0.1 slice.24
  62.7 0.1 collective-permute-start.5
  62.8 0.1 slice.25
  62.9 2.7 %collective-permute-start.7 = (bf16[160,2048]{1,0:T(8,128)(2,1)S(1)}, bf16[160,2048]{1,0:T(8,128)(2,1)S(1)}, u32[]{:S(2)}, u32[]{:S(2)}) collective-permute-start(bf16[160,2048]{1,0:T(8,128)(2,1)S(1)} %slice.25), channel_id=1, source_target_pairs={{0,6},{2,0},{4,2},{6,4},{8,14},{10,8},{12,10},{14,12},{1,7},{3,1},... | collective-permute-start | bytes 1966088 | tf_op jit(solution)/shard_map/ppermute | solution.py:25
  65.6 11.6 %collective-permute-done.7.refs_3_ = bf16[160,2048]{1,0:T(8,128)(2,1)S(1)} collective-permute-done((bf16[160,2048]{1,0:T(8,128)(2,1)S(1)}, bf16[160,2048]{1,0:T(8,128)(2,1)S(1)}, u32[]{:S(2)}, u32[]{:S(2)}) %collective-permute-start.7) | collective-permute-done | bytes 655392 | tf_op jit(solution)/shard_map/ppermute | solution.py:25
  77.2 2.3 %collective-permute-done.5.refs_2_ = bf16[176,2048]{1,0:T(8,128)(2,1)S(1)} collective-permute-done((bf16[176,2048]{1,0:T(8,128)(2,1)S(1)}, bf16[176,2048]{1,0:T(8,128)(2,1)S(1)}, u32[]{:S(2)}, u32[]{:S(2)}) %collective-permute-start.5) | collective-permute-done | bytes 720928 | tf_op jit(solution)/shard_map/ppermute | solution.py:25
  79.5 5.2 %shard_map.79 = (f32[3,1024,512]{2,1,0:T(8,128)S(1)}, bf16[1024,1024]{1,0:T(8,128)(2,1)S(1)}, bf16[256,1024]{1,0:T(8,128)(2,1)S(1)}, bf16[4,16,128]{2,1,0:T(8,128)(2,1)S(1)}) custom-call(s32[5]{0:T(128)S(1)} %stack.46.where, bf16[336,2048]{1,0:T(8,128)(2,1)S(1)} %get-tuple-element.47.refs_0_, bf16[336,2048]{1,0:T(8,128)(2,1)S(1)} %collective-permute-done.4.refs_1_, ...), custom_call_target="tpu_custom_call" | custom-call | flops 1 | bytes 1 | tf_op jit(solution)/shard_map/pallas_call | solution.py:280
  84.7 2.7 %collective-permute-start.10 = (bf16[2048,256]{1,0:T(8,128)(2,1)S(1)}, bf16[2048,256]{1,0:T(8,128)(2,1)S(1)}, u32[]{:S(2)}, u32[]{:S(2)}) collective-permute-start(bf16[2048,256]{1,0:T(8,128)(2,1)S(1)} %pad_maximum_fusion.1), channel_id=1, source_target_pairs={{0,6},{2,0},{4,2},{6,4},{8,14},{10,8},{12,10},{14,12},{1,7},{3,1},... | collective-permute-start | bytes 3145736 | tf_op jit(solution)/shard_map/ppermute | solution.py:25
  87.4 0.1 fusion
  87.5 21.9 %collective-permute-start.12 = (bf16[2,3,256,256]{3,2,1,0:T(8,128)(2,1)S(1)}, bf16[2,3,256,256]{3,2,1,0:T(8,128)(2,1)S(1)}, u32[]{:S(2)}, u32[]{:S(2)}) collective-permute-start(bf16[2,3,256,256]{3,2,1,0:T(8,128)(2,1)S(1)} %get-tuple-element.56), channel_id=1, source_target_pairs={{0,1},{1,0},{2,3},{3,2},{4,5},{5,4},{6,7},{7,6},{8,9},{9,8},{10,11... | collective-permute-start | bytes 2359304 | tf_op jit(solution)/shard_map/ppermute | solution.py:33
  109.4 0.1 collective-permute-start.13
  109.5 0.1 collective-permute-start.17
  109.6 2.7 %collective-permute-start.18 = (bf16[1024,256]{1,0:T(8,128)(2,1)S(1)}, bf16[1024,256]{1,0:T(8,128)(2,1)S(1)}, u32[]{:S(2)}, u32[]{:S(2)}) collective-permute-start(bf16[1024,256]{1,0:T(8,128)(2,1)S(1)} %slice.29), channel_id=1, source_target_pairs={{0,6},{2,0},{4,2},{6,4},{8,14},{10,8},{12,10},{14,12},{1,7},{3,1},... | collective-permute-start | bytes 1572872 | tf_op jit(solution)/shard_map/ppermute | solution.py:25
  112.4 0.0 collective-permute-done.13.refs_2_
  112.4 9.2 %shard_map.80 = (bf16[256,512]{1,0:T(8,128)(2,1)S(1)}, bf16[256,512]{1,0:T(8,128)(2,1)S(1)}, bf16[256,512]{1,0:T(8,128)(2,1)S(1)}, bf16[256,512]{1,0:T(8,128)(2,1)S(1)}) custom-call(s32[5]{0:T(128)S(1)} %stack.46.where, f32[3,1024,512]{2,1,0:T(8,128)S(1)} %get-tuple-element.49.total, bf16[1024,1024]{1,0:T(8,128)(2,1)S(1)} %get-tuple-element.52.rows, ...), custom_call_target="tpu_custom_call" | custom-call | flops 1 | bytes 1 | tf_op jit(solution)/shard_map/pallas_call | solution.py:304
  121.6 2.3 %collective-permute-done.17 = bf16[1024,256]{1,0:T(8,128)(2,1)S(1)} collective-permute-done((bf16[1024,256]{1,0:T(8,128)(2,1)S(1)}, bf16[1024,256]{1,0:T(8,128)(2,1)S(1)}, u32[]{:S(2)}, u32[]{:S(2)}) %collective-permute-start.17) | collective-permute-done | bytes 524320 | tf_op jit(solution)/shard_map/ppermute | solution.py:25
  123.9 0.1 constant_dynamic-update-slice_fusion.4
  124.0 0.1 constant_dynamic-update-slice_fusion.3
  124.0 0.0 copy-start.1
  124.1 0.0 copy-start.3
  124.2 0.1 constant_dynamic-update-slice_fusion.refs_4_
  124.2 1.3 collective-permute-start.19
  125.6 4.0 %collective-permute-start.27 = (bf16[256,2048]{1,0:T(8,128)(2,1)S(1)}, bf16[256,2048]{1,0:T(8,128)(2,1)S(1)}, u32[]{:S(2)}, u32[]{:S(2)}) collective-permute-start(bf16[256,2048]{1,0:T(8,128)(2,1)S(1)} %get-tuple-element.76), channel_id=1, source_target_pairs={{128,144},{144,160},{160,176},{176,192},{192,208},{208,224},{224,2... | collective-permute-start | bytes 3145736 | tf_op jit(solution)/shard_map/ppermute | solution.py:37
  129.5 2.9 %collective-permute-start.14 = (bf16[256,512]{1,0:T(8,128)(2,1)S(1)}, bf16[256,512]{1,0:T(8,128)(2,1)S(1)}, u32[]{:S(2)}, u32[]{:S(2)}) collective-permute-start(bf16[256,512]{1,0:T(8,128)(2,1)S(1)} %get-tuple-element.59), channel_id=1, source_target_pairs={{0,6},{2,0},{4,2},{6,4},{8,14},{10,8},{12,10},{14,12},{1,7},{3,1},... | collective-permute-start | bytes 786440 | tf_op jit(solution)/shard_map/ppermute | solution.py:25
  132.4 0.7 collective-permute-start.16
  133.1 10.0 %collective-permute-done.14.refs_1_ = bf16[256,512]{1,0:T(8,128)(2,1)S(1)} collective-permute-done((bf16[256,512]{1,0:T(8,128)(2,1)S(1)}, bf16[256,512]{1,0:T(8,128)(2,1)S(1)}, u32[]{:S(2)}, u32[]{:S(2)}) %collective-permute-start.14) | collective-permute-done | bytes 262176 | tf_op jit(solution)/shard_map/ppermute | solution.py:25
  143.1 4.0 %collective-permute-done.16.refs_3_ = bf16[256,512]{1,0:T(8,128)(2,1)S(1)} collective-permute-done((bf16[256,512]{1,0:T(8,128)(2,1)S(1)}, bf16[256,512]{1,0:T(8,128)(2,1)S(1)}, u32[]{:S(2)}, u32[]{:S(2)}) %collective-permute-start.16) | collective-permute-done | bytes 262176 | tf_op jit(solution)/shard_map/ppermute | solution.py:25
  147.1 1.3 collective-permute-start.22
  148.5 2.2 %shard_map.81 = (bf16[256,1024]{1,0:T(8,128)(2,1)S(1)}, bf16[64,1024]{1,0:T(8,128)(2,1)S(1)}) custom-call(s32[5]{0:T(128)S(1)} %stack.46.where, bf16[2,256,2048]{2,1,0:T(8,128)(2,1)S(1)} %bitcast.19, bf16[2,64,2048]{2,1,0:T(8,128)(2,1)S(1)} %bitcast.22, bf16[256,512]{1,0:T(8,128)(2,1)S(1)} %get-tuple-element.58.refs_0_, ...), custom_call_target="tpu_custom_call" | custom-call | flops 1 | bytes 1 | tf_op jit(solution)/shard_map/pallas_call | solution.py:388
  150.6 1.3 collective-permute-start.20
  151.9 6.8 %collective-permute-done.22.refs_6_ = bf16[64,2048]{1,0:T(8,128)(2,1)S(1)} collective-permute-done((bf16[64,2048]{1,0:T(8,128)(2,1)S(1)}, bf16[64,2048]{1,0:T(8,128)(2,1)S(1)}, u32[]{:S(2)}, u32[]{:S(2)}) %collective-permute-start.22) | collective-permute-done | bytes 262176 | tf_op jit(solution)/shard_map/ppermute | solution.py:37
  158.7 3.0 %collective-permute-start.23 = (bf16[64,2048]{1,0:T(8,128)(2,1)S(1)}, bf16[64,2048]{1,0:T(8,128)(2,1)S(1)}, u32[]{:S(2)}, u32[]{:S(2)}) collective-permute-start(bf16[64,2048]{1,0:T(8,128)(2,1)S(1)} %collective-permute-done.22.refs_6_), channel_id=1, source_target_pairs={{0,1},{1,0},{2,3},{3,2},{4,5},{5,4},{6,7},{7,6},{8,9},{9,8},{10,11... | collective-permute-start | bytes 786440 | tf_op jit(solution)/shard_map/ppermute | solution.py:33
  161.7 2.2 %shard_map.82 = (bf16[256,1024]{1,0:T(8,128)(2,1)S(1)}, bf16[64,2048]{1,0:T(8,128)(2,1)S(1)}) custom-call(s32[5]{0:T(128)S(1)} %stack.46.where, bf16[2,256,2048]{2,1,0:T(8,128)(2,1)S(1)} %bitcast.20, bf16[2,64,2048]{2,1,0:T(8,128)(2,1)S(1)} %bitcast.23, bf16[256,512]{1,0:T(8,128)(2,1)S(1)} %get-tuple-element.58.refs_0_, ...), custom_call_target="tpu_custom_call" | custom-call | flops 1 | bytes 1 | tf_op jit(solution)/shard_map/pallas_call | solution.py:388
  163.9 1.3 collective-permute-start.25
  165.2 1.3 collective-permute-start.24
  166.5 4.6 %collective-permute-done.25.refs_8_ = bf16[64,2048]{1,0:T(8,128)(2,1)S(1)} collective-permute-done((bf16[64,2048]{1,0:T(8,128)(2,1)S(1)}, bf16[64,2048]{1,0:T(8,128)(2,1)S(1)}, u32[]{:S(2)}, u32[]{:S(2)}) %collective-permute-start.25) | collective-permute-done | bytes 262176 | tf_op jit(solution)/shard_map/ppermute | solution.py:37
  171.1 0.6 collective-permute-start.28
  171.7 11.7 %collective-permute-done.24.refs_2_ = bf16[256,1024]{1,0:T(8,128)(2,1)S(1)} collective-permute-done((bf16[256,1024]{1,0:T(8,128)(2,1)S(1)}, bf16[256,1024]{1,0:T(8,128)(2,1)S(1)}, u32[]{:S(2)}, u32[]{:S(2)}) %collective-permute-start.24) | collective-permute-done | bytes 524320 | tf_op jit(solution)/shard_map/ppermute | solution.py:37
  183.4 0.8 collective-permute-start.21
  184.1 0.0 collective-permute-start.26
  184.2 0.5 collective-permute-start.29
  184.7 2.2 %collective-permute-done.29.refs_9_ = bf16[64,2048]{1,0:T(8,128)(2,1)S(1)} collective-permute-done((bf16[64,2048]{1,0:T(8,128)(2,1)S(1)}, bf16[64,2048]{1,0:T(8,128)(2,1)S(1)}, u32[]{:S(2)}, u32[]{:S(2)}) %collective-permute-start.29) | collective-permute-done | bytes 262176 | tf_op jit(solution)/shard_map/ppermute | solution.py:33
  186.8 2.3 %shard_map.83 = (bf16[2,256,2048]{2,1,0:T(8,128)(2,1)}, bf16[2,64,2048]{2,1,0:T(8,128)(2,1)}) custom-call(s32[5]{0:T(128)S(1)} %stack.46.where, bf16[256,1024]{1,0:T(8,128)(2,1)S(1)} %collective-permute-done.20.refs_0_, bf16[256,1024]{1,0:T(8,128)(2,1)S(1)} %collective-permute-done.21.refs_1_, bf16[256,1024]{1,0:T(8,128)(2,1)S(1)} %collective-permute-done.24.refs_2_, ...), custom_call_target="tpu_custom_call" | custom-call | flops 1 | bytes 1 | tf_op jit(solution)/shard_map/pallas_call | solution.py:447
  (32 shorter events, 0.2 us)
Async XLA Ops:
  0.6 21.0 %collective-permute-start = (bf16[1024,256]{1,0:T(8,128)(2,1)}, bf16[1024,256]{1,0:T(8,128)(2,1)S(1)}, u32[]{:S(2)}, u32[]{:S(2)}) collective-permute-start(bf16[1024,256]{1,0:T(8,128)(2,1)} %bitcast.27), channel_id=1, source_target_pairs={{0,8},{2,10},{4,12},{6,14},{8,0},{10,2},{12,4},{14,6},{1,9},{3,11}... | collective-permute-start | bytes 1572872 | tf_op jit(solution)/shard_map/ppermute | solution.py:29
  7.7 1.4 copy-start.4
  9.1 12.5 %copy-start.7 = (bf16[1,1024,256]{2,1,0:T(8,128)(2,1)S(1)}, bf16[1,1024,256]{2,1,0:T(8,128)(2,1)}, u32[]{:S(2)}) copy-start(bf16[1,1024,256]{2,1,0:T(8,128)(2,1)} %param.11) | copy-start | bytes 1572868
  9.9 11.8 %collective-permute-start.1 = (bf16[3,256,256]{2,1,0:T(8,128)(2,1)S(1)}, bf16[3,256,256]{2,1,0:T(8,128)(2,1)S(1)}, u32[]{:S(2)}, u32[]{:S(2)}) collective-permute-start(bf16[3,256,256]{2,1,0:T(8,128)(2,1)S(1)} %get-tuple-element.42), channel_id=1, source_target_pairs={{0,2},{2,4},{4,6},{6,0},{8,10},{10,12},{12,14},{14,8},{1,3},{3,5},... | collective-permute-start | bytes 1179656 | tf_op jit(solution)/shard_map/ppermute | solution.py:25
  11.2 19.1 %collective-permute-start.2 = (bf16[3,256,256]{2,1,0:T(8,128)(2,1)S(1)}, bf16[3,256,256]{2,1,0:T(8,128)(2,1)S(1)}, u32[]{:S(2)}, u32[]{:S(2)}) collective-permute-start(bf16[3,256,256]{2,1,0:T(8,128)(2,1)S(1)} %get-tuple-element.43), channel_id=1, source_target_pairs={{0,4},{2,6},{4,0},{6,2},{8,12},{10,14},{12,8},{14,10},{1,5},{3,7},... | collective-permute-start | bytes 1179656 | tf_op jit(solution)/shard_map/ppermute | solution.py:25
  13.6 16.6 %collective-permute-start.3 = (bf16[3,256,256]{2,1,0:T(8,128)(2,1)S(1)}, bf16[3,256,256]{2,1,0:T(8,128)(2,1)S(1)}, u32[]{:S(2)}, u32[]{:S(2)}) collective-permute-start(bf16[3,256,256]{2,1,0:T(8,128)(2,1)S(1)} %get-tuple-element.44), channel_id=1, source_target_pairs={{0,6},{2,0},{4,2},{6,4},{8,14},{10,8},{12,10},{14,12},{1,7},{3,1},... | collective-permute-start | bytes 1179656 | tf_op jit(solution)/shard_map/ppermute | solution.py:25
  14.8 1.6 copy-start
  16.4 1.0 copy-start.2
  17.4 0.7 copy-start.5
  18.1 0.7 copy-start.6
  30.2 32.4 %collective-permute-start.4 = (bf16[336,2048]{1,0:T(8,128)(2,1)S(1)}, bf16[336,2048]{1,0:T(8,128)(2,1)S(1)}, u32[]{:S(2)}, u32[]{:S(2)}) collective-permute-start(bf16[336,2048]{1,0:T(8,128)(2,1)S(1)} %get-tuple-element.47.refs_0_), channel_id=1, source_target_pairs={{0,2},{2,4},{4,6},{6,0},{8,10},{10,12},{12,14},{14,8},{1,3},{3,5},... | collective-permute-start | bytes 4128776 | tf_op jit(solution)/shard_map/ppermute | solution.py:25
  31.9 30.9 %collective-permute-start.6 = (bf16[336,2048]{1,0:T(8,128)(2,1)S(1)}, bf16[336,2048]{1,0:T(8,128)(2,1)S(1)}, u32[]{:S(2)}, u32[]{:S(2)}) collective-permute-start(bf16[336,2048]{1,0:T(8,128)(2,1)S(1)} %get-tuple-element.47.refs_0_), channel_id=1, source_target_pairs={{0,6},{2,0},{4,2},{6,4},{8,14},{10,8},{12,10},{14,12},{1,7},{3,1},... | collective-permute-start | bytes 4128776 | tf_op jit(solution)/shard_map/ppermute | solution.py:25
  33.8 45.7 %collective-permute-start.9 = (bf16[4,3,256,256]{3,2,1,0:T(8,128)(2,1)S(1)}, bf16[4,3,256,256]{3,2,1,0:T(8,128)(2,1)S(1)}, u32[]{:S(2)}, u32[]{:S(2)}) collective-permute-start(bf16[4,3,256,256]{3,2,1,0:T(8,128)(2,1)S(1)} %pad_maximum_fusion.refs_5_), channel_id=1, source_target_pairs={{0,1},{1,0},{2,3},{3,2},{4,5},{5,4},{6,7},{7,6},{8,9},{9,8},{10,11... | collective-permute-start | bytes 4718600 | tf_op jit(solution)/shard_map/ppermute | solution.py:33
  35.6 51.8 %collective-permute-start.11 = (bf16[4,3,256,256]{3,2,1,0:T(8,128)(2,1)S(1)}, bf16[4,3,256,256]{3,2,1,0:T(8,128)(2,1)S(1)}, u32[]{:S(2)}, u32[]{:S(2)}) collective-permute-start(bf16[4,3,256,256]{3,2,1,0:T(8,128)(2,1)S(1)} %pad_maximum_fusion.refs_5_), channel_id=1, source_target_pairs={{0,8},{2,10},{4,12},{6,14},{8,0},{10,2},{12,4},{14,6},{1,9},{3,11}... | collective-permute-start | bytes 4718600 | tf_op jit(solution)/shard_map/ppermute | solution.py:29
  62.7 16.8 %collective-permute-start.5 = (bf16[176,2048]{1,0:T(8,128)(2,1)S(1)}, bf16[176,2048]{1,0:T(8,128)(2,1)S(1)}, u32[]{:S(2)}, u32[]{:S(2)}) collective-permute-start(bf16[176,2048]{1,0:T(8,128)(2,1)S(1)} %slice.24), channel_id=1, source_target_pairs={{0,2},{2,4},{4,6},{6,0},{8,10},{10,12},{12,14},{14,8},{1,3},{3,5},... | collective-permute-start | bytes 2162696 | tf_op jit(solution)/shard_map/ppermute | solution.py:25
  62.9 14.4 %collective-permute-start.7 = (bf16[160,2048]{1,0:T(8,128)(2,1)S(1)}, bf16[160,2048]{1,0:T(8,128)(2,1)S(1)}, u32[]{:S(2)}, u32[]{:S(2)}) collective-permute-start(bf16[160,2048]{1,0:T(8,128)(2,1)S(1)} %slice.25), channel_id=1, source_target_pairs={{0,6},{2,0},{4,2},{6,4},{8,14},{10,8},{12,10},{14,12},{1,7},{3,1},... | collective-permute-start | bytes 1966088 | tf_op jit(solution)/shard_map/ppermute | solution.py:25
  79.5 30.0 %collective-permute-start.8 = (bf16[2048,256]{1,0:T(8,128)(2,1)S(1)}, bf16[2048,256]{1,0:T(8,128)(2,1)S(1)}, u32[]{:S(2)}, u32[]{:S(2)}) collective-permute-start(bf16[2048,256]{1,0:T(8,128)(2,1)S(1)} %pad_maximum_fusion.1), channel_id=1, source_target_pairs={{0,2},{2,4},{4,6},{6,0},{8,10},{10,12},{12,14},{14,8},{1,3},{3,5},... | collective-permute-start | bytes 3145736 | tf_op jit(solution)/shard_map/ppermute | solution.py:25
  84.7 24.9 %collective-permute-start.10 = (bf16[2048,256]{1,0:T(8,128)(2,1)S(1)}, bf16[2048,256]{1,0:T(8,128)(2,1)S(1)}, u32[]{:S(2)}, u32[]{:S(2)}) collective-permute-start(bf16[2048,256]{1,0:T(8,128)(2,1)S(1)} %pad_maximum_fusion.1), channel_id=1, source_target_pairs={{0,6},{2,0},{4,2},{6,4},{8,14},{10,8},{12,10},{14,12},{1,7},{3,1},... | collective-permute-start | bytes 3145736 | tf_op jit(solution)/shard_map/ppermute | solution.py:25
  87.5 24.9 %collective-permute-start.12 = (bf16[2,3,256,256]{3,2,1,0:T(8,128)(2,1)S(1)}, bf16[2,3,256,256]{3,2,1,0:T(8,128)(2,1)S(1)}, u32[]{:S(2)}, u32[]{:S(2)}) collective-permute-start(bf16[2,3,256,256]{3,2,1,0:T(8,128)(2,1)S(1)} %get-tuple-element.56), channel_id=1, source_target_pairs={{0,1},{1,0},{2,3},{3,2},{4,5},{5,4},{6,7},{7,6},{8,9},{9,8},{10,11... | collective-permute-start | bytes 2359304 | tf_op jit(solution)/shard_map/ppermute | solution.py:33
  109.4 3.0 %collective-permute-start.13 = (bf16[2,3,256,256]{3,2,1,0:T(8,128)(2,1)S(1)}, bf16[2,3,256,256]{3,2,1,0:T(8,128)(2,1)S(1)}, u32[]{:S(2)}, u32[]{:S(2)}) collective-permute-start(bf16[2,3,256,256]{3,2,1,0:T(8,128)(2,1)S(1)} %get-tuple-element.57), channel_id=1, source_target_pairs={{0,1},{1,0},{2,3},{3,2},{4,5},{5,4},{6,7},{7,6},{8,9},{9,8},{10,11... | collective-permute-start | bytes 2359304 | tf_op jit(solution)/shard_map/ppermute | solution.py:33
  109.5 14.4 %collective-permute-start.17 = (bf16[1024,256]{1,0:T(8,128)(2,1)S(1)}, bf16[1024,256]{1,0:T(8,128)(2,1)S(1)}, u32[]{:S(2)}, u32[]{:S(2)}) collective-permute-start(bf16[1024,256]{1,0:T(8,128)(2,1)S(1)} %slice.28), channel_id=1, source_target_pairs={{0,2},{2,4},{4,6},{6,0},{8,10},{10,12},{12,14},{14,8},{1,3},{3,5},... | collective-permute-start | bytes 1572872 | tf_op jit(solution)/shard_map/ppermute | solution.py:25
  109.6 14.2 %collective-permute-start.18 = (bf16[1024,256]{1,0:T(8,128)(2,1)S(1)}, bf16[1024,256]{1,0:T(8,128)(2,1)S(1)}, u32[]{:S(2)}, u32[]{:S(2)}) collective-permute-start(bf16[1024,256]{1,0:T(8,128)(2,1)S(1)} %slice.29), channel_id=1, source_target_pairs={{0,6},{2,0},{4,2},{6,4},{8,14},{10,8},{12,10},{14,12},{1,7},{3,1},... | collective-permute-start | bytes 1572872 | tf_op jit(solution)/shard_map/ppermute | solution.py:25
  124.0 24.4 %copy-start.1 = (bf16[1,2,256,2048]{3,2,1,0:T(8,128)(2,1)S(1)}, bf16[1,2,256,2048]{3,2,1,0:T(8,128)(2,1)}, u32[]{:S(2)}) copy-start(bf16[1,2,256,2048]{3,2,1,0:T(8,128)(2,1)} %param.6) | copy-start | bytes 6291460
  124.1 24.4 %copy-start.3 = (bf16[1,2,64,2048]{3,2,1,0:T(8,128)(2,1)S(1)}, bf16[1,2,64,2048]{3,2,1,0:T(8,128)(2,1)}, u32[]{:S(2)}) copy-start(bf16[1,2,64,2048]{3,2,1,0:T(8,128)(2,1)} %param.7) | copy-start | bytes 1572868
  124.2 24.2 %collective-permute-start.19 = (bf16[8192,256]{1,0:T(8,128)(2,1)S(1)}, bf16[8192,256]{1,0:T(8,128)(2,1)S(1)}, u32[]{:S(2)}, u32[]{:S(2)}) collective-permute-start(bf16[8192,256]{1,0:T(8,128)(2,1)S(1)} %constant_dynamic-update-slice_fusion.refs_4_), channel_id=1, source_target_pairs={{0,1},{1,0},{2,3},{3,2},{4,5},{5,4},{6,7},{7,6},{8,9},{9,8},{10,11... | collective-permute-start | bytes 12582920 | tf_op jit(solution)/shard_map/ppermute | solution.py:33
  125.6 41.0 %collective-permute-start.27 = (bf16[256,2048]{1,0:T(8,128)(2,1)S(1)}, bf16[256,2048]{1,0:T(8,128)(2,1)S(1)}, u32[]{:S(2)}, u32[]{:S(2)}) collective-permute-start(bf16[256,2048]{1,0:T(8,128)(2,1)S(1)} %get-tuple-element.76), channel_id=1, source_target_pairs={{128,144},{144,160},{160,176},{176,192},{192,208},{208,224},{224,2... | collective-permute-start | bytes 3145736 | tf_op jit(solution)/shard_map/ppermute | solution.py:37
  129.5 13.6 %collective-permute-start.14 = (bf16[256,512]{1,0:T(8,128)(2,1)S(1)}, bf16[256,512]{1,0:T(8,128)(2,1)S(1)}, u32[]{:S(2)}, u32[]{:S(2)}) collective-permute-start(bf16[256,512]{1,0:T(8,128)(2,1)S(1)} %get-tuple-element.59), channel_id=1, source_target_pairs={{0,6},{2,0},{4,2},{6,4},{8,14},{10,8},{12,10},{14,12},{1,7},{3,1},... | collective-permute-start | bytes 786440 | tf_op jit(solution)/shard_map/ppermute | solution.py:25
  132.4 10.7 %collective-permute-start.15 = (bf16[256,512]{1,0:T(8,128)(2,1)S(1)}, bf16[256,512]{1,0:T(8,128)(2,1)S(1)}, u32[]{:S(2)}, u32[]{:S(2)}) collective-permute-start(bf16[256,512]{1,0:T(8,128)(2,1)S(1)} %get-tuple-element.60), channel_id=1, source_target_pairs={{0,4},{2,6},{4,0},{6,2},{8,12},{10,14},{12,8},{14,10},{1,5},{3,7},... | collective-permute-start | bytes 786440 | tf_op jit(solution)/shard_map/ppermute | solution.py:25
  132.4 14.7 %collective-permute-start.16 = (bf16[256,512]{1,0:T(8,128)(2,1)S(1)}, bf16[256,512]{1,0:T(8,128)(2,1)S(1)}, u32[]{:S(2)}, u32[]{:S(2)}) collective-permute-start(bf16[256,512]{1,0:T(8,128)(2,1)S(1)} %get-tuple-element.61), channel_id=1, source_target_pairs={{0,2},{2,4},{4,6},{6,0},{8,10},{10,12},{12,14},{14,8},{1,3},{3,5},... | collective-permute-start | bytes 786440 | tf_op jit(solution)/shard_map/ppermute | solution.py:25
  147.1 11.6 %collective-permute-start.22 = (bf16[64,2048]{1,0:T(8,128)(2,1)S(1)}, bf16[64,2048]{1,0:T(8,128)(2,1)S(1)}, u32[]{:S(2)}, u32[]{:S(2)}) collective-permute-start(bf16[64,2048]{1,0:T(8,128)(2,1)S(1)} %get-tuple-element.71), channel_id=1, source_target_pairs={{0,16},{16,32},{32,48},{48,64},{64,80},{80,96},{96,112},{112,128},... | collective-permute-start | bytes 786440 | tf_op jit(solution)/shard_map/ppermute | solution.py:37
  150.6 20.5 %collective-permute-start.20 = (bf16[256,1024]{1,0:T(8,128)(2,1)S(1)}, bf16[256,1024]{1,0:T(8,128)(2,1)S(1)}, u32[]{:S(2)}, u32[]{:S(2)}) collective-permute-start(bf16[256,1024]{1,0:T(8,128)(2,1)S(1)} %get-tuple-element.67), channel_id=1, source_target_pairs={{0,16},{16,32},{32,48},{48,64},{64,80},{80,96},{96,112},{112,128},... | collective-permute-start | bytes 1572872 | tf_op jit(solution)/shard_map/ppermute | solution.py:37
  158.7 6.5 %collective-permute-start.23 = (bf16[64,2048]{1,0:T(8,128)(2,1)S(1)}, bf16[64,2048]{1,0:T(8,128)(2,1)S(1)}, u32[]{:S(2)}, u32[]{:S(2)}) collective-permute-start(bf16[64,2048]{1,0:T(8,128)(2,1)S(1)} %collective-permute-done.22.refs_6_), channel_id=1, source_target_pairs={{0,1},{1,0},{2,3},{3,2},{4,5},{5,4},{6,7},{7,6},{8,9},{9,8},{10,11... | collective-permute-start | bytes 786440 | tf_op jit(solution)/shard_map/ppermute | solution.py:33
  163.9 7.2 %collective-permute-start.25 = (bf16[64,2048]{1,0:T(8,128)(2,1)S(1)}, bf16[64,2048]{1,0:T(8,128)(2,1)S(1)}, u32[]{:S(2)}, u32[]{:S(2)}) collective-permute-start(bf16[64,2048]{1,0:T(8,128)(2,1)S(1)} %get-tuple-element.73), channel_id=1, source_target_pairs={{128,144},{144,160},{160,176},{176,192},{192,208},{208,224},{224,2... | collective-permute-start | bytes 786440 | tf_op jit(solution)/shard_map/ppermute | solution.py:37
  165.2 18.1 %collective-permute-start.24 = (bf16[256,1024]{1,0:T(8,128)(2,1)S(1)}, bf16[256,1024]{1,0:T(8,128)(2,1)S(1)}, u32[]{:S(2)}, u32[]{:S(2)}) collective-permute-start(bf16[256,1024]{1,0:T(8,128)(2,1)S(1)} %get-tuple-element.72), channel_id=1, source_target_pairs={{0,16},{16,32},{32,48},{48,64},{64,80},{80,96},{96,112},{112,128},... | collective-permute-start | bytes 1572872 | tf_op jit(solution)/shard_map/ppermute | solution.py:37
  171.1 15.7 %collective-permute-start.28 = (bf16[256,2048]{1,0:T(8,128)(2,1)S(1)}, bf16[256,2048]{1,0:T(8,128)(2,1)S(1)}, u32[]{:S(2)}, u32[]{:S(2)}) collective-permute-start(bf16[256,2048]{1,0:T(8,128)(2,1)S(1)} %collective-permute-done.27.refs_4_), channel_id=1, source_target_pairs={{0,1},{1,0},{2,3},{3,2},{4,5},{5,4},{6,7},{7,6},{8,9},{9,8},{10,11... | collective-permute-start | bytes 3145736 | tf_op jit(solution)/shard_map/ppermute | solution.py:33
  183.4 3.4 %collective-permute-start.21 = (bf16[256,1024]{1,0:T(8,128)(2,1)S(1)}, bf16[256,1024]{1,0:T(8,128)(2,1)S(1)}, u32[]{:S(2)}, u32[]{:S(2)}) collective-permute-start(bf16[256,1024]{1,0:T(8,128)(2,1)S(1)} %collective-permute-done.20.refs_0_), channel_id=1, source_target_pairs={{0,1},{1,0},{2,3},{3,2},{4,5},{5,4},{6,7},{7,6},{8,9},{9,8},{10,11... | collective-permute-start | bytes 1572872 | tf_op jit(solution)/shard_map/ppermute | solution.py:33
  184.1 2.7 %collective-permute-start.26 = (bf16[256,1024]{1,0:T(8,128)(2,1)S(1)}, bf16[256,1024]{1,0:T(8,128)(2,1)S(1)}, u32[]{:S(2)}, u32[]{:S(2)}) collective-permute-start(bf16[256,1024]{1,0:T(8,128)(2,1)S(1)} %collective-permute-done.24.refs_2_), channel_id=1, source_target_pairs={{0,1},{1,0},{2,3},{3,2},{4,5},{5,4},{6,7},{7,6},{8,9},{9,8},{10,11... | collective-permute-start | bytes 1572872 | tf_op jit(solution)/shard_map/ppermute | solution.py:33
  184.2 2.7 %collective-permute-start.29 = (bf16[64,2048]{1,0:T(8,128)(2,1)S(1)}, bf16[64,2048]{1,0:T(8,128)(2,1)S(1)}, u32[]{:S(2)}, u32[]{:S(2)}) collective-permute-start(bf16[64,2048]{1,0:T(8,128)(2,1)S(1)} %collective-permute-done.25.refs_8_), channel_id=1, source_target_pairs={{0,1},{1,0},{2,3},{3,2},{4,5},{5,4},{6,7},{7,6},{8,9},{9,8},{10,11... | collective-permute-start | bytes 786440 | tf_op jit(solution)/shard_map/ppermute | solution.py:33

commit v8 on v7

--- a/solution.py
+++ b/solution.py
@@ -256,7 +256,8 @@
                 )
                 scores = jnp.where(valid, scores, -1e30)
                 expo = jnp.exp(scores - jnp.max(scores, axis=-1, keepdims=True))
-                probs = (expo / jnp.sum(expo, axis=-1, keepdims=True)).astype(BF16)
+                inverse = 1.0 / jnp.sum(expo, axis=-1, keepdims=True)
+                probs = (expo * inverse).astype(BF16)
                 mixed[slot, pl.ds(0, count), at] = jnp.dot(
                     probs, low[2, keys, at], preferred_element_type=F32
                 ).astype(BF16)

time: 190 us -> 190 us (level)
  no operation moved by 1% of the time
where the time goes in v8:
time: 190 us; the launch traced here: 189 us
  waiting for transfers between devices  87.1 us (46%)
  starting transfers between devices  71 us (37%)
  Pallas kernels  23.7 us (12%)
  local copies, waits for them, and re-layouts  6.06 us (3%)
    ppermute x14, waiting for transfers between devices, around_x(): return lax.ppermute(array, 'dp', pairs)  61 us
    ppermute x9, starting transfers between devices, other_core(): return lax.ppermute(array, 'tensor', [(0, 1), (1, 0)])  30 us
    ppermute x5, waiting for transfers between devices, relay(): lax.ppermute(array, 'section', [(s, (s + 1) % count) for s in sections])  23.1 us
    ppermute x14, starting transfers between devices, around_x(): return lax.ppermute(array, 'dp', pairs)  20.1 us
    ppermute x2, starting transfers between devices, across_z(): lax.ppermute(array, 'dp', [(d, (d + RING) % (2 * RING)) for d in range(2...  11.8 us
    pallas_call x1, Pallas kernels, attend(): call(attend_kernel, (out,) * RING, [SMEM] + [VMEM] * 7, (VMEM,) * RING, [...  9.23 us
    ppermute x5, starting transfers between devices, relay(): lax.ppermute(array, 'section', [(s, (s + 1) % count) for s in sections])  9.12 us
    unnamed x20, local copies, waits for them, and re-layouts  5.62 us
  transfers between devices with their start and end apart: 30, of which 12 were waited for; matrix products, arithmetic and copies ran while one was open for 0% of the time, Pallas kernels for 11%

profile of v8, /device:TPU:17, one launch (start us, length us, event | category | flops | bytes accessed | tf_op | source)
XLA Modules:
  0.0 189.3 jit_solution(16341732557106101794)
XLA Ops:
  0.6 7.0 %collective-permute-start = (bf16[1024,256]{1,0:T(8,128)(2,1)}, bf16[1024,256]{1,0:T(8,128)(2,1)S(1)}, u32[]{:S(2)}, u32[]{:S(2)}) collective-permute-start(bf16[1024,256]{1,0:T(8,128)(2,1)} %bitcast.27), channel_id=1, source_target_pairs={{0,8},{2,10},{4,12},{6,14},{8,0},{10,2},{12,4},{14,6},{1,9},{3,11}... | collective-permute-start | bytes 1572872 | tf_op jit(solution)/shard_map/ppermute | solution.py:29
  7.6 0.1 stack.46.where
  7.7 1.4 copy-done.4
  9.1 0.8 shard_map.77
  9.9 1.3 collective-permute-start.1
  11.2 2.5 %collective-permute-start.2 = (bf16[3,256,256]{2,1,0:T(8,128)(2,1)S(1)}, bf16[3,256,256]{2,1,0:T(8,128)(2,1)S(1)}, u32[]{:S(2)}, u32[]{:S(2)}) collective-permute-start(bf16[3,256,256]{2,1,0:T(8,128)(2,1)S(1)} %get-tuple-element.43), channel_id=1, source_target_pairs={{0,4},{2,6},{4,0},{6,2},{8,12},{10,14},{12,8},{14,10},{1,5},{3,7},... | collective-permute-start | bytes 1179656 | tf_op jit(solution)/shard_map/ppermute | solution.py:25
  13.6 1.2 collective-permute-start.3
  14.8 1.6 copy-done
  16.4 1.0 copy-done.2
  17.4 0.7 copy-done.5
  18.1 0.7 copy-done.6
  18.8 2.0 %shard_map.78 = (bf16[256,2048]{1,0:T(8,128)(2,1)S(1)}, bf16[64,2048]{1,0:T(8,128)(2,1)S(1)}, bf16[336,2048]{1,0:T(8,128)(2,1)S(1)}) custom-call(s32[5]{0:T(128)S(1)} %stack.46.where, bf16[2,256,2048]{2,1,0:T(8,128)(2,1)S(1)} %bitcast.18, bf16[2,64,2048]{2,1,0:T(8,128)(2,1)S(1)} %bitcast.21, f32[1,2048]{1,0:T(1,128)S(1)} %copy-done.5, s32[2]{0:T(128)S(1)} %bitcast.26), custom_call_target="tpu_custom_call" | custom-call | flops 1 | bytes 1 | tf_op jit(solution)/shard_map/pallas_call | solution.py:125
  20.8 0.8 collective-permute-done
  21.6 0.1 pad_maximum_fusion.1
  21.7 8.6 %collective-permute-done.2 = bf16[3,256,256]{2,1,0:T(8,128)(2,1)S(1)} collective-permute-done((bf16[3,256,256]{2,1,0:T(8,128)(2,1)S(1)}, bf16[3,256,256]{2,1,0:T(8,128)(2,1)S(1)}, u32[]{:S(2)}, u32[]{:S(2)}) %collective-permute-start.2) | collective-permute-done | bytes 393248 | tf_op jit(solution)/shard_map/ppermute | solution.py:25
  30.2 1.7 collective-permute-start.4
  31.9 1.7 collective-permute-start.6
  33.6 0.2 pad_maximum_fusion.refs_5_
  33.8 1.8 collective-permute-start.9
  35.6 4.8 %collective-permute-start.11 = (bf16[4,3,256,256]{3,2,1,0:T(8,128)(2,1)S(1)}, bf16[4,3,256,256]{3,2,1,0:T(8,128)(2,1)S(1)}, u32[]{:S(2)}, u32[]{:S(2)}) collective-permute-start(bf16[4,3,256,256]{3,2,1,0:T(8,128)(2,1)S(1)} %pad_maximum_fusion.refs_5_), channel_id=1, source_target_pairs={{0,8},{2,10},{4,12},{6,14},{8,0},{10,2},{12,4},{14,6},{1,9},{3,11}... | collective-permute-start | bytes 4718600 | tf_op jit(solution)/shard_map/ppermute | solution.py:29
  40.4 22.2 %collective-permute-done.4.refs_1_ = bf16[336,2048]{1,0:T(8,128)(2,1)S(1)} collective-permute-done((bf16[336,2048]{1,0:T(8,128)(2,1)S(1)}, bf16[336,2048]{1,0:T(8,128)(2,1)S(1)}, u32[]{:S(2)}, u32[]{:S(2)}) %collective-permute-start.4) | collective-permute-done | bytes 1376288 | tf_op jit(solution)/shard_map/ppermute | solution.py:25
  62.6 0.1 slice.24
  62.7 0.1 collective-permute-start.5
  62.8 0.1 slice.25
  62.9 2.7 %collective-permute-start.7 = (bf16[160,2048]{1,0:T(8,128)(2,1)S(1)}, bf16[160,2048]{1,0:T(8,128)(2,1)S(1)}, u32[]{:S(2)}, u32[]{:S(2)}) collective-permute-start(bf16[160,2048]{1,0:T(8,128)(2,1)S(1)} %slice.25), channel_id=1, source_target_pairs={{0,6},{2,0},{4,2},{6,4},{8,14},{10,8},{12,10},{14,12},{1,7},{3,1},... | collective-permute-start | bytes 1966088 | tf_op jit(solution)/shard_map/ppermute | solution.py:25
  65.6 11.6 %collective-permute-done.7.refs_3_ = bf16[160,2048]{1,0:T(8,128)(2,1)S(1)} collective-permute-done((bf16[160,2048]{1,0:T(8,128)(2,1)S(1)}, bf16[160,2048]{1,0:T(8,128)(2,1)S(1)}, u32[]{:S(2)}, u32[]{:S(2)}) %collective-permute-start.7) | collective-permute-done | bytes 655392 | tf_op jit(solution)/shard_map/ppermute | solution.py:25
  77.2 2.3 %collective-permute-done.5.refs_2_ = bf16[176,2048]{1,0:T(8,128)(2,1)S(1)} collective-permute-done((bf16[176,2048]{1,0:T(8,128)(2,1)S(1)}, bf16[176,2048]{1,0:T(8,128)(2,1)S(1)}, u32[]{:S(2)}, u32[]{:S(2)}) %collective-permute-start.5) | collective-permute-done | bytes 720928 | tf_op jit(solution)/shard_map/ppermute | solution.py:25
  79.5 5.2 %shard_map.79 = (f32[3,1024,512]{2,1,0:T(8,128)S(1)}, bf16[1024,1024]{1,0:T(8,128)(2,1)S(1)}, bf16[256,1024]{1,0:T(8,128)(2,1)S(1)}, bf16[4,16,128]{2,1,0:T(8,128)(2,1)S(1)}) custom-call(s32[5]{0:T(128)S(1)} %stack.46.where, bf16[336,2048]{1,0:T(8,128)(2,1)S(1)} %get-tuple-element.47.refs_0_, bf16[336,2048]{1,0:T(8,128)(2,1)S(1)} %collective-permute-done.4.refs_1_, ...), custom_call_target="tpu_custom_call" | custom-call | flops 1 | bytes 1 | tf_op jit(solution)/shard_map/pallas_call | solution.py:281
  84.7 2.7 %collective-permute-start.10 = (bf16[2048,256]{1,0:T(8,128)(2,1)S(1)}, bf16[2048,256]{1,0:T(8,128)(2,1)S(1)}, u32[]{:S(2)}, u32[]{:S(2)}) collective-permute-start(bf16[2048,256]{1,0:T(8,128)(2,1)S(1)} %pad_maximum_fusion.1), channel_id=1, source_target_pairs={{0,6},{2,0},{4,2},{6,4},{8,14},{10,8},{12,10},{14,12},{1,7},{3,1},... | collective-permute-start | bytes 3145736 | tf_op jit(solution)/shard_map/ppermute | solution.py:25
  87.4 0.1 fusion
  87.5 21.9 %collective-permute-start.12 = (bf16[2,3,256,256]{3,2,1,0:T(8,128)(2,1)S(1)}, bf16[2,3,256,256]{3,2,1,0:T(8,128)(2,1)S(1)}, u32[]{:S(2)}, u32[]{:S(2)}) collective-permute-start(bf16[2,3,256,256]{3,2,1,0:T(8,128)(2,1)S(1)} %get-tuple-element.56), channel_id=1, source_target_pairs={{0,1},{1,0},{2,3},{3,2},{4,5},{5,4},{6,7},{7,6},{8,9},{9,8},{10,11... | collective-permute-start | bytes 2359304 | tf_op jit(solution)/shard_map/ppermute | solution.py:33
  109.4 0.1 collective-permute-start.13
  109.5 0.1 collective-permute-start.17
  109.6 2.7 %collective-permute-start.18 = (bf16[1024,256]{1,0:T(8,128)(2,1)S(1)}, bf16[1024,256]{1,0:T(8,128)(2,1)S(1)}, u32[]{:S(2)}, u32[]{:S(2)}) collective-permute-start(bf16[1024,256]{1,0:T(8,128)(2,1)S(1)} %slice.29), channel_id=1, source_target_pairs={{0,6},{2,0},{4,2},{6,4},{8,14},{10,8},{12,10},{14,12},{1,7},{3,1},... | collective-permute-start | bytes 1572872 | tf_op jit(solution)/shard_map/ppermute | solution.py:25
  112.4 0.0 collective-permute-done.13.refs_2_
  112.4 9.2 %shard_map.80 = (bf16[256,512]{1,0:T(8,128)(2,1)S(1)}, bf16[256,512]{1,0:T(8,128)(2,1)S(1)}, bf16[256,512]{1,0:T(8,128)(2,1)S(1)}, bf16[256,512]{1,0:T(8,128)(2,1)S(1)}) custom-call(s32[5]{0:T(128)S(1)} %stack.46.where, f32[3,1024,512]{2,1,0:T(8,128)S(1)} %get-tuple-element.49.total, bf16[1024,1024]{1,0:T(8,128)(2,1)S(1)} %get-tuple-element.52.rows, ...), custom_call_target="tpu_custom_call" | custom-call | flops 1 | bytes 1 | tf_op jit(solution)/shard_map/pallas_call | solution.py:305
  121.6 2.3 %collective-permute-done.17 = bf16[1024,256]{1,0:T(8,128)(2,1)S(1)} collective-permute-done((bf16[1024,256]{1,0:T(8,128)(2,1)S(1)}, bf16[1024,256]{1,0:T(8,128)(2,1)S(1)}, u32[]{:S(2)}, u32[]{:S(2)}) %collective-permute-start.17) | collective-permute-done | bytes 524320 | tf_op jit(solution)/shard_map/ppermute | solution.py:25
  123.9 0.1 constant_dynamic-update-slice_fusion.4
  124.0 0.1 constant_dynamic-update-slice_fusion.3
  124.0 0.0 copy-start.1
  124.1 0.0 copy-start.3
  124.2 0.1 constant_dynamic-update-slice_fusion.refs_4_
  124.2 1.3 collective-permute-start.19
  125.6 4.0 %collective-permute-start.27 = (bf16[256,2048]{1,0:T(8,128)(2,1)S(1)}, bf16[256,2048]{1,0:T(8,128)(2,1)S(1)}, u32[]{:S(2)}, u32[]{:S(2)}) collective-permute-start(bf16[256,2048]{1,0:T(8,128)(2,1)S(1)} %get-tuple-element.76), channel_id=1, source_target_pairs={{128,144},{144,160},{160,176},{176,192},{192,208},{208,224},{224,2... | collective-permute-start | bytes 3145736 | tf_op jit(solution)/shard_map/ppermute | solution.py:37
  129.5 2.9 %collective-permute-start.14 = (bf16[256,512]{1,0:T(8,128)(2,1)S(1)}, bf16[256,512]{1,0:T(8,128)(2,1)S(1)}, u32[]{:S(2)}, u32[]{:S(2)}) collective-permute-start(bf16[256,512]{1,0:T(8,128)(2,1)S(1)} %get-tuple-element.59), channel_id=1, source_target_pairs={{0,6},{2,0},{4,2},{6,4},{8,14},{10,8},{12,10},{14,12},{1,7},{3,1},... | collective-permute-start | bytes 786440 | tf_op jit(solution)/shard_map/ppermute | solution.py:25
  132.4 0.7 collective-permute-start.16
  133.1 10.0 %collective-permute-done.14.refs_1_ = bf16[256,512]{1,0:T(8,128)(2,1)S(1)} collective-permute-done((bf16[256,512]{1,0:T(8,128)(2,1)S(1)}, bf16[256,512]{1,0:T(8,128)(2,1)S(1)}, u32[]{:S(2)}, u32[]{:S(2)}) %collective-permute-start.14) | collective-permute-done | bytes 262176 | tf_op jit(solution)/shard_map/ppermute | solution.py:25
  143.1 4.0 %collective-permute-done.16.refs_3_ = bf16[256,512]{1,0:T(8,128)(2,1)S(1)} collective-permute-done((bf16[256,512]{1,0:T(8,128)(2,1)S(1)}, bf16[256,512]{1,0:T(8,128)(2,1)S(1)}, u32[]{:S(2)}, u32[]{:S(2)}) %collective-permute-start.16) | collective-permute-done | bytes 262176 | tf_op jit(solution)/shard_map/ppermute | solution.py:25
  147.1 1.3 collective-permute-start.22
  148.5 2.2 %shard_map.81 = (bf16[256,1024]{1,0:T(8,128)(2,1)S(1)}, bf16[64,1024]{1,0:T(8,128)(2,1)S(1)}) custom-call(s32[5]{0:T(128)S(1)} %stack.46.where, bf16[2,256,2048]{2,1,0:T(8,128)(2,1)S(1)} %bitcast.19, bf16[2,64,2048]{2,1,0:T(8,128)(2,1)S(1)} %bitcast.22, bf16[256,512]{1,0:T(8,128)(2,1)S(1)} %get-tuple-element.58.refs_0_, ...), custom_call_target="tpu_custom_call" | custom-call | flops 1 | bytes 1 | tf_op jit(solution)/shard_map/pallas_call | solution.py:389
  150.6 1.3 collective-permute-start.20
  151.9 6.8 %collective-permute-done.22.refs_6_ = bf16[64,2048]{1,0:T(8,128)(2,1)S(1)} collective-permute-done((bf16[64,2048]{1,0:T(8,128)(2,1)S(1)}, bf16[64,2048]{1,0:T(8,128)(2,1)S(1)}, u32[]{:S(2)}, u32[]{:S(2)}) %collective-permute-start.22) | collective-permute-done | bytes 262176 | tf_op jit(solution)/shard_map/ppermute | solution.py:37
  158.7 3.0 %collective-permute-start.23 = (bf16[64,2048]{1,0:T(8,128)(2,1)S(1)}, bf16[64,2048]{1,0:T(8,128)(2,1)S(1)}, u32[]{:S(2)}, u32[]{:S(2)}) collective-permute-start(bf16[64,2048]{1,0:T(8,128)(2,1)S(1)} %collective-permute-done.22.refs_6_), channel_id=1, source_target_pairs={{0,1},{1,0},{2,3},{3,2},{4,5},{5,4},{6,7},{7,6},{8,9},{9,8},{10,11... | collective-permute-start | bytes 786440 | tf_op jit(solution)/shard_map/ppermute | solution.py:33
  161.7 2.2 %shard_map.82 = (bf16[256,1024]{1,0:T(8,128)(2,1)S(1)}, bf16[64,2048]{1,0:T(8,128)(2,1)S(1)}) custom-call(s32[5]{0:T(128)S(1)} %stack.46.where, bf16[2,256,2048]{2,1,0:T(8,128)(2,1)S(1)} %bitcast.20, bf16[2,64,2048]{2,1,0:T(8,128)(2,1)S(1)} %bitcast.23, bf16[256,512]{1,0:T(8,128)(2,1)S(1)} %get-tuple-element.58.refs_0_, ...), custom_call_target="tpu_custom_call" | custom-call | flops 1 | bytes 1 | tf_op jit(solution)/shard_map/pallas_call | solution.py:389
  163.9 1.3 collective-permute-start.25
  165.2 1.3 collective-permute-start.24
  166.5 4.6 %collective-permute-done.25.refs_8_ = bf16[64,2048]{1,0:T(8,128)(2,1)S(1)} collective-permute-done((bf16[64,2048]{1,0:T(8,128)(2,1)S(1)}, bf16[64,2048]{1,0:T(8,128)(2,1)S(1)}, u32[]{:S(2)}, u32[]{:S(2)}) %collective-permute-start.25) | collective-permute-done | bytes 262176 | tf_op jit(solution)/shard_map/ppermute | solution.py:37
  171.1 0.6 collective-permute-start.28
  171.7 11.7 %collective-permute-done.24.refs_2_ = bf16[256,1024]{1,0:T(8,128)(2,1)S(1)} collective-permute-done((bf16[256,1024]{1,0:T(8,128)(2,1)S(1)}, bf16[256,1024]{1,0:T(8,128)(2,1)S(1)}, u32[]{:S(2)}, u32[]{:S(2)}) %collective-permute-start.24) | collective-permute-done | bytes 524320 | tf_op jit(solution)/shard_map/ppermute | solution.py:37
  183.4 0.8 collective-permute-start.21
  184.1 0.0 collective-permute-start.26
  184.2 0.5 collective-permute-start.29
  184.7 2.2 %collective-permute-done.29.refs_9_ = bf16[64,2048]{1,0:T(8,128)(2,1)S(1)} collective-permute-done((bf16[64,2048]{1,0:T(8,128)(2,1)S(1)}, bf16[64,2048]{1,0:T(8,128)(2,1)S(1)}, u32[]{:S(2)}, u32[]{:S(2)}) %collective-permute-start.29) | collective-permute-done | bytes 262176 | tf_op jit(solution)/shard_map/ppermute | solution.py:33
  186.8 2.3 %shard_map.83 = (bf16[2,256,2048]{2,1,0:T(8,128)(2,1)}, bf16[2,64,2048]{2,1,0:T(8,128)(2,1)}) custom-call(s32[5]{0:T(128)S(1)} %stack.46.where, bf16[256,1024]{1,0:T(8,128)(2,1)S(1)} %collective-permute-done.20.refs_0_, bf16[256,1024]{1,0:T(8,128)(2,1)S(1)} %collective-permute-done.21.refs_1_, bf16[256,1024]{1,0:T(8,128)(2,1)S(1)} %collective-permute-done.24.refs_2_, ...), custom_call_target="tpu_custom_call" | custom-call | flops 1 | bytes 1 | tf_op jit(solution)/shard_map/pallas_call | solution.py:448
  (32 shorter events, 0.2 us)
Async XLA Ops:
  0.6 21.0 %collective-permute-start = (bf16[1024,256]{1,0:T(8,128)(2,1)}, bf16[1024,256]{1,0:T(8,128)(2,1)S(1)}, u32[]{:S(2)}, u32[]{:S(2)}) collective-permute-start(bf16[1024,256]{1,0:T(8,128)(2,1)} %bitcast.27), channel_id=1, source_target_pairs={{0,8},{2,10},{4,12},{6,14},{8,0},{10,2},{12,4},{14,6},{1,9},{3,11}... | collective-permute-start | bytes 1572872 | tf_op jit(solution)/shard_map/ppermute | solution.py:29
  7.7 1.4 copy-start.4
  9.1 12.5 %copy-start.7 = (bf16[1,1024,256]{2,1,0:T(8,128)(2,1)S(1)}, bf16[1,1024,256]{2,1,0:T(8,128)(2,1)}, u32[]{:S(2)}) copy-start(bf16[1,1024,256]{2,1,0:T(8,128)(2,1)} %param.11) | copy-start | bytes 1572868
  9.9 11.8 %collective-permute-start.1 = (bf16[3,256,256]{2,1,0:T(8,128)(2,1)S(1)}, bf16[3,256,256]{2,1,0:T(8,128)(2,1)S(1)}, u32[]{:S(2)}, u32[]{:S(2)}) collective-permute-start(bf16[3,256,256]{2,1,0:T(8,128)(2,1)S(1)} %get-tuple-element.42), channel_id=1, source_target_pairs={{0,2},{2,4},{4,6},{6,0},{8,10},{10,12},{12,14},{14,8},{1,3},{3,5},... | collective-permute-start | bytes 1179656 | tf_op jit(solution)/shard_map/ppermute | solution.py:25
  11.2 19.1 %collective-permute-start.2 = (bf16[3,256,256]{2,1,0:T(8,128)(2,1)S(1)}, bf16[3,256,256]{2,1,0:T(8,128)(2,1)S(1)}, u32[]{:S(2)}, u32[]{:S(2)}) collective-permute-start(bf16[3,256,256]{2,1,0:T(8,128)(2,1)S(1)} %get-tuple-element.43), channel_id=1, source_target_pairs={{0,4},{2,6},{4,0},{6,2},{8,12},{10,14},{12,8},{14,10},{1,5},{3,7},... | collective-permute-start | bytes 1179656 | tf_op jit(solution)/shard_map/ppermute | solution.py:25
  13.6 16.6 %collective-permute-start.3 = (bf16[3,256,256]{2,1,0:T(8,128)(2,1)S(1)}, bf16[3,256,256]{2,1,0:T(8,128)(2,1)S(1)}, u32[]{:S(2)}, u32[]{:S(2)}) collective-permute-start(bf16[3,256,256]{2,1,0:T(8,128)(2,1)S(1)} %get-tuple-element.44), channel_id=1, source_target_pairs={{0,6},{2,0},{4,2},{6,4},{8,14},{10,8},{12,10},{14,12},{1,7},{3,1},... | collective-permute-start | bytes 1179656 | tf_op jit(solution)/shard_map/ppermute | solution.py:25
  14.8 1.6 copy-start
  16.4 1.0 copy-start.2
  17.4 0.7 copy-start.5
  18.1 0.7 copy-start.6
  30.2 32.4 %collective-permute-start.4 = (bf16[336,2048]{1,0:T(8,128)(2,1)S(1)}, bf16[336,2048]{1,0:T(8,128)(2,1)S(1)}, u32[]{:S(2)}, u32[]{:S(2)}) collective-permute-start(bf16[336,2048]{1,0:T(8,128)(2,1)S(1)} %get-tuple-element.47.refs_0_), channel_id=1, source_target_pairs={{0,2},{2,4},{4,6},{6,0},{8,10},{10,12},{12,14},{14,8},{1,3},{3,5},... | collective-permute-start | bytes 4128776 | tf_op jit(solution)/shard_map/ppermute | solution.py:25
  31.9 30.9 %collective-permute-start.6 = (bf16[336,2048]{1,0:T(8,128)(2,1)S(1)}, bf16[336,2048]{1,0:T(8,128)(2,1)S(1)}, u32[]{:S(2)}, u32[]{:S(2)}) collective-permute-start(bf16[336,2048]{1,0:T(8,128)(2,1)S(1)} %get-tuple-element.47.refs_0_), channel_id=1, source_target_pairs={{0,6},{2,0},{4,2},{6,4},{8,14},{10,8},{12,10},{14,12},{1,7},{3,1},... | collective-permute-start | bytes 4128776 | tf_op jit(solution)/shard_map/ppermute | solution.py:25
  33.8 45.7 %collective-permute-start.9 = (bf16[4,3,256,256]{3,2,1,0:T(8,128)(2,1)S(1)}, bf16[4,3,256,256]{3,2,1,0:T(8,128)(2,1)S(1)}, u32[]{:S(2)}, u32[]{:S(2)}) collective-permute-start(bf16[4,3,256,256]{3,2,1,0:T(8,128)(2,1)S(1)} %pad_maximum_fusion.refs_5_), channel_id=1, source_target_pairs={{0,1},{1,0},{2,3},{3,2},{4,5},{5,4},{6,7},{7,6},{8,9},{9,8},{10,11... | collective-permute-start | bytes 4718600 | tf_op jit(solution)/shard_map/ppermute | solution.py:33
  35.6 51.8 %collective-permute-start.11 = (bf16[4,3,256,256]{3,2,1,0:T(8,128)(2,1)S(1)}, bf16[4,3,256,256]{3,2,1,0:T(8,128)(2,1)S(1)}, u32[]{:S(2)}, u32[]{:S(2)}) collective-permute-start(bf16[4,3,256,256]{3,2,1,0:T(8,128)(2,1)S(1)} %pad_maximum_fusion.refs_5_), channel_id=1, source_target_pairs={{0,8},{2,10},{4,12},{6,14},{8,0},{10,2},{12,4},{14,6},{1,9},{3,11}... | collective-permute-start | bytes 4718600 | tf_op jit(solution)/shard_map/ppermute | solution.py:29
  62.7 16.8 %collective-permute-start.5 = (bf16[176,2048]{1,0:T(8,128)(2,1)S(1)}, bf16[176,2048]{1,0:T(8,128)(2,1)S(1)}, u32[]{:S(2)}, u32[]{:S(2)}) collective-permute-start(bf16[176,2048]{1,0:T(8,128)(2,1)S(1)} %slice.24), channel_id=1, source_target_pairs={{0,2},{2,4},{4,6},{6,0},{8,10},{10,12},{12,14},{14,8},{1,3},{3,5},... | collective-permute-start | bytes 2162696 | tf_op jit(solution)/shard_map/ppermute | solution.py:25
  62.9 14.4 %collective-permute-start.7 = (bf16[160,2048]{1,0:T(8,128)(2,1)S(1)}, bf16[160,2048]{1,0:T(8,128)(2,1)S(1)}, u32[]{:S(2)}, u32[]{:S(2)}) collective-permute-start(bf16[160,2048]{1,0:T(8,128)(2,1)S(1)} %slice.25), channel_id=1, source_target_pairs={{0,6},{2,0},{4,2},{6,4},{8,14},{10,8},{12,10},{14,12},{1,7},{3,1},... | collective-permute-start | bytes 1966088 | tf_op jit(solution)/shard_map/ppermute | solution.py:25
  79.5 30.0 %collective-permute-start.8 = (bf16[2048,256]{1,0:T(8,128)(2,1)S(1)}, bf16[2048,256]{1,0:T(8,128)(2,1)S(1)}, u32[]{:S(2)}, u32[]{:S(2)}) collective-permute-start(bf16[2048,256]{1,0:T(8,128)(2,1)S(1)} %pad_maximum_fusion.1), channel_id=1, source_target_pairs={{0,2},{2,4},{4,6},{6,0},{8,10},{10,12},{12,14},{14,8},{1,3},{3,5},... | collective-permute-start | bytes 3145736 | tf_op jit(solution)/shard_map/ppermute | solution.py:25
  84.7 24.9 %collective-permute-start.10 = (bf16[2048,256]{1,0:T(8,128)(2,1)S(1)}, bf16[2048,256]{1,0:T(8,128)(2,1)S(1)}, u32[]{:S(2)}, u32[]{:S(2)}) collective-permute-start(bf16[2048,256]{1,0:T(8,128)(2,1)S(1)} %pad_maximum_fusion.1), channel_id=1, source_target_pairs={{0,6},{2,0},{4,2},{6,4},{8,14},{10,8},{12,10},{14,12},{1,7},{3,1},... | collective-permute-start | bytes 3145736 | tf_op jit(solution)/shard_map/ppermute | solution.py:25
  87.5 24.9 %collective-permute-start.12 = (bf16[2,3,256,256]{3,2,1,0:T(8,128)(2,1)S(1)}, bf16[2,3,256,256]{3,2,1,0:T(8,128)(2,1)S(1)}, u32[]{:S(2)}, u32[]{:S(2)}) collective-permute-start(bf16[2,3,256,256]{3,2,1,0:T(8,128)(2,1)S(1)} %get-tuple-element.56), channel_id=1, source_target_pairs={{0,1},{1,0},{2,3},{3,2},{4,5},{5,4},{6,7},{7,6},{8,9},{9,8},{10,11... | collective-permute-start | bytes 2359304 | tf_op jit(solution)/shard_map/ppermute | solution.py:33
  109.4 3.0 %collective-permute-start.13 = (bf16[2,3,256,256]{3,2,1,0:T(8,128)(2,1)S(1)}, bf16[2,3,256,256]{3,2,1,0:T(8,128)(2,1)S(1)}, u32[]{:S(2)}, u32[]{:S(2)}) collective-permute-start(bf16[2,3,256,256]{3,2,1,0:T(8,128)(2,1)S(1)} %get-tuple-element.57), channel_id=1, source_target_pairs={{0,1},{1,0},{2,3},{3,2},{4,5},{5,4},{6,7},{7,6},{8,9},{9,8},{10,11... | collective-permute-start | bytes 2359304 | tf_op jit(solution)/shard_map/ppermute | solution.py:33
  109.5 14.4 %collective-permute-start.17 = (bf16[1024,256]{1,0:T(8,128)(2,1)S(1)}, bf16[1024,256]{1,0:T(8,128)(2,1)S(1)}, u32[]{:S(2)}, u32[]{:S(2)}) collective-permute-start(bf16[1024,256]{1,0:T(8,128)(2,1)S(1)} %slice.28), channel_id=1, source_target_pairs={{0,2},{2,4},{4,6},{6,0},{8,10},{10,12},{12,14},{14,8},{1,3},{3,5},... | collective-permute-start | bytes 1572872 | tf_op jit(solution)/shard_map/ppermute | solution.py:25
  109.6 14.2 %collective-permute-start.18 = (bf16[1024,256]{1,0:T(8,128)(2,1)S(1)}, bf16[1024,256]{1,0:T(8,128)(2,1)S(1)}, u32[]{:S(2)}, u32[]{:S(2)}) collective-permute-start(bf16[1024,256]{1,0:T(8,128)(2,1)S(1)} %slice.29), channel_id=1, source_target_pairs={{0,6},{2,0},{4,2},{6,4},{8,14},{10,8},{12,10},{14,12},{1,7},{3,1},... | collective-permute-start | bytes 1572872 | tf_op jit(solution)/shard_map/ppermute | solution.py:25
  124.0 24.4 %copy-start.1 = (bf16[1,2,256,2048]{3,2,1,0:T(8,128)(2,1)S(1)}, bf16[1,2,256,2048]{3,2,1,0:T(8,128)(2,1)}, u32[]{:S(2)}) copy-start(bf16[1,2,256,2048]{3,2,1,0:T(8,128)(2,1)} %param.6) | copy-start | bytes 6291460
  124.1 24.4 %copy-start.3 = (bf16[1,2,64,2048]{3,2,1,0:T(8,128)(2,1)S(1)}, bf16[1,2,64,2048]{3,2,1,0:T(8,128)(2,1)}, u32[]{:S(2)}) copy-start(bf16[1,2,64,2048]{3,2,1,0:T(8,128)(2,1)} %param.7) | copy-start | bytes 1572868
  124.2 24.2 %collective-permute-start.19 = (bf16[8192,256]{1,0:T(8,128)(2,1)S(1)}, bf16[8192,256]{1,0:T(8,128)(2,1)S(1)}, u32[]{:S(2)}, u32[]{:S(2)}) collective-permute-start(bf16[8192,256]{1,0:T(8,128)(2,1)S(1)} %constant_dynamic-update-slice_fusion.refs_4_), channel_id=1, source_target_pairs={{0,1},{1,0},{2,3},{3,2},{4,5},{5,4},{6,7},{7,6},{8,9},{9,8},{10,11... | collective-permute-start | bytes 12582920 | tf_op jit(solution)/shard_map/ppermute | solution.py:33
  125.6 41.0 %collective-permute-start.27 = (bf16[256,2048]{1,0:T(8,128)(2,1)S(1)}, bf16[256,2048]{1,0:T(8,128)(2,1)S(1)}, u32[]{:S(2)}, u32[]{:S(2)}) collective-permute-start(bf16[256,2048]{1,0:T(8,128)(2,1)S(1)} %get-tuple-element.76), channel_id=1, source_target_pairs={{128,144},{144,160},{160,176},{176,192},{192,208},{208,224},{224,2... | collective-permute-start | bytes 3145736 | tf_op jit(solution)/shard_map/ppermute | solution.py:37
  129.5 13.6 %collective-permute-start.14 = (bf16[256,512]{1,0:T(8,128)(2,1)S(1)}, bf16[256,512]{1,0:T(8,128)(2,1)S(1)}, u32[]{:S(2)}, u32[]{:S(2)}) collective-permute-start(bf16[256,512]{1,0:T(8,128)(2,1)S(1)} %get-tuple-element.59), channel_id=1, source_target_pairs={{0,6},{2,0},{4,2},{6,4},{8,14},{10,8},{12,10},{14,12},{1,7},{3,1},... | collective-permute-start | bytes 786440 | tf_op jit(solution)/shard_map/ppermute | solution.py:25
  132.4 10.7 %collective-permute-start.15 = (bf16[256,512]{1,0:T(8,128)(2,1)S(1)}, bf16[256,512]{1,0:T(8,128)(2,1)S(1)}, u32[]{:S(2)}, u32[]{:S(2)}) collective-permute-start(bf16[256,512]{1,0:T(8,128)(2,1)S(1)} %get-tuple-element.60), channel_id=1, source_target_pairs={{0,4},{2,6},{4,0},{6,2},{8,12},{10,14},{12,8},{14,10},{1,5},{3,7},... | collective-permute-start | bytes 786440 | tf_op jit(solution)/shard_map/ppermute | solution.py:25
  132.4 14.7 %collective-permute-start.16 = (bf16[256,512]{1,0:T(8,128)(2,1)S(1)}, bf16[256,512]{1,0:T(8,128)(2,1)S(1)}, u32[]{:S(2)}, u32[]{:S(2)}) collective-permute-start(bf16[256,512]{1,0:T(8,128)(2,1)S(1)} %get-tuple-element.61), channel_id=1, source_target_pairs={{0,2},{2,4},{4,6},{6,0},{8,10},{10,12},{12,14},{14,8},{1,3},{3,5},... | collective-permute-start | bytes 786440 | tf_op jit(solution)/shard_map/ppermute | solution.py:25
  147.1 11.6 %collective-permute-start.22 = (bf16[64,2048]{1,0:T(8,128)(2,1)S(1)}, bf16[64,2048]{1,0:T(8,128)(2,1)S(1)}, u32[]{:S(2)}, u32[]{:S(2)}) collective-permute-start(bf16[64,2048]{1,0:T(8,128)(2,1)S(1)} %get-tuple-element.71), channel_id=1, source_target_pairs={{0,16},{16,32},{32,48},{48,64},{64,80},{80,96},{96,112},{112,128},... | collective-permute-start | bytes 786440 | tf_op jit(solution)/shard_map/ppermute | solution.py:37
  150.6 20.5 %collective-permute-start.20 = (bf16[256,1024]{1,0:T(8,128)(2,1)S(1)}, bf16[256,1024]{1,0:T(8,128)(2,1)S(1)}, u32[]{:S(2)}, u32[]{:S(2)}) collective-permute-start(bf16[256,1024]{1,0:T(8,128)(2,1)S(1)} %get-tuple-element.67), channel_id=1, source_target_pairs={{0,16},{16,32},{32,48},{48,64},{64,80},{80,96},{96,112},{112,128},... | collective-permute-start | bytes 1572872 | tf_op jit(solution)/shard_map/ppermute | solution.py:37
  158.7 6.5 %collective-permute-start.23 = (bf16[64,2048]{1,0:T(8,128)(2,1)S(1)}, bf16[64,2048]{1,0:T(8,128)(2,1)S(1)}, u32[]{:S(2)}, u32[]{:S(2)}) collective-permute-start(bf16[64,2048]{1,0:T(8,128)(2,1)S(1)} %collective-permute-done.22.refs_6_), channel_id=1, source_target_pairs={{0,1},{1,0},{2,3},{3,2},{4,5},{5,4},{6,7},{7,6},{8,9},{9,8},{10,11... | collective-permute-start | bytes 786440 | tf_op jit(solution)/shard_map/ppermute | solution.py:33
  163.9 7.2 %collective-permute-start.25 = (bf16[64,2048]{1,0:T(8,128)(2,1)S(1)}, bf16[64,2048]{1,0:T(8,128)(2,1)S(1)}, u32[]{:S(2)}, u32[]{:S(2)}) collective-permute-start(bf16[64,2048]{1,0:T(8,128)(2,1)S(1)} %get-tuple-element.73), channel_id=1, source_target_pairs={{128,144},{144,160},{160,176},{176,192},{192,208},{208,224},{224,2... | collective-permute-start | bytes 786440 | tf_op jit(solution)/shard_map/ppermute | solution.py:37
  165.2 18.1 %collective-permute-start.24 = (bf16[256,1024]{1,0:T(8,128)(2,1)S(1)}, bf16[256,1024]{1,0:T(8,128)(2,1)S(1)}, u32[]{:S(2)}, u32[]{:S(2)}) collective-permute-start(bf16[256,1024]{1,0:T(8,128)(2,1)S(1)} %get-tuple-element.72), channel_id=1, source_target_pairs={{0,16},{16,32},{32,48},{48,64},{64,80},{80,96},{96,112},{112,128},... | collective-permute-start | bytes 1572872 | tf_op jit(solution)/shard_map/ppermute | solution.py:37
  171.1 15.7 %collective-permute-start.28 = (bf16[256,2048]{1,0:T(8,128)(2,1)S(1)}, bf16[256,2048]{1,0:T(8,128)(2,1)S(1)}, u32[]{:S(2)}, u32[]{:S(2)}) collective-permute-start(bf16[256,2048]{1,0:T(8,128)(2,1)S(1)} %collective-permute-done.27.refs_4_), channel_id=1, source_target_pairs={{0,1},{1,0},{2,3},{3,2},{4,5},{5,4},{6,7},{7,6},{8,9},{9,8},{10,11... | collective-permute-start | bytes 3145736 | tf_op jit(solution)/shard_map/ppermute | solution.py:33
  183.4 3.4 %collective-permute-start.21 = (bf16[256,1024]{1,0:T(8,128)(2,1)S(1)}, bf16[256,1024]{1,0:T(8,128)(2,1)S(1)}, u32[]{:S(2)}, u32[]{:S(2)}) collective-permute-start(bf16[256,1024]{1,0:T(8,128)(2,1)S(1)} %collective-permute-done.20.refs_0_), channel_id=1, source_target_pairs={{0,1},{1,0},{2,3},{3,2},{4,5},{5,4},{6,7},{7,6},{8,9},{9,8},{10,11... | collective-permute-start | bytes 1572872 | tf_op jit(solution)/shard_map/ppermute | solution.py:33
  184.1 2.7 %collective-permute-start.26 = (bf16[256,1024]{1,0:T(8,128)(2,1)S(1)}, bf16[256,1024]{1,0:T(8,128)(2,1)S(1)}, u32[]{:S(2)}, u32[]{:S(2)}) collective-permute-start(bf16[256,1024]{1,0:T(8,128)(2,1)S(1)} %collective-permute-done.24.refs_2_), channel_id=1, source_target_pairs={{0,1},{1,0},{2,3},{3,2},{4,5},{5,4},{6,7},{7,6},{8,9},{9,8},{10,11... | collective-permute-start | bytes 1572872 | tf_op jit(solution)/shard_map/ppermute | solution.py:33
  184.2 2.7 %collective-permute-start.29 = (bf16[64,2048]{1,0:T(8,128)(2,1)S(1)}, bf16[64,2048]{1,0:T(8,128)(2,1)S(1)}, u32[]{:S(2)}, u32[]{:S(2)}) collective-permute-start(bf16[64,2048]{1,0:T(8,128)(2,1)S(1)} %collective-permute-done.25.refs_8_), channel_id=1, source_target_pairs={{0,1},{1,0},{2,3},{3,2},{4,5},{5,4},{6,7},{7,6},{8,9},{9,8},{10,11... | collective-permute-start | bytes 786440 | tf_op jit(solution)/shard_map/ppermute | solution.py:33
